TPU v7x, 128 devices: a whole 4x4x4 slice. The times are simulated.
128 devices in a mesh: gen: 32 (over z, y, core), ref: 4 (over x).
Axes of the slice: x: 4, y: 4, z: 4, core: 2. Of those that a mesh axis runs over, the one named last changes fastest.
Arguments:
- gen_features: bfloat16 [16384, 2048], P('gen'), may hold values from 0 to 40
- gen_weight: float32 [16384], P('gen'), may hold values from 0.5 to 18
- ref_features: bfloat16 [16384, 2048], P('ref'), may hold values from 0 to 40
- ref_weight: float32 [16384], P('ref'), may hold values from 0.5 to 18
- ref_self: float32 [16384], P('ref'), may hold values from 0 to 2
Outputs:
- gen_gap: float32 [16384], P('gen')
- ref_gap: float32 [16384], P('ref')
- divergence: float32 [], replicated
All inputs are finite; a program needn't handle non-finite values.
Results may differ from a plain program's by a relative error of at most 0.0003.
Values may be sent and summed in bfloat16 or wider, within the bound.
No kernel may reach another device: no remote copies, remote signals or barrier semaphores. Data moves between devices by JAX's collectives and lax.ppermute only.
A program may use at most 128 MiB of HBM per device.

v0:
```python
import jax
import jax.numpy as jnp
from jax import lax
from jax.sharding import PartitionSpec as P

ITERS = 2


blur_scale = 0.1


def half_norms(features, feature_width):
    values = features.astype(jnp.float32)
    return 0.5 * jnp.sum(values * values, axis=1) / feature_width


def pair_cost(left_rows, left_half, right_rows, right_half, feature_width):
    inner_dots = lax.dot_general(
        left_rows, right_rows, (((1,), (1,)), ((), ())), preferred_element_type=jnp.float32
    )
    return left_half[:, None] + right_half[None, :] - inner_dots / feature_width


def local_sum(scores, local_peak, reduce_axis):
    return jnp.sum(jnp.exp(scores - jnp.expand_dims(local_peak, reduce_axis)), axis=reduce_axis)


def per_device(gen_features, gen_weight, ref_features, ref_weight, ref_self):
    gen_count, feature_width = gen_features.shape
    ref_parts = lax.axis_size("ref")
    ref_place = lax.axis_index("ref")
    gen_place = lax.axis_index("gen")
    quarter = gen_count // ref_parts
    gen_local = jnp.sum(gen_weight)
    ref_local = jnp.sum(ref_weight)
    gen_mass = lax.psum(gen_local, "gen")
    ref_mass = lax.psum(ref_local, "ref")
    gen_share = gen_weight / gen_mass
    ref_share = ref_weight / ref_mass
    gen_log = jnp.log(gen_weight) - jnp.log(gen_mass)
    ref_log = jnp.log(ref_weight) - jnp.log(ref_mass)
    gen_half = half_norms(gen_features, feature_width)
    ref_half = half_norms(ref_features, feature_width)
    cross_cost = pair_cost(gen_features, gen_half, ref_features, ref_half, feature_width)
    own_rows = lax.dynamic_slice_in_dim(gen_features, ref_place * quarter, quarter, 0)
    piece_rows = lax.all_gather(own_rows, "gen", axis=0, tiled=True)
    self_cost = pair_cost(
        gen_features, gen_half, piece_rows, half_norms(piece_rows, feature_width), feature_width
    )
    self_axis = 1
    cross_gen = jnp.zeros((gen_count,), jnp.float32)
    cross_ref = jnp.zeros((ref_features.shape[0],), jnp.float32)
    self_gen = jnp.zeros((gen_count,), jnp.float32)
    for pass_index in range(ITERS + 1):
        ref_terms = ref_log + cross_ref / blur_scale
        gen_terms = gen_log + cross_gen / blur_scale
        self_terms = gen_log + self_gen / blur_scale
        own_terms = lax.dynamic_slice_in_dim(self_terms, ref_place * quarter, quarter, 0)
        column_terms = lax.all_gather(own_terms, "gen", axis=0, tiled=True)
        self_scores = column_terms[None, :] - self_cost / blur_scale
        row_scores = ref_terms[None, :] - cross_cost / blur_scale
        column_scores = gen_terms[:, None] - cross_cost / blur_scale
        row_top, self_top = lax.pmax(
            (jnp.max(row_scores, axis=1), jnp.max(self_scores, axis=self_axis)), "ref"
        )
        column_top = lax.pmax(jnp.max(column_scores, axis=0), "gen")
        row_sum, self_sum = lax.psum(
            (local_sum(row_scores, row_top, 1), local_sum(self_scores, self_top, self_axis)), "ref"
        )
        column_sum = lax.psum(local_sum(column_scores, column_top, 0), "gen")
        new_gen = -blur_scale * (row_top + jnp.log(row_sum))
        new_self = -blur_scale * (self_top + jnp.log(self_sum))
        new_ref = -blur_scale * (column_top + jnp.log(column_sum))
        if pass_index == 0:
            cross_gen, cross_ref, self_gen = (new_gen, new_ref, new_self)
        else:
            cross_gen = 0.5 * (cross_gen + new_gen)
            cross_ref = 0.5 * (cross_ref + new_ref)
            self_gen = 0.5 * (self_gen + new_self)
    gen_gap = cross_gen - self_gen
    ref_gap = cross_ref - ref_self
    gen_part = jnp.sum(gen_share * gen_gap)
    ref_part = jnp.sum(ref_share * ref_gap)
    divergence = lax.psum(
        jnp.where(ref_place == 0, gen_part, 0.0) + jnp.where(gen_place == 0, ref_part, 0.0),
        ("gen", "ref"),
    )
    return (gen_gap, ref_gap, divergence)


def solution(mesh):
    placed = (P("gen", None), P("gen"), P("ref", None), P("ref"), P("ref"))
    return jax.shard_map(
        per_device, mesh=mesh, in_specs=placed, out_specs=(P("gen"), P("ref"), P()), check_vma=False
    )
```

profile of v0, /device:TPU:1, one launch (start us, length us, event | category | flops | bytes accessed | tf_op | source)
XLA Modules:
  0.0 874.9 jit_solution(8693917594896283207)
XLA Ops:
  7.2 0.0 all-gather.5.cloned.1.call-start
  7.2 1.9 constant_dynamic-slice_fusion
  9.1 0.0 all-gather.5.cloned.1.call-update
  9.1 1.3 reduce_sum.148
  10.4 67.3 %psum.86 = f32[]{:T(128)} all-reduce(f32[]{:T(128)} %reduce_sum.148), channel_id=1, replica_groups=mesh['gen'=32,'ref'=4] {'gen'}, use_global_device_ids=true, to_apply=%region_9.0 | all-reduce | flops 1 | bytes 8 | tf_op jit(solution)/shard_map/psum | solution.py:36
  78.4 1.3 reduce_sum.144
  79.7 0.7 log_subtract_fusion.1
  80.4 0.1 dynamic-slice_bitcast_fusion.2
  80.5 22.6 %all-gather = f32[32,1,128]{2,1,0:T(1,128)S(1)} all-gather(f32[1,1,128]{2,1,0:T(1,128)S(1)} %dynamic-slice_bitcast_fusion.2), channel_id=1, replica_groups=mesh['gen'=32,'ref'=4] {'gen'}, dimensions={0}, use_global_device_ids=true | all-gather | bytes 16896 | tf_op jit(solution)/shard_map/all_gather | solution.py:59
  103.1 2.1 multiply_reduce_fusion.2
  105.2 0.0 copy-start.1
  105.2 7.3 multiply_reduce_fusion.1
  112.5 0.0 all-gather.5.cloned.1.call-done
  112.5 0.0 copy-start
  112.6 7.5 multiply_reduce_fusion
  120.1 0.0 copy-done.1
  120.1 3.1 copy-done
  123.2 11.7 %subtract_reduce_fusion.3 = (f32[512]{0:T(512)S(1)}, f32[512,4096]{1,0:T(8,128)}) fusion(f32[4096]{0:T(1024)S(1)} %bitcast.21, bf16[4096,2048]{1,0:T(8,128)(2,1)S(1)} %copy-done, bf16[512,2048]{1,0:T(8,128)(2,1)S(1)} %copy-done.1, f32[4096]{0:T(1024)S(1)} %broadcast_multiply_fusion, f32[512]{0:T(512)S(1)} %broadcast_multiply_fusion.2), kind=kOutput, calls=%fused_computation.17 | convolution fusion | flops 8602517504 | bytes 27299840 | tf_op jit(solution)/shard_map/dot_general | solution.py:18
  134.9 0.0 copy-start.2
  134.9 8.6 pmax.68
  143.5 4.9 exponential_reduce_fusion.3
  148.3 6.6 all-reduce.4
  155.7 0.0 copy-done.2
  155.7 15.3 %subtract_reduce_fusion.8 = (f32[512]{0:T(512)S(1)}, f32[4096]{0:T(1024)S(1)}, f32[512,4096]{1,0:T(8,128)}) fusion(f32[4096]{0:T(1024)S(1)} %log_subtract_fusion, f32[512]{0:T(512)S(1)} %log_subtract_fusion.1, bf16[512,2048]{1,0:T(8,128)(2,1)S(1)} %copy-done.1, bf16[4096,2048]{1,0:T(8,128)(2,1)} %param.7, f32[4096]{0:T(1024)S(1)} %broadcast_multiply_fusion.1, ...), kind=kOutput, calls=%fused_computation.22 | convolution fusion | flops 8606707712 | bytes 27318272 | tf_op jit(solution)/shard_map/dot_general | solution.py:18
  171.0 122.4 %pmax.64 = f32[4096]{0:T(1024)S(1)} all-reduce(f32[4096]{0:T(1024)S(1)} %get-tuple-element.10), channel_id=1, replica_groups=mesh['gen'=32,'ref'=4] {'gen'}, use_global_device_ids=true, to_apply=%region_11.0 | all-reduce | flops 4096 | bytes 32768 | tf_op jit(solution)/shard_map/pmax | solution.py:66
  293.4 8.0 pmax.63
  301.3 0.0 copy-start.3
  301.3 7.0 exponential_reduce_fusion.8
  308.4 125.5 %psum.87 = f32[4096]{0:T(1024)S(1)} all-reduce(f32[4096]{0:T(1024)S(1)} %get-tuple-element.8), channel_id=1, replica_groups=mesh['gen'=32,'ref'=4] {'gen'}, use_global_device_ids=true, to_apply=%region_13.0 | all-reduce | flops 4096 | bytes 32768 | tf_op jit(solution)/shard_map/psum | solution.py:70
  433.9 4.0 subtract_reduce_fusion.6
  437.9 0.0 copy-done.3
  437.9 0.1 dynamic-slice_bitcast_fusion.1
  438.0 22.9 %all-gather.1 = f32[32,1,128]{2,1,0:T(1,128)S(1)} all-gather(f32[1,1,128]{2,1,0:T(1,128)S(1)} %dynamic-slice_bitcast_fusion.1), channel_id=1, replica_groups=mesh['gen'=32,'ref'=4] {'gen'}, dimensions={0}, use_global_device_ids=true | all-gather | bytes 16896 | tf_op jit(solution)/shard_map/all_gather | solution.py:59
  460.9 4.0 subtract_reduce_fusion.2
  464.9 6.1 all-reduce.6
  471.0 7.4 exponential_reduce_fusion.2
  478.4 7.8 all-reduce.3
  486.2 0.0 copy-start.4
  486.2 4.4 subtract_reduce_fusion
  490.6 122.2 %all-reduce.1 = (f32[4096]{0:T(1024)S(1)}, f32[4096]{0:T(1024)S(1)}) all-reduce(f32[4096]{0:T(1024)S(1)} %get-tuple-element.6, f32[4096]{0:T(1024)S(1)} %get-tuple-element.5), channel_id=1, replica_groups=mesh['gen'=32,'ref'=4] {'gen'}, use_global_device_ids=true, to_apply=%region_19.0 | all-reduce | flops 8192 | bytes 65536 | tf_op jit(solution)/shard_map/pmax | solution.py:66
  612.8 5.3 exponential_reduce_fusion
  618.1 123.8 %all-reduce = (f32[4096]{0:T(1024)S(1)}, f32[4096]{0:T(1024)S(1)}) all-reduce(f32[4096]{0:T(1024)S(1)} %get-tuple-element.4, f32[4096]{0:T(1024)S(1)} %get-tuple-element.3), channel_id=1, replica_groups=mesh['gen'=32,'ref'=4] {'gen'}, use_global_device_ids=true, to_apply=%region_21.0 | all-reduce | flops 8192 | bytes 65536 | tf_op jit(solution)/shard_map/psum | solution.py:70
  741.9 0.0 copy-done.4
  741.9 1.9 multiply_reduce_fusion.3
  743.7 4.0 subtract_reduce_fusion.4
  747.7 0.1 dynamic-slice_bitcast_fusion
  747.8 22.9 %all-gather.2 = f32[32,1,128]{2,1,0:T(1,128)S(1)} all-gather(f32[1,1,128]{2,1,0:T(1,128)S(1)} %dynamic-slice_bitcast_fusion), channel_id=1, replica_groups=mesh['gen'=32,'ref'=4] {'gen'}, dimensions={0}, use_global_device_ids=true | all-gather | bytes 16896 | tf_op jit(solution)/shard_map/all_gather | solution.py:59
  770.7 4.0 subtract_reduce_fusion.1
  774.7 6.3 all-reduce.5
  781.1 4.9 exponential_reduce_fusion.4
  786.0 4.9 exponential_reduce_fusion.1
  790.8 7.4 all-reduce.2
  798.2 1.9 fusion.6
  801.4 66.7 %psum.95 = f32[]{:T(128)} all-reduce(f32[]{:T(128)S(6)} %add.147), channel_id=1, replica_groups=mesh['gen'=32,'ref'=4] {'gen','ref'}, use_global_device_ids=true, to_apply=%region_45.46 | all-reduce | flops 1 | bytes 8 | tf_op jit(solution)/shard_map/psum | solution.py:84
  (8 shorter events, 0.1 us)
Async XLA Ops:
  7.2 105.4 %all-gather.5.cloned.1.call-start = ((), (), s32[]{:S(2)}) async-start(), calls=%async_computation | async-start | bytes 17301504 | tf_op jit(solution)/shard_map/all_gather | solution.py:46
  105.2 14.9 %copy-start.1 = (bf16[512,2048]{1,0:T(8,128)(2,1)S(1)}, bf16[512,2048]{1,0:T(8,128)(2,1)}, u32[]{:S(2)}) copy-start(bf16[512,2048]{1,0:T(8,128)(2,1)} %param.5) | copy-start | bytes 6291460
  112.5 10.7 %copy-start = (bf16[4096,2048]{1,0:T(8,128)(2,1)S(1)}, bf16[4096,2048]{1,0:T(8,128)(2,1)}, u32[]{:S(2)}) copy-start(bf16[4096,2048]{1,0:T(8,128)(2,1)} %all-gather.5.cloned.1.call-done) | copy-start | bytes 50331652
  134.9 20.8 %copy-start.2 = (f32[4096]{0:T(1024)S(1)}, f32[4096]{0:T(1024)}, u32[]{:S(2)}) copy-start(f32[4096]{0:T(1024)} %param.8) | copy-start | bytes 49156
  301.3 136.6 %copy-start.3 = (f32[512]{0:T(512)S(1)}, f32[512]{0:T(512)}, u32[]{:S(2)}) copy-start(f32[512]{0:T(512)} %param.6) | copy-start | bytes 6148
  486.2 255.7 %copy-start.4 = (f32[4096]{0:T(1024)S(1)}, f32[4096]{0:T(1024)}, u32[]{:S(2)}) copy-start(f32[4096]{0:T(1024)} %param.9) | copy-start | bytes 49156
Sparse Core Ops, SparseCore 0:
  10.2 76.6 all-gather.4
where the time goes:
time: 876 us; the launch traced here: 875 us
  blocking collectives  747 us (85%)
  other arithmetic  78.9 us (9%)
  matrix products  26.9 us (3%)
  between operations  16.8 us (2%)
    psum x2, blocking collectives, per_device(): column_sum = lax.psum(local_sum(column_scores, column_top, 0), 'gen')  249 us
    pmax x2, blocking collectives, per_device(): column_top = lax.pmax(jnp.max(column_scores, axis=0), 'gen')  245 us
    all_gather x3, blocking collectives, per_device(): column_terms = lax.all_gather(own_terms, 'gen', axis=0, tiled=True)  68.4 us
    psum x1, blocking collectives, per_device(): gen_mass = lax.psum(gen_local, 'gen')  67.3 us
    psum x1, blocking collectives, per_device(): lax.psum(jnp.where(ref_place == 0, gen_part, 0.0) + jnp.where(gen_place =...  66.7 us
    reduce_sum x6, other arithmetic, local_sum(): jnp.sum(jnp.exp(scores - jnp.expand_dims(local_peak, reduce_axis)), axis=...  34.3 us
    pmax x4, blocking collectives, per_device(): lax.pmax((jnp.max(row_scores, axis=1), jnp.max(self_scores, axis=self_axi...  29 us
    dot_general x2, matrix products, pair_cost(): lax.dot_general(left_rows, right_rows, (((1,), (1,)), ((), ())), preferre...  26.9 us
  transfers between devices with their start and end apart: 1, of which 0 were waited for; matrix products, arithmetic and copies ran while one was open for 1% of the time, Pallas kernels for 0%

commit v1 on v0

v1 whole, which is shorter than its diff:
```python
import functools

import jax
import jax.numpy as jnp
from jax import lax
from jax.experimental import pallas as pl
from jax.experimental.pallas import tpu as pltpu
from jax.sharding import PartitionSpec as P


EPS = 0.1
LOG2E = 1.4426950408889634
F32 = jnp.float32
LANES = 128
TILE = 512
ROWS = 32
LOW = 2.0**-80
HIGH = 2.0**120


def vmem_array(x):
    return pltpu.with_memory_space_constraint(x, pltpu.VMEM)


def hbm_array(x):
    return pltpu.with_memory_space_constraint(x, pltpu.HBM)


def spread(vec_ref, out_ref, count, first=0, at=0):
    for q in range(count):
        block = jnp.broadcast_to(vec_ref[first + q : first + q + 1, :], (LANES, LANES))
        out_ref[(at + q) * LANES : (at + q + 1) * LANES, :] = block.T


def lane_fold(acc, op):
    return op(acc.T, axis=0, keepdims=True)


def norms(feat_ref, start, count, scale):
    width = feat_ref.shape[1]
    out = []
    for q in range(count):
        acc = jnp.zeros((LANES, LANES), F32)
        for c in range(width // LANES):
            x = feat_ref[start + q * LANES : start + (q + 1) * LANES, c * LANES : (c + 1) * LANES].astype(F32)
            acc = acc + x * x
        out.append(lane_fold(acc, jnp.sum) * scale)
    return out


def sweep(d_ref, base, chunks, u, vs_ref, rowacc_ref):
    rows = d_ref.shape[0]

    def body(r, cols):
        at = pl.ds(pl.multiple_of(r * ROWS, ROWS), ROWS)
        vs = vs_ref[at, :]
        racc = rowacc_ref[at, :]
        out = []
        for c in range(chunks):
            p = jnp.exp2((d_ref[at, pl.ds(base + c * LANES, LANES)] + u[c]) + vs)
            racc = racc + p
            out.append(cols[c] + jnp.sum(p.reshape(ROWS // 8, 8, LANES), axis=0))
        rowacc_ref[at, :] = racc
        return tuple(out)

    zero = jnp.zeros((8, LANES), F32)
    cols = lax.fori_loop(0, rows // ROWS, body, (zero,) * chunks, unroll=2)
    return [jnp.sum(c, axis=0, keepdims=True) for c in cols]


def tile_peak(d_ref, u, vs_ref):
    rows = d_ref.shape[0]
    best = jnp.full((8, LANES), -3.0e38, F32)

    def body(r, best):
        at = pl.ds(pl.multiple_of(r * ROWS, ROWS), ROWS)
        val = (d_ref[at, 0:LANES] + u) + vs_ref[at, :]
        return jnp.maximum(best, jnp.max(val.reshape(ROWS // 8, 8, LANES), axis=0))

    best = lax.fori_loop(0, rows // ROWS, body, best, unroll=2)
    return jnp.max(jnp.max(best, axis=0, keepdims=True), axis=1, keepdims=True)


def start_peak(d_ref, u0, v_ref, vs_ref, peak_ref, rowacc_ref):
    rows = d_ref.shape[0]
    spread(v_ref, vs_ref, rows // LANES)
    peak = jnp.broadcast_to(tile_peak(d_ref, u0, vs_ref), (8, LANES))
    peak_ref[...] = peak
    vs_ref[...] = vs_ref[...] - peak[0:1, :]
    rowacc_ref[...] = jnp.zeros_like(rowacc_ref)


def finish(d_refs, u_ref, v_ref, vs_ref, rowacc_ref, colsum_ref, peak_ref, lrow_ref, lcol_ref):
    rows = d_refs[0].shape[0]
    nq = rows // LANES
    rowsum = [lane_fold(rowacc_ref[q * LANES : (q + 1) * LANES, :], jnp.sum) for q in range(nq)]
    rowsum = jnp.concatenate(rowsum, axis=0)
    colsum = colsum_ref[...]
    low = jnp.minimum(jnp.min(rowsum), jnp.min(colsum))
    high = jnp.maximum(jnp.max(rowsum), jnp.max(colsum))
    good = jnp.logical_and(low >= LOW, high <= HIGH)
    peak = peak_ref[0:1, :]

    @pl.when(good)
    def _():
        lrow_ref[0:nq, :] = (jnp.log2(rowsum) + peak) - v_ref[...]
        lcol_ref[...] = (jnp.log2(colsum) + peak) - u_ref[...]

    @pl.when(jnp.logical_not(good))
    def _():
        spread(v_ref, vs_ref, nq)

        def row_block(q, carry):
            part = pl.ds(pl.multiple_of(q * LANES, LANES), LANES)

            def scores(d_ref, first, c):
                at = pl.ds(pl.multiple_of(c * LANES, LANES), LANES)
                return d_ref[part, at] + u_ref[pl.ds(first + c, 1), :]

            best = jnp.full((LANES, LANES), -3.0e38, F32)
            first = 0
            for d_ref in d_refs:
                count = d_ref.shape[1] // LANES
                best = lax.fori_loop(
                    0, count, lambda c, best: jnp.maximum(best, scores(d_ref, first, c)), best
                )
                first += count
            top = jnp.max(best, axis=1, keepdims=True)
            acc = jnp.zeros((LANES, LANES), F32)
            first = 0
            for d_ref in d_refs:
                count = d_ref.shape[1] // LANES
                acc = lax.fori_loop(
                    0, count, lambda c, acc: acc + jnp.exp2(scores(d_ref, first, c) - top), acc
                )
                first += count
            log_sum = jnp.log2(jnp.sum(acc, axis=1, keepdims=True)) + top
            lrow_ref[pl.ds(q, 1), :] = lane_fold(jnp.broadcast_to(log_sum, (LANES, LANES)), jnp.max)
            return carry

        lax.fori_loop(0, nq, row_block, 0)
        first = 0
        for d_ref in d_refs:
            count = d_ref.shape[1] // LANES

            def column(c, carry):
                at = pl.ds(pl.multiple_of(c * LANES, LANES), LANES)

                def block(r):
                    part = pl.ds(pl.multiple_of(r * ROWS, ROWS), ROWS)
                    return d_ref[part, at] + vs_ref[part, :]

                top = lax.fori_loop(
                    0,
                    rows // ROWS,
                    lambda r, best: jnp.maximum(best, jnp.max(block(r), axis=0, keepdims=True)),
                    jnp.full((1, LANES), -3.0e38, F32),
                )
                total = lax.fori_loop(
                    0,
                    rows // ROWS,
                    lambda r, acc: acc + jnp.sum(jnp.exp2(block(r) - top), axis=0, keepdims=True),
                    jnp.zeros((1, LANES), F32),
                )
                lcol_ref[pl.ds(first + c, 1), :] = top + jnp.log2(total)
                return carry

            lax.fori_loop(0, count, column, 0)
            first += count


def first_kernel(
    offset, gen_ref, ref_hbm, gweight_ref, rweight_ref, d_ref, lrow_ref, lcol_ref, hrow_ref, hcol_ref, mass_ref,
    tile_ref, u_ref, v_ref, vs_ref, rowacc_ref, colsum_ref, peak_ref, sem,
):
    rows, width = gen_ref.shape
    nq, nc = rows // LANES, d_ref.shape[1] // LANES
    chunks = TILE // LANES
    steps = d_ref.shape[1] // TILE
    half_scale = 0.5 * LOG2E / (EPS * width)
    dot_scale = LOG2E / (EPS * width)

    def load(j, slot):
        at = pl.ds(pl.multiple_of((offset * steps + j) * TILE, TILE), TILE)
        return pltpu.make_async_copy(ref_hbm.at[at, :], tile_ref.at[slot], sem.at[slot])

    load(0, 0).start()
    for q, part in enumerate(norms(gen_ref, 0, nq, half_scale)):
        hrow_ref[q : q + 1, :] = part
        v_ref[q : q + 1, :] = jnp.log2(gweight_ref[q : q + 1, :]) - part
        hrow_ref[nq + q : nq + q + 1, :] = gweight_ref[q : q + 1, :]
    lrow_ref[nq : 2 * nq, :] = jnp.broadcast_to(jnp.sum(rweight_ref[...]).reshape(1, 1), (nq, LANES))
    mass_ref[...] = jnp.broadcast_to(jnp.sum(gweight_ref[...]).reshape(1, 1), (8, LANES))

    def step(j, carry):
        slot = lax.rem(j, 2)

        @pl.when(j + 1 < steps)
        def _():
            load(j + 1, 1 - slot).start()

        load(j, slot).wait()
        tile = tile_ref.at[slot]
        half = norms(tile, 0, chunks, half_scale)
        u = []
        for c in range(chunks):
            row = pl.ds(j * chunks + c, 1)
            hcol_ref[row, :] = half[c]
            u.append(jnp.log2(rweight_ref[pl.ds(offset * nc + j * chunks + c, 1), :]) - half[c])
            u_ref[row, :] = u[c]
        base = pl.multiple_of(j * TILE, TILE)
        dots = lax.dot_general(
            gen_ref[...], tile[...], (((1,), (1,)), ((), ())), preferred_element_type=F32
        )
        d_ref[:, pl.ds(base, TILE)] = dots * dot_scale

        @pl.when(j == 0)
        def _():
            start_peak(d_ref, u[0], v_ref, vs_ref, peak_ref, rowacc_ref)

        for c, part in enumerate(sweep(d_ref, base, chunks, u, vs_ref, rowacc_ref)):
            colsum_ref[pl.ds(j * chunks + c, 1), :] = part
        return carry

    lax.fori_loop(0, steps, step, 0)
    finish([d_ref], u_ref, v_ref, vs_ref, rowacc_ref, colsum_ref, peak_ref, lrow_ref, lcol_ref)


def first_pass(gen, ref, gweight, rweight, piece, pieces):
    rows, width = gen.shape
    cols = ref.shape[0] // pieces
    nq, nc = rows // LANES, cols // LANES
    vmem = pl.BlockSpec(memory_space=pltpu.VMEM)
    vec = lambda n: jax.ShapeDtypeStruct((n, LANES), F32)
    return pl.pallas_call(
        functools.partial(first_kernel, piece),
        in_specs=[vmem, pl.BlockSpec(memory_space=pltpu.HBM), vmem, vmem],
        out_shape=(pltpu.VMEM((rows, cols), F32), vec(2 * nq), vec(nc), vec(2 * nq), vec(nc), vec(8)),
        out_specs=(vmem,) * 6,
        scratch_shapes=[
            pltpu.VMEM((2, TILE, width), jnp.bfloat16),
            pltpu.VMEM((nc, LANES), F32),
            pltpu.VMEM((nq, LANES), F32),
            pltpu.VMEM((rows, LANES), F32),
            pltpu.VMEM((rows, LANES), F32),
            pltpu.VMEM((nc, LANES), F32),
            pltpu.VMEM((8, LANES), F32),
            pltpu.SemaphoreType.DMA((2,)),
        ],
        compiler_params=pltpu.CompilerParams(vmem_limit_bytes=16 << 20),
    )(vmem_array(gen), hbm_array(ref), gweight, rweight)


def next_kernel(count, *refs):
    sources = refs[:count]
    u_ref, v_ref, lrow_ref, lcol_ref, vs_ref, rowacc_ref, colsum_ref, peak_ref = refs[count:]
    chunks = TILE // LANES
    start_peak(sources[0], u_ref[0:1, :], v_ref, vs_ref, peak_ref, rowacc_ref)
    first = 0
    for d_ref in sources:
        steps = d_ref.shape[1] // TILE

        def step(j, carry):
            u = [u_ref[pl.ds(first + j * chunks + c, 1), :] for c in range(chunks)]
            base = pl.multiple_of(j * TILE, TILE)
            for c, part in enumerate(sweep(d_ref, base, chunks, u, vs_ref, rowacc_ref)):
                colsum_ref[pl.ds(first + j * chunks + c, 1), :] = part
            return carry

        lax.fori_loop(0, steps, step, 0)
        first += steps * chunks
    finish(sources, u_ref, v_ref, vs_ref, rowacc_ref, colsum_ref, peak_ref, lrow_ref, lcol_ref)


def next_pass(parts, u, v):
    rows = parts[0].shape[0]
    cols = sum(part.shape[1] for part in parts)
    nq, nc = rows // LANES, cols // LANES
    vmem = pl.BlockSpec(memory_space=pltpu.VMEM)
    return pl.pallas_call(
        functools.partial(next_kernel, len(parts)),
        in_specs=[vmem] * (len(parts) + 2),
        out_shape=(jax.ShapeDtypeStruct((nq, LANES), F32), jax.ShapeDtypeStruct((nc, LANES), F32)),
        out_specs=(vmem, vmem),
        scratch_shapes=[
            pltpu.VMEM((rows, LANES), F32),
            pltpu.VMEM((rows, LANES), F32),
            pltpu.VMEM((nc, LANES), F32),
            pltpu.VMEM((8, LANES), F32),
        ],
        compiler_params=pltpu.CompilerParams(vmem_limit_bytes=8 << 20),
    )(*[vmem_array(part) for part in parts], u, v)


def self_first_kernel(count, first, *refs):
    own_ref, mate_ref = refs[:2]
    sources = refs[2 : 2 + count]
    mine_ref, theirs_ref, place_ref, e_ref, z_ref = refs[2 + count : 7 + count]
    piece_ref, hs_ref, ws_ref, sem = refs[7 + count :]
    half, width = own_ref.shape
    rows = 2 * half
    tall = piece_ref.shape[0] // count
    chunks = tall // LANES
    half_scale = 0.5 * LOG2E / (EPS * width)
    dot_scale = LOG2E / (EPS * width)

    def load(t, src):
        at = pl.ds(pl.multiple_of(t * tall, tall), tall)
        return pltpu.make_async_copy(src, piece_ref.at[at, :], sem.at[t])

    for t, src in enumerate(sources):
        load(t, src).start()
    nq = half // LANES
    for at, vec_ref in ((0, mine_ref), (nq, theirs_ref)):
        spread(vec_ref, hs_ref, nq, 0, at)
        spread(vec_ref, ws_ref, nq, nq, at)
    z_ref[...] = jnp.zeros_like(z_ref)
    zero = jnp.zeros((8, LANES), F32)

    def tile(t, carry):
        load(t, sources[0]).wait()
        base = pl.multiple_of(t * tall, tall)
        view = piece_ref.at[pl.ds(base, tall), :]
        piece_half = norms(view, 0, chunks, half_scale)
        for h, rows_ref in enumerate((own_ref, mate_ref)):
            e_ref[h * half : (h + 1) * half, pl.ds(base, tall)] = lax.dot_general(
                rows_ref[...], view[...], (((1,), (1,)), ((), ())), preferred_element_type=F32
            )

        def body(r, acc):
            at = pl.ds(pl.multiple_of(r * ROWS, ROWS), ROWS)
            hs = hs_ref[at, :]
            ws = ws_ref[at, :]
            out = []
            for c in range(chunks):
                part = pl.ds(base + c * LANES, LANES)
                e = jnp.exp2(e_ref[at, part] * dot_scale - (hs + piece_half[c]))
                e_ref[at, part] = e
                out.append(acc[c] + jnp.sum((e * ws).reshape(ROWS // 8, 8, LANES), axis=0))
            return tuple(out)

        acc = lax.fori_loop(0, rows // ROWS, body, (zero,) * chunks, unroll=2)
        for c in range(chunks):
            z_ref[pl.ds(place_ref[first + t * chunks + c], 1), :] = jnp.sum(acc[c], axis=0, keepdims=True)
        return carry

    lax.fori_loop(0, count, tile, 0)


def self_first(own, mate, sources, mine, theirs, place, first):
    rows, width = 2 * own.shape[0], own.shape[1]
    count, tall = len(sources), sources[0].shape[0]
    cols = count * tall
    vmem = pl.BlockSpec(memory_space=pltpu.VMEM)
    return pl.pallas_call(
        functools.partial(self_first_kernel, count, first),
        in_specs=[vmem, vmem]
        + [pl.BlockSpec(memory_space=pl.ANY)] * count
        + [vmem, vmem, pl.BlockSpec(memory_space=pltpu.SMEM)],
        out_shape=(pltpu.VMEM((rows, cols), F32), jax.ShapeDtypeStruct((place.shape[0], LANES), F32)),
        out_specs=(vmem, vmem),
        scratch_shapes=[
            pltpu.VMEM((cols, width), jnp.bfloat16),
            pltpu.VMEM((rows, LANES), F32),
            pltpu.VMEM((rows, LANES), F32),
            pltpu.SemaphoreType.DMA((count,)),
        ],
        compiler_params=pltpu.CompilerParams(vmem_limit_bytes=16 << 20),
    )(vmem_array(own), vmem_array(mate), *sources, mine, theirs, place)


def self_cols_kernel(count, *refs):
    w_ref, place_ref, z_ref, ws_ref = refs[count:]
    rows = refs[0].shape[0]
    chunks = 256 // LANES
    spread(w_ref, ws_ref, rows // LANES)
    zero = jnp.zeros((8, LANES), F32)
    first = 0
    for e_ref in refs[:count]:
        steps = e_ref.shape[1] // 256

        def tile(t, carry):
            base = pl.multiple_of(t * 256, 256)

            def body(r, acc):
                at = pl.ds(pl.multiple_of(r * ROWS, ROWS), ROWS)
                ws = ws_ref[at, :]
                out = []
                for c in range(chunks):
                    e = e_ref[at, pl.ds(base + c * LANES, LANES)] * ws
                    out.append(acc[c] + jnp.sum(e.reshape(ROWS // 8, 8, LANES), axis=0))
                return tuple(out)

            acc = lax.fori_loop(0, rows // ROWS, body, (zero,) * chunks, unroll=4)
            for c in range(chunks):
                z_ref[pl.ds(place_ref[first + t * chunks + c], 1), :] = jnp.sum(acc[c], axis=0, keepdims=True)
            return carry

        lax.fori_loop(0, steps, tile, 0)
        first += steps * chunks


def self_rows_kernel(count, *refs):
    w_ref, place_ref, y_ref, rowacc_ref = refs[count:]
    rows = refs[0].shape[0]
    chunks = 512 // LANES
    rowacc_ref[...] = jnp.zeros_like(rowacc_ref)
    first = 0
    for e_ref in refs[:count]:
        steps = e_ref.shape[1] // 512

        def tile(t, carry):
            base = pl.multiple_of(t * 512, 512)
            w = [w_ref[pl.ds(place_ref[first + t * chunks + c], 1), :] for c in range(chunks)]

            def body(r, carry):
                at = pl.ds(pl.multiple_of(r * ROWS, ROWS), ROWS)
                acc = rowacc_ref[at, :]
                for c in range(chunks):
                    acc = acc + e_ref[at, pl.ds(base + c * LANES, LANES)] * w[c]
                rowacc_ref[at, :] = acc
                return carry

            return lax.fori_loop(0, rows // ROWS, body, carry, unroll=4)

        lax.fori_loop(0, steps, tile, 0)
        first += steps * chunks
    for q in range(rows // LANES):
        y_ref[q : q + 1, :] = lane_fold(rowacc_ref[q * LANES : (q + 1) * LANES, :], jnp.sum)


def self_apply(kernel, parts, w, place, out_rows):
    rows = parts[0].shape[0]
    vmem = pl.BlockSpec(memory_space=pltpu.VMEM)
    return pl.pallas_call(
        functools.partial(kernel, len(parts)),
        in_specs=[vmem] * (len(parts) + 1) + [pl.BlockSpec(memory_space=pltpu.SMEM)],
        out_shape=jax.ShapeDtypeStruct((out_rows, LANES), F32),
        out_specs=vmem,
        scratch_shapes=[pltpu.VMEM((rows, LANES), F32)],
        compiler_params=pltpu.CompilerParams(vmem_limit_bytes=8 << 20),
    )(*[vmem_array(part) for part in parts], w, place)


def log_add(parts):
    top = functools.reduce(jnp.maximum, parts)
    return top + jnp.log2(sum(jnp.exp2(part - top) for part in parts))


def build(n_z, n_y, n_core, n_ref):
    n_zy = n_z * n_y
    n_gen = n_zy * n_core
    assert n_z == n_y == n_ref == 4 and n_core == 2

    def place_of(g):
        return g // (n_y * n_core), (g // n_core) % n_y, g % n_core

    def gen_perm(move):
        out = []
        for g in range(n_gen):
            z, y, c = move(*place_of(g))
            out.append((g, ((z % n_z) * n_y + y % n_y) * n_core + c % n_core))
        return out

    core_stage = [gen_perm(lambda z, y, c: (z, y, c + 1))]
    y_stage = [gen_perm(lambda z, y, c: (z, y + k, c)) for k in (1, 2, 3)]
    z_stage = [gen_perm(lambda z, y, c: (z + k, y, c)) for k in (1, 2, 3)]
    ref_stage = [[(i, (i + k) % n_ref) for i in range(n_ref)] for k in (1, 2, 3)]
    first_axis = {k: gen_perm(lambda z, y, c: (z, y + k, c) if c == 0 else (z + k, y, c)) for k in (1, 2, 3)}
    second_axis = {k: gen_perm(lambda z, y, c: (z + k, y, c) if c == 0 else (z, y + k, c)) for k in (1, 3)}
    order = [(0, 0), (0, 1), (0, 2), (0, 3)]
    order += [(1, 0), (1, 1), (1, 2), (1, 3), (3, 0), (3, 1), (3, 2), (3, 3)]
    order += [(2, 0), (2, 1), (2, 2), (2, 3)]

    def shift(value, axis, perms):
        return [lax.ppermute(value, axis, perm) for perm in perms]

    def merge(parts, logs):
        top = log_add([part[:logs] for part in parts])
        if parts[0].shape[0] == logs:
            return top
        return jnp.concatenate([top, sum(part[logs:] for part in parts)], axis=0)

    def stage(value, axis, perms, logs):
        return merge([value] + shift(value, axis, perms), logs)

    def run(gen_features, gen_weight, ref_features, ref_weight, ref_self):
        gen_count = gen_features.shape[0]
        ref_count = ref_features.shape[0]
        nq, nc = gen_count // LANES, ref_count // LANES
        g = lax.axis_index("gen")
        x = lax.axis_index("ref")
        z, y, core = place_of(g)
        zy = z * n_y + y
        b, a = (lax.broadcasted_iota(jnp.int32, (len(order),), 0) for _ in range(2))
        b = functools.reduce(lambda v, k: jnp.where(a == k, order[k][0], v), range(len(order)), b)
        a = a % 4
        mine = ((z - b + n_z) % n_z) * n_y + (y - a + n_y) % n_y
        other = ((z - a + n_z) % n_z) * n_y + (y - b + n_y) % n_y
        place = jnp.where(core == 0, mine, other)
        wg = gen_weight.reshape(nq, LANES)
        wr = ref_weight.reshape(nc, LANES)
        at_zy = (lax.broadcasted_iota(jnp.int32, (n_zy, LANES), 0) == zy).astype(F32)
        at_x = (lax.broadcasted_iota(jnp.int32, (n_ref, LANES), 0) == x).astype(F32)
        wg, place, at_zy, at_x = lax.optimization_barrier((wg, place, at_zy, at_x))

        def to_cols(rows):
            picked = jnp.sum(jnp.where(at_x > 0, rows, 0.0), axis=0, keepdims=True)
            return jnp.where(at_zy > 0, picked, 0.0)

        def to_rows(cols):
            picked = jnp.sum(jnp.where(at_zy > 0, cols, 0.0), axis=0, keepdims=True)
            return jnp.where(at_x > 0, picked, 0.0)

        own = lax.dynamic_slice_in_dim(gen_features, x * LANES, LANES, 0)
        got = [lax.ppermute(own, "gen", first_axis[k]) for k in (1, 2, 3)]
        mate = lax.ppermute(gen_features, "gen", core_stage[0])
        near = jnp.concatenate([own] + got, axis=0)
        up = lax.ppermute(near, "gen", second_axis[1])
        down = lax.ppermute(near, "gen", second_axis[3])
        low_far = lax.ppermute(up[: 2 * LANES], "gen", second_axis[1])
        high_far = lax.ppermute(down[2 * LANES :], "gen", second_axis[3])

        d0, row0, lcol0, mine, hcol0, gmass = first_pass(gen_features, ref_features, wg, wr, 0, 2)
        theirs = lax.ppermute(mine, "gen", core_stage[0])
        d1, row1, lcol1, _, hcol1, _ = first_pass(gen_features, ref_features, wg, wr, 1, 2)
        hcol = jnp.concatenate([hcol0, hcol1], axis=0)
        hrow = mine[:nq]
        weight = jnp.concatenate([wg, theirs[nq:]], axis=0)
        e0, z1_0 = self_first(gen_features, mate, [near], mine, theirs, place, 0)
        e1, z1_1 = self_first(gen_features, mate, [up, down], mine, theirs, place, 4)
        e2, z1_2 = self_first(gen_features, mate, [low_far, high_far], mine, theirs, place, 12)
        e = [e0, e1, e2]

        row_part = jnp.concatenate([log_add([row0[:nq], row1[:nq]]), row0[nq:]], axis=0)
        row_part = stage(row_part, "ref", ref_stage, nq)
        col_part = jnp.concatenate([lcol0, lcol1, gmass], axis=0)
        col_part = stage(col_part, "gen", core_stage, nc)
        col_part = jnp.concatenate([col_part, to_cols(wg)], axis=0)
        col_part = stage(col_part, "gen", y_stage, nc)
        col_part = stage(col_part, "gen", z_stage, nc)
        gmass = col_part[nc : nc + 1]
        rmass = row_part[nq : nq + 1]
        wcols = col_part[nc + 8 :] / gmass
        gmass_log = jnp.log2(gmass)
        rmass_log = jnp.log2(rmass)
        f = hrow - (row_part[:nq] - rmass_log)
        c = hcol - (col_part[:nc] - gmass_log)
        ubase = jnp.log2(wr) - rmass_log - hcol
        vbase = jnp.log2(wg) - gmass_log - hrow
        share = wg / gmass

        lrow, lcol = next_pass([d0, d1], ubase + c, vbase + f)
        lrow = stage(lrow, "ref", ref_stage, nq)
        lcol = stage(lcol, "gen", core_stage, nc)
        col_part = jnp.concatenate([lcol, z1_0 + z1_1 + z1_2], axis=0)
        col_part = stage(col_part, "gen", y_stage, nc)
        col_part = stage(col_part, "gen", z_stage, nc)
        f = 0.5 * (f + (hrow - lrow))
        c = 0.5 * (c + (hcol - col_part[:nc]))
        y1 = col_part[nc:] / gmass

        lrow, lcol = next_pass([d0, d1], ubase + c, vbase + f)
        y2 = self_apply(self_rows_kernel, e, wcols / y1, place, 2 * nq)
        row_part = jnp.concatenate([lrow, y2, to_rows(-jnp.log2(y1))], axis=0)
        row_part = stage(row_part, "ref", ref_stage, nq)
        f = 0.5 * (f + (hrow - row_part[:nq]))
        f_part = share * f
        f_part = jnp.concatenate([f_part, f_part], axis=0)
        mine = jnp.concatenate([lcol, f_part, row_part[nq:]], axis=0)
        theirs = shift(mine, "gen", core_stage)[0]
        lcol = log_add([lcol, theirs[:nc]])
        f_part = f_part + theirs[nc : nc + 8]
        y2, y2_mate, s1 = row_part[nq : 2 * nq], row_part[2 * nq : 3 * nq], row_part[3 * nq :]
        at = nc + 8
        y2 = y2 + theirs[at + nq : at + 2 * nq]
        y2_mate = y2_mate + theirs[at : at + nq]
        s1 = jnp.concatenate([s1, theirs[at + 2 * nq :]], axis=0)
        s2 = 0.5 * (s1 - jnp.log2(jnp.concatenate([y2, y2_mate], axis=0)))
        w3 = weight / gmass * jnp.exp2(s2)
        z3 = self_apply(self_cols_kernel, e, w3, place, n_zy)
        col_part = jnp.concatenate([lcol, f_part, z3, to_cols(s2[:nq])], axis=0)
        col_part = stage(col_part, "gen", y_stage, nc)
        col_part = stage(col_part, "gen", z_stage, nc)
        c = 0.5 * (c + (hcol - col_part[:nc]))
        f_part = col_part[nc : nc + nq]
        z3, s2 = col_part[nc + 8 : nc + 8 + n_zy], col_part[nc + 8 + n_zy :]

        unit = EPS / LOG2E
        ref_gap = c * unit - ref_self.reshape(nc, LANES)
        s3 = 0.5 * (s2 - jnp.log2(z3))
        s_part = jnp.sum((wcols * s3).reshape(2, 8, LANES), axis=0)
        s_part = s_part + shift(s_part, "gen", core_stage)[0]
        part = jnp.sum(((wr / rmass) * ref_gap).reshape(nc // 8, 8, LANES), axis=0) - unit * s_part
        row_part = jnp.concatenate([to_rows(s3), part], axis=0)
        row_part = row_part + sum(shift(row_part, "ref", ref_stage))
        gen_gap = (f - row_part[:nq]) * unit
        divergence = unit * jnp.sum(f_part) + jnp.sum(row_part[nq:])
        return gen_gap.reshape(gen_count), ref_gap.reshape(ref_count), divergence

    return run


def solution(mesh):
    n_gen, n_ref = mesh.shape["gen"], mesh.shape["ref"]
    n_core = 2
    n_y = 1
    while n_y * n_y * n_core < n_gen:
        n_y *= 2
    placed = (P("gen", None), P("gen"), P("ref", None), P("ref"), P("ref"))
    return jax.shard_map(
        build(n_gen // (n_y * n_core), n_y, n_core, n_ref),
        mesh=mesh,
        in_specs=placed,
        out_specs=(P("gen"), P("ref"), P()),
        check_vma=False,
    )
```

time: 876 us -> 230 us (0.26)
  blocking collectives: 747 us -> 0 us
  Pallas kernels: 0 us -> 124 us
  other arithmetic: 78.9 us -> 3.38 us
  starting transfers between devices: 0.04 us -> 61.7 us
  waiting for transfers between devices: 0.04 us -> 31.8 us
  matrix products: 26.9 us -> 0 us
  between operations: 16.8 us -> 3.51 us
    psum x7 -> x0, blocking collectives: 405 us -> none  [the longest x2 249 us: per_device(): column_sum = lax.psum(local_sum(column_scores, column_top, 0), 'gen')]
    pmax x6 -> x0, blocking collectives: 274 us -> none  [the longest x2 245 us: per_device(): column_top = lax.pmax(jnp.max(column_scores, axis=0), 'gen')]
    pallas_call x0 -> x9, Pallas kernels: none -> 124 us  [the longest x2 54 us: next_pass(): pl.pallas_call(functools.partial(next_kernel, len(parts)), in_specs=[vmem...]
    all_gather x3 -> x0, blocking collectives: 68.4 us -> none  [per_device(): column_terms = lax.all_gather(own_terms, 'gen', axis=0, tiled=True)]
    ppermute x0 -> x43, starting transfers between devices: none -> 61.7 us  [the longest x34 46.6 us: shift(): return [lax.ppermute(value, axis, perm) for perm in perms]]
    reduce_sum x13 -> x8, other arithmetic: 57.6 us -> 1.95 us  [the longest x2 1.2 us: run(): divergence = unit * jnp.sum(f_part) + jnp.sum(row_part[nq:])]
    ppermute x0 -> x43, waiting for transfers between devices: none -> 31.8 us  [the longest x34 31.7 us: shift(): return [lax.ppermute(value, axis, perm) for perm in perms]]
    dot_general x2 -> x0, matrix products: 26.9 us -> none  [pair_cost(): lax.dot_general(left_rows, right_rows, (((1,), (1,)), ((), ())), preferre...]
  transfers between devices with their start and end apart: 1 -> 43, of which waited for: 0 -> 18; matrix products, arithmetic and copies ran while one was open for 1% -> 1% of each run, Pallas kernels for 0% -> 38%
where the time goes in v1:
time: 230 us; the launch traced here: 229 us
  Pallas kernels  124 us (54%)
  starting transfers between devices  61.7 us (27%)
  waiting for transfers between devices  31.8 us (14%)
  local copies, waits for them, and re-layouts  4.41 us (2%)
  between operations  3.51 us (2%)
  other arithmetic  3.38 us (1%)
    pallas_call x2, Pallas kernels, next_pass(): pl.pallas_call(functools.partial(next_kernel, len(parts)), in_specs=[vmem...  54 us
    ppermute x34, starting transfers between devices, shift(): return [lax.ppermute(value, axis, perm) for perm in perms]  46.6 us
    pallas_call x2, Pallas kernels, first_pass(): pl.pallas_call(functools.partial(first_kernel, piece), in_specs=[vmem, pl...  44.7 us
    ppermute x34, waiting for transfers between devices, shift(): return [lax.ppermute(value, axis, perm) for perm in perms]  31.7 us
    pallas_call x3, Pallas kernels, self_first(): pl.pallas_call(functools.partial(self_first_kernel, count, first), in_spe...  20.8 us
    ppermute x3, starting transfers between devices, run(): got = [lax.ppermute(own, 'gen', first_axis[k]) for k in (1, 2, 3)]  6.55 us
  transfers between devices with their start and end apart: 43, of which 18 were waited for; matrix products, arithmetic and copies ran while one was open for 1% of the time, Pallas kernels for 38%

profile of v1, /device:TPU:1, one launch (start us, length us, event | category | flops | bytes accessed | tf_op | source)
XLA Modules:
  0.0 228.9 jit_solution(6762326305992946911)
XLA Ops:
  0.6 1.1 constant_dynamic-slice_fusion
  1.7 2.5 %collective-permute-start.15 = (bf16[128,2048]{1,0:T(8,128)(2,1)S(1)}, bf16[128,2048]{1,0:T(8,128)(2,1)S(1)}, u32[]{:S(2)}, u32[]{:S(2)}) collective-permute-start(bf16[128,2048]{1,0:T(8,128)(2,1)S(1)} %constant_dynamic-slice_fusion), channel_id=1, source_target_pairs={{0,8},{4,36},{8,16},{12,44},{16,24},{20,52},{24,0},{28,60},{32,40}... | collective-permute-start | bytes 1572872 | tf_op jit(solution)/shard_map/ppermute | solution.py:516
  4.2 3.3 %collective-permute-start.16 = (bf16[128,2048]{1,0:T(8,128)(2,1)S(1)}, bf16[128,2048]{1,0:T(8,128)(2,1)S(1)}, u32[]{:S(2)}, u32[]{:S(2)}) collective-permute-start(bf16[128,2048]{1,0:T(8,128)(2,1)S(1)} %constant_dynamic-slice_fusion), channel_id=1, source_target_pairs={{0,16},{4,68},{8,24},{12,76},{16,0},{20,84},{24,8},{28,92},{32,48}... | collective-permute-start | bytes 1572872 | tf_op jit(solution)/shard_map/ppermute | solution.py:516
  7.5 0.7 collective-permute-start.17
  8.4 1.6 copy-done
  10.0 0.7 copy-done.2
  10.8 0.7 copy-done.4
  11.4 22.0 %shard_map.76 = (f32[512,2048]{1,0:T(8,128)S(1)}, f32[8,128]{1,0:T(8,128)S(1)}, f32[16,128]{1,0:T(8,128)S(1)}, f32[8,128]{1,0:T(8,128)S(1)}, f32[16,128]{1,0:T(8,128)S(1)}, /*index=5*/f32[8,128]{1,0:T(8,128)S(1)}) custom-call(bf16[512,2048]{1,0:T(8,128)(2,1)S(1)} %copy-done, bf16[4096,2048]{1,0:T(8,128)(2,1)} %ref_hbm.3, f32[4,128]{1,0:T(4,128)S(1)} %bitcast.25, ...), custom_call_target="tpu_custom_call" | custom-call | tf_op jit(solution)/shard_map/pallas_call | solution.py:235
  33.5 22.7 %shard_map.77 = (f32[512,2048]{1,0:T(8,128)S(1)}, f32[8,128]{1,0:T(8,128)S(1)}, f32[16,128]{1,0:T(8,128)S(1)}, f32[8,128]{1,0:T(8,128)}, f32[16,128]{1,0:T(8,128)S(1)}, /*index=5*/f32[8,128]{1,0:T(8,128)}) custom-call(bf16[512,2048]{1,0:T(8,128)(2,1)S(1)} %copy-done, bf16[4096,2048]{1,0:T(8,128)(2,1)} %ref_hbm.3, f32[4,128]{1,0:T(4,128)S(1)} %bitcast.26, ...), custom_call_target="tpu_custom_call" | custom-call | tf_op jit(solution)/shard_map/pallas_call | solution.py:235
  56.2 1.3 collective-permute-start
  57.5 2.5 %collective-permute-start.1 = (f32[8,128]{1,0:T(8,128)S(1)}, f32[8,128]{1,0:T(8,128)S(1)}, u32[]{:S(2)}, u32[]{:S(2)}) collective-permute-start(f32[8,128]{1,0:T(8,128)S(1)} %pad_maximum_fusion.11), channel_id=1, source_target_pairs={{0,2},{1,3},{2,0},{3,1},{4,6},{5,7},{6,4},{7,5},{8,10},{9,11},{10,... | collective-permute-start | bytes 12296 | tf_op jit(solution)/shard_map/ppermute | solution.py:476
  59.9 1.5 collective-permute-start.3
  61.7 0.5 collective-permute-start.19
  62.1 2.3 %collective-permute-start.20 = (bf16[512,2048]{1,0:T(8,128)(2,1)S(1)}, bf16[512,2048]{1,0:T(8,128)(2,1)S(1)}, u32[]{:S(2)}, u32[]{:S(2)}) collective-permute-start(bf16[512,2048]{1,0:T(8,128)(2,1)S(1)} %pad_maximum_fusion.refs_2_), channel_id=1, source_target_pairs={{0,96},{4,28},{8,104},{12,4},{16,112},{20,12},{24,120},{28,20},{32... | collective-permute-start | bytes 6291464 | tf_op jit(solution)/shard_map/ppermute | solution.py:520
  64.5 1.2 collective-permute-start.2
  65.9 2.6 %collective-permute-start.14 = (bf16[512,2048]{1,0:T(8,128)(2,1)S(1)}, bf16[512,2048]{1,0:T(8,128)(2,1)S(1)}, u32[]{:S(2)}, u32[]{:S(2)}) collective-permute-start(bf16[512,2048]{1,0:T(8,128)(2,1)S(1)} %copy-done.1), channel_id=1, source_target_pairs={{0,4},{4,0},{8,12},{12,8},{16,20},{20,16},{24,28},{28,24},{32,36},... | collective-permute-start | bytes 6291464 | tf_op jit(solution)/shard_map/ppermute | solution.py:517
  68.5 1.6 collective-permute-start.5
  70.1 19.2 %collective-permute-done.4 = f32[56,128]{1,0:T(8,128)S(1)} collective-permute-done((f32[56,128]{1,0:T(8,128)S(1)}, f32[56,128]{1,0:T(8,128)S(1)}, u32[]{:S(2)}, u32[]{:S(2)}) %collective-permute-start.4) | collective-permute-done | bytes 28704 | tf_op jit(solution)/shard_map/ppermute | solution.py:476
  89.4 2.7 %collective-permute-done.6 = f32[56,128]{1,0:T(8,128)S(1)} collective-permute-done((f32[56,128]{1,0:T(8,128)S(1)}, f32[56,128]{1,0:T(8,128)S(1)}, u32[]{:S(2)}, u32[]{:S(2)}) %collective-permute-start.6) | collective-permute-done | bytes 28704 | tf_op jit(solution)/shard_map/ppermute | solution.py:476
  92.1 1.4 collective-permute-start.7
  93.5 3.8 %collective-permute-start.8 = (f32[56,128]{1,0:T(8,128)S(1)}, f32[56,128]{1,0:T(8,128)S(1)}, u32[]{:S(2)}, u32[]{:S(2)}) collective-permute-start(f32[56,128]{1,0:T(8,128)S(1)} %pad_maximum_fusion.4), channel_id=1, source_target_pairs={{0,64},{4,68},{8,72},{12,76},{16,80},{20,84},{24,88},{28,92},{32,9... | collective-permute-start | bytes 86024 | tf_op jit(solution)/shard_map/ppermute | solution.py:476
  98.0 2.6 %collective-permute-start.22 = (bf16[256,2048]{1,0:T(8,128)(2,1)S(1)}, bf16[256,2048]{1,0:T(8,128)(2,1)S(1)}, u32[]{:S(2)}, u32[]{:S(2)}) collective-permute-start(bf16[256,2048]{1,0:T(8,128)(2,1)S(1)} %slice.320), channel_id=1, source_target_pairs={{0,96},{4,28},{8,104},{12,4},{16,112},{20,12},{24,120},{28,20},{32... | collective-permute-start | bytes 3145736 | tf_op jit(solution)/shard_map/ppermute | solution.py:522
  100.7 27.1 %shard_map.78 = (f32[4,128]{1,0:T(4,128)S(1)}, f32[32,128]{1,0:T(8,128)S(1)}) custom-call(f32[512,2048]{1,0:T(8,128)S(1)} %get-tuple-element.31.refs_0_, f32[512,2048]{1,0:T(8,128)S(1)} %get-tuple-element.32.refs_1_, f32[32,128]{1,0:T(8,128)S(1)} %get-tuple-element.63.refs_2_, f32[4,128]{1,0:T(4,128)S(1)} %get-tuple-element.61.refs_3_), custom_call_target="tpu_custom_call" | custom-call | tf_op jit(solution)/shard_map/pallas_call | solution.py:280
  127.9 0.5 collective-permute-start.18
  128.4 0.7 collective-permute-done.13
  129.2 5.4 %shard_map.79 = (f32[1024,512]{1,0:T(8,128)S(1)}, f32[16,128]{1,0:T(8,128)S(1)}) custom-call(bf16[512,2048]{1,0:T(8,128)(2,1)S(1)} %copy-done.1, bf16[512,2048]{1,0:T(8,128)(2,1)S(1)} %collective-permute-done.14.refs_1_, bf16[512,2048]{1,0:T(8,128)(2,1)S(1)} %pad_maximum_fusion.refs_2_, f32[8,128]{1,0:T(8,128)S(1)} %get-tuple-element.28.refs_3_.refs_4_, ...), custom_call_target="tpu_custom_call" | custom-call | tf_op jit(solution)/shard_map/pallas_call | solution.py:355
  134.6 9.9 %shard_map.80 = (f32[1024,1024]{1,0:T(8,128)S(1)}, f32[16,128]{1,0:T(8,128)S(1)}) custom-call(bf16[512,2048]{1,0:T(8,128)(2,1)S(1)} %copy-done.1, bf16[512,2048]{1,0:T(8,128)(2,1)S(1)} %collective-permute-done.14.refs_1_, bf16[512,2048]{1,0:T(8,128)(2,1)S(1)} %collective-permute-done.19.refs_2_, bf16[512,2048]{1,0:T(8,128)(2,1)S(1)} %collective-permute-done.20.refs_3_, ...), custom_call_target="tpu_custom_call" | custom-call | tf_op jit(solution)/shard_map/pallas_call | solution.py:355
  144.5 5.5 %shard_map.81 = (f32[1024,512]{1,0:T(8,128)S(1)}, f32[16,128]{1,0:T(8,128)S(1)}) custom-call(bf16[512,2048]{1,0:T(8,128)(2,1)S(1)} %copy-done.1, bf16[512,2048]{1,0:T(8,128)(2,1)S(1)} %collective-permute-done.14.refs_1_, bf16[256,2048]{1,0:T(8,128)(2,1)S(1)} %collective-permute-done.21.refs_2_, bf16[256,2048]{1,0:T(8,128)(2,1)S(1)} %collective-permute-done.22.refs_3_, ...), custom_call_target="tpu_custom_call" | custom-call | tf_op jit(solution)/shard_map/pallas_call | solution.py:355
  150.2 2.1 collective-permute-start.24
  152.3 0.6 collective-permute-start.25
  152.8 2.3 %collective-permute-start.11 = (f32[4,128]{1,0:T(4,128)S(1)}, f32[4,128]{1,0:T(4,128)S(1)}, u32[]{:S(2)}, u32[]{:S(2)}) collective-permute-start(f32[4,128]{1,0:T(4,128)S(1)} %get-tuple-element.40), channel_id=1, source_target_pairs={{0,2},{1,3},{2,0},{3,1},{4,6},{5,7},{6,4},{7,5},{8,10},{9,11},{10,... | collective-permute-start | bytes 6152 | tf_op jit(solution)/shard_map/ppermute | solution.py:476
  155.2 0.3 collective-permute-start.12
  155.6 1.3 collective-permute-start.26
  156.8 1.5 collective-permute-start.27
  158.3 1.0 collective-permute-start.28
  159.5 1.5 collective-permute-done.27
  161.1 26.9 %shard_map.82 = (f32[4,128]{1,0:T(4,128)S(1)}, f32[32,128]{1,0:T(8,128)S(1)}) custom-call(f32[512,2048]{1,0:T(8,128)S(1)} %get-tuple-element.31.refs_0_, f32[512,2048]{1,0:T(8,128)S(1)} %get-tuple-element.32.refs_1_, f32[32,128]{1,0:T(8,128)S(1)} %get-tuple-element.59.refs_2_, f32[4,128]{1,0:T(4,128)S(1)} %get-tuple-element.57.refs_3_), custom_call_target="tpu_custom_call" | custom-call | tf_op jit(solution)/shard_map/pallas_call | solution.py:280
  188.0 2.2 shard_map.83
  190.4 2.6 %collective-permute-start.31 = (f32[16,128]{1,0:T(8,128)S(1)}, f32[16,128]{1,0:T(8,128)S(1)}, u32[]{:S(2)}, u32[]{:S(2)}) collective-permute-start(f32[16,128]{1,0:T(8,128)S(1)} %pad_maximum_fusion.9), channel_id=1, source_target_pairs={{0,3},{1,0},{2,1},{3,2},{4,7},{5,4},{6,5},{7,6},{8,11},{9,8},{10,9... | collective-permute-start | bytes 24584 | tf_op jit(solution)/shard_map/ppermute | solution.py:476
  193.0 1.0 collective-permute-done.29
  194.0 0.4 collective-permute-done.30
  194.4 0.3 collective-permute-done.31
  194.7 4.9 %collective-permute-start.32 = (f32[52,128]{1,0:T(8,128)S(1)}, f32[52,128]{1,0:T(8,128)S(1)}, u32[]{:S(2)}, u32[]{:S(2)}) collective-permute-start(f32[52,128]{1,0:T(8,128)S(1)} %pad_maximum_fusion.5), channel_id=1, source_target_pairs={{0,4},{4,0},{8,12},{12,8},{16,20},{20,16},{24,28},{28,24},{32,36},... | collective-permute-start | bytes 79880 | tf_op jit(solution)/shard_map/ppermute | solution.py:476
  199.6 0.9 collective-permute-done.32
  200.5 2.4 %shard_map.84 = f32[16,128]{1,0:T(8,128)S(1)} custom-call(f32[1024,512]{1,0:T(8,128)S(1)} %get-tuple-element.47.refs_0_, f32[1024,1024]{1,0:T(8,128)S(1)} %get-tuple-element.48.refs_1_, f32[1024,512]{1,0:T(8,128)S(1)} %get-tuple-element.49.refs_2_, f32[8,128]{1,0:T(8,128)S(1)} %get-tuple-element.75.refs_3_, s32[16]{0:T(128)S(1)} %broadcast_select_fusion.4.refs_5_.refs_6_.refs_4_), custom_call_target="tpu_custom_call" | custom-call | tf_op jit(solution)/shard_map/pallas_call | solution.py:435
  203.0 1.4 collective-permute-start.33
  204.5 1.3 collective-permute-start.34
  205.8 1.9 collective-permute-start.35
  207.7 1.1 collective-permute-done.34
  208.8 0.3 collective-permute-done.35
  209.2 0.8 collective-permute-start.36
  210.0 2.5 %collective-permute-start.37 = (f32[72,128]{1,0:T(8,128)S(1)}, f32[72,128]{1,0:T(8,128)S(1)}, u32[]{:S(2)}, u32[]{:S(2)}) collective-permute-start(f32[72,128]{1,0:T(8,128)S(1)} %pad_maximum_fusion.2), channel_id=1, source_target_pairs={{0,64},{4,68},{8,72},{12,76},{16,80},{20,84},{24,88},{28,92},{32,9... | collective-permute-start | bytes 110600 | tf_op jit(solution)/shard_map/ppermute | solution.py:476
  212.5 1.0 collective-permute-start.38
  213.5 0.8 collective-permute-done.37
  214.3 1.3 collective-permute-done.38
  215.6 3.0 %collective-permute-start.39 = (f32[8,128]{1,0:T(8,128)S(1)}, f32[8,128]{1,0:T(8,128)S(1)}, u32[]{:S(2)}, u32[]{:S(2)}) collective-permute-start(f32[8,128]{1,0:T(8,128)S(1)} %bitcast_reduce_fusion.1), channel_id=1, source_target_pairs={{0,4},{4,0},{8,12},{12,8},{16,20},{20,16},{24,28},{28,24},{32,36},... | collective-permute-start | bytes 12296 | tf_op jit(solution)/shard_map/ppermute | solution.py:476
  218.6 0.6 bitcast_reduce_fusion
  219.4 1.7 collective-permute-start.40
  221.2 1.9 collective-permute-start.41
  223.1 0.5 collective-permute-start.42
  223.6 0.6 slice_reduce_fusion.1
  225.2 0.7 collective-permute-done.42
  225.9 0.6 slice_reduce_fusion
  226.5 0.6 fusion.14
  (112 shorter events, 3.0 us)
Async XLA Ops:
  1.7 58.2 %collective-permute-start.15 = (bf16[128,2048]{1,0:T(8,128)(2,1)S(1)}, bf16[128,2048]{1,0:T(8,128)(2,1)S(1)}, u32[]{:S(2)}, u32[]{:S(2)}) collective-permute-start(bf16[128,2048]{1,0:T(8,128)(2,1)S(1)} %constant_dynamic-slice_fusion), channel_id=1, source_target_pairs={{0,8},{4,36},{8,16},{12,44},{16,24},{20,52},{24,0},{28,60},{32,40}... | collective-permute-start | bytes 1572872 | tf_op jit(solution)/shard_map/ppermute | solution.py:516
  4.2 57.2 %collective-permute-start.16 = (bf16[128,2048]{1,0:T(8,128)(2,1)S(1)}, bf16[128,2048]{1,0:T(8,128)(2,1)S(1)}, u32[]{:S(2)}, u32[]{:S(2)}) collective-permute-start(bf16[128,2048]{1,0:T(8,128)(2,1)S(1)} %constant_dynamic-slice_fusion), channel_id=1, source_target_pairs={{0,16},{4,68},{8,24},{12,76},{16,0},{20,84},{24,8},{28,92},{32,48}... | collective-permute-start | bytes 1572872 | tf_op jit(solution)/shard_map/ppermute | solution.py:516
  7.5 53.9 %collective-permute-start.17 = (bf16[128,2048]{1,0:T(8,128)(2,1)S(1)}, bf16[128,2048]{1,0:T(8,128)(2,1)S(1)}, u32[]{:S(2)}, u32[]{:S(2)}) collective-permute-start(bf16[128,2048]{1,0:T(8,128)(2,1)S(1)} %constant_dynamic-slice_fusion), channel_id=1, source_target_pairs={{0,24},{4,100},{8,0},{12,108},{16,8},{20,116},{24,16},{28,124},{32... | collective-permute-start | bytes 1572872 | tf_op jit(solution)/shard_map/ppermute | solution.py:516
  8.4 1.6 copy-start
  10.0 0.7 copy-start.2
  10.8 0.7 copy-start.4
  56.2 9.6 %collective-permute-start = (f32[8,128]{1,0:T(8,128)S(1)}, f32[8,128]{1,0:T(8,128)S(1)}, u32[]{:S(2)}, u32[]{:S(2)}) collective-permute-start(f32[8,128]{1,0:T(8,128)S(1)} %pad_maximum_fusion.11), channel_id=1, source_target_pairs={{0,1},{1,2},{2,3},{3,0},{4,5},{5,6},{6,7},{7,4},{8,9},{9,10},{10,1... | collective-permute-start | bytes 12296 | tf_op jit(solution)/shard_map/ppermute | solution.py:476
  57.5 8.4 %collective-permute-start.1 = (f32[8,128]{1,0:T(8,128)S(1)}, f32[8,128]{1,0:T(8,128)S(1)}, u32[]{:S(2)}, u32[]{:S(2)}) collective-permute-start(f32[8,128]{1,0:T(8,128)S(1)} %pad_maximum_fusion.11), channel_id=1, source_target_pairs={{0,2},{1,3},{2,0},{3,1},{4,6},{5,7},{6,4},{7,5},{8,10},{9,11},{10,... | collective-permute-start | bytes 12296 | tf_op jit(solution)/shard_map/ppermute | solution.py:476
  59.9 2.2 copy-start.5
  59.9 6.0 %copy-start.1 = (bf16[512,2048]{1,0:T(8,128)(2,1)S(1)}, bf16[512,2048]{1,0:T(8,128)(2,1)}, u32[]{:S(2)}) copy-start(bf16[512,2048]{1,0:T(8,128)(2,1)} %refs_0_.5) | copy-start | bytes 6291460
  59.9 4.6 %collective-permute-start.3 = (f32[40,128]{1,0:T(8,128)S(1)}, f32[40,128]{1,0:T(8,128)S(1)}, u32[]{:S(2)}, u32[]{:S(2)}) collective-permute-start(f32[40,128]{1,0:T(8,128)S(1)} %pad_maximum_fusion.8), channel_id=1, source_target_pairs={{0,4},{4,0},{8,12},{12,8},{16,20},{20,16},{24,28},{28,24},{32,36},... | collective-permute-start | bytes 61448 | tf_op jit(solution)/shard_map/ppermute | solution.py:476
  61.7 35.7 %collective-permute-start.19 = (bf16[512,2048]{1,0:T(8,128)(2,1)S(1)}, bf16[512,2048]{1,0:T(8,128)(2,1)S(1)}, u32[]{:S(2)}, u32[]{:S(2)}) collective-permute-start(bf16[512,2048]{1,0:T(8,128)(2,1)S(1)} %pad_maximum_fusion.refs_2_), channel_id=1, source_target_pairs={{0,32},{4,12},{8,40},{12,20},{16,48},{20,28},{24,56},{28,4},{32,64... | collective-permute-start | bytes 6291464 | tf_op jit(solution)/shard_map/ppermute | solution.py:519
  62.1 35.5 %collective-permute-start.20 = (bf16[512,2048]{1,0:T(8,128)(2,1)S(1)}, bf16[512,2048]{1,0:T(8,128)(2,1)S(1)}, u32[]{:S(2)}, u32[]{:S(2)}) collective-permute-start(bf16[512,2048]{1,0:T(8,128)(2,1)S(1)} %pad_maximum_fusion.refs_2_), channel_id=1, source_target_pairs={{0,96},{4,28},{8,104},{12,4},{16,112},{20,12},{24,120},{28,20},{32... | collective-permute-start | bytes 6291464 | tf_op jit(solution)/shard_map/ppermute | solution.py:520
  64.5 4.0 %collective-permute-start.2 = (f32[8,128]{1,0:T(8,128)S(1)}, f32[8,128]{1,0:T(8,128)S(1)}, u32[]{:S(2)}, u32[]{:S(2)}) collective-permute-start(f32[8,128]{1,0:T(8,128)S(1)} %pad_maximum_fusion.11), channel_id=1, source_target_pairs={{0,3},{1,0},{2,1},{3,2},{4,7},{5,4},{6,5},{7,6},{8,11},{9,8},{10,9... | collective-permute-start | bytes 12296 | tf_op jit(solution)/shard_map/ppermute | solution.py:476
  65.8 23.6 %collective-permute-start.4 = (f32[56,128]{1,0:T(8,128)S(1)}, f32[56,128]{1,0:T(8,128)S(1)}, u32[]{:S(2)}, u32[]{:S(2)}) collective-permute-start(f32[56,128]{1,0:T(8,128)S(1)} %pad_maximum_fusion.3), channel_id=1, source_target_pairs={{0,8},{4,12},{8,16},{12,20},{16,24},{20,28},{24,0},{28,4},{32,40},... | collective-permute-start | bytes 86024 | tf_op jit(solution)/shard_map/ppermute | solution.py:476
  65.9 63.3 %collective-permute-start.14 = (bf16[512,2048]{1,0:T(8,128)(2,1)S(1)}, bf16[512,2048]{1,0:T(8,128)(2,1)S(1)}, u32[]{:S(2)}, u32[]{:S(2)}) collective-permute-start(bf16[512,2048]{1,0:T(8,128)(2,1)S(1)} %copy-done.1), channel_id=1, source_target_pairs={{0,4},{4,0},{8,12},{12,8},{16,20},{20,16},{24,28},{28,24},{32,36},... | collective-permute-start | bytes 6291464 | tf_op jit(solution)/shard_map/ppermute | solution.py:517
  68.5 20.8 %collective-permute-start.5 = (f32[56,128]{1,0:T(8,128)S(1)}, f32[56,128]{1,0:T(8,128)S(1)}, u32[]{:S(2)}, u32[]{:S(2)}) collective-permute-start(f32[56,128]{1,0:T(8,128)S(1)} %pad_maximum_fusion.3), channel_id=1, source_target_pairs={{0,16},{4,20},{8,24},{12,28},{16,0},{20,4},{24,8},{28,12},{32,48},... | collective-permute-start | bytes 86024 | tf_op jit(solution)/shard_map/ppermute | solution.py:476
  89.3 2.7 %collective-permute-start.6 = (f32[56,128]{1,0:T(8,128)S(1)}, f32[56,128]{1,0:T(8,128)S(1)}, u32[]{:S(2)}, u32[]{:S(2)}) collective-permute-start(f32[56,128]{1,0:T(8,128)S(1)} %pad_maximum_fusion.3), channel_id=1, source_target_pairs={{0,24},{4,28},{8,0},{12,4},{16,8},{20,12},{24,16},{28,20},{32,56},... | collective-permute-start | bytes 86024 | tf_op jit(solution)/shard_map/ppermute | solution.py:476
  92.1 5.9 %collective-permute-start.7 = (f32[56,128]{1,0:T(8,128)S(1)}, f32[56,128]{1,0:T(8,128)S(1)}, u32[]{:S(2)}, u32[]{:S(2)}) collective-permute-start(f32[56,128]{1,0:T(8,128)S(1)} %pad_maximum_fusion.4), channel_id=1, source_target_pairs={{0,32},{4,36},{8,40},{12,44},{16,48},{20,52},{24,56},{28,60},{32,6... | collective-permute-start | bytes 86024 | tf_op jit(solution)/shard_map/ppermute | solution.py:476
  93.5 7.1 %collective-permute-start.8 = (f32[56,128]{1,0:T(8,128)S(1)}, f32[56,128]{1,0:T(8,128)S(1)}, u32[]{:S(2)}, u32[]{:S(2)}) collective-permute-start(f32[56,128]{1,0:T(8,128)S(1)} %pad_maximum_fusion.4), channel_id=1, source_target_pairs={{0,64},{4,68},{8,72},{12,76},{16,80},{20,84},{24,88},{28,92},{32,9... | collective-permute-start | bytes 86024 | tf_op jit(solution)/shard_map/ppermute | solution.py:476
  97.3 3.3 %collective-permute-start.9 = (f32[56,128]{1,0:T(8,128)S(1)}, f32[56,128]{1,0:T(8,128)S(1)}, u32[]{:S(2)}, u32[]{:S(2)}) collective-permute-start(f32[56,128]{1,0:T(8,128)S(1)} %pad_maximum_fusion.4), channel_id=1, source_target_pairs={{0,96},{4,100},{8,104},{12,108},{16,112},{20,116},{24,120},{28,124... | collective-permute-start | bytes 86024 | tf_op jit(solution)/shard_map/ppermute | solution.py:476
  97.6 3.1 %copy-start.3 = (f32[4096]{0:T(1024)S(1)}, f32[4096]{0:T(1024)}, u32[]{:S(2)}) copy-start(f32[4096]{0:T(1024)} %param.8) | copy-start | bytes 49156
  97.7 46.8 %collective-permute-start.21 = (bf16[256,2048]{1,0:T(8,128)(2,1)S(1)}, bf16[256,2048]{1,0:T(8,128)(2,1)S(1)}, u32[]{:S(2)}, u32[]{:S(2)}) collective-permute-start(bf16[256,2048]{1,0:T(8,128)(2,1)S(1)} %slice.319), channel_id=1, source_target_pairs={{0,32},{4,12},{8,40},{12,20},{16,48},{20,28},{24,56},{28,4},{32,64... | collective-permute-start | bytes 3145736 | tf_op jit(solution)/shard_map/ppermute | solution.py:521
  98.0 46.5 %collective-permute-start.22 = (bf16[256,2048]{1,0:T(8,128)(2,1)S(1)}, bf16[256,2048]{1,0:T(8,128)(2,1)S(1)}, u32[]{:S(2)}, u32[]{:S(2)}) collective-permute-start(bf16[256,2048]{1,0:T(8,128)(2,1)S(1)} %slice.320), channel_id=1, source_target_pairs={{0,96},{4,28},{8,104},{12,4},{16,112},{20,12},{24,120},{28,20},{32... | collective-permute-start | bytes 3145736 | tf_op jit(solution)/shard_map/ppermute | solution.py:522
  127.8 1.3 collective-permute-start.13
  127.9 1.3 collective-permute-start.18
  150.1 5.1 %collective-permute-start.23 = (f32[48,128]{1,0:T(8,128)S(1)}, f32[48,128]{1,0:T(8,128)S(1)}, u32[]{:S(2)}, u32[]{:S(2)}) collective-permute-start(f32[48,128]{1,0:T(8,128)S(1)} %pad_maximum_fusion.6), channel_id=1, source_target_pairs={{0,8},{4,12},{8,16},{12,20},{16,24},{20,28},{24,0},{28,4},{32,40},... | collective-permute-start | bytes 73736 | tf_op jit(solution)/shard_map/ppermute | solution.py:476
  150.2 5.4 %collective-permute-start.24 = (f32[48,128]{1,0:T(8,128)S(1)}, f32[48,128]{1,0:T(8,128)S(1)}, u32[]{:S(2)}, u32[]{:S(2)}) collective-permute-start(f32[48,128]{1,0:T(8,128)S(1)} %pad_maximum_fusion.6), channel_id=1, source_target_pairs={{0,16},{4,20},{8,24},{12,28},{16,0},{20,4},{24,8},{28,12},{32,48},... | collective-permute-start | bytes 73736 | tf_op jit(solution)/shard_map/ppermute | solution.py:476
  152.3 3.3 %collective-permute-start.25 = (f32[48,128]{1,0:T(8,128)S(1)}, f32[48,128]{1,0:T(8,128)S(1)}, u32[]{:S(2)}, u32[]{:S(2)}) collective-permute-start(f32[48,128]{1,0:T(8,128)S(1)} %pad_maximum_fusion.6), channel_id=1, source_target_pairs={{0,24},{4,28},{8,0},{12,4},{16,8},{20,12},{24,16},{28,20},{32,56},... | collective-permute-start | bytes 73736 | tf_op jit(solution)/shard_map/ppermute | solution.py:476
  152.8 5.5 %collective-permute-start.10 = (f32[4,128]{1,0:T(4,128)S(1)}, f32[4,128]{1,0:T(4,128)S(1)}, u32[]{:S(2)}, u32[]{:S(2)}) collective-permute-start(f32[4,128]{1,0:T(4,128)S(1)} %get-tuple-element.40), channel_id=1, source_target_pairs={{0,1},{1,2},{2,3},{3,0},{4,5},{5,6},{6,7},{7,4},{8,9},{9,10},{10,1... | collective-permute-start | bytes 6152 | tf_op jit(solution)/shard_map/ppermute | solution.py:476
  152.8 6.5 %collective-permute-start.11 = (f32[4,128]{1,0:T(4,128)S(1)}, f32[4,128]{1,0:T(4,128)S(1)}, u32[]{:S(2)}, u32[]{:S(2)}) collective-permute-start(f32[4,128]{1,0:T(4,128)S(1)} %get-tuple-element.40), channel_id=1, source_target_pairs={{0,2},{1,3},{2,0},{3,1},{4,6},{5,7},{6,4},{7,5},{8,10},{9,11},{10,... | collective-permute-start | bytes 6152 | tf_op jit(solution)/shard_map/ppermute | solution.py:476
  155.2 4.2 %collective-permute-start.12 = (f32[4,128]{1,0:T(4,128)S(1)}, f32[4,128]{1,0:T(4,128)S(1)}, u32[]{:S(2)}, u32[]{:S(2)}) collective-permute-start(f32[4,128]{1,0:T(4,128)S(1)} %get-tuple-element.40), channel_id=1, source_target_pairs={{0,3},{1,0},{2,1},{3,2},{4,7},{5,4},{6,5},{7,6},{8,11},{9,8},{10,9... | collective-permute-start | bytes 6152 | tf_op jit(solution)/shard_map/ppermute | solution.py:476
  155.6 4.0 %collective-permute-start.26 = (f32[48,128]{1,0:T(8,128)S(1)}, f32[48,128]{1,0:T(8,128)S(1)}, u32[]{:S(2)}, u32[]{:S(2)}) collective-permute-start(f32[48,128]{1,0:T(8,128)S(1)} %pad_maximum_fusion.7), channel_id=1, source_target_pairs={{0,32},{4,36},{8,40},{12,44},{16,48},{20,52},{24,56},{28,60},{32,6... | collective-permute-start | bytes 73736 | tf_op jit(solution)/shard_map/ppermute | solution.py:476
  156.8 4.2 %collective-permute-start.27 = (f32[48,128]{1,0:T(8,128)S(1)}, f32[48,128]{1,0:T(8,128)S(1)}, u32[]{:S(2)}, u32[]{:S(2)}) collective-permute-start(f32[48,128]{1,0:T(8,128)S(1)} %pad_maximum_fusion.7), channel_id=1, source_target_pairs={{0,64},{4,68},{8,72},{12,76},{16,80},{20,84},{24,88},{28,92},{32,9... | collective-permute-start | bytes 73736 | tf_op jit(solution)/shard_map/ppermute | solution.py:476
  158.3 2.7 %collective-permute-start.28 = (f32[48,128]{1,0:T(8,128)S(1)}, f32[48,128]{1,0:T(8,128)S(1)}, u32[]{:S(2)}, u32[]{:S(2)}) collective-permute-start(f32[48,128]{1,0:T(8,128)S(1)} %pad_maximum_fusion.7), channel_id=1, source_target_pairs={{0,96},{4,100},{8,104},{12,108},{16,112},{20,116},{24,120},{28,124... | collective-permute-start | bytes 73736 | tf_op jit(solution)/shard_map/ppermute | solution.py:476
  190.2 3.8 %collective-permute-start.29 = (f32[16,128]{1,0:T(8,128)S(1)}, f32[16,128]{1,0:T(8,128)S(1)}, u32[]{:S(2)}, u32[]{:S(2)}) collective-permute-start(f32[16,128]{1,0:T(8,128)S(1)} %pad_maximum_fusion.9), channel_id=1, source_target_pairs={{0,1},{1,2},{2,3},{3,0},{4,5},{5,6},{6,7},{7,4},{8,9},{9,10},{10,1... | collective-permute-start | bytes 24584 | tf_op jit(solution)/shard_map/ppermute | solution.py:476
  190.3 4.1 %collective-permute-start.30 = (f32[16,128]{1,0:T(8,128)S(1)}, f32[16,128]{1,0:T(8,128)S(1)}, u32[]{:S(2)}, u32[]{:S(2)}) collective-permute-start(f32[16,128]{1,0:T(8,128)S(1)} %pad_maximum_fusion.9), channel_id=1, source_target_pairs={{0,2},{1,3},{2,0},{3,1},{4,6},{5,7},{6,4},{7,5},{8,10},{9,11},{10,... | collective-permute-start | bytes 24584 | tf_op jit(solution)/shard_map/ppermute | solution.py:476
  190.4 4.3 %collective-permute-start.31 = (f32[16,128]{1,0:T(8,128)S(1)}, f32[16,128]{1,0:T(8,128)S(1)}, u32[]{:S(2)}, u32[]{:S(2)}) collective-permute-start(f32[16,128]{1,0:T(8,128)S(1)} %pad_maximum_fusion.9), channel_id=1, source_target_pairs={{0,3},{1,0},{2,1},{3,2},{4,7},{5,4},{6,5},{7,6},{8,11},{9,8},{10,9... | collective-permute-start | bytes 24584 | tf_op jit(solution)/shard_map/ppermute | solution.py:476
  194.7 5.8 %collective-permute-start.32 = (f32[52,128]{1,0:T(8,128)S(1)}, f32[52,128]{1,0:T(8,128)S(1)}, u32[]{:S(2)}, u32[]{:S(2)}) collective-permute-start(f32[52,128]{1,0:T(8,128)S(1)} %pad_maximum_fusion.5), channel_id=1, source_target_pairs={{0,4},{4,0},{8,12},{12,8},{16,20},{20,16},{24,28},{28,24},{32,36},... | collective-permute-start | bytes 79880 | tf_op jit(solution)/shard_map/ppermute | solution.py:476
  200.5 18.1 %copy-start.6 = (f32[4096]{0:T(1024)S(1)}, f32[4096]{0:T(1024)}, u32[]{:S(2)}) copy-start(f32[4096]{0:T(1024)} %param.9) | copy-start | bytes 49156
  203.0 4.7 %collective-permute-start.33 = (f32[72,128]{1,0:T(8,128)S(1)}, f32[72,128]{1,0:T(8,128)S(1)}, u32[]{:S(2)}, u32[]{:S(2)}) collective-permute-start(f32[72,128]{1,0:T(8,128)S(1)} %pad_maximum_fusion.1), channel_id=1, source_target_pairs={{0,8},{4,12},{8,16},{12,20},{16,24},{20,28},{24,0},{28,4},{32,40},... | collective-permute-start | bytes 110600 | tf_op jit(solution)/shard_map/ppermute | solution.py:476
  204.5 4.3 %collective-permute-start.34 = (f32[72,128]{1,0:T(8,128)S(1)}, f32[72,128]{1,0:T(8,128)S(1)}, u32[]{:S(2)}, u32[]{:S(2)}) collective-permute-start(f32[72,128]{1,0:T(8,128)S(1)} %pad_maximum_fusion.1), channel_id=1, source_target_pairs={{0,16},{4,20},{8,24},{12,28},{16,0},{20,4},{24,8},{28,12},{32,48},... | collective-permute-start | bytes 110600 | tf_op jit(solution)/shard_map/ppermute | solution.py:476
  205.8 3.3 %collective-permute-start.35 = (f32[72,128]{1,0:T(8,128)S(1)}, f32[72,128]{1,0:T(8,128)S(1)}, u32[]{:S(2)}, u32[]{:S(2)}) collective-permute-start(f32[72,128]{1,0:T(8,128)S(1)} %pad_maximum_fusion.1), channel_id=1, source_target_pairs={{0,24},{4,28},{8,0},{12,4},{16,8},{20,12},{24,16},{28,20},{32,56},... | collective-permute-start | bytes 110600 | tf_op jit(solution)/shard_map/ppermute | solution.py:476
  209.2 4.3 %collective-permute-start.36 = (f32[72,128]{1,0:T(8,128)S(1)}, f32[72,128]{1,0:T(8,128)S(1)}, u32[]{:S(2)}, u32[]{:S(2)}) collective-permute-start(f32[72,128]{1,0:T(8,128)S(1)} %pad_maximum_fusion.2), channel_id=1, source_target_pairs={{0,32},{4,36},{8,40},{12,44},{16,48},{20,52},{24,56},{28,60},{32,6... | collective-permute-start | bytes 110600 | tf_op jit(solution)/shard_map/ppermute | solution.py:476
  210.0 4.3 %collective-permute-start.37 = (f32[72,128]{1,0:T(8,128)S(1)}, f32[72,128]{1,0:T(8,128)S(1)}, u32[]{:S(2)}, u32[]{:S(2)}) collective-permute-start(f32[72,128]{1,0:T(8,128)S(1)} %pad_maximum_fusion.2), channel_id=1, source_target_pairs={{0,64},{4,68},{8,72},{12,76},{16,80},{20,84},{24,88},{28,92},{32,9... | collective-permute-start | bytes 110600 | tf_op jit(solution)/shard_map/ppermute | solution.py:476
  212.5 3.1 %collective-permute-start.38 = (f32[72,128]{1,0:T(8,128)S(1)}, f32[72,128]{1,0:T(8,128)S(1)}, u32[]{:S(2)}, u32[]{:S(2)}) collective-permute-start(f32[72,128]{1,0:T(8,128)S(1)} %pad_maximum_fusion.2), channel_id=1, source_target_pairs={{0,96},{4,100},{8,104},{12,108},{16,112},{20,116},{24,120},{28,124... | collective-permute-start | bytes 110600 | tf_op jit(solution)/shard_map/ppermute | solution.py:476
  215.6 3.8 %collective-permute-start.39 = (f32[8,128]{1,0:T(8,128)S(1)}, f32[8,128]{1,0:T(8,128)S(1)}, u32[]{:S(2)}, u32[]{:S(2)}) collective-permute-start(f32[8,128]{1,0:T(8,128)S(1)} %bitcast_reduce_fusion.1), channel_id=1, source_target_pairs={{0,4},{4,0},{8,12},{12,8},{16,20},{20,16},{24,28},{28,24},{32,36},... | collective-permute-start | bytes 12296 | tf_op jit(solution)/shard_map/ppermute | solution.py:476
  219.4 5.5 %collective-permute-start.40 = (f32[12,128]{1,0:T(8,128)S(1)}, f32[12,128]{1,0:T(8,128)S(1)}, u32[]{:S(2)}, u32[]{:S(2)}) collective-permute-start(f32[12,128]{1,0:T(8,128)S(1)} %pad_maximum_fusion.10), channel_id=1, source_target_pairs={{0,1},{1,2},{2,3},{3,0},{4,5},{5,6},{6,7},{7,4},{8,9},{9,10},{10,1... | collective-permute-start | bytes 18440 | tf_op jit(solution)/shard_map/ppermute | solution.py:476
  221.2 4.0 %collective-permute-start.41 = (f32[12,128]{1,0:T(8,128)S(1)}, f32[12,128]{1,0:T(8,128)S(1)}, u32[]{:S(2)}, u32[]{:S(2)}) collective-permute-start(f32[12,128]{1,0:T(8,128)S(1)} %pad_maximum_fusion.10), channel_id=1, source_target_pairs={{0,2},{1,3},{2,0},{3,1},{4,6},{5,7},{6,4},{7,5},{8,10},{9,11},{10,... | collective-permute-start | bytes 18440 | tf_op jit(solution)/shard_map/ppermute | solution.py:476
  223.1 2.8 %collective-permute-start.42 = (f32[12,128]{1,0:T(8,128)S(1)}, f32[12,128]{1,0:T(8,128)S(1)}, u32[]{:S(2)}, u32[]{:S(2)}) collective-permute-start(f32[12,128]{1,0:T(8,128)S(1)} %pad_maximum_fusion.10), channel_id=1, source_target_pairs={{0,3},{1,0},{2,1},{3,2},{4,7},{5,4},{6,5},{7,6},{8,11},{9,8},{10,9... | collective-permute-start | bytes 18440 | tf_op jit(solution)/shard_map/ppermute | solution.py:476

commit v2 on v1

--- a/solution.py
+++ b/solution.py
@@ -48,23 +48,36 @@
     return out
 
 
-def sweep(d_ref, base, chunks, u, vs_ref, rowacc_ref):
+def row_block(r):
+    if isinstance(r, int):
+        return slice(r * ROWS, (r + 1) * ROWS)
+    return pl.ds(pl.multiple_of(r * ROWS, ROWS), ROWS)
+
+
+def sweep(d_ref, base, chunks, u, vs_ref, rowacc_ref, straight=False, keep=None):
     rows = d_ref.shape[0]
 
     def body(r, cols):
-        at = pl.ds(pl.multiple_of(r * ROWS, ROWS), ROWS)
+        at = row_block(r)
         vs = vs_ref[at, :]
         racc = rowacc_ref[at, :]
         out = []
         for c in range(chunks):
-            p = jnp.exp2((d_ref[at, pl.ds(base + c * LANES, LANES)] + u[c]) + vs)
+            d = d_ref[at, pl.ds(base + c * LANES, LANES)]
+            if keep is not None:
+                keep[0][at, pl.ds(pl.multiple_of(keep[1] + c * LANES, LANES), LANES)] = d
+            p = jnp.exp2((d + u[c]) + vs)
             racc = racc + p
             out.append(cols[c] + jnp.sum(p.reshape(ROWS // 8, 8, LANES), axis=0))
         rowacc_ref[at, :] = racc
         return tuple(out)
 
-    zero = jnp.zeros((8, LANES), F32)
-    cols = lax.fori_loop(0, rows // ROWS, body, (zero,) * chunks, unroll=2)
+    cols = (jnp.zeros((8, LANES), F32),) * chunks
+    if straight:
+        for r in range(rows // ROWS):
+            cols = body(r, cols)
+    else:
+        cols = lax.fori_loop(0, rows // ROWS, body, cols, unroll=2)
     return [jnp.sum(c, axis=0, keepdims=True) for c in cols]
 
 
@@ -170,21 +183,34 @@
 
 
 def first_kernel(
-    offset, gen_ref, ref_hbm, gweight_ref, rweight_ref, d_ref, lrow_ref, lcol_ref, hrow_ref, hcol_ref, mass_ref,
-    tile_ref, u_ref, v_ref, vs_ref, rowacc_ref, colsum_ref, peak_ref, sem,
+    offset, gen_ref, ref_hbm, gweight_hbm, rweight_hbm,
+    d_ref, lrow_ref, lcol_ref, hrow_ref, hcol_ref, mass_ref, *refs,
 ):
+    if offset == 0:
+        held_ref, *refs = refs
+    tile_ref, stage_ref, gweight_ref, rweight_ref, u_ref, v_ref, vs_ref, rowacc_ref, colsum_ref, peak_ref, sem = refs
     rows, width = gen_ref.shape
     nq, nc = rows // LANES, d_ref.shape[1] // LANES
     chunks = TILE // LANES
     steps = d_ref.shape[1] // TILE
     half_scale = 0.5 * LOG2E / (EPS * width)
     dot_scale = LOG2E / (EPS * width)
-
-    def load(j, slot):
+    loads = []
+    if offset == 0:
+        loads.append(pltpu.make_async_copy(gen_ref, held_ref, sem.at[steps + 2]))
+        gen_ref = held_ref
+    loads.append(pltpu.make_async_copy(gweight_hbm, gweight_ref, sem.at[steps]))
+    loads.append(pltpu.make_async_copy(rweight_hbm, rweight_ref, sem.at[steps + 1]))
+
+    def load(j):
         at = pl.ds(pl.multiple_of((offset * steps + j) * TILE, TILE), TILE)
-        return pltpu.make_async_copy(ref_hbm.at[at, :], tile_ref.at[slot], sem.at[slot])
-
-    load(0, 0).start()
+        return pltpu.make_async_copy(ref_hbm.at[at, :], tile_ref.at[j], sem.at[j])
+
+    tiles = [load(j) for j in range(steps)]
+    for copy in loads[:1] + tiles[:1] + loads[1:] + tiles[1:]:
+        copy.start()
+    for copy in loads:
+        copy.wait()
     for q, part in enumerate(norms(gen_ref, 0, nq, half_scale)):
         hrow_ref[q : q + 1, :] = part
         v_ref[q : q + 1, :] = jnp.log2(gweight_ref[q : q + 1, :]) - part
@@ -192,37 +218,34 @@
     lrow_ref[nq : 2 * nq, :] = jnp.broadcast_to(jnp.sum(rweight_ref[...]).reshape(1, 1), (nq, LANES))
     mass_ref[...] = jnp.broadcast_to(jnp.sum(gweight_ref[...]).reshape(1, 1), (8, LANES))
 
+    def product(j):
+        for c, half in enumerate(norms(tile_ref.at[j], 0, chunks, half_scale)):
+            row = pl.ds(j * chunks + c, 1)
+            hcol_ref[row, :] = half
+            u_ref[row, :] = jnp.log2(rweight_ref[pl.ds(offset * nc + j * chunks + c, 1), :]) - half
+        dots = lax.dot_general(
+            gen_ref[...], tile_ref[j], (((1,), (1,)), ((), ())), preferred_element_type=F32
+        )
+        stage_ref[...] = dots * dot_scale
+
+    def sums(j, straight):
+        mine = [u_ref[pl.ds(j * chunks + c, 1), :] for c in range(chunks)]
+        found = sweep(stage_ref, 0, chunks, mine, vs_ref, rowacc_ref, straight, (d_ref, j * TILE))
+        for c, part in enumerate(found):
+            colsum_ref[pl.ds(j * chunks + c, 1), :] = part
+
+    tiles[0].wait()
+    product(0)
+    start_peak(stage_ref, u_ref[0:1, :], v_ref, vs_ref, peak_ref, rowacc_ref)
+
     def step(j, carry):
-        slot = lax.rem(j, 2)
-
-        @pl.when(j + 1 < steps)
-        def _():
-            load(j + 1, 1 - slot).start()
-
-        load(j, slot).wait()
-        tile = tile_ref.at[slot]
-        half = norms(tile, 0, chunks, half_scale)
-        u = []
-        for c in range(chunks):
-            row = pl.ds(j * chunks + c, 1)
-            hcol_ref[row, :] = half[c]
-            u.append(jnp.log2(rweight_ref[pl.ds(offset * nc + j * chunks + c, 1), :]) - half[c])
-            u_ref[row, :] = u[c]
-        base = pl.multiple_of(j * TILE, TILE)
-        dots = lax.dot_general(
-            gen_ref[...], tile[...], (((1,), (1,)), ((), ())), preferred_element_type=F32
-        )
-        d_ref[:, pl.ds(base, TILE)] = dots * dot_scale
-
-        @pl.when(j == 0)
-        def _():
-            start_peak(d_ref, u[0], v_ref, vs_ref, peak_ref, rowacc_ref)
-
-        for c, part in enumerate(sweep(d_ref, base, chunks, u, vs_ref, rowacc_ref)):
-            colsum_ref[pl.ds(j * chunks + c, 1), :] = part
+        load(j).wait()
+        sums(j - 1, True)
+        product(j)
         return carry
 
-    lax.fori_loop(0, steps, step, 0)
+    lax.fori_loop(1, steps, step, 0)
+    sums(steps - 1, False)
     finish([d_ref], u_ref, v_ref, vs_ref, rowacc_ref, colsum_ref, peak_ref, lrow_ref, lcol_ref)
 
 
@@ -231,24 +254,29 @@
     cols = ref.shape[0] // pieces
     nq, nc = rows // LANES, cols // LANES
     vmem = pl.BlockSpec(memory_space=pltpu.VMEM)
+    hbm = pl.BlockSpec(memory_space=pltpu.HBM)
     vec = lambda n: jax.ShapeDtypeStruct((n, LANES), F32)
+    held = () if piece else (pltpu.VMEM((rows, width), gen.dtype),)
     return pl.pallas_call(
         functools.partial(first_kernel, piece),
-        in_specs=[vmem, pl.BlockSpec(memory_space=pltpu.HBM), vmem, vmem],
-        out_shape=(pltpu.VMEM((rows, cols), F32), vec(2 * nq), vec(nc), vec(2 * nq), vec(nc), vec(8)),
-        out_specs=(vmem,) * 6,
+        in_specs=[vmem if piece else hbm, hbm, hbm, hbm],
+        out_shape=(pltpu.VMEM((rows, cols), F32), vec(2 * nq), vec(nc), vec(2 * nq), vec(nc), vec(8)) + held,
+        out_specs=(vmem,) * (6 + len(held)),
         scratch_shapes=[
-            pltpu.VMEM((2, TILE, width), jnp.bfloat16),
+            pltpu.VMEM((cols // TILE, TILE, width), jnp.bfloat16),
+            pltpu.VMEM((rows, TILE), F32),
+            pltpu.VMEM((nq, LANES), F32),
+            pltpu.VMEM(rweight.shape, F32),
             pltpu.VMEM((nc, LANES), F32),
             pltpu.VMEM((nq, LANES), F32),
             pltpu.VMEM((rows, LANES), F32),
             pltpu.VMEM((rows, LANES), F32),
             pltpu.VMEM((nc, LANES), F32),
             pltpu.VMEM((8, LANES), F32),
-            pltpu.SemaphoreType.DMA((2,)),
+            pltpu.SemaphoreType.DMA((cols // TILE + 3,)),
         ],
         compiler_params=pltpu.CompilerParams(vmem_limit_bytes=16 << 20),
-    )(vmem_array(gen), hbm_array(ref), gweight, rweight)
+    )(vmem_array(gen) if piece else hbm_array(gen), hbm_array(ref), gweight, rweight)
 
 
 def next_kernel(count, *refs):
@@ -295,78 +323,76 @@
 def self_first_kernel(count, first, *refs):
     own_ref, mate_ref = refs[:2]
     sources = refs[2 : 2 + count]
-    mine_ref, theirs_ref, place_ref, e_ref, z_ref = refs[2 + count : 7 + count]
-    piece_ref, hs_ref, ws_ref, sem = refs[7 + count :]
+    rest = refs[2 + count :]
     half, width = own_ref.shape
-    rows = 2 * half
-    tall = piece_ref.shape[0] // count
-    chunks = tall // LANES
+    nq = half // LANES
+    if first == 0:
+        mine_ref, theirs_ref, place_ref, e_ref, z_ref, hs_ref, ws_ref = rest
+        for at, vec_ref in ((0, mine_ref), (nq, theirs_ref)):
+            spread(vec_ref, hs_ref, nq, 0, at)
+            spread(vec_ref, ws_ref, nq, nq, at)
+    else:
+        hs_ref, ws_ref, place_ref, e_ref, z_ref = rest
+    wide = 256
+    chunks = wide // LANES
     half_scale = 0.5 * LOG2E / (EPS * width)
     dot_scale = LOG2E / (EPS * width)
-
-    def load(t, src):
-        at = pl.ds(pl.multiple_of(t * tall, tall), tall)
-        return pltpu.make_async_copy(src, piece_ref.at[at, :], sem.at[t])
-
-    for t, src in enumerate(sources):
-        load(t, src).start()
-    nq = half // LANES
-    for at, vec_ref in ((0, mine_ref), (nq, theirs_ref)):
-        spread(vec_ref, hs_ref, nq, 0, at)
-        spread(vec_ref, ws_ref, nq, nq, at)
     z_ref[...] = jnp.zeros_like(z_ref)
-    zero = jnp.zeros((8, LANES), F32)
-
-    def tile(t, carry):
-        load(t, sources[0]).wait()
-        base = pl.multiple_of(t * tall, tall)
-        view = piece_ref.at[pl.ds(base, tall), :]
-        piece_half = norms(view, 0, chunks, half_scale)
+    tiles = [(src, k) for src in sources for k in range(src.shape[0] // wide)]
+    piece_half = {}
+
+    def product(t):
+        src, k = tiles[t]
+        view = src.at[k * wide : (k + 1) * wide, :]
+        piece_half[t] = norms(view, 0, chunks, half_scale)
         for h, rows_ref in enumerate((own_ref, mate_ref)):
-            e_ref[h * half : (h + 1) * half, pl.ds(base, tall)] = lax.dot_general(
+            e_ref[h * half : (h + 1) * half, t * wide : (t + 1) * wide] = lax.dot_general(
                 rows_ref[...], view[...], (((1,), (1,)), ((), ())), preferred_element_type=F32
             )
 
+    def sums(t, straight):
         def body(r, acc):
-            at = pl.ds(pl.multiple_of(r * ROWS, ROWS), ROWS)
+            at = row_block(r)
             hs = hs_ref[at, :]
             ws = ws_ref[at, :]
             out = []
             for c in range(chunks):
-                part = pl.ds(base + c * LANES, LANES)
-                e = jnp.exp2(e_ref[at, part] * dot_scale - (hs + piece_half[c]))
+                part = slice(t * wide + c * LANES, t * wide + (c + 1) * LANES)
+                e = jnp.exp2(e_ref[at, part] * dot_scale - (hs + piece_half[t][c]))
                 e_ref[at, part] = e
                 out.append(acc[c] + jnp.sum((e * ws).reshape(ROWS // 8, 8, LANES), axis=0))
             return tuple(out)
 
-        acc = lax.fori_loop(0, rows // ROWS, body, (zero,) * chunks, unroll=2)
+        acc = (jnp.zeros((8, LANES), F32),) * chunks
+        if straight:
+            for r in range(2 * half // ROWS):
+                acc = body(r, acc)
+        else:
+            acc = lax.fori_loop(0, 2 * half // ROWS, body, acc, unroll=2)
         for c in range(chunks):
             z_ref[pl.ds(place_ref[first + t * chunks + c], 1), :] = jnp.sum(acc[c], axis=0, keepdims=True)
-        return carry
-
-    lax.fori_loop(0, count, tile, 0)
-
-
-def self_first(own, mate, sources, mine, theirs, place, first):
-    rows, width = 2 * own.shape[0], own.shape[1]
-    count, tall = len(sources), sources[0].shape[0]
-    cols = count * tall
+
+    product(0)
+    for t in range(1, len(tiles)):
+        sums(t - 1, True)
+        product(t)
+    sums(len(tiles) - 1, False)
+
+
+def self_first(own, mate, sources, left, right, place, first):
+    rows = 2 * own.shape[0]
+    cols = sum(src.shape[0] for src in sources)
     vmem = pl.BlockSpec(memory_space=pltpu.VMEM)
+    lanes = () if first else (pltpu.VMEM((rows, LANES), F32),) * 2
+    if first:
+        left, right = vmem_array(left), vmem_array(right)
     return pl.pallas_call(
-        functools.partial(self_first_kernel, count, first),
-        in_specs=[vmem, vmem]
-        + [pl.BlockSpec(memory_space=pl.ANY)] * count
-        + [vmem, vmem, pl.BlockSpec(memory_space=pltpu.SMEM)],
-        out_shape=(pltpu.VMEM((rows, cols), F32), jax.ShapeDtypeStruct((place.shape[0], LANES), F32)),
-        out_specs=(vmem, vmem),
-        scratch_shapes=[
-            pltpu.VMEM((cols, width), jnp.bfloat16),
-            pltpu.VMEM((rows, LANES), F32),
-            pltpu.VMEM((rows, LANES), F32),
-            pltpu.SemaphoreType.DMA((count,)),
-        ],
-        compiler_params=pltpu.CompilerParams(vmem_limit_bytes=16 << 20),
-    )(vmem_array(own), vmem_array(mate), *sources, mine, theirs, place)
+        functools.partial(self_first_kernel, len(sources), first),
+        in_specs=[vmem] * (4 + len(sources)) + [pl.BlockSpec(memory_space=pltpu.SMEM)],
+        out_shape=(pltpu.VMEM((rows, cols), F32), jax.ShapeDtypeStruct((place.shape[0], LANES), F32)) + lanes,
+        out_specs=(vmem,) * (2 + len(lanes)),
+        compiler_params=pltpu.CompilerParams(vmem_limit_bytes=8 << 20),
+    )(vmem_array(own), vmem_array(mate), *[vmem_array(src) for src in sources], left, right, place)
 
 
 def self_cols_kernel(count, *refs):
@@ -483,6 +509,11 @@
 
     def stage(value, axis, perms, logs):
         return merge([value] + shift(value, axis, perms), logs)
+
+    def doubled(value, logs):
+        for bit in (1, 2):
+            value = merge([value, lax.ppermute(value, "ref", [(i, i ^ bit) for i in range(n_ref)])], logs)
+        return value
 
     def run(gen_features, gen_weight, ref_features, ref_weight, ref_self):
         gen_count = gen_features.shape[0]
@@ -521,19 +552,19 @@
         low_far = lax.ppermute(up[: 2 * LANES], "gen", second_axis[1])
         high_far = lax.ppermute(down[2 * LANES :], "gen", second_axis[3])
 
-        d0, row0, lcol0, mine, hcol0, gmass = first_pass(gen_features, ref_features, wg, wr, 0, 2)
+        d0, row0, lcol0, mine, hcol0, gmass, held = first_pass(gen_features, ref_features, wg, wr, 0, 2)
         theirs = lax.ppermute(mine, "gen", core_stage[0])
-        d1, row1, lcol1, _, hcol1, _ = first_pass(gen_features, ref_features, wg, wr, 1, 2)
+        d1, row1, lcol1, _, hcol1, _ = first_pass(held, ref_features, wg, wr, 1, 2)
         hcol = jnp.concatenate([hcol0, hcol1], axis=0)
         hrow = mine[:nq]
         weight = jnp.concatenate([wg, theirs[nq:]], axis=0)
-        e0, z1_0 = self_first(gen_features, mate, [near], mine, theirs, place, 0)
-        e1, z1_1 = self_first(gen_features, mate, [up, down], mine, theirs, place, 4)
-        e2, z1_2 = self_first(gen_features, mate, [low_far, high_far], mine, theirs, place, 12)
+        e0, z1_0, hs, ws = self_first(held, mate, [near], mine, theirs, place, 0)
+        e1, z1_1 = self_first(held, mate, [up, down], hs, ws, place, 4)
+        e2, z1_2 = self_first(held, mate, [low_far, high_far], hs, ws, place, 12)
         e = [e0, e1, e2]
 
         row_part = jnp.concatenate([log_add([row0[:nq], row1[:nq]]), row0[nq:]], axis=0)
-        row_part = stage(row_part, "ref", ref_stage, nq)
+        row_part = doubled(row_part, nq)
         col_part = jnp.concatenate([lcol0, lcol1, gmass], axis=0)
         col_part = stage(col_part, "gen", core_stage, nc)
         col_part = jnp.concatenate([col_part, to_cols(wg)], axis=0)
@@ -551,7 +582,7 @@
         share = wg / gmass
 
         lrow, lcol = next_pass([d0, d1], ubase + c, vbase + f)
-        lrow = stage(lrow, "ref", ref_stage, nq)
+        lrow = doubled(lrow, nq)
         lcol = stage(lcol, "gen", core_stage, nc)
         col_part = jnp.concatenate([lcol, z1_0 + z1_1 + z1_2], axis=0)
         col_part = stage(col_part, "gen", y_stage, nc)
@@ -595,7 +626,7 @@
         row_part = jnp.concatenate([to_rows(s3), part], axis=0)
         row_part = row_part + sum(shift(row_part, "ref", ref_stage))
         gen_gap = (f - row_part[:nq]) * unit
-        divergence = unit * jnp.sum(f_part) + jnp.sum(row_part[nq:])
+        divergence = jnp.sum(unit * f_part + row_part[nq : 2 * nq] + row_part[2 * nq :])
         return gen_gap.reshape(gen_count), ref_gap.reshape(ref_count), divergence
 
     return run

time: 230 us -> 218 us (0.948)
  Pallas kernels: 124 us -> 117 us
  starting transfers between devices: 61.7 us -> 57.5 us
  waiting for transfers between devices: 31.8 us -> 34.7 us
  between operations: 3.51 us -> 1.09 us
    ppermute x34 -> x28, starting transfers between devices: 46.6 us -> 37.1 us  [shift(): return [lax.ppermute(value, axis, perm) for perm in perms]]
    pallas_call x5, Pallas kernels: 65.5 us -> 58.5 us  [the longest x2 44.4 us: first_pass(): pl.pallas_call(functools.partial(first_kernel, piece), in_specs=[vmem if...]
    ppermute x0 -> x4, starting transfers between devices: none -> 6.9 us  [doubled(): lax.ppermute(value, 'ref', [(i, i ^ bit) for i in range(n_ref)])]
    ppermute x34 -> x28, waiting for transfers between devices: 31.7 us -> 33.3 us  [shift(): return [lax.ppermute(value, axis, perm) for perm in perms]]
  transfers between devices with their start and end apart: 43 -> 41, of which waited for: 18 -> 19; matrix products, arithmetic and copies ran while one was open for 1% -> 1% of each run, Pallas kernels for 38% -> 39%
where the time goes in v2:
time: 218 us; the launch traced here: 217 us
  Pallas kernels  117 us (54%)
  starting transfers between devices  57.5 us (26%)
  waiting for transfers between devices  34.7 us (16%)
  other arithmetic  4.13 us (2%)
  local copies, waits for them, and re-layouts  2.85 us (1%)
    pallas_call x2, Pallas kernels, next_pass(): pl.pallas_call(functools.partial(next_kernel, len(parts)), in_specs=[vmem...  53.8 us
    pallas_call x2, Pallas kernels, first_pass(): pl.pallas_call(functools.partial(first_kernel, piece), in_specs=[vmem if...  44.4 us
    ppermute x28, starting transfers between devices, shift(): return [lax.ppermute(value, axis, perm) for perm in perms]  37.1 us
    ppermute x28, waiting for transfers between devices, shift(): return [lax.ppermute(value, axis, perm) for perm in perms]  33.3 us
    pallas_call x3, Pallas kernels, self_first(): pl.pallas_call(functools.partial(self_first_kernel, len(sources), first),...  14 us
    ppermute x4, starting transfers between devices, doubled(): lax.ppermute(value, 'ref', [(i, i ^ bit) for i in range(n_ref)])  6.9 us
    ppermute x3, starting transfers between devices, run(): got = [lax.ppermute(own, 'gen', first_axis[k]) for k in (1, 2, 3)]  6.55 us
    pallas_call x2, Pallas kernels, self_apply(): pl.pallas_call(functools.partial(kernel, len(parts)), in_specs=[vmem] * (...  4.54 us
  transfers between devices with their start and end apart: 41, of which 19 were waited for; matrix products, arithmetic and copies ran while one was open for 1% of the time, Pallas kernels for 39%

profile of v2, /device:TPU:1, one launch (start us, length us, event | category | flops | bytes accessed | tf_op | source)
XLA Modules:
  0.0 217.1 jit_solution(5857074597934466152)
XLA Ops:
  0.6 1.1 constant_dynamic-slice_fusion
  1.7 2.5 %collective-permute-start.13 = (bf16[128,2048]{1,0:T(8,128)(2,1)S(1)}, bf16[128,2048]{1,0:T(8,128)(2,1)S(1)}, u32[]{:S(2)}, u32[]{:S(2)}) collective-permute-start(bf16[128,2048]{1,0:T(8,128)(2,1)S(1)} %constant_dynamic-slice_fusion), channel_id=1, source_target_pairs={{0,8},{4,36},{8,16},{12,44},{16,24},{20,52},{24,0},{28,60},{32,40}... | collective-permute-start | bytes 1572872 | tf_op jit(solution)/shard_map/ppermute | solution.py:547
  4.2 3.3 %collective-permute-start.14 = (bf16[128,2048]{1,0:T(8,128)(2,1)S(1)}, bf16[128,2048]{1,0:T(8,128)(2,1)}, u32[]{:S(2)}, u32[]{:S(2)}) collective-permute-start(bf16[128,2048]{1,0:T(8,128)(2,1)S(1)} %constant_dynamic-slice_fusion), channel_id=1, source_target_pairs={{0,16},{4,68},{8,24},{12,76},{16,0},{20,84},{24,8},{28,92},{32,48}... | collective-permute-start | bytes 1572872 | tf_op jit(solution)/shard_map/ppermute | solution.py:547
  7.5 0.7 collective-permute-start.15
  8.3 0.8 collective-permute-start.12
  9.3 0.7 copy-done
  10.0 0.7 copy-done.2
  10.7 22.2 %shard_map.76 = (f32[512,2048]{1,0:T(8,128)S(1)}, f32[8,128]{1,0:T(8,128)S(1)}, f32[16,128]{1,0:T(8,128)S(1)}, f32[8,128]{1,0:T(8,128)S(1)}, f32[16,128]{1,0:T(8...) custom-call(bf16[512,2048]{1,0:T(8,128)(2,1)} %gen_ref.1, bf16[4096,2048]{1,0:T(8,128)(2,1)} %ref_hbm.3, ...), custom_call_target="tpu_custom_call" | custom-call | tf_op jit(solution)/shard_map/pallas_call | solution.py:260
  32.9 22.2 %shard_map.77 = (f32[512,2048]{1,0:T(8,128)S(1)}, f32[8,128]{1,0:T(8,128)S(1)}, f32[16,128]{1,0:T(8,128)S(1)}, f32[8,128]{1,0:T(8,128)}, f32[16,128]{1,0:T(8,128)S(1)}, /*index=5*/f32[8,128]{1,0:T(8,128)}) custom-call(bf16[512,2048]{1,0:T(8,128)(2,1)S(1)} %get-tuple-element.33.gen_ref.refs_0_, bf16[4096,2048]{1,0:T(8,128)(2,1)} %ref_hbm.3, ...), custom_call_target="tpu_custom_call" | custom-call | tf_op jit(solution)/shard_map/pallas_call | solution.py:260
  55.3 1.3 collective-permute-start
  56.6 1.6 pad_maximum_fusion.refs_2_
  58.2 1.0 collective-permute-start.17
  59.2 1.7 collective-permute-start.18
  61.0 2.5 %collective-permute-start.1 = (f32[8,128]{1,0:T(8,128)S(1)}, f32[8,128]{1,0:T(8,128)S(1)}, u32[]{:S(2)}, u32[]{:S(2)}) collective-permute-start(f32[8,128]{1,0:T(8,128)S(1)} %pad_maximum_fusion.12), channel_id=1, source_target_pairs={{0,2},{1,3},{2,0},{3,1},{4,6},{5,7},{6,4},{7,5},{8,10},{9,11},{10,... | collective-permute-start | bytes 12296 | tf_op jit(solution)/shard_map/ppermute | solution.py:515
  63.6 1.4 collective-permute-done.1
  65.0 1.4 collective-permute-start.4
  66.4 19.2 %collective-permute-done.3 = f32[56,128]{1,0:T(8,128)S(1)} collective-permute-done((f32[56,128]{1,0:T(8,128)S(1)}, f32[56,128]{1,0:T(8,128)S(1)}, u32[]{:S(2)}, u32[]{:S(2)}) %collective-permute-start.3) | collective-permute-done | bytes 28704 | tf_op jit(solution)/shard_map/ppermute | solution.py:502
  85.6 1.2 collective-permute-start.5
  86.7 1.8 collective-permute-done.5
  88.6 1.3 collective-permute-start.6
  89.9 3.9 %collective-permute-start.7 = (f32[56,128]{1,0:T(8,128)S(1)}, f32[56,128]{1,0:T(8,128)S(1)}, u32[]{:S(2)}, u32[]{:S(2)}) collective-permute-start(f32[56,128]{1,0:T(8,128)S(1)} %pad_maximum_fusion.4), channel_id=1, source_target_pairs={{0,64},{4,68},{8,72},{12,76},{16,80},{20,84},{24,88},{28,92},{32,9... | collective-permute-start | bytes 86024 | tf_op jit(solution)/shard_map/ppermute | solution.py:502
  93.8 0.7 collective-permute-start.8
  94.9 2.7 %collective-permute-start.20 = (bf16[256,2048]{1,0:T(8,128)(2,1)S(1)}, bf16[256,2048]{1,0:T(8,128)(2,1)S(1)}, u32[]{:S(2)}, u32[]{:S(2)}) collective-permute-start(bf16[256,2048]{1,0:T(8,128)(2,1)S(1)} %slice.316), channel_id=1, source_target_pairs={{0,96},{4,28},{8,104},{12,4},{16,112},{20,12},{24,120},{28,20},{32... | collective-permute-start | bytes 3145736 | tf_op jit(solution)/shard_map/ppermute | solution.py:553
  97.7 26.9 %shard_map.78 = (f32[4,128]{1,0:T(4,128)S(1)}, f32[32,128]{1,0:T(8,128)S(1)}) custom-call(f32[512,2048]{1,0:T(8,128)S(1)} %get-tuple-element.35.refs_0_, f32[512,2048]{1,0:T(8,128)S(1)} %get-tuple-element.36.refs_1_, f32[32,128]{1,0:T(8,128)S(1)} %get-tuple-element.69.refs_2_, f32[4,128]{1,0:T(4,128)S(1)} %get-tuple-element.67.refs_3_), custom_call_target="tpu_custom_call" | custom-call | tf_op jit(solution)/shard_map/pallas_call | solution.py:308
  124.8 0.5 collective-permute-start.16
  125.3 0.7 collective-permute-done.11
  126.2 3.8 %shard_map.79 = (f32[1024,512]{1,0:T(8,128)S(1)}, f32[16,128]{1,0:T(8,128)S(1)}, f32[1024,128]{1,0:T(8,128)S(1)}, f32[1024,128]{1,0:T(8,128)S(1)}) custom-call(bf16[512,2048]{1,0:T(8,128)(2,1)S(1)} %get-tuple-element.33.gen_ref.refs_0_, bf16[512,2048]{1,0:T(8,128)(2,1)S(1)} %collective-permute-done.12.refs_1_, ...), custom_call_target="tpu_custom_call" | custom-call | tf_op jit(solution)/shard_map/pallas_call | solution.py:389
  130.0 6.5 %shard_map.80 = (f32[1024,1024]{1,0:T(8,128)S(1)}, f32[16,128]{1,0:T(8,128)S(1)}) custom-call(bf16[512,2048]{1,0:T(8,128)(2,1)S(1)} %get-tuple-element.33.gen_ref.refs_0_, bf16[512,2048]{1,0:T(8,128)(2,1)S(1)} %collective-permute-done.12.refs_1_, bf16[512,2048]{1,0:T(8,128)(2,1)S(1)} %collective-permute-done.17.refs_2_, ...), custom_call_target="tpu_custom_call" | custom-call | tf_op jit(solution)/shard_map/pallas_call | solution.py:389
  136.5 3.8 %shard_map.81 = (f32[1024,512]{1,0:T(8,128)S(1)}, f32[16,128]{1,0:T(8,128)S(1)}) custom-call(bf16[512,2048]{1,0:T(8,128)(2,1)S(1)} %get-tuple-element.33.gen_ref.refs_0_, bf16[512,2048]{1,0:T(8,128)(2,1)S(1)} %collective-permute-done.12.refs_1_, bf16[256,2048]{1,0:T(8,128)(2,1)S(1)} %collective-permute-done.19.refs_2_, ...), custom_call_target="tpu_custom_call" | custom-call | tf_op jit(solution)/shard_map/pallas_call | solution.py:389
  140.6 1.9 collective-permute-start.22
  142.5 0.8 collective-permute-start.23
  143.3 2.8 %collective-permute-start.10 = (f32[4,128]{1,0:T(4,128)S(1)}, f32[4,128]{1,0:T(4,128)S(1)}, u32[]{:S(2)}, u32[]{:S(2)}) collective-permute-start(f32[4,128]{1,0:T(4,128)S(1)} %multiply_add_fusion.6), channel_id=1, source_target_pairs={{0,2},{1,3},{2,0},{3,1},{4,6},{5,7},{6,4},{7,5},{8,10},{9,11},{10,... | collective-permute-start | bytes 6152 | tf_op jit(solution)/shard_map/ppermute | solution.py:515
  146.2 0.8 collective-permute-start.24
  147.0 1.9 collective-permute-start.25
  148.9 0.6 collective-permute-start.26
  149.5 0.7 collective-permute-done.24
  150.2 1.0 collective-permute-done.25
  151.2 0.7 collective-permute-done.26
  152.0 26.9 %shard_map.82 = (f32[4,128]{1,0:T(4,128)S(1)}, f32[32,128]{1,0:T(8,128)S(1)}) custom-call(f32[512,2048]{1,0:T(8,128)S(1)} %get-tuple-element.35.refs_0_, f32[512,2048]{1,0:T(8,128)S(1)} %get-tuple-element.36.refs_1_, f32[32,128]{1,0:T(8,128)S(1)} %get-tuple-element.65.refs_2_, f32[4,128]{1,0:T(4,128)S(1)} %get-tuple-element.63.refs_3_), custom_call_target="tpu_custom_call" | custom-call | tf_op jit(solution)/shard_map/pallas_call | solution.py:308
  178.9 2.1 shard_map.83
  181.2 2.6 %collective-permute-start.29 = (f32[16,128]{1,0:T(8,128)S(1)}, f32[16,128]{1,0:T(8,128)S(1)}, u32[]{:S(2)}, u32[]{:S(2)}) collective-permute-start(f32[16,128]{1,0:T(8,128)S(1)} %pad_maximum_fusion.9), channel_id=1, source_target_pairs={{0,3},{1,0},{2,1},{3,2},{4,7},{5,4},{6,5},{7,6},{8,11},{9,8},{10,9... | collective-permute-start | bytes 24584 | tf_op jit(solution)/shard_map/ppermute | solution.py:502
  183.8 1.0 collective-permute-done.27
  185.6 4.3 %collective-permute-start.30 = (f32[52,128]{1,0:T(8,128)S(1)}, f32[52,128]{1,0:T(8,128)S(1)}, u32[]{:S(2)}, u32[]{:S(2)}) collective-permute-start(f32[52,128]{1,0:T(8,128)S(1)} %pad_maximum_fusion.5), channel_id=1, source_target_pairs={{0,4},{4,0},{8,12},{12,8},{16,20},{20,16},{24,28},{28,24},{32,36},... | collective-permute-start | bytes 79880 | tf_op jit(solution)/shard_map/ppermute | solution.py:502
  189.9 0.9 collective-permute-done.30
  190.8 2.4 %shard_map.84 = f32[16,128]{1,0:T(8,128)S(1)} custom-call(f32[1024,512]{1,0:T(8,128)S(1)} %get-tuple-element.53.refs_0_, f32[1024,1024]{1,0:T(8,128)S(1)} %get-tuple-element.54.refs_1_, f32[1024,512]{1,0:T(8,128)S(1)} %get-tuple-element.55.refs_2_, f32[8,128]{1,0:T(8,128)S(1)} %get-tuple-element.83.refs_3_, s32[16]{0:T(128)S(1)} %broadcast_select_fusion.4.refs_5_.refs_6_.refs_4_), custom_call_target="tpu_custom_call" | custom-call | tf_op jit(solution)/shard_map/pallas_call | solution.py:461
  193.3 1.2 collective-permute-start.31
  194.5 1.8 collective-permute-start.32
  196.3 1.6 collective-permute-start.33
  197.9 0.9 collective-permute-done.32
  198.9 0.8 collective-permute-done.33
  199.8 0.6 collective-permute-start.34
  200.3 2.5 %collective-permute-start.35 = (f32[72,128]{1,0:T(8,128)S(1)}, f32[72,128]{1,0:T(8,128)S(1)}, u32[]{:S(2)}, u32[]{:S(2)}) collective-permute-start(f32[72,128]{1,0:T(8,128)S(1)} %pad_maximum_fusion.2), channel_id=1, source_target_pairs={{0,64},{4,68},{8,72},{12,76},{16,80},{20,84},{24,88},{28,92},{32,9... | collective-permute-start | bytes 110600 | tf_op jit(solution)/shard_map/ppermute | solution.py:502
  202.8 0.5 collective-permute-start.36
  203.3 0.6 collective-permute-done.34
  203.9 0.8 collective-permute-done.35
  204.7 1.2 collective-permute-done.36
  206.0 3.2 %collective-permute-start.37 = (f32[8,128]{1,0:T(8,128)S(1)}, f32[8,128]{1,0:T(8,128)S(1)}, u32[]{:S(2)}, u32[]{:S(2)}) collective-permute-start(f32[8,128]{1,0:T(8,128)S(1)} %bitcast_reduce_fusion.1), channel_id=1, source_target_pairs={{0,4},{4,0},{8,12},{12,8},{16,20},{20,16},{24,28},{28,24},{32,36},... | collective-permute-start | bytes 12296 | tf_op jit(solution)/shard_map/ppermute | solution.py:502
  209.2 0.6 bitcast_reduce_fusion
  210.0 1.3 collective-permute-start.38
  211.3 1.8 collective-permute-start.39
  213.1 0.7 collective-permute-start.40
  213.8 1.5 collective-permute-done.39
  215.3 0.6 collective-permute-done.40
  215.9 1.2 fusion.13
  (105 shorter events, 3.1 us)
Async XLA Ops:
  1.7 53.6 %collective-permute-start.13 = (bf16[128,2048]{1,0:T(8,128)(2,1)S(1)}, bf16[128,2048]{1,0:T(8,128)(2,1)S(1)}, u32[]{:S(2)}, u32[]{:S(2)}) collective-permute-start(bf16[128,2048]{1,0:T(8,128)(2,1)S(1)} %constant_dynamic-slice_fusion), channel_id=1, source_target_pairs={{0,8},{4,36},{8,16},{12,44},{16,24},{20,52},{24,0},{28,60},{32,40}... | collective-permute-start | bytes 1572872 | tf_op jit(solution)/shard_map/ppermute | solution.py:547
  4.2 52.4 %collective-permute-start.14 = (bf16[128,2048]{1,0:T(8,128)(2,1)S(1)}, bf16[128,2048]{1,0:T(8,128)(2,1)}, u32[]{:S(2)}, u32[]{:S(2)}) collective-permute-start(bf16[128,2048]{1,0:T(8,128)(2,1)S(1)} %constant_dynamic-slice_fusion), channel_id=1, source_target_pairs={{0,16},{4,68},{8,24},{12,76},{16,0},{20,84},{24,8},{28,92},{32,48}... | collective-permute-start | bytes 1572872 | tf_op jit(solution)/shard_map/ppermute | solution.py:547
  7.5 49.1 %collective-permute-start.15 = (bf16[128,2048]{1,0:T(8,128)(2,1)S(1)}, bf16[128,2048]{1,0:T(8,128)(2,1)}, u32[]{:S(2)}, u32[]{:S(2)}) collective-permute-start(bf16[128,2048]{1,0:T(8,128)(2,1)S(1)} %constant_dynamic-slice_fusion), channel_id=1, source_target_pairs={{0,24},{4,100},{8,0},{12,108},{16,8},{20,116},{24,16},{28,124},{32... | collective-permute-start | bytes 1572872 | tf_op jit(solution)/shard_map/ppermute | solution.py:547
  8.3 118.0 %collective-permute-start.12 = (bf16[512,2048]{1,0:T(8,128)(2,1)}, bf16[512,2048]{1,0:T(8,128)(2,1)S(1)}, u32[]{:S(2)}, u32[]{:S(2)}) collective-permute-start(bf16[512,2048]{1,0:T(8,128)(2,1)} %gen_ref.1), channel_id=1, source_target_pairs={{0,4},{4,0},{8,12},{12,8},{16,20},{20,16},{24,28},{28,24},{32,36},... | collective-permute-start | bytes 6291464 | tf_op jit(solution)/shard_map/ppermute | solution.py:548
  9.3 0.7 copy-start
  10.0 0.7 copy-start.2
  55.1 8.4 %collective-permute-start.2 = (f32[40,128]{1,0:T(8,128)S(1)}, f32[40,128]{1,0:T(8,128)S(1)}, u32[]{:S(2)}, u32[]{:S(2)}) collective-permute-start(f32[40,128]{1,0:T(8,128)S(1)} %pad_maximum_fusion.8), channel_id=1, source_target_pairs={{0,4},{4,0},{8,12},{12,8},{16,20},{20,16},{24,28},{28,24},{32,36},... | collective-permute-start | bytes 61448 | tf_op jit(solution)/shard_map/ppermute | solution.py:502
  55.3 5.6 %collective-permute-start = (f32[8,128]{1,0:T(8,128)S(1)}, f32[8,128]{1,0:T(8,128)S(1)}, u32[]{:S(2)}, u32[]{:S(2)}) collective-permute-start(f32[8,128]{1,0:T(8,128)S(1)} %pad_maximum_fusion.11), channel_id=1, source_target_pairs={{0,1},{1,0},{2,3},{3,2},{4,5},{5,4},{6,7},{7,6},{8,9},{9,8},{10,11... | collective-permute-start | bytes 12296 | tf_op jit(solution)/shard_map/ppermute | solution.py:515
  58.2 35.7 %collective-permute-start.17 = (bf16[512,2048]{1,0:T(8,128)(2,1)S(1)}, bf16[512,2048]{1,0:T(8,128)(2,1)S(1)}, u32[]{:S(2)}, u32[]{:S(2)}) collective-permute-start(bf16[512,2048]{1,0:T(8,128)(2,1)S(1)} %pad_maximum_fusion.refs_2_), channel_id=1, source_target_pairs={{0,32},{4,12},{8,40},{12,20},{16,48},{20,28},{24,56},{28,4},{32,64... | collective-permute-start | bytes 6291464 | tf_op jit(solution)/shard_map/ppermute | solution.py:550
  59.2 35.5 %collective-permute-start.18 = (bf16[512,2048]{1,0:T(8,128)(2,1)S(1)}, bf16[512,2048]{1,0:T(8,128)(2,1)S(1)}, u32[]{:S(2)}, u32[]{:S(2)}) collective-permute-start(bf16[512,2048]{1,0:T(8,128)(2,1)S(1)} %pad_maximum_fusion.refs_2_), channel_id=1, source_target_pairs={{0,96},{4,28},{8,104},{12,4},{16,112},{20,12},{24,120},{28,20},{32... | collective-permute-start | bytes 6291464 | tf_op jit(solution)/shard_map/ppermute | solution.py:551
  61.0 4.0 %collective-permute-start.1 = (f32[8,128]{1,0:T(8,128)S(1)}, f32[8,128]{1,0:T(8,128)S(1)}, u32[]{:S(2)}, u32[]{:S(2)}) collective-permute-start(f32[8,128]{1,0:T(8,128)S(1)} %pad_maximum_fusion.12), channel_id=1, source_target_pairs={{0,2},{1,3},{2,0},{3,1},{4,6},{5,7},{6,4},{7,5},{8,10},{9,11},{10,... | collective-permute-start | bytes 12296 | tf_op jit(solution)/shard_map/ppermute | solution.py:515
  63.5 22.0 %collective-permute-start.3 = (f32[56,128]{1,0:T(8,128)S(1)}, f32[56,128]{1,0:T(8,128)S(1)}, u32[]{:S(2)}, u32[]{:S(2)}) collective-permute-start(f32[56,128]{1,0:T(8,128)S(1)} %pad_maximum_fusion.3), channel_id=1, source_target_pairs={{0,8},{4,12},{8,16},{12,20},{16,24},{20,28},{24,0},{28,4},{32,40},... | collective-permute-start | bytes 86024 | tf_op jit(solution)/shard_map/ppermute | solution.py:502
  65.0 21.7 %collective-permute-start.4 = (f32[56,128]{1,0:T(8,128)S(1)}, f32[56,128]{1,0:T(8,128)S(1)}, u32[]{:S(2)}, u32[]{:S(2)}) collective-permute-start(f32[56,128]{1,0:T(8,128)S(1)} %pad_maximum_fusion.3), channel_id=1, source_target_pairs={{0,16},{4,20},{8,24},{12,28},{16,0},{20,4},{24,8},{28,12},{32,48},... | collective-permute-start | bytes 86024 | tf_op jit(solution)/shard_map/ppermute | solution.py:502
  85.6 3.0 %collective-permute-start.5 = (f32[56,128]{1,0:T(8,128)S(1)}, f32[56,128]{1,0:T(8,128)S(1)}, u32[]{:S(2)}, u32[]{:S(2)}) collective-permute-start(f32[56,128]{1,0:T(8,128)S(1)} %pad_maximum_fusion.3), channel_id=1, source_target_pairs={{0,24},{4,28},{8,0},{12,4},{16,8},{20,12},{24,16},{28,20},{32,56},... | collective-permute-start | bytes 86024 | tf_op jit(solution)/shard_map/ppermute | solution.py:502
  88.6 6.3 %collective-permute-start.6 = (f32[56,128]{1,0:T(8,128)S(1)}, f32[56,128]{1,0:T(8,128)S(1)}, u32[]{:S(2)}, u32[]{:S(2)}) collective-permute-start(f32[56,128]{1,0:T(8,128)S(1)} %pad_maximum_fusion.4), channel_id=1, source_target_pairs={{0,32},{4,36},{8,40},{12,44},{16,48},{20,52},{24,56},{28,60},{32,6... | collective-permute-start | bytes 86024 | tf_op jit(solution)/shard_map/ppermute | solution.py:502
  89.9 7.7 %collective-permute-start.7 = (f32[56,128]{1,0:T(8,128)S(1)}, f32[56,128]{1,0:T(8,128)S(1)}, u32[]{:S(2)}, u32[]{:S(2)}) collective-permute-start(f32[56,128]{1,0:T(8,128)S(1)} %pad_maximum_fusion.4), channel_id=1, source_target_pairs={{0,64},{4,68},{8,72},{12,76},{16,80},{20,84},{24,88},{28,92},{32,9... | collective-permute-start | bytes 86024 | tf_op jit(solution)/shard_map/ppermute | solution.py:502
  93.8 3.8 %collective-permute-start.8 = (f32[56,128]{1,0:T(8,128)S(1)}, f32[56,128]{1,0:T(8,128)S(1)}, u32[]{:S(2)}, u32[]{:S(2)}) collective-permute-start(f32[56,128]{1,0:T(8,128)S(1)} %pad_maximum_fusion.4), channel_id=1, source_target_pairs={{0,96},{4,100},{8,104},{12,108},{16,112},{20,116},{24,120},{28,124... | collective-permute-start | bytes 86024 | tf_op jit(solution)/shard_map/ppermute | solution.py:502
  94.6 3.1 %copy-start.3 = (f32[512]{0:T(512)S(1)}, f32[512]{0:T(512)}, u32[]{:S(2)}) copy-start(f32[512]{0:T(512)} %param.6) | copy-start | bytes 6148
  94.6 3.1 %copy-start.1 = (f32[4096]{0:T(1024)S(1)}, f32[4096]{0:T(1024)}, u32[]{:S(2)}) copy-start(f32[4096]{0:T(1024)} %param.8) | copy-start | bytes 49156
  94.7 41.8 %collective-permute-start.19 = (bf16[256,2048]{1,0:T(8,128)(2,1)S(1)}, bf16[256,2048]{1,0:T(8,128)(2,1)S(1)}, u32[]{:S(2)}, u32[]{:S(2)}) collective-permute-start(bf16[256,2048]{1,0:T(8,128)(2,1)S(1)} %slice.315), channel_id=1, source_target_pairs={{0,32},{4,12},{8,40},{12,20},{16,48},{20,28},{24,56},{28,4},{32,64... | collective-permute-start | bytes 3145736 | tf_op jit(solution)/shard_map/ppermute | solution.py:552
  94.9 41.6 %collective-permute-start.20 = (bf16[256,2048]{1,0:T(8,128)(2,1)S(1)}, bf16[256,2048]{1,0:T(8,128)(2,1)S(1)}, u32[]{:S(2)}, u32[]{:S(2)}) collective-permute-start(bf16[256,2048]{1,0:T(8,128)(2,1)S(1)} %slice.316), channel_id=1, source_target_pairs={{0,96},{4,28},{8,104},{12,4},{16,112},{20,12},{24,120},{28,20},{32... | collective-permute-start | bytes 3145736 | tf_op jit(solution)/shard_map/ppermute | solution.py:553
  124.7 1.3 collective-permute-start.11
  124.8 1.5 collective-permute-start.16
  125.9 17.4 %collective-permute-start.9 = (f32[4,128]{1,0:T(4,128)S(1)}, f32[4,128]{1,0:T(4,128)S(1)}, u32[]{:S(2)}, u32[]{:S(2)}) collective-permute-start(f32[4,128]{1,0:T(4,128)S(1)} %get-tuple-element.44), channel_id=1, source_target_pairs={{0,1},{1,0},{2,3},{3,2},{4,5},{5,4},{6,7},{7,6},{8,9},{9,8},{10,11... | collective-permute-start | bytes 6152 | tf_op jit(solution)/shard_map/ppermute | solution.py:515
  140.3 5.8 %collective-permute-start.21 = (f32[48,128]{1,0:T(8,128)S(1)}, f32[48,128]{1,0:T(8,128)S(1)}, u32[]{:S(2)}, u32[]{:S(2)}) collective-permute-start(f32[48,128]{1,0:T(8,128)S(1)} %pad_maximum_fusion.6), channel_id=1, source_target_pairs={{0,8},{4,12},{8,16},{12,20},{16,24},{20,28},{24,0},{28,4},{32,40},... | collective-permute-start | bytes 73736 | tf_op jit(solution)/shard_map/ppermute | solution.py:502
  140.6 5.5 %collective-permute-start.22 = (f32[48,128]{1,0:T(8,128)S(1)}, f32[48,128]{1,0:T(8,128)S(1)}, u32[]{:S(2)}, u32[]{:S(2)}) collective-permute-start(f32[48,128]{1,0:T(8,128)S(1)} %pad_maximum_fusion.6), channel_id=1, source_target_pairs={{0,16},{4,20},{8,24},{12,28},{16,0},{20,4},{24,8},{28,12},{32,48},... | collective-permute-start | bytes 73736 | tf_op jit(solution)/shard_map/ppermute | solution.py:502
  142.5 3.6 %collective-permute-start.23 = (f32[48,128]{1,0:T(8,128)S(1)}, f32[48,128]{1,0:T(8,128)S(1)}, u32[]{:S(2)}, u32[]{:S(2)}) collective-permute-start(f32[48,128]{1,0:T(8,128)S(1)} %pad_maximum_fusion.6), channel_id=1, source_target_pairs={{0,24},{4,28},{8,0},{12,4},{16,8},{20,12},{24,16},{28,20},{32,56},... | collective-permute-start | bytes 73736 | tf_op jit(solution)/shard_map/ppermute | solution.py:502
  143.3 6.2 %collective-permute-start.10 = (f32[4,128]{1,0:T(4,128)S(1)}, f32[4,128]{1,0:T(4,128)S(1)}, u32[]{:S(2)}, u32[]{:S(2)}) collective-permute-start(f32[4,128]{1,0:T(4,128)S(1)} %multiply_add_fusion.6), channel_id=1, source_target_pairs={{0,2},{1,3},{2,0},{3,1},{4,6},{5,7},{6,4},{7,5},{8,10},{9,11},{10,... | collective-permute-start | bytes 6152 | tf_op jit(solution)/shard_map/ppermute | solution.py:515
  146.2 4.0 %collective-permute-start.24 = (f32[48,128]{1,0:T(8,128)S(1)}, f32[48,128]{1,0:T(8,128)S(1)}, u32[]{:S(2)}, u32[]{:S(2)}) collective-permute-start(f32[48,128]{1,0:T(8,128)S(1)} %pad_maximum_fusion.7), channel_id=1, source_target_pairs={{0,32},{4,36},{8,40},{12,44},{16,48},{20,52},{24,56},{28,60},{32,6... | collective-permute-start | bytes 73736 | tf_op jit(solution)/shard_map/ppermute | solution.py:502
  147.0 4.2 %collective-permute-start.25 = (f32[48,128]{1,0:T(8,128)S(1)}, f32[48,128]{1,0:T(8,128)S(1)}, u32[]{:S(2)}, u32[]{:S(2)}) collective-permute-start(f32[48,128]{1,0:T(8,128)S(1)} %pad_maximum_fusion.7), channel_id=1, source_target_pairs={{0,64},{4,68},{8,72},{12,76},{16,80},{20,84},{24,88},{28,92},{32,9... | collective-permute-start | bytes 73736 | tf_op jit(solution)/shard_map/ppermute | solution.py:502
  148.9 3.0 %collective-permute-start.26 = (f32[48,128]{1,0:T(8,128)S(1)}, f32[48,128]{1,0:T(8,128)S(1)}, u32[]{:S(2)}, u32[]{:S(2)}) collective-permute-start(f32[48,128]{1,0:T(8,128)S(1)} %pad_maximum_fusion.7), channel_id=1, source_target_pairs={{0,96},{4,100},{8,104},{12,108},{16,112},{20,116},{24,120},{28,124... | collective-permute-start | bytes 73736 | tf_op jit(solution)/shard_map/ppermute | solution.py:502
  181.1 3.8 %collective-permute-start.27 = (f32[16,128]{1,0:T(8,128)S(1)}, f32[16,128]{1,0:T(8,128)S(1)}, u32[]{:S(2)}, u32[]{:S(2)}) collective-permute-start(f32[16,128]{1,0:T(8,128)S(1)} %pad_maximum_fusion.9), channel_id=1, source_target_pairs={{0,1},{1,2},{2,3},{3,0},{4,5},{5,6},{6,7},{7,4},{8,9},{9,10},{10,1... | collective-permute-start | bytes 24584 | tf_op jit(solution)/shard_map/ppermute | solution.py:502
  181.1 4.1 %collective-permute-start.28 = (f32[16,128]{1,0:T(8,128)S(1)}, f32[16,128]{1,0:T(8,128)S(1)}, u32[]{:S(2)}, u32[]{:S(2)}) collective-permute-start(f32[16,128]{1,0:T(8,128)S(1)} %pad_maximum_fusion.9), channel_id=1, source_target_pairs={{0,2},{1,3},{2,0},{3,1},{4,6},{5,7},{6,4},{7,5},{8,10},{9,11},{10,... | collective-permute-start | bytes 24584 | tf_op jit(solution)/shard_map/ppermute | solution.py:502
  181.2 4.3 %collective-permute-start.29 = (f32[16,128]{1,0:T(8,128)S(1)}, f32[16,128]{1,0:T(8,128)S(1)}, u32[]{:S(2)}, u32[]{:S(2)}) collective-permute-start(f32[16,128]{1,0:T(8,128)S(1)} %pad_maximum_fusion.9), channel_id=1, source_target_pairs={{0,3},{1,0},{2,1},{3,2},{4,7},{5,4},{6,5},{7,6},{8,11},{9,8},{10,9... | collective-permute-start | bytes 24584 | tf_op jit(solution)/shard_map/ppermute | solution.py:502
  185.6 5.2 %collective-permute-start.30 = (f32[52,128]{1,0:T(8,128)S(1)}, f32[52,128]{1,0:T(8,128)S(1)}, u32[]{:S(2)}, u32[]{:S(2)}) collective-permute-start(f32[52,128]{1,0:T(8,128)S(1)} %pad_maximum_fusion.5), channel_id=1, source_target_pairs={{0,4},{4,0},{8,12},{12,8},{16,20},{20,16},{24,28},{28,24},{32,36},... | collective-permute-start | bytes 79880 | tf_op jit(solution)/shard_map/ppermute | solution.py:502
  190.7 18.4 %copy-start.4 = (f32[4096]{0:T(1024)S(1)}, f32[4096]{0:T(1024)}, u32[]{:S(2)}) copy-start(f32[4096]{0:T(1024)} %param.9) | copy-start | bytes 49156
  193.3 4.7 %collective-permute-start.31 = (f32[72,128]{1,0:T(8,128)S(1)}, f32[72,128]{1,0:T(8,128)S(1)}, u32[]{:S(2)}, u32[]{:S(2)}) collective-permute-start(f32[72,128]{1,0:T(8,128)S(1)} %pad_maximum_fusion.1), channel_id=1, source_target_pairs={{0,8},{4,12},{8,16},{12,20},{16,24},{20,28},{24,0},{28,4},{32,40},... | collective-permute-start | bytes 110600 | tf_op jit(solution)/shard_map/ppermute | solution.py:502
  194.5 4.4 %collective-permute-start.32 = (f32[72,128]{1,0:T(8,128)S(1)}, f32[72,128]{1,0:T(8,128)S(1)}, u32[]{:S(2)}, u32[]{:S(2)}) collective-permute-start(f32[72,128]{1,0:T(8,128)S(1)} %pad_maximum_fusion.1), channel_id=1, source_target_pairs={{0,16},{4,20},{8,24},{12,28},{16,0},{20,4},{24,8},{28,12},{32,48},... | collective-permute-start | bytes 110600 | tf_op jit(solution)/shard_map/ppermute | solution.py:502
  196.3 3.4 %collective-permute-start.33 = (f32[72,128]{1,0:T(8,128)S(1)}, f32[72,128]{1,0:T(8,128)S(1)}, u32[]{:S(2)}, u32[]{:S(2)}) collective-permute-start(f32[72,128]{1,0:T(8,128)S(1)} %pad_maximum_fusion.1), channel_id=1, source_target_pairs={{0,24},{4,28},{8,0},{12,4},{16,8},{20,12},{24,16},{28,20},{32,56},... | collective-permute-start | bytes 110600 | tf_op jit(solution)/shard_map/ppermute | solution.py:502
  199.8 4.1 %collective-permute-start.34 = (f32[72,128]{1,0:T(8,128)S(1)}, f32[72,128]{1,0:T(8,128)S(1)}, u32[]{:S(2)}, u32[]{:S(2)}) collective-permute-start(f32[72,128]{1,0:T(8,128)S(1)} %pad_maximum_fusion.2), channel_id=1, source_target_pairs={{0,32},{4,36},{8,40},{12,44},{16,48},{20,52},{24,56},{28,60},{32,6... | collective-permute-start | bytes 110600 | tf_op jit(solution)/shard_map/ppermute | solution.py:502
  200.3 4.3 %collective-permute-start.35 = (f32[72,128]{1,0:T(8,128)S(1)}, f32[72,128]{1,0:T(8,128)S(1)}, u32[]{:S(2)}, u32[]{:S(2)}) collective-permute-start(f32[72,128]{1,0:T(8,128)S(1)} %pad_maximum_fusion.2), channel_id=1, source_target_pairs={{0,64},{4,68},{8,72},{12,76},{16,80},{20,84},{24,88},{28,92},{32,9... | collective-permute-start | bytes 110600 | tf_op jit(solution)/shard_map/ppermute | solution.py:502
  202.8 3.1 %collective-permute-start.36 = (f32[72,128]{1,0:T(8,128)S(1)}, f32[72,128]{1,0:T(8,128)S(1)}, u32[]{:S(2)}, u32[]{:S(2)}) collective-permute-start(f32[72,128]{1,0:T(8,128)S(1)} %pad_maximum_fusion.2), channel_id=1, source_target_pairs={{0,96},{4,100},{8,104},{12,108},{16,112},{20,116},{24,120},{28,124... | collective-permute-start | bytes 110600 | tf_op jit(solution)/shard_map/ppermute | solution.py:502
  206.0 4.0 %collective-permute-start.37 = (f32[8,128]{1,0:T(8,128)S(1)}, f32[8,128]{1,0:T(8,128)S(1)}, u32[]{:S(2)}, u32[]{:S(2)}) collective-permute-start(f32[8,128]{1,0:T(8,128)S(1)} %bitcast_reduce_fusion.1), channel_id=1, source_target_pairs={{0,4},{4,0},{8,12},{12,8},{16,20},{20,16},{24,28},{28,24},{32,36},... | collective-permute-start | bytes 12296 | tf_op jit(solution)/shard_map/ppermute | solution.py:502
  210.0 3.8 %collective-permute-start.38 = (f32[12,128]{1,0:T(8,128)S(1)}, f32[12,128]{1,0:T(8,128)S(1)}, u32[]{:S(2)}, u32[]{:S(2)}) collective-permute-start(f32[12,128]{1,0:T(8,128)S(1)} %pad_maximum_fusion.10), channel_id=1, source_target_pairs={{0,1},{1,2},{2,3},{3,0},{4,5},{5,6},{6,7},{7,4},{8,9},{9,10},{10,1... | collective-permute-start | bytes 18440 | tf_op jit(solution)/shard_map/ppermute | solution.py:502
  211.3 4.0 %collective-permute-start.39 = (f32[12,128]{1,0:T(8,128)S(1)}, f32[12,128]{1,0:T(8,128)S(1)}, u32[]{:S(2)}, u32[]{:S(2)}) collective-permute-start(f32[12,128]{1,0:T(8,128)S(1)} %pad_maximum_fusion.10), channel_id=1, source_target_pairs={{0,2},{1,3},{2,0},{3,1},{4,6},{5,7},{6,4},{7,5},{8,10},{9,11},{10,... | collective-permute-start | bytes 18440 | tf_op jit(solution)/shard_map/ppermute | solution.py:502
  213.1 2.8 %collective-permute-start.40 = (f32[12,128]{1,0:T(8,128)S(1)}, f32[12,128]{1,0:T(8,128)S(1)}, u32[]{:S(2)}, u32[]{:S(2)}) collective-permute-start(f32[12,128]{1,0:T(8,128)S(1)} %pad_maximum_fusion.10), channel_id=1, source_target_pairs={{0,3},{1,0},{2,1},{3,2},{4,7},{5,4},{6,5},{7,6},{8,11},{9,8},{10,9... | collective-permute-start | bytes 18440 | tf_op jit(solution)/shard_map/ppermute | solution.py:502

commit v3 on v2

--- a/solution.py
+++ b/solution.py
@@ -77,7 +77,7 @@
         for r in range(rows // ROWS):
             cols = body(r, cols)
     else:
-        cols = lax.fori_loop(0, rows // ROWS, body, cols, unroll=2)
+        cols = lax.fori_loop(0, rows // ROWS, body, cols, unroll=4)
     return [jnp.sum(c, axis=0, keepdims=True) for c in cols]
 
 
@@ -182,50 +182,59 @@
             first += count
 
 
-def first_kernel(
-    offset, gen_ref, ref_hbm, gweight_hbm, rweight_hbm,
-    d_ref, lrow_ref, lcol_ref, hrow_ref, hcol_ref, mass_ref, *refs,
-):
+def first_kernel(offset, steps, *refs):
     if offset == 0:
-        held_ref, *refs = refs
-    tile_ref, stage_ref, gweight_ref, rweight_ref, u_ref, v_ref, vs_ref, rowacc_ref, colsum_ref, peak_ref, sem = refs
+        gen_hbm, ref_hbm, gweight_hbm, rweight_hbm, *refs = refs
+        d_ref, lrow_ref, lcol_ref, hcol_ref, hrow_ref, mass_ref, gen_ref, ahead_ref, *refs = refs
+        gweight_ref, *refs = refs
+    else:
+        gen_ref, ref_hbm, rweight_hbm, hrow_ref, first_ref, d_ref, lrow_ref, lcol_ref, hcol_ref, *refs = refs
+    tile_ref, stage_ref, rweight_ref, u_ref, v_ref, vs_ref, rowacc_ref, colsum_ref, peak_ref, sem = refs
     rows, width = gen_ref.shape
     nq, nc = rows // LANES, d_ref.shape[1] // LANES
     chunks = TILE // LANES
-    steps = d_ref.shape[1] // TILE
     half_scale = 0.5 * LOG2E / (EPS * width)
     dot_scale = LOG2E / (EPS * width)
-    loads = []
+    first_tile = offset * steps
+
+    def load(j):
+        at = pl.ds(pl.multiple_of((first_tile + j) * TILE, TILE), TILE)
+        return pltpu.make_async_copy(ref_hbm.at[at, :], tile_ref.at[j], sem.at[j])
+
+    rload = pltpu.make_async_copy(rweight_hbm, rweight_ref, sem.at[steps])
     if offset == 0:
-        loads.append(pltpu.make_async_copy(gen_ref, held_ref, sem.at[steps + 2]))
-        gen_ref = held_ref
-    loads.append(pltpu.make_async_copy(gweight_hbm, gweight_ref, sem.at[steps]))
-    loads.append(pltpu.make_async_copy(rweight_hbm, rweight_ref, sem.at[steps + 1]))
-
-    def load(j):
-        at = pl.ds(pl.multiple_of((offset * steps + j) * TILE, TILE), TILE)
-        return pltpu.make_async_copy(ref_hbm.at[at, :], tile_ref.at[j], sem.at[j])
-
-    tiles = [load(j) for j in range(steps)]
-    for copy in loads[:1] + tiles[:1] + loads[1:] + tiles[1:]:
-        copy.start()
-    for copy in loads:
-        copy.wait()
-    for q, part in enumerate(norms(gen_ref, 0, nq, half_scale)):
-        hrow_ref[q : q + 1, :] = part
-        v_ref[q : q + 1, :] = jnp.log2(gweight_ref[q : q + 1, :]) - part
-        hrow_ref[nq + q : nq + q + 1, :] = gweight_ref[q : q + 1, :]
-    lrow_ref[nq : 2 * nq, :] = jnp.broadcast_to(jnp.sum(rweight_ref[...]).reshape(1, 1), (nq, LANES))
-    mass_ref[...] = jnp.broadcast_to(jnp.sum(gweight_ref[...]).reshape(1, 1), (8, LANES))
-
-    def product(j):
-        for c, half in enumerate(norms(tile_ref.at[j], 0, chunks, half_scale)):
+        own = pltpu.make_async_copy(gen_hbm, gen_ref, sem.at[steps + 1])
+        gload = pltpu.make_async_copy(gweight_hbm, gweight_ref, sem.at[steps + 2])
+        ahead = pltpu.make_async_copy(
+            ref_hbm.at[steps * TILE : (steps + 1) * TILE, :], ahead_ref, sem.at[steps + 3]
+        )
+        for copy in (own, load(0), gload, rload):
+            copy.start()
+        own.wait()
+        load(1).start()
+        gload.wait()
+        rload.wait()
+        for q, part in enumerate(norms(gen_ref, 0, nq, half_scale)):
+            hrow_ref[q : q + 1, :] = part
+            v_ref[q : q + 1, :] = jnp.log2(gweight_ref[q : q + 1, :]) - part
+            hrow_ref[nq + q : nq + q + 1, :] = gweight_ref[q : q + 1, :]
+        lrow_ref[nq : 2 * nq, :] = jnp.broadcast_to(jnp.sum(rweight_ref[...]).reshape(1, 1), (nq, LANES))
+        mass_ref[...] = jnp.broadcast_to(jnp.sum(gweight_ref[...]).reshape(1, 1), (8, LANES))
+        load(0).wait()
+        tile0_ref = tile_ref.at[0]
+    else:
+        rload.start()
+        load(1).start()
+        v_ref[...] = jnp.log2(hrow_ref[nq : 2 * nq, :]) - hrow_ref[0:nq, :]
+        rload.wait()
+        tile0_ref = first_ref
+
+    def product(j, tile):
+        for c, half in enumerate(norms(tile, 0, chunks, half_scale)):
             row = pl.ds(j * chunks + c, 1)
             hcol_ref[row, :] = half
             u_ref[row, :] = jnp.log2(rweight_ref[pl.ds(offset * nc + j * chunks + c, 1), :]) - half
-        dots = lax.dot_general(
-            gen_ref[...], tile_ref[j], (((1,), (1,)), ((), ())), preferred_element_type=F32
-        )
+        dots = lax.dot_general(gen_ref[...], tile[...], (((1,), (1,)), ((), ())), preferred_element_type=F32)
         stage_ref[...] = dots * dot_scale
 
     def sums(j, straight):
@@ -234,38 +243,62 @@
         for c, part in enumerate(found):
             colsum_ref[pl.ds(j * chunks + c, 1), :] = part
 
-    tiles[0].wait()
-    product(0)
+    product(0, tile0_ref)
     start_peak(stage_ref, u_ref[0:1, :], v_ref, vs_ref, peak_ref, rowacc_ref)
 
     def step(j, carry):
         load(j).wait()
+
+        @pl.when(j + 1 < steps)
+        def _():
+            load(j + 1).start()
+
+        if offset == 0:
+
+            @pl.when(j + 1 == steps)
+            def _():
+                ahead.start()
+
         sums(j - 1, True)
-        product(j)
+        product(j, tile_ref.at[j])
         return carry
 
     lax.fori_loop(1, steps, step, 0)
     sums(steps - 1, False)
     finish([d_ref], u_ref, v_ref, vs_ref, rowacc_ref, colsum_ref, peak_ref, lrow_ref, lcol_ref)
-
-
-def first_pass(gen, ref, gweight, rweight, piece, pieces):
+    if offset == 0:
+        ahead.wait()
+
+
+def first_pass(offset, pieces, gen, ref, rweight, *more):
     rows, width = gen.shape
     cols = ref.shape[0] // pieces
+    steps = cols // TILE
     nq, nc = rows // LANES, cols // LANES
     vmem = pl.BlockSpec(memory_space=pltpu.VMEM)
     hbm = pl.BlockSpec(memory_space=pltpu.HBM)
     vec = lambda n: jax.ShapeDtypeStruct((n, LANES), F32)
-    held = () if piece else (pltpu.VMEM((rows, width), gen.dtype),)
+    outs = (pltpu.VMEM((rows, cols), F32), vec(nq if offset else 2 * nq), vec(nc), vec(nc))
+    if offset == 0:
+        (gweight,) = more
+        outs += (vec(2 * nq), vec(8), pltpu.VMEM((rows, width), gen.dtype), pltpu.VMEM((TILE, width), ref.dtype))
+        specs = [hbm] * 4
+        operands = [hbm_array(gen), hbm_array(ref), hbm_array(gweight), hbm_array(rweight)]
+        weights = [pltpu.VMEM((nq, LANES), F32)]
+    else:
+        hrow, first = more
+        specs = [vmem, hbm, hbm, vmem, vmem]
+        operands = [vmem_array(gen), hbm_array(ref), hbm_array(rweight), hrow, vmem_array(first)]
+        weights = []
     return pl.pallas_call(
-        functools.partial(first_kernel, piece),
-        in_specs=[vmem if piece else hbm, hbm, hbm, hbm],
-        out_shape=(pltpu.VMEM((rows, cols), F32), vec(2 * nq), vec(nc), vec(2 * nq), vec(nc), vec(8)) + held,
-        out_specs=(vmem,) * (6 + len(held)),
-        scratch_shapes=[
-            pltpu.VMEM((cols // TILE, TILE, width), jnp.bfloat16),
+        functools.partial(first_kernel, offset, steps),
+        in_specs=specs,
+        out_shape=outs,
+        out_specs=(vmem,) * len(outs),
+        scratch_shapes=weights
+        + [
+            pltpu.VMEM((steps, TILE, width), jnp.bfloat16),
             pltpu.VMEM((rows, TILE), F32),
-            pltpu.VMEM((nq, LANES), F32),
             pltpu.VMEM(rweight.shape, F32),
             pltpu.VMEM((nc, LANES), F32),
             pltpu.VMEM((nq, LANES), F32),
@@ -273,10 +306,10 @@
             pltpu.VMEM((rows, LANES), F32),
             pltpu.VMEM((nc, LANES), F32),
             pltpu.VMEM((8, LANES), F32),
-            pltpu.SemaphoreType.DMA((cols // TILE + 3,)),
+            pltpu.SemaphoreType.DMA((steps + 4,)),
         ],
         compiler_params=pltpu.CompilerParams(vmem_limit_bytes=16 << 20),
-    )(vmem_array(gen) if piece else hbm_array(gen), hbm_array(ref), gweight, rweight)
+    )(*operands)
 
 
 def next_kernel(count, *refs):
@@ -552,9 +585,9 @@
         low_far = lax.ppermute(up[: 2 * LANES], "gen", second_axis[1])
         high_far = lax.ppermute(down[2 * LANES :], "gen", second_axis[3])
 
-        d0, row0, lcol0, mine, hcol0, gmass, held = first_pass(gen_features, ref_features, wg, wr, 0, 2)
+        d0, row0, lcol0, hcol0, mine, gmass, held, ahead = first_pass(0, 2, gen_features, ref_features, wr, wg)
         theirs = lax.ppermute(mine, "gen", core_stage[0])
-        d1, row1, lcol1, _, hcol1, _ = first_pass(held, ref_features, wg, wr, 1, 2)
+        d1, row1, lcol1, hcol1 = first_pass(1, 2, held, ref_features, wr, mine, ahead)
         hcol = jnp.concatenate([hcol0, hcol1], axis=0)
         hrow = mine[:nq]
         weight = jnp.concatenate([wg, theirs[nq:]], axis=0)
@@ -563,7 +596,7 @@
         e2, z1_2 = self_first(held, mate, [low_far, high_far], hs, ws, place, 12)
         e = [e0, e1, e2]
 
-        row_part = jnp.concatenate([log_add([row0[:nq], row1[:nq]]), row0[nq:]], axis=0)
+        row_part = jnp.concatenate([log_add([row0[:nq], row1]), row0[nq:]], axis=0)
         row_part = doubled(row_part, nq)
         col_part = jnp.concatenate([lcol0, lcol1, gmass], axis=0)
         col_part = stage(col_part, "gen", core_stage, nc)

time: 218 us -> 214 us (0.982)
  transfers between devices with their start and end apart: 41 -> 41, of which waited for: 19 -> 20; matrix products, arithmetic and copies ran while one was open for 1% -> 1% of each run, Pallas kernels for 39% -> 39%
where the time goes in v3:
time: 214 us; the launch traced here: 213 us
  Pallas kernels  115 us (54%)
  starting transfers between devices  57 us (27%)
  waiting for transfers between devices  34.9 us (16%)
  other arithmetic  4.13 us (2%)
    pallas_call x2, Pallas kernels, next_pass(): pl.pallas_call(functools.partial(next_kernel, len(parts)), in_specs=[vmem...  52.8 us
    pallas_call x2, Pallas kernels, first_pass(): pl.pallas_call(functools.partial(first_kernel, offset, steps), in_specs=s...  43.3 us
    ppermute x28, starting transfers between devices, shift(): return [lax.ppermute(value, axis, perm) for perm in perms]  36.6 us
    ppermute x28, waiting for transfers between devices, shift(): return [lax.ppermute(value, axis, perm) for perm in perms]  33.5 us
    pallas_call x3, Pallas kernels, self_first(): pl.pallas_call(functools.partial(self_first_kernel, len(sources), first),...  14.1 us
    ppermute x4, starting transfers between devices, doubled(): lax.ppermute(value, 'ref', [(i, i ^ bit) for i in range(n_ref)])  6.89 us
    ppermute x3, starting transfers between devices, run(): got = [lax.ppermute(own, 'gen', first_axis[k]) for k in (1, 2, 3)]  6.55 us
    pallas_call x2, Pallas kernels, self_apply(): pl.pallas_call(functools.partial(kernel, len(parts)), in_specs=[vmem] * (...  4.54 us
  transfers between devices with their start and end apart: 41, of which 20 were waited for; matrix products, arithmetic and copies ran while one was open for 1% of the time, Pallas kernels for 39%

profile of v3, /device:TPU:1, one launch (start us, length us, event | category | flops | bytes accessed | tf_op | source)
XLA Modules:
  0.0 213.2 jit_solution(2348952559805285263)
XLA Ops:
  0.6 1.1 constant_dynamic-slice_fusion
  1.7 2.5 %collective-permute-start.13 = (bf16[128,2048]{1,0:T(8,128)(2,1)S(1)}, bf16[128,2048]{1,0:T(8,128)(2,1)S(1)}, u32[]{:S(2)}, u32[]{:S(2)}) collective-permute-start(bf16[128,2048]{1,0:T(8,128)(2,1)S(1)} %constant_dynamic-slice_fusion), channel_id=1, source_target_pairs={{0,8},{4,36},{8,16},{12,44},{16,24},{20,52},{24,0},{28,60},{32,40}... | collective-permute-start | bytes 1572872 | tf_op jit(solution)/shard_map/ppermute | solution.py:580
  4.2 3.3 %collective-permute-start.14 = (bf16[128,2048]{1,0:T(8,128)(2,1)S(1)}, bf16[128,2048]{1,0:T(8,128)(2,1)}, u32[]{:S(2)}, u32[]{:S(2)}) collective-permute-start(bf16[128,2048]{1,0:T(8,128)(2,1)S(1)} %constant_dynamic-slice_fusion), channel_id=1, source_target_pairs={{0,16},{4,68},{8,24},{12,76},{16,0},{20,84},{24,8},{28,92},{32,48}... | collective-permute-start | bytes 1572872 | tf_op jit(solution)/shard_map/ppermute | solution.py:580
  7.5 0.7 collective-permute-start.15
  8.3 0.8 collective-permute-start.12
  9.3 22.5 %shard_map.76 = (f32[512,2048]{1,0:T(8,128)S(1)}, f32[8,128]{1,0:T(8,128)S(1)}, f32[16,128]{1,0:T(8,128)S(1)}, f32[16,128]{1,0:T(8,128)S(1)}, f32[8,128]{1,0:T(8...) custom-call(bf16[512,2048]{1,0:T(8,128)(2,1)} %refs_0_.1, ...), custom_call_target="tpu_custom_call" | custom-call | tf_op jit(solution)/shard_map/pallas_call | solution.py:293
  31.8 20.8 %shard_map.77 = (f32[512,2048]{1,0:T(8,128)S(1)}, f32[4,128]{1,0:T(4,128)S(1)}, f32[16,128]{1,0:T(8,128)S(1)}, f32[16,128]{1,0:T(8,128)S(1)}) custom-call(bf16[512,2048]{1,0:T(8,128)(2,1)S(1)} %get-tuple-element.34.refs_0_, bf16[4096,2048]{1,0:T(8,128)(2,1)} %refs_1_.3, f32[32,128]{1,0:T(8,128)} %bitcast.24, f32[8,128]{1,0:T(8,128)S(1)} %get-tuple-element.32.refs_3_, ...), custom_call_target="tpu_custom_call" | custom-call | tf_op jit(solution)/shard_map/pallas_call | solution.py:293
  52.8 1.3 collective-permute-start
  54.1 1.6 pad_maximum_fusion.refs_2_
  55.7 1.0 collective-permute-start.17
  56.7 1.7 collective-permute-start.18
  58.5 2.5 %collective-permute-start.1 = (f32[8,128]{1,0:T(8,128)S(1)}, f32[8,128]{1,0:T(8,128)S(1)}, u32[]{:S(2)}, u32[]{:S(2)}) collective-permute-start(f32[8,128]{1,0:T(8,128)S(1)} %pad_maximum_fusion.12), channel_id=1, source_target_pairs={{0,2},{1,3},{2,0},{3,1},{4,6},{5,7},{6,4},{7,5},{8,10},{9,11},{10,... | collective-permute-start | bytes 12296 | tf_op jit(solution)/shard_map/ppermute | solution.py:548
  61.1 1.4 collective-permute-done.1
  62.5 1.4 collective-permute-start.4
  63.9 19.2 %collective-permute-done.3 = f32[56,128]{1,0:T(8,128)S(1)} collective-permute-done((f32[56,128]{1,0:T(8,128)S(1)}, f32[56,128]{1,0:T(8,128)S(1)}, u32[]{:S(2)}, u32[]{:S(2)}) %collective-permute-start.3) | collective-permute-done | bytes 28704 | tf_op jit(solution)/shard_map/ppermute | solution.py:535
  83.0 1.2 collective-permute-start.5
  84.2 1.8 collective-permute-done.5
  86.1 1.1 collective-permute-start.6
  87.2 3.9 %collective-permute-start.7 = (f32[56,128]{1,0:T(8,128)S(1)}, f32[56,128]{1,0:T(8,128)S(1)}, u32[]{:S(2)}, u32[]{:S(2)}) collective-permute-start(f32[56,128]{1,0:T(8,128)S(1)} %pad_maximum_fusion.4), channel_id=1, source_target_pairs={{0,64},{4,68},{8,72},{12,76},{16,80},{20,84},{24,88},{28,92},{32,9... | collective-permute-start | bytes 86024 | tf_op jit(solution)/shard_map/ppermute | solution.py:535
  91.1 0.7 collective-permute-start.8
  92.1 2.7 %collective-permute-start.20 = (bf16[256,2048]{1,0:T(8,128)(2,1)S(1)}, bf16[256,2048]{1,0:T(8,128)(2,1)S(1)}, u32[]{:S(2)}, u32[]{:S(2)}) collective-permute-start(bf16[256,2048]{1,0:T(8,128)(2,1)S(1)} %slice.312), channel_id=1, source_target_pairs={{0,96},{4,28},{8,104},{12,4},{16,112},{20,12},{24,120},{28,20},{32... | collective-permute-start | bytes 3145736 | tf_op jit(solution)/shard_map/ppermute | solution.py:586
  95.0 26.4 %shard_map.78 = (f32[4,128]{1,0:T(4,128)S(1)}, f32[32,128]{1,0:T(8,128)S(1)}) custom-call(f32[512,2048]{1,0:T(8,128)S(1)} %get-tuple-element.37.refs_0_, f32[512,2048]{1,0:T(8,128)S(1)} %get-tuple-element.38.refs_1_, f32[32,128]{1,0:T(8,128)S(1)} %get-tuple-element.71.refs_2_, f32[4,128]{1,0:T(4,128)S(1)} %get-tuple-element.69.refs_3_), custom_call_target="tpu_custom_call" | custom-call | tf_op jit(solution)/shard_map/pallas_call | solution.py:341
  121.5 0.5 collective-permute-start.16
  122.0 0.7 collective-permute-done.11
  123.0 3.8 %shard_map.79 = (f32[1024,512]{1,0:T(8,128)S(1)}, f32[16,128]{1,0:T(8,128)S(1)}, f32[1024,128]{1,0:T(8,128)S(1)}, f32[1024,128]{1,0:T(8,128)S(1)}) custom-call(bf16[512,2048]{1,0:T(8,128)(2,1)S(1)} %get-tuple-element.34.refs_0_, bf16[512,2048]{1,0:T(8,128)(2,1)S(1)} %collective-permute-done.12.refs_1_, bf16[512,2048]{1,0:T(8,128)(2,1)S(1)} %pad_maximum_fusion.refs_2_, ...), custom_call_target="tpu_custom_call" | custom-call | tf_op jit(solution)/shard_map/pallas_call | solution.py:422
  126.7 6.5 %shard_map.80 = (f32[1024,1024]{1,0:T(8,128)S(1)}, f32[16,128]{1,0:T(8,128)S(1)}) custom-call(bf16[512,2048]{1,0:T(8,128)(2,1)S(1)} %get-tuple-element.34.refs_0_, bf16[512,2048]{1,0:T(8,128)(2,1)S(1)} %collective-permute-done.12.refs_1_, bf16[512,2048]{1,0:T(8,128)(2,1)S(1)} %collective-permute-done.17.refs_2_, ...), custom_call_target="tpu_custom_call" | custom-call | tf_op jit(solution)/shard_map/pallas_call | solution.py:422
  133.3 3.8 %shard_map.81 = (f32[1024,512]{1,0:T(8,128)S(1)}, f32[16,128]{1,0:T(8,128)S(1)}) custom-call(bf16[512,2048]{1,0:T(8,128)(2,1)S(1)} %get-tuple-element.34.refs_0_, bf16[512,2048]{1,0:T(8,128)(2,1)S(1)} %collective-permute-done.12.refs_1_, bf16[256,2048]{1,0:T(8,128)(2,1)S(1)} %collective-permute-done.19.refs_2_, ...), custom_call_target="tpu_custom_call" | custom-call | tf_op jit(solution)/shard_map/pallas_call | solution.py:422
  137.2 2.0 collective-permute-start.22
  139.2 0.7 collective-permute-start.23
  139.9 2.8 %collective-permute-start.10 = (f32[4,128]{1,0:T(4,128)S(1)}, f32[4,128]{1,0:T(4,128)S(1)}, u32[]{:S(2)}, u32[]{:S(2)}) collective-permute-start(f32[4,128]{1,0:T(4,128)S(1)} %multiply_add_fusion.6), channel_id=1, source_target_pairs={{0,2},{1,3},{2,0},{3,1},{4,6},{5,7},{6,4},{7,5},{8,10},{9,11},{10,... | collective-permute-start | bytes 6152 | tf_op jit(solution)/shard_map/ppermute | solution.py:548
  142.8 0.8 collective-permute-start.24
  143.6 2.0 collective-permute-start.25
  145.6 0.5 collective-permute-start.26
  146.1 0.6 collective-permute-done.24
  146.7 1.0 collective-permute-done.25
  147.8 0.7 collective-permute-done.26
  148.6 26.4 %shard_map.82 = (f32[4,128]{1,0:T(4,128)S(1)}, f32[32,128]{1,0:T(8,128)S(1)}) custom-call(f32[512,2048]{1,0:T(8,128)S(1)} %get-tuple-element.37.refs_0_, f32[512,2048]{1,0:T(8,128)S(1)} %get-tuple-element.38.refs_1_, f32[32,128]{1,0:T(8,128)S(1)} %get-tuple-element.67.refs_2_, f32[4,128]{1,0:T(4,128)S(1)} %get-tuple-element.65.refs_3_), custom_call_target="tpu_custom_call" | custom-call | tf_op jit(solution)/shard_map/pallas_call | solution.py:341
  175.1 2.1 %shard_map.83 = f32[8,128]{1,0:T(8,128)S(1)} custom-call(f32[1024,512]{1,0:T(8,128)S(1)} %get-tuple-element.55.refs_0_, f32[1024,1024]{1,0:T(8,128)S(1)} %get-tuple-element.56.refs_1_, f32[1024,512]{1,0:T(8,128)S(1)} %get-tuple-element.57.refs_2_, f32[16,128]{1,0:T(8,128)S(1)} %get-tuple-element.63.refs_3_, s32[16]{0:T(128)S(1)} %broadcast_select_fusion.4.refs_5_.refs_6_.refs_4_), custom_call_target="tpu_custom_call" | custom-call | tf_op jit(solution)/shard_map/pallas_call | solution.py:494
  177.4 2.6 %collective-permute-start.29 = (f32[16,128]{1,0:T(8,128)S(1)}, f32[16,128]{1,0:T(8,128)S(1)}, u32[]{:S(2)}, u32[]{:S(2)}) collective-permute-start(f32[16,128]{1,0:T(8,128)S(1)} %pad_maximum_fusion.9), channel_id=1, source_target_pairs={{0,3},{1,0},{2,1},{3,2},{4,7},{5,4},{6,5},{7,6},{8,11},{9,8},{10,9... | collective-permute-start | bytes 24584 | tf_op jit(solution)/shard_map/ppermute | solution.py:535
  180.0 1.0 collective-permute-done.27
  181.0 0.4 collective-permute-done.28
  181.4 0.3 collective-permute-done.29
  181.7 4.3 %collective-permute-start.30 = (f32[52,128]{1,0:T(8,128)S(1)}, f32[52,128]{1,0:T(8,128)S(1)}, u32[]{:S(2)}, u32[]{:S(2)}) collective-permute-start(f32[52,128]{1,0:T(8,128)S(1)} %pad_maximum_fusion.5), channel_id=1, source_target_pairs={{0,4},{4,0},{8,12},{12,8},{16,20},{20,16},{24,28},{28,24},{32,36},... | collective-permute-start | bytes 79880 | tf_op jit(solution)/shard_map/ppermute | solution.py:535
  186.0 0.9 collective-permute-done.30
  186.9 2.4 %shard_map.84 = f32[16,128]{1,0:T(8,128)S(1)} custom-call(f32[1024,512]{1,0:T(8,128)S(1)} %get-tuple-element.55.refs_0_, f32[1024,1024]{1,0:T(8,128)S(1)} %get-tuple-element.56.refs_1_, f32[1024,512]{1,0:T(8,128)S(1)} %get-tuple-element.57.refs_2_, f32[8,128]{1,0:T(8,128)S(1)} %get-tuple-element.85.refs_3_, s32[16]{0:T(128)S(1)} %broadcast_select_fusion.4.refs_5_.refs_6_.refs_4_), custom_call_target="tpu_custom_call" | custom-call | tf_op jit(solution)/shard_map/pallas_call | solution.py:494
  189.4 1.2 collective-permute-start.31
  190.6 1.8 collective-permute-start.32
  192.5 1.6 collective-permute-start.33
  194.1 0.9 collective-permute-done.32
  195.0 0.8 collective-permute-done.33
  195.9 0.5 collective-permute-start.34
  196.4 2.5 %collective-permute-start.35 = (f32[72,128]{1,0:T(8,128)S(1)}, f32[72,128]{1,0:T(8,128)S(1)}, u32[]{:S(2)}, u32[]{:S(2)}) collective-permute-start(f32[72,128]{1,0:T(8,128)S(1)} %pad_maximum_fusion.2), channel_id=1, source_target_pairs={{0,64},{4,68},{8,72},{12,76},{16,80},{20,84},{24,88},{28,92},{32,9... | collective-permute-start | bytes 110600 | tf_op jit(solution)/shard_map/ppermute | solution.py:535
  199.0 0.4 collective-permute-start.36
  199.4 0.6 collective-permute-done.34
  200.0 0.8 collective-permute-done.35
  200.8 1.3 collective-permute-done.36
  202.2 3.2 %collective-permute-start.37 = (f32[8,128]{1,0:T(8,128)S(1)}, f32[8,128]{1,0:T(8,128)S(1)}, u32[]{:S(2)}, u32[]{:S(2)}) collective-permute-start(f32[8,128]{1,0:T(8,128)S(1)} %bitcast_reduce_fusion.1), channel_id=1, source_target_pairs={{0,4},{4,0},{8,12},{12,8},{16,20},{20,16},{24,28},{28,24},{32,36},... | collective-permute-start | bytes 12296 | tf_op jit(solution)/shard_map/ppermute | solution.py:535
  205.3 0.6 bitcast_reduce_fusion
  206.2 1.2 collective-permute-start.38
  207.3 1.8 collective-permute-start.39
  209.2 0.7 collective-permute-start.40
  210.0 1.4 collective-permute-done.39
  211.3 0.7 collective-permute-done.40
  212.0 1.2 fusion.13
  (101 shorter events, 2.3 us)
Async XLA Ops:
  1.7 51.1 %collective-permute-start.13 = (bf16[128,2048]{1,0:T(8,128)(2,1)S(1)}, bf16[128,2048]{1,0:T(8,128)(2,1)S(1)}, u32[]{:S(2)}, u32[]{:S(2)}) collective-permute-start(bf16[128,2048]{1,0:T(8,128)(2,1)S(1)} %constant_dynamic-slice_fusion), channel_id=1, source_target_pairs={{0,8},{4,36},{8,16},{12,44},{16,24},{20,52},{24,0},{28,60},{32,40}... | collective-permute-start | bytes 1572872 | tf_op jit(solution)/shard_map/ppermute | solution.py:580
  4.2 49.9 %collective-permute-start.14 = (bf16[128,2048]{1,0:T(8,128)(2,1)S(1)}, bf16[128,2048]{1,0:T(8,128)(2,1)}, u32[]{:S(2)}, u32[]{:S(2)}) collective-permute-start(bf16[128,2048]{1,0:T(8,128)(2,1)S(1)} %constant_dynamic-slice_fusion), channel_id=1, source_target_pairs={{0,16},{4,68},{8,24},{12,76},{16,0},{20,84},{24,8},{28,92},{32,48}... | collective-permute-start | bytes 1572872 | tf_op jit(solution)/shard_map/ppermute | solution.py:580
  7.5 46.6 %collective-permute-start.15 = (bf16[128,2048]{1,0:T(8,128)(2,1)S(1)}, bf16[128,2048]{1,0:T(8,128)(2,1)}, u32[]{:S(2)}, u32[]{:S(2)}) collective-permute-start(bf16[128,2048]{1,0:T(8,128)(2,1)S(1)} %constant_dynamic-slice_fusion), channel_id=1, source_target_pairs={{0,24},{4,100},{8,0},{12,108},{16,8},{20,116},{24,16},{28,124},{32... | collective-permute-start | bytes 1572872 | tf_op jit(solution)/shard_map/ppermute | solution.py:580
  8.3 114.7 %collective-permute-start.12 = (bf16[512,2048]{1,0:T(8,128)(2,1)}, bf16[512,2048]{1,0:T(8,128)(2,1)S(1)}, u32[]{:S(2)}, u32[]{:S(2)}) collective-permute-start(bf16[512,2048]{1,0:T(8,128)(2,1)} %refs_0_.1), channel_id=1, source_target_pairs={{0,4},{4,0},{8,12},{12,8},{16,20},{20,16},{24,28},{28,24},{32,36},... | collective-permute-start | bytes 6291464 | tf_op jit(solution)/shard_map/ppermute | solution.py:581
  31.8 20.9 %copy-start.1 = (f32[512]{0:T(512)S(1)}, f32[512]{0:T(512)}, u32[]{:S(2)}) copy-start(f32[512]{0:T(512)} %param.6) | copy-start | bytes 6148
  52.6 8.4 %collective-permute-start.2 = (f32[40,128]{1,0:T(8,128)S(1)}, f32[40,128]{1,0:T(8,128)S(1)}, u32[]{:S(2)}, u32[]{:S(2)}) collective-permute-start(f32[40,128]{1,0:T(8,128)S(1)} %pad_maximum_fusion.8), channel_id=1, source_target_pairs={{0,4},{4,0},{8,12},{12,8},{16,20},{20,16},{24,28},{28,24},{32,36},... | collective-permute-start | bytes 61448 | tf_op jit(solution)/shard_map/ppermute | solution.py:535
  52.8 5.6 %collective-permute-start = (f32[8,128]{1,0:T(8,128)S(1)}, f32[8,128]{1,0:T(8,128)S(1)}, u32[]{:S(2)}, u32[]{:S(2)}) collective-permute-start(f32[8,128]{1,0:T(8,128)S(1)} %pad_maximum_fusion.11), channel_id=1, source_target_pairs={{0,1},{1,0},{2,3},{3,2},{4,5},{5,4},{6,7},{7,6},{8,9},{9,8},{10,11... | collective-permute-start | bytes 12296 | tf_op jit(solution)/shard_map/ppermute | solution.py:548
  55.7 35.5 %collective-permute-start.17 = (bf16[512,2048]{1,0:T(8,128)(2,1)S(1)}, bf16[512,2048]{1,0:T(8,128)(2,1)S(1)}, u32[]{:S(2)}, u32[]{:S(2)}) collective-permute-start(bf16[512,2048]{1,0:T(8,128)(2,1)S(1)} %pad_maximum_fusion.refs_2_), channel_id=1, source_target_pairs={{0,32},{4,12},{8,40},{12,20},{16,48},{20,28},{24,56},{28,4},{32,64... | collective-permute-start | bytes 6291464 | tf_op jit(solution)/shard_map/ppermute | solution.py:583
  56.7 35.3 %collective-permute-start.18 = (bf16[512,2048]{1,0:T(8,128)(2,1)S(1)}, bf16[512,2048]{1,0:T(8,128)(2,1)S(1)}, u32[]{:S(2)}, u32[]{:S(2)}) collective-permute-start(bf16[512,2048]{1,0:T(8,128)(2,1)S(1)} %pad_maximum_fusion.refs_2_), channel_id=1, source_target_pairs={{0,96},{4,28},{8,104},{12,4},{16,112},{20,12},{24,120},{28,20},{32... | collective-permute-start | bytes 6291464 | tf_op jit(solution)/shard_map/ppermute | solution.py:584
  58.5 4.0 %collective-permute-start.1 = (f32[8,128]{1,0:T(8,128)S(1)}, f32[8,128]{1,0:T(8,128)S(1)}, u32[]{:S(2)}, u32[]{:S(2)}) collective-permute-start(f32[8,128]{1,0:T(8,128)S(1)} %pad_maximum_fusion.12), channel_id=1, source_target_pairs={{0,2},{1,3},{2,0},{3,1},{4,6},{5,7},{6,4},{7,5},{8,10},{9,11},{10,... | collective-permute-start | bytes 12296 | tf_op jit(solution)/shard_map/ppermute | solution.py:548
  61.0 22.0 %collective-permute-start.3 = (f32[56,128]{1,0:T(8,128)S(1)}, f32[56,128]{1,0:T(8,128)S(1)}, u32[]{:S(2)}, u32[]{:S(2)}) collective-permute-start(f32[56,128]{1,0:T(8,128)S(1)} %pad_maximum_fusion.3), channel_id=1, source_target_pairs={{0,8},{4,12},{8,16},{12,20},{16,24},{20,28},{24,0},{28,4},{32,40},... | collective-permute-start | bytes 86024 | tf_op jit(solution)/shard_map/ppermute | solution.py:535
  62.5 21.7 %collective-permute-start.4 = (f32[56,128]{1,0:T(8,128)S(1)}, f32[56,128]{1,0:T(8,128)S(1)}, u32[]{:S(2)}, u32[]{:S(2)}) collective-permute-start(f32[56,128]{1,0:T(8,128)S(1)} %pad_maximum_fusion.3), channel_id=1, source_target_pairs={{0,16},{4,20},{8,24},{12,28},{16,0},{20,4},{24,8},{28,12},{32,48},... | collective-permute-start | bytes 86024 | tf_op jit(solution)/shard_map/ppermute | solution.py:535
  83.0 3.0 %collective-permute-start.5 = (f32[56,128]{1,0:T(8,128)S(1)}, f32[56,128]{1,0:T(8,128)S(1)}, u32[]{:S(2)}, u32[]{:S(2)}) collective-permute-start(f32[56,128]{1,0:T(8,128)S(1)} %pad_maximum_fusion.3), channel_id=1, source_target_pairs={{0,24},{4,28},{8,0},{12,4},{16,8},{20,12},{24,16},{28,20},{32,56},... | collective-permute-start | bytes 86024 | tf_op jit(solution)/shard_map/ppermute | solution.py:535
  86.1 6.0 %collective-permute-start.6 = (f32[56,128]{1,0:T(8,128)S(1)}, f32[56,128]{1,0:T(8,128)S(1)}, u32[]{:S(2)}, u32[]{:S(2)}) collective-permute-start(f32[56,128]{1,0:T(8,128)S(1)} %pad_maximum_fusion.4), channel_id=1, source_target_pairs={{0,32},{4,36},{8,40},{12,44},{16,48},{20,52},{24,56},{28,60},{32,6... | collective-permute-start | bytes 86024 | tf_op jit(solution)/shard_map/ppermute | solution.py:535
  87.2 7.6 %collective-permute-start.7 = (f32[56,128]{1,0:T(8,128)S(1)}, f32[56,128]{1,0:T(8,128)S(1)}, u32[]{:S(2)}, u32[]{:S(2)}) collective-permute-start(f32[56,128]{1,0:T(8,128)S(1)} %pad_maximum_fusion.4), channel_id=1, source_target_pairs={{0,64},{4,68},{8,72},{12,76},{16,80},{20,84},{24,88},{28,92},{32,9... | collective-permute-start | bytes 86024 | tf_op jit(solution)/shard_map/ppermute | solution.py:535
  91.1 3.7 %collective-permute-start.8 = (f32[56,128]{1,0:T(8,128)S(1)}, f32[56,128]{1,0:T(8,128)S(1)}, u32[]{:S(2)}, u32[]{:S(2)}) collective-permute-start(f32[56,128]{1,0:T(8,128)S(1)} %pad_maximum_fusion.4), channel_id=1, source_target_pairs={{0,96},{4,100},{8,104},{12,108},{16,112},{20,116},{24,120},{28,124... | collective-permute-start | bytes 86024 | tf_op jit(solution)/shard_map/ppermute | solution.py:535
  91.9 3.0 %copy-start = (f32[4096]{0:T(1024)S(1)}, f32[4096]{0:T(1024)}, u32[]{:S(2)}) copy-start(f32[4096]{0:T(1024)} %param.8) | copy-start | bytes 49156
  92.0 41.3 %collective-permute-start.19 = (bf16[256,2048]{1,0:T(8,128)(2,1)S(1)}, bf16[256,2048]{1,0:T(8,128)(2,1)S(1)}, u32[]{:S(2)}, u32[]{:S(2)}) collective-permute-start(bf16[256,2048]{1,0:T(8,128)(2,1)S(1)} %slice.311), channel_id=1, source_target_pairs={{0,32},{4,12},{8,40},{12,20},{16,48},{20,28},{24,56},{28,4},{32,64... | collective-permute-start | bytes 3145736 | tf_op jit(solution)/shard_map/ppermute | solution.py:585
  92.1 41.1 %collective-permute-start.20 = (bf16[256,2048]{1,0:T(8,128)(2,1)S(1)}, bf16[256,2048]{1,0:T(8,128)(2,1)S(1)}, u32[]{:S(2)}, u32[]{:S(2)}) collective-permute-start(bf16[256,2048]{1,0:T(8,128)(2,1)S(1)} %slice.312), channel_id=1, source_target_pairs={{0,96},{4,28},{8,104},{12,4},{16,112},{20,12},{24,120},{28,20},{32... | collective-permute-start | bytes 3145736 | tf_op jit(solution)/shard_map/ppermute | solution.py:586
  121.4 1.3 collective-permute-start.11
  121.5 1.4 collective-permute-start.16
  122.7 17.2 %collective-permute-start.9 = (f32[4,128]{1,0:T(4,128)S(1)}, f32[4,128]{1,0:T(4,128)S(1)}, u32[]{:S(2)}, u32[]{:S(2)}) collective-permute-start(f32[4,128]{1,0:T(4,128)S(1)} %get-tuple-element.46), channel_id=1, source_target_pairs={{0,1},{1,0},{2,3},{3,2},{4,5},{5,4},{6,7},{7,6},{8,9},{9,8},{10,11... | collective-permute-start | bytes 6152 | tf_op jit(solution)/shard_map/ppermute | solution.py:548
  137.1 5.6 %collective-permute-start.21 = (f32[48,128]{1,0:T(8,128)S(1)}, f32[48,128]{1,0:T(8,128)S(1)}, u32[]{:S(2)}, u32[]{:S(2)}) collective-permute-start(f32[48,128]{1,0:T(8,128)S(1)} %pad_maximum_fusion.6), channel_id=1, source_target_pairs={{0,8},{4,12},{8,16},{12,20},{16,24},{20,28},{24,0},{28,4},{32,40},... | collective-permute-start | bytes 73736 | tf_op jit(solution)/shard_map/ppermute | solution.py:535
  137.2 5.5 %collective-permute-start.22 = (f32[48,128]{1,0:T(8,128)S(1)}, f32[48,128]{1,0:T(8,128)S(1)}, u32[]{:S(2)}, u32[]{:S(2)}) collective-permute-start(f32[48,128]{1,0:T(8,128)S(1)} %pad_maximum_fusion.6), channel_id=1, source_target_pairs={{0,16},{4,20},{8,24},{12,28},{16,0},{20,4},{24,8},{28,12},{32,48},... | collective-permute-start | bytes 73736 | tf_op jit(solution)/shard_map/ppermute | solution.py:535
  139.2 3.5 %collective-permute-start.23 = (f32[48,128]{1,0:T(8,128)S(1)}, f32[48,128]{1,0:T(8,128)S(1)}, u32[]{:S(2)}, u32[]{:S(2)}) collective-permute-start(f32[48,128]{1,0:T(8,128)S(1)} %pad_maximum_fusion.6), channel_id=1, source_target_pairs={{0,24},{4,28},{8,0},{12,4},{16,8},{20,12},{24,16},{28,20},{32,56},... | collective-permute-start | bytes 73736 | tf_op jit(solution)/shard_map/ppermute | solution.py:535
  139.9 6.2 %collective-permute-start.10 = (f32[4,128]{1,0:T(4,128)S(1)}, f32[4,128]{1,0:T(4,128)S(1)}, u32[]{:S(2)}, u32[]{:S(2)}) collective-permute-start(f32[4,128]{1,0:T(4,128)S(1)} %multiply_add_fusion.6), channel_id=1, source_target_pairs={{0,2},{1,3},{2,0},{3,1},{4,6},{5,7},{6,4},{7,5},{8,10},{9,11},{10,... | collective-permute-start | bytes 6152 | tf_op jit(solution)/shard_map/ppermute | solution.py:548
  142.8 4.0 %collective-permute-start.24 = (f32[48,128]{1,0:T(8,128)S(1)}, f32[48,128]{1,0:T(8,128)S(1)}, u32[]{:S(2)}, u32[]{:S(2)}) collective-permute-start(f32[48,128]{1,0:T(8,128)S(1)} %pad_maximum_fusion.7), channel_id=1, source_target_pairs={{0,32},{4,36},{8,40},{12,44},{16,48},{20,52},{24,56},{28,60},{32,6... | collective-permute-start | bytes 73736 | tf_op jit(solution)/shard_map/ppermute | solution.py:535
  143.6 4.2 %collective-permute-start.25 = (f32[48,128]{1,0:T(8,128)S(1)}, f32[48,128]{1,0:T(8,128)S(1)}, u32[]{:S(2)}, u32[]{:S(2)}) collective-permute-start(f32[48,128]{1,0:T(8,128)S(1)} %pad_maximum_fusion.7), channel_id=1, source_target_pairs={{0,64},{4,68},{8,72},{12,76},{16,80},{20,84},{24,88},{28,92},{32,9... | collective-permute-start | bytes 73736 | tf_op jit(solution)/shard_map/ppermute | solution.py:535
  145.6 3.0 %collective-permute-start.26 = (f32[48,128]{1,0:T(8,128)S(1)}, f32[48,128]{1,0:T(8,128)S(1)}, u32[]{:S(2)}, u32[]{:S(2)}) collective-permute-start(f32[48,128]{1,0:T(8,128)S(1)} %pad_maximum_fusion.7), channel_id=1, source_target_pairs={{0,96},{4,100},{8,104},{12,108},{16,112},{20,116},{24,120},{28,124... | collective-permute-start | bytes 73736 | tf_op jit(solution)/shard_map/ppermute | solution.py:535
  177.2 3.8 %collective-permute-start.27 = (f32[16,128]{1,0:T(8,128)S(1)}, f32[16,128]{1,0:T(8,128)S(1)}, u32[]{:S(2)}, u32[]{:S(2)}) collective-permute-start(f32[16,128]{1,0:T(8,128)S(1)} %pad_maximum_fusion.9), channel_id=1, source_target_pairs={{0,1},{1,2},{2,3},{3,0},{4,5},{5,6},{6,7},{7,4},{8,9},{9,10},{10,1... | collective-permute-start | bytes 24584 | tf_op jit(solution)/shard_map/ppermute | solution.py:535
  177.3 4.1 %collective-permute-start.28 = (f32[16,128]{1,0:T(8,128)S(1)}, f32[16,128]{1,0:T(8,128)S(1)}, u32[]{:S(2)}, u32[]{:S(2)}) collective-permute-start(f32[16,128]{1,0:T(8,128)S(1)} %pad_maximum_fusion.9), channel_id=1, source_target_pairs={{0,2},{1,3},{2,0},{3,1},{4,6},{5,7},{6,4},{7,5},{8,10},{9,11},{10,... | collective-permute-start | bytes 24584 | tf_op jit(solution)/shard_map/ppermute | solution.py:535
  177.4 4.3 %collective-permute-start.29 = (f32[16,128]{1,0:T(8,128)S(1)}, f32[16,128]{1,0:T(8,128)S(1)}, u32[]{:S(2)}, u32[]{:S(2)}) collective-permute-start(f32[16,128]{1,0:T(8,128)S(1)} %pad_maximum_fusion.9), channel_id=1, source_target_pairs={{0,3},{1,0},{2,1},{3,2},{4,7},{5,4},{6,5},{7,6},{8,11},{9,8},{10,9... | collective-permute-start | bytes 24584 | tf_op jit(solution)/shard_map/ppermute | solution.py:535
  181.7 5.2 %collective-permute-start.30 = (f32[52,128]{1,0:T(8,128)S(1)}, f32[52,128]{1,0:T(8,128)S(1)}, u32[]{:S(2)}, u32[]{:S(2)}) collective-permute-start(f32[52,128]{1,0:T(8,128)S(1)} %pad_maximum_fusion.5), channel_id=1, source_target_pairs={{0,4},{4,0},{8,12},{12,8},{16,20},{20,16},{24,28},{28,24},{32,36},... | collective-permute-start | bytes 79880 | tf_op jit(solution)/shard_map/ppermute | solution.py:535
  186.9 18.4 %copy-start.2 = (f32[4096]{0:T(1024)S(1)}, f32[4096]{0:T(1024)}, u32[]{:S(2)}) copy-start(f32[4096]{0:T(1024)} %param.9) | copy-start | bytes 49156
  189.4 4.7 %collective-permute-start.31 = (f32[72,128]{1,0:T(8,128)S(1)}, f32[72,128]{1,0:T(8,128)S(1)}, u32[]{:S(2)}, u32[]{:S(2)}) collective-permute-start(f32[72,128]{1,0:T(8,128)S(1)} %pad_maximum_fusion.1), channel_id=1, source_target_pairs={{0,8},{4,12},{8,16},{12,20},{16,24},{20,28},{24,0},{28,4},{32,40},... | collective-permute-start | bytes 110600 | tf_op jit(solution)/shard_map/ppermute | solution.py:535
  190.6 4.4 %collective-permute-start.32 = (f32[72,128]{1,0:T(8,128)S(1)}, f32[72,128]{1,0:T(8,128)S(1)}, u32[]{:S(2)}, u32[]{:S(2)}) collective-permute-start(f32[72,128]{1,0:T(8,128)S(1)} %pad_maximum_fusion.1), channel_id=1, source_target_pairs={{0,16},{4,20},{8,24},{12,28},{16,0},{20,4},{24,8},{28,12},{32,48},... | collective-permute-start | bytes 110600 | tf_op jit(solution)/shard_map/ppermute | solution.py:535
  192.5 3.4 %collective-permute-start.33 = (f32[72,128]{1,0:T(8,128)S(1)}, f32[72,128]{1,0:T(8,128)S(1)}, u32[]{:S(2)}, u32[]{:S(2)}) collective-permute-start(f32[72,128]{1,0:T(8,128)S(1)} %pad_maximum_fusion.1), channel_id=1, source_target_pairs={{0,24},{4,28},{8,0},{12,4},{16,8},{20,12},{24,16},{28,20},{32,56},... | collective-permute-start | bytes 110600 | tf_op jit(solution)/shard_map/ppermute | solution.py:535
  195.9 4.1 %collective-permute-start.34 = (f32[72,128]{1,0:T(8,128)S(1)}, f32[72,128]{1,0:T(8,128)S(1)}, u32[]{:S(2)}, u32[]{:S(2)}) collective-permute-start(f32[72,128]{1,0:T(8,128)S(1)} %pad_maximum_fusion.2), channel_id=1, source_target_pairs={{0,32},{4,36},{8,40},{12,44},{16,48},{20,52},{24,56},{28,60},{32,6... | collective-permute-start | bytes 110600 | tf_op jit(solution)/shard_map/ppermute | solution.py:535
  196.4 4.3 %collective-permute-start.35 = (f32[72,128]{1,0:T(8,128)S(1)}, f32[72,128]{1,0:T(8,128)S(1)}, u32[]{:S(2)}, u32[]{:S(2)}) collective-permute-start(f32[72,128]{1,0:T(8,128)S(1)} %pad_maximum_fusion.2), channel_id=1, source_target_pairs={{0,64},{4,68},{8,72},{12,76},{16,80},{20,84},{24,88},{28,92},{32,9... | collective-permute-start | bytes 110600 | tf_op jit(solution)/shard_map/ppermute | solution.py:535
  199.0 3.1 %collective-permute-start.36 = (f32[72,128]{1,0:T(8,128)S(1)}, f32[72,128]{1,0:T(8,128)S(1)}, u32[]{:S(2)}, u32[]{:S(2)}) collective-permute-start(f32[72,128]{1,0:T(8,128)S(1)} %pad_maximum_fusion.2), channel_id=1, source_target_pairs={{0,96},{4,100},{8,104},{12,108},{16,112},{20,116},{24,120},{28,124... | collective-permute-start | bytes 110600 | tf_op jit(solution)/shard_map/ppermute | solution.py:535
  202.2 4.0 %collective-permute-start.37 = (f32[8,128]{1,0:T(8,128)S(1)}, f32[8,128]{1,0:T(8,128)S(1)}, u32[]{:S(2)}, u32[]{:S(2)}) collective-permute-start(f32[8,128]{1,0:T(8,128)S(1)} %bitcast_reduce_fusion.1), channel_id=1, source_target_pairs={{0,4},{4,0},{8,12},{12,8},{16,20},{20,16},{24,28},{28,24},{32,36},... | collective-permute-start | bytes 12296 | tf_op jit(solution)/shard_map/ppermute | solution.py:535
  206.2 3.8 %collective-permute-start.38 = (f32[12,128]{1,0:T(8,128)S(1)}, f32[12,128]{1,0:T(8,128)S(1)}, u32[]{:S(2)}, u32[]{:S(2)}) collective-permute-start(f32[12,128]{1,0:T(8,128)S(1)} %pad_maximum_fusion.10), channel_id=1, source_target_pairs={{0,1},{1,2},{2,3},{3,0},{4,5},{5,6},{6,7},{7,4},{8,9},{9,10},{10,1... | collective-permute-start | bytes 18440 | tf_op jit(solution)/shard_map/ppermute | solution.py:535
  207.3 4.0 %collective-permute-start.39 = (f32[12,128]{1,0:T(8,128)S(1)}, f32[12,128]{1,0:T(8,128)S(1)}, u32[]{:S(2)}, u32[]{:S(2)}) collective-permute-start(f32[12,128]{1,0:T(8,128)S(1)} %pad_maximum_fusion.10), channel_id=1, source_target_pairs={{0,2},{1,3},{2,0},{3,1},{4,6},{5,7},{6,4},{7,5},{8,10},{9,11},{10,... | collective-permute-start | bytes 18440 | tf_op jit(solution)/shard_map/ppermute | solution.py:535
  209.2 2.8 %collective-permute-start.40 = (f32[12,128]{1,0:T(8,128)S(1)}, f32[12,128]{1,0:T(8,128)S(1)}, u32[]{:S(2)}, u32[]{:S(2)}) collective-permute-start(f32[12,128]{1,0:T(8,128)S(1)} %pad_maximum_fusion.10), channel_id=1, source_target_pairs={{0,3},{1,0},{2,1},{3,2},{4,7},{5,4},{6,5},{7,6},{8,11},{9,8},{10,9... | collective-permute-start | bytes 18440 | tf_op jit(solution)/shard_map/ppermute | solution.py:535

commit v4 on v3

--- a/solution.py
+++ b/solution.py
@@ -182,14 +182,57 @@
             first += count
 
 
+def entry_kernel(gen_hbm, ref_hbm, gweight_hbm, rweight_hbm, own_ref, gen_ref, tile_ref, gweight_ref, rweight_ref, sem):
+    count = own_ref.shape[0]
+    at = pl.ds(pl.multiple_of(lax.axis_index("ref") * count, count), count)
+    pairs = (
+        (gen_hbm.at[at, :], own_ref),
+        (gweight_hbm, gweight_ref),
+        (rweight_hbm, rweight_ref),
+        (gen_hbm, gen_ref),
+        (ref_hbm.at[: tile_ref.shape[0], :], tile_ref),
+    )
+    copies = [pltpu.make_async_copy(src, dst, sem.at[k]) for k, (src, dst) in enumerate(pairs)]
+    for copy in copies:
+        copy.start()
+    for copy in copies:
+        copy.wait()
+
+
+def entry(gen, ref, gweight, rweight):
+    vmem = pl.BlockSpec(memory_space=pltpu.VMEM)
+    hbm = pl.BlockSpec(memory_space=pltpu.HBM)
+    width = gen.shape[1]
+    return pl.pallas_call(
+        entry_kernel,
+        in_specs=[hbm] * 4,
+        out_shape=(
+            pltpu.VMEM((LANES, width), gen.dtype),
+            pltpu.VMEM(gen.shape, gen.dtype),
+            pltpu.VMEM((TILE, width), ref.dtype),
+            pltpu.VMEM(gweight.shape, F32),
+            pltpu.VMEM(rweight.shape, F32),
+        ),
+        out_specs=(vmem,) * 5,
+        scratch_shapes=[pltpu.SemaphoreType.DMA((5,))],
+        compiler_params=pltpu.CompilerParams(vmem_limit_bytes=4 << 20),
+        name="entry",
+    )(*[hbm_array(x) for x in (gen, ref, gweight, rweight)])
+
+
+def total(x):
+    return jnp.sum(jnp.sum(x, axis=0, keepdims=True), axis=1, keepdims=True)
+
+
 def first_kernel(offset, steps, *refs):
     if offset == 0:
-        gen_hbm, ref_hbm, gweight_hbm, rweight_hbm, *refs = refs
-        d_ref, lrow_ref, lcol_ref, hcol_ref, hrow_ref, mass_ref, gen_ref, ahead_ref, *refs = refs
-        gweight_ref, *refs = refs
+        gen_ref, first_ref, gweight_ref, rweight_ref, ref_hbm, *refs = refs
+        d_ref, hcol_ref, hrow_ref, mass_ref, ahead_ref, vs_ref, rowacc_ref, u_ref, colsum_ref, peak_ref, *refs = refs
+        tile_ref, stage_ref, v_ref, sem = refs
     else:
-        gen_ref, ref_hbm, rweight_hbm, hrow_ref, first_ref, d_ref, lrow_ref, lcol_ref, hcol_ref, *refs = refs
-    tile_ref, stage_ref, rweight_ref, u_ref, v_ref, vs_ref, rowacc_ref, colsum_ref, peak_ref, sem = refs
+        gen_ref, first_ref, rweight_ref, hrow_ref, ref_hbm, before_ref, *refs = refs
+        hcol0_ref, vs_ref, rowacc0_ref, u0_ref, colsum0_ref, peak_ref, *refs = refs
+        d_ref, lrow_ref, lcol_ref, hcol_ref, tile_ref, stage_ref, v_ref, rowacc_ref, u_ref, colsum_ref, sem = refs
     rows, width = gen_ref.shape
     nq, nc = rows // LANES, d_ref.shape[1] // LANES
     chunks = TILE // LANES
@@ -201,50 +244,39 @@
         at = pl.ds(pl.multiple_of((first_tile + j) * TILE, TILE), TILE)
         return pltpu.make_async_copy(ref_hbm.at[at, :], tile_ref.at[j], sem.at[j])
 
-    rload = pltpu.make_async_copy(rweight_hbm, rweight_ref, sem.at[steps])
+    def product(j, tile, out_ref, columns):
+        for c, half in enumerate(norms(tile, 0, chunks, half_scale)):
+            row = pl.ds((first_tile + j) * chunks + c, 1)
+            hcol_ref[row, :] = half
+            u_ref[row, :] = jnp.log2(rweight_ref[row, :]) - half
+        dots = lax.dot_general(gen_ref[...], tile[...], (((1,), (1,)), ((), ())), preferred_element_type=F32)
+        out_ref[:, columns] = dots * dot_scale
+
+    def sums(j, straight, src_ref, base, keep):
+        mine = [u_ref[pl.ds(j * chunks + c, 1), :] for c in range(chunks)]
+        for c, part in enumerate(sweep(src_ref, base, chunks, mine, vs_ref, rowacc_ref, straight, keep)):
+            colsum_ref[pl.ds(j * chunks + c, 1), :] = part
+
+    whole = slice(0, TILE)
+    load(1).start()
     if offset == 0:
-        own = pltpu.make_async_copy(gen_hbm, gen_ref, sem.at[steps + 1])
-        gload = pltpu.make_async_copy(gweight_hbm, gweight_ref, sem.at[steps + 2])
-        ahead = pltpu.make_async_copy(
-            ref_hbm.at[steps * TILE : (steps + 1) * TILE, :], ahead_ref, sem.at[steps + 3]
-        )
-        for copy in (own, load(0), gload, rload):
-            copy.start()
-        own.wait()
-        load(1).start()
-        gload.wait()
-        rload.wait()
+        ahead = pltpu.make_async_copy(ref_hbm.at[steps * TILE : (steps + 1) * TILE, :], ahead_ref, sem.at[steps])
         for q, part in enumerate(norms(gen_ref, 0, nq, half_scale)):
             hrow_ref[q : q + 1, :] = part
             v_ref[q : q + 1, :] = jnp.log2(gweight_ref[q : q + 1, :]) - part
             hrow_ref[nq + q : nq + q + 1, :] = gweight_ref[q : q + 1, :]
-        lrow_ref[nq : 2 * nq, :] = jnp.broadcast_to(jnp.sum(rweight_ref[...]).reshape(1, 1), (nq, LANES))
-        mass_ref[...] = jnp.broadcast_to(jnp.sum(gweight_ref[...]).reshape(1, 1), (8, LANES))
-        load(0).wait()
-        tile0_ref = tile_ref.at[0]
+        mass_ref[...] = jnp.broadcast_to(total(gweight_ref[...]), (8, LANES))
+        product(0, first_ref, stage_ref, whole)
+        start_peak(stage_ref, u_ref[0:1, :], v_ref, vs_ref, peak_ref, rowacc_ref)
     else:
-        rload.start()
-        load(1).start()
         v_ref[...] = jnp.log2(hrow_ref[nq : 2 * nq, :]) - hrow_ref[0:nq, :]
-        rload.wait()
-        tile0_ref = first_ref
-
-    def product(j, tile):
-        for c, half in enumerate(norms(tile, 0, chunks, half_scale)):
-            row = pl.ds(j * chunks + c, 1)
-            hcol_ref[row, :] = half
-            u_ref[row, :] = jnp.log2(rweight_ref[pl.ds(offset * nc + j * chunks + c, 1), :]) - half
-        dots = lax.dot_general(gen_ref[...], tile[...], (((1,), (1,)), ((), ())), preferred_element_type=F32)
-        stage_ref[...] = dots * dot_scale
-
-    def sums(j, straight):
-        mine = [u_ref[pl.ds(j * chunks + c, 1), :] for c in range(chunks)]
-        found = sweep(stage_ref, 0, chunks, mine, vs_ref, rowacc_ref, straight, (d_ref, j * TILE))
-        for c, part in enumerate(found):
-            colsum_ref[pl.ds(j * chunks + c, 1), :] = part
-
-    product(0, tile0_ref)
-    start_peak(stage_ref, u_ref[0:1, :], v_ref, vs_ref, peak_ref, rowacc_ref)
+        lrow_ref[nq : 2 * nq, :] = jnp.broadcast_to(total(rweight_ref[...]), (nq, LANES))
+        hcol_ref[0:nc, :] = hcol0_ref[...]
+        rowacc_ref[...] = rowacc0_ref[...]
+        u_ref[0:nc, :] = u0_ref[...]
+        colsum_ref[0:nc, :] = colsum0_ref[...]
+        sums(steps - 1, True, before_ref, (steps - 1) * TILE, None)
+        product(0, first_ref, stage_ref, whole)
 
     def step(j, carry):
         load(j).wait()
@@ -253,24 +285,25 @@
         def _():
             load(j + 1).start()
 
-        if offset == 0:
-
-            @pl.when(j + 1 == steps)
-            def _():
-                ahead.start()
-
-        sums(j - 1, True)
-        product(j, tile_ref.at[j])
+        sums(first_tile + j - 1, True, stage_ref, 0, (d_ref, (j - 1) * TILE))
+        product(j, tile_ref.at[j], stage_ref, whole)
         return carry
 
-    lax.fori_loop(1, steps, step, 0)
-    sums(steps - 1, False)
-    finish([d_ref], u_ref, v_ref, vs_ref, rowacc_ref, colsum_ref, peak_ref, lrow_ref, lcol_ref)
     if offset == 0:
+        lax.fori_loop(1, steps - 1, step, 0)
+        load(steps - 1).wait()
+        ahead.start()
+        sums(steps - 2, True, stage_ref, 0, (d_ref, (steps - 2) * TILE))
+        product(steps - 1, tile_ref.at[steps - 1], d_ref, slice((steps - 1) * TILE, steps * TILE))
+        colsum_ref[(steps - 1) * chunks : steps * chunks, :] = jnp.zeros((chunks, LANES), F32)
         ahead.wait()
-
-
-def first_pass(offset, pieces, gen, ref, rweight, *more):
+    else:
+        lax.fori_loop(1, steps, step, 0)
+        sums(first_tile + steps - 1, False, stage_ref, 0, (d_ref, (steps - 1) * TILE))
+        finish([before_ref, d_ref], u_ref, v_ref, vs_ref, rowacc_ref, colsum_ref, peak_ref, lrow_ref, lcol_ref)
+
+
+def first_pass(offset, pieces, gen, first, ref, *more):
     rows, width = gen.shape
     cols = ref.shape[0] // pieces
     steps = cols // TILE
@@ -278,36 +311,37 @@
     vmem = pl.BlockSpec(memory_space=pltpu.VMEM)
     hbm = pl.BlockSpec(memory_space=pltpu.HBM)
     vec = lambda n: jax.ShapeDtypeStruct((n, LANES), F32)
-    outs = (pltpu.VMEM((rows, cols), F32), vec(nq if offset else 2 * nq), vec(nc), vec(nc))
+    lanes = pltpu.VMEM((rows, LANES), F32)
+    scratch = [
+        pltpu.VMEM((steps, TILE, width), jnp.bfloat16),
+        pltpu.VMEM((rows, TILE), F32),
+        pltpu.VMEM((nq, LANES), F32),
+    ]
     if offset == 0:
-        (gweight,) = more
-        outs += (vec(2 * nq), vec(8), pltpu.VMEM((rows, width), gen.dtype), pltpu.VMEM((TILE, width), ref.dtype))
-        specs = [hbm] * 4
-        operands = [hbm_array(gen), hbm_array(ref), hbm_array(gweight), hbm_array(rweight)]
-        weights = [pltpu.VMEM((nq, LANES), F32)]
+        gweight, rweight = more
+        operands = [vmem_array(gen), vmem_array(first), gweight, rweight, hbm_array(ref)]
+        outs = (
+            pltpu.VMEM((rows, cols), F32), vec(nc), vec(2 * nq), vec(8), pltpu.VMEM((TILE, width), ref.dtype),
+            lanes, lanes, vec(nc), vec(nc), vec(8),
+        )
+        specs = [vmem] * 4 + [hbm]
     else:
-        hrow, first = more
-        specs = [vmem, hbm, hbm, vmem, vmem]
-        operands = [vmem_array(gen), hbm_array(ref), hbm_array(rweight), hrow, vmem_array(first)]
-        weights = []
+        rweight, hrow, before, hcol, vs, rowacc, u, colsum, peak = more
+        operands = [vmem_array(gen), vmem_array(first), rweight, hrow, hbm_array(ref), vmem_array(before)]
+        operands += [hcol, vmem_array(vs), vmem_array(rowacc), u, colsum, peak]
+        outs = (pltpu.VMEM((rows, cols), F32), vec(2 * nq), vec(2 * nc), vec(2 * nc))
+        specs = [vmem] * 4 + [hbm] + [vmem] * 7
+        scratch += [
+            pltpu.VMEM((rows, LANES), F32),
+            pltpu.VMEM((2 * nc, LANES), F32),
+            pltpu.VMEM((2 * nc, LANES), F32),
+        ]
     return pl.pallas_call(
         functools.partial(first_kernel, offset, steps),
         in_specs=specs,
         out_shape=outs,
         out_specs=(vmem,) * len(outs),
-        scratch_shapes=weights
-        + [
-            pltpu.VMEM((steps, TILE, width), jnp.bfloat16),
-            pltpu.VMEM((rows, TILE), F32),
-            pltpu.VMEM(rweight.shape, F32),
-            pltpu.VMEM((nc, LANES), F32),
-            pltpu.VMEM((nq, LANES), F32),
-            pltpu.VMEM((rows, LANES), F32),
-            pltpu.VMEM((rows, LANES), F32),
-            pltpu.VMEM((nc, LANES), F32),
-            pltpu.VMEM((8, LANES), F32),
-            pltpu.SemaphoreType.DMA((steps + 4,)),
-        ],
+        scratch_shapes=scratch + [pltpu.SemaphoreType.DMA((steps + 1,))],
         compiler_params=pltpu.CompilerParams(vmem_limit_bytes=16 << 20),
     )(*operands)
 
@@ -544,8 +578,8 @@
         return merge([value] + shift(value, axis, perms), logs)
 
     def doubled(value, logs):
-        for bit in (1, 2):
-            value = merge([value, lax.ppermute(value, "ref", [(i, i ^ bit) for i in range(n_ref)])], logs)
+        for flip in (1, n_ref - 1):
+            value = merge([value, lax.ppermute(value, "ref", [(i, i ^ flip) for i in range(n_ref)])], logs)
         return value
 
     def run(gen_features, gen_weight, ref_features, ref_weight, ref_self):
@@ -562,11 +596,13 @@
         mine = ((z - b + n_z) % n_z) * n_y + (y - a + n_y) % n_y
         other = ((z - a + n_z) % n_z) * n_y + (y - b + n_y) % n_y
         place = jnp.where(core == 0, mine, other)
-        wg = gen_weight.reshape(nq, LANES)
-        wr = ref_weight.reshape(nc, LANES)
         at_zy = (lax.broadcasted_iota(jnp.int32, (n_zy, LANES), 0) == zy).astype(F32)
         at_x = (lax.broadcasted_iota(jnp.int32, (n_ref, LANES), 0) == x).astype(F32)
+        wg = gen_weight.reshape(nq, LANES)
         wg, place, at_zy, at_x = lax.optimization_barrier((wg, place, at_zy, at_x))
+        own, held, tile0, wg, wr = entry(
+            gen_features, ref_features, wg, ref_weight.reshape(nc, LANES)
+        )
 
         def to_cols(rows):
             picked = jnp.sum(jnp.where(at_x > 0, rows, 0.0), axis=0, keepdims=True)
@@ -576,19 +612,17 @@
             picked = jnp.sum(jnp.where(at_zy > 0, cols, 0.0), axis=0, keepdims=True)
             return jnp.where(at_x > 0, picked, 0.0)
 
-        own = lax.dynamic_slice_in_dim(gen_features, x * LANES, LANES, 0)
         got = [lax.ppermute(own, "gen", first_axis[k]) for k in (1, 2, 3)]
-        mate = lax.ppermute(gen_features, "gen", core_stage[0])
+        mate = lax.ppermute(held, "gen", core_stage[0])
         near = jnp.concatenate([own] + got, axis=0)
         up = lax.ppermute(near, "gen", second_axis[1])
         down = lax.ppermute(near, "gen", second_axis[3])
         low_far = lax.ppermute(up[: 2 * LANES], "gen", second_axis[1])
         high_far = lax.ppermute(down[2 * LANES :], "gen", second_axis[3])
 
-        d0, row0, lcol0, hcol0, mine, gmass, held, ahead = first_pass(0, 2, gen_features, ref_features, wr, wg)
+        d0, hcol, mine, gmass, ahead, *carried = first_pass(0, 2, held, tile0, ref_features, wg, wr)
         theirs = lax.ppermute(mine, "gen", core_stage[0])
-        d1, row1, lcol1, hcol1 = first_pass(1, 2, held, ref_features, wr, mine, ahead)
-        hcol = jnp.concatenate([hcol0, hcol1], axis=0)
+        d1, row_part, lcol, hcol = first_pass(1, 2, held, ahead, ref_features, wr, mine, d0, hcol, *carried)
         hrow = mine[:nq]
         weight = jnp.concatenate([wg, theirs[nq:]], axis=0)
         e0, z1_0, hs, ws = self_first(held, mate, [near], mine, theirs, place, 0)
@@ -596,9 +630,8 @@
         e2, z1_2 = self_first(held, mate, [low_far, high_far], hs, ws, place, 12)
         e = [e0, e1, e2]
 
-        row_part = jnp.concatenate([log_add([row0[:nq], row1]), row0[nq:]], axis=0)
         row_part = doubled(row_part, nq)
-        col_part = jnp.concatenate([lcol0, lcol1, gmass], axis=0)
+        col_part = jnp.concatenate([lcol, gmass], axis=0)
         col_part = stage(col_part, "gen", core_stage, nc)
         col_part = jnp.concatenate([col_part, to_cols(wg)], axis=0)
         col_part = stage(col_part, "gen", y_stage, nc)

time: 214 us -> 211 us (0.986)
  starting transfers between devices: 57 us -> 60.3 us
  waiting for transfers between devices: 34.9 us -> 31.7 us
    pallas_call x2, Pallas kernels: 43.3 us -> 40 us  [first_pass(): pl.pallas_call(functools.partial(first_kernel, offset, steps), in_specs=s...]
    ppermute x28, starting transfers between devices: 36.6 us -> 39.2 us  [shift(): return [lax.ppermute(value, axis, perm) for perm in perms]]
    pallas_call x0 -> x1, Pallas kernels: none -> 2.48 us  [entry(): pl.pallas_call(entry_kernel, in_specs=[hbm] * 4, out_shape=(pltpu.VMEM((L...]
  transfers between devices with their start and end apart: 41 -> 41, of which waited for: 20 -> 18; matrix products, arithmetic and copies ran while one was open for 1% -> 1% of each run, Pallas kernels for 39% -> 38%
where the time goes in v4:
time: 211 us; the launch traced here: 210 us
  Pallas kernels  114 us (54%)
  starting transfers between devices  60.3 us (29%)
  waiting for transfers between devices  31.7 us (15%)
  other arithmetic  2.55 us (1%)
    pallas_call x2, Pallas kernels, next_pass(): pl.pallas_call(functools.partial(next_kernel, len(parts)), in_specs=[vmem...  53.1 us
    pallas_call x2, Pallas kernels, first_pass(): pl.pallas_call(functools.partial(first_kernel, offset, steps), in_specs=s...  40 us
    ppermute x28, starting transfers between devices, shift(): return [lax.ppermute(value, axis, perm) for perm in perms]  39.2 us
    ppermute x28, waiting for transfers between devices, shift(): return [lax.ppermute(value, axis, perm) for perm in perms]  31.6 us
    pallas_call x3, Pallas kernels, self_first(): pl.pallas_call(functools.partial(self_first_kernel, len(sources), first),...  14 us
    ppermute x3, starting transfers between devices, run(): got = [lax.ppermute(own, 'gen', first_axis[k]) for k in (1, 2, 3)]  6.55 us
    ppermute x4, starting transfers between devices, doubled(): lax.ppermute(value, 'ref', [(i, i ^ flip) for i in range(n_ref)])  5.92 us
    pallas_call x2, Pallas kernels, self_apply(): pl.pallas_call(functools.partial(kernel, len(parts)), in_specs=[vmem] * (...  4.54 us
  transfers between devices with their start and end apart: 41, of which 18 were waited for; matrix products, arithmetic and copies ran while one was open for 1% of the time, Pallas kernels for 38%

profile of v4, /device:TPU:1, one launch (start us, length us, event | category | flops | bytes accessed | tf_op | source)
XLA Modules:
  0.0 210.3 jit_solution(6085077139480140917)
XLA Ops:
  0.9 2.5 %entry.1 = (bf16[128,2048]{1,0:T(8,128)(2,1)S(1)}, bf16[512,2048]{1,0:T(8,128)(2,1)S(1)}, bf16[512,2048]{1,0:T(8,128)(2,1)S(1)}, f32[4,128]{1,0:T(4,128)S(1)}, f32[32,128]{1,0:T(8,128)S(1)}) custom-call(bf16[512,2048]{1,0:T(8,128)(2,1)} %gen_hbm.1, bf16[4096,2048]{1,0:T(8,128)(2,1)} %refs_4_.3, f32[4,128]{1,0:T(4,128)} %bitcast.22, f32[32,128]{1,0:T(8,128)} %bitcast.21), custom_call_target="tpu_custom_call" | custom-call | tf_op jit(solution)/shard_map/entry/pallas_call | solution.py:206
  3.4 2.5 %collective-permute-start.13 = (bf16[128,2048]{1,0:T(8,128)(2,1)S(1)}, bf16[128,2048]{1,0:T(8,128)(2,1)S(1)}, u32[]{:S(2)}, u32[]{:S(2)}) collective-permute-start(bf16[128,2048]{1,0:T(8,128)(2,1)S(1)} %get-tuple-element.61), channel_id=1, source_target_pairs={{0,8},{4,36},{8,16},{12,44},{16,24},{20,52},{24,0},{28,60},{32,40}... | collective-permute-start | bytes 1572872 | tf_op jit(solution)/shard_map/ppermute | solution.py:615
  5.9 3.3 %collective-permute-start.14 = (bf16[128,2048]{1,0:T(8,128)(2,1)S(1)}, bf16[128,2048]{1,0:T(8,128)(2,1)S(1)}, u32[]{:S(2)}, u32[]{:S(2)}) collective-permute-start(bf16[128,2048]{1,0:T(8,128)(2,1)S(1)} %get-tuple-element.61), channel_id=1, source_target_pairs={{0,16},{4,68},{8,24},{12,76},{16,0},{20,84},{24,8},{28,92},{32,48}... | collective-permute-start | bytes 1572872 | tf_op jit(solution)/shard_map/ppermute | solution.py:615
  9.2 0.7 collective-permute-start.15
  9.9 7.3 %shard_map.76 = (f32[512,2048]{1,0:T(8,128)S(1)}, f32[16,128]{1,0:T(8,128)S(1)}, f32[8,128]{1,0:T(8,128)S(1)}, f32[8,128]{1,0:T(8,128)S(1)}, bf16[512,2048]{1,0:...) custom-call(bf16[512,2048]{1,0:T(8,128)(2,1)S(1)} %get-tuple-element, ...), custom_call_target="tpu_custom_call" | custom-call | tf_op jit(solution)/shard_map/pallas_call | solution.py:339
  17.2 32.7 %shard_map.77 = (f32[512,2048]{1,0:T(8,128)S(1)}, f32[8,128]{1,0:T(8,128)S(1)}, f32[32,128]{1,0:T(8,128)S(1)}, f32[32,128]{1,0:T(8,128)S(1)}) custom-call(bf16[512,2048]{1,0:T(8,128)(2,1)S(1)} %get-tuple-element.39.refs_0_, bf16[512,2048]{1,0:T(8,128)(2,1)S(1)} %get-tuple-element.44.refs_1_, f32[32,128]{1,0:T(8,128)S(1)} %get-tuple-element.42.refs_3_.refs_2_, ...), custom_call_target="tpu_custom_call" | custom-call | tf_op jit(solution)/shard_map/pallas_call | solution.py:339
  50.0 0.9 collective-permute-start.2
  50.9 1.2 collective-permute-start
  52.3 0.6 collective-permute-start.17
  53.0 2.2 %collective-permute-start.18 = (bf16[512,2048]{1,0:T(8,128)(2,1)S(1)}, bf16[512,2048]{1,0:T(8,128)(2,1)S(1)}, u32[]{:S(2)}, u32[]{:S(2)}) collective-permute-start(bf16[512,2048]{1,0:T(8,128)(2,1)S(1)} %constant_dynamic-update-slice_fusion.refs_2_), channel_id=1, source_target_pairs={{0,96},{4,28},{8,104},{12,4},{16,112},{20,12},{24,120},{28,20},{32... | collective-permute-start | bytes 6291464 | tf_op jit(solution)/shard_map/ppermute | solution.py:619
  55.3 1.9 collective-permute-start.1
  57.2 2.6 %collective-permute-start.12 = (bf16[512,2048]{1,0:T(8,128)(2,1)S(1)}, bf16[512,2048]{1,0:T(8,128)(2,1)S(1)}, u32[]{:S(2)}, u32[]{:S(2)}) collective-permute-start(bf16[512,2048]{1,0:T(8,128)(2,1)S(1)} %get-tuple-element.39.refs_0_), channel_id=1, source_target_pairs={{0,4},{4,0},{8,12},{12,8},{16,20},{20,16},{24,28},{28,24},{32,36},... | collective-permute-start | bytes 6291464 | tf_op jit(solution)/shard_map/ppermute | solution.py:616
  59.8 2.3 %collective-permute-start.4 = (f32[56,128]{1,0:T(8,128)S(1)}, f32[56,128]{1,0:T(8,128)S(1)}, u32[]{:S(2)}, u32[]{:S(2)}) collective-permute-start(f32[56,128]{1,0:T(8,128)S(1)} %pad_maximum_fusion.2), channel_id=1, source_target_pairs={{0,16},{4,20},{8,24},{12,28},{16,0},{20,4},{24,8},{28,12},{32,48},... | collective-permute-start | bytes 86024 | tf_op jit(solution)/shard_map/ppermute | solution.py:569
  62.1 17.6 %collective-permute-done.3 = f32[56,128]{1,0:T(8,128)S(1)} collective-permute-done((f32[56,128]{1,0:T(8,128)S(1)}, f32[56,128]{1,0:T(8,128)S(1)}, u32[]{:S(2)}, u32[]{:S(2)}) %collective-permute-start.3) | collective-permute-done | bytes 28704 | tf_op jit(solution)/shard_map/ppermute | solution.py:569
  79.7 0.8 collective-permute-start.5
  80.5 2.0 collective-permute-done.5
  82.5 1.7 collective-permute-start.6
  84.2 3.8 %collective-permute-start.7 = (f32[56,128]{1,0:T(8,128)S(1)}, f32[56,128]{1,0:T(8,128)S(1)}, u32[]{:S(2)}, u32[]{:S(2)}) collective-permute-start(f32[56,128]{1,0:T(8,128)S(1)} %pad_maximum_fusion.3), channel_id=1, source_target_pairs={{0,64},{4,68},{8,72},{12,76},{16,80},{20,84},{24,88},{28,92},{32,9... | collective-permute-start | bytes 86024 | tf_op jit(solution)/shard_map/ppermute | solution.py:569
  88.1 0.3 collective-permute-start.8
  88.8 2.6 %collective-permute-start.20 = (bf16[256,2048]{1,0:T(8,128)(2,1)S(1)}, bf16[256,2048]{1,0:T(8,128)(2,1)S(1)}, u32[]{:S(2)}, u32[]{:S(2)}) collective-permute-start(bf16[256,2048]{1,0:T(8,128)(2,1)S(1)} %slice.310), channel_id=1, source_target_pairs={{0,96},{4,28},{8,104},{12,4},{16,112},{20,12},{24,120},{28,20},{32... | collective-permute-start | bytes 3145736 | tf_op jit(solution)/shard_map/ppermute | solution.py:621
  91.5 26.4 %shard_map.78 = (f32[4,128]{1,0:T(4,128)S(1)}, f32[32,128]{1,0:T(8,128)S(1)}) custom-call(f32[512,2048]{1,0:T(8,128)S(1)} %get-tuple-element.45.refs_5_.refs_0_, f32[512,2048]{1,0:T(8,128)S(1)} %get-tuple-element.53.refs_1_, f32[32,128]{1,0:T(8,128)S(1)} %get-tuple-element.85.refs_2_, f32[4,128]{1,0:T(4,128)S(1)} %get-tuple-element.83.refs_3_), custom_call_target="tpu_custom_call" | custom-call | tf_op jit(solution)/shard_map/pallas_call | solution.py:375
  118.0 0.5 collective-permute-start.16
  118.5 0.7 collective-permute-done.11
  119.2 0.3 collective-permute-start.9
  119.5 3.8 %shard_map.79 = (f32[1024,512]{1,0:T(8,128)S(1)}, f32[16,128]{1,0:T(8,128)S(1)}, f32[1024,128]{1,0:T(8,128)S(1)}, f32[1024,128]{1,0:T(8,128)S(1)}) custom-call(bf16[512,2048]{1,0:T(8,128)(2,1)S(1)} %get-tuple-element.39.refs_0_, bf16[512,2048]{1,0:T(8,128)(2,1)S(1)} %collective-permute-done.12.refs_1_, ...), custom_call_target="tpu_custom_call" | custom-call | tf_op jit(solution)/shard_map/pallas_call | solution.py:456
  123.3 6.5 %shard_map.80 = (f32[1024,1024]{1,0:T(8,128)S(1)}, f32[16,128]{1,0:T(8,128)S(1)}) custom-call(bf16[512,2048]{1,0:T(8,128)(2,1)S(1)} %get-tuple-element.39.refs_0_, bf16[512,2048]{1,0:T(8,128)(2,1)S(1)} %collective-permute-done.12.refs_1_, bf16[512,2048]{1,0:T(8,128)(2,1)S(1)} %collective-permute-done.17.refs_2_, ...), custom_call_target="tpu_custom_call" | custom-call | tf_op jit(solution)/shard_map/pallas_call | solution.py:456
  129.8 3.8 %shard_map.81 = (f32[1024,512]{1,0:T(8,128)S(1)}, f32[16,128]{1,0:T(8,128)S(1)}) custom-call(bf16[512,2048]{1,0:T(8,128)(2,1)S(1)} %get-tuple-element.39.refs_0_, bf16[512,2048]{1,0:T(8,128)(2,1)S(1)} %collective-permute-done.12.refs_1_, bf16[256,2048]{1,0:T(8,128)(2,1)S(1)} %collective-permute-done.19.refs_2_, ...), custom_call_target="tpu_custom_call" | custom-call | tf_op jit(solution)/shard_map/pallas_call | solution.py:456
  133.6 2.1 collective-permute-start.22
  135.7 0.6 collective-permute-start.23
  136.3 2.6 %collective-permute-start.10 = (f32[4,128]{1,0:T(4,128)S(1)}, f32[4,128]{1,0:T(4,128)S(1)}, u32[]{:S(2)}, u32[]{:S(2)}) collective-permute-start(f32[4,128]{1,0:T(4,128)S(1)} %multiply_add_fusion.6), channel_id=1, source_target_pairs={{0,3},{1,2},{2,1},{3,0},{4,7},{5,6},{6,5},{7,4},{8,11},{9,10},{10,... | collective-permute-start | bytes 6152 | tf_op jit(solution)/shard_map/ppermute | solution.py:582
  139.0 1.2 collective-permute-start.24
  140.2 1.5 collective-permute-start.25
  141.7 1.0 collective-permute-start.26
  142.7 0.2 collective-permute-done.24
  142.9 1.5 collective-permute-done.25
  144.5 26.7 %shard_map.82 = (f32[4,128]{1,0:T(4,128)S(1)}, f32[32,128]{1,0:T(8,128)S(1)}) custom-call(f32[512,2048]{1,0:T(8,128)S(1)} %get-tuple-element.45.refs_5_.refs_0_, f32[512,2048]{1,0:T(8,128)S(1)} %get-tuple-element.53.refs_1_, f32[32,128]{1,0:T(8,128)S(1)} %get-tuple-element.81.refs_2_, f32[4,128]{1,0:T(4,128)S(1)} %get-tuple-element.79.refs_3_), custom_call_target="tpu_custom_call" | custom-call | tf_op jit(solution)/shard_map/pallas_call | solution.py:375
  171.2 2.1 %shard_map.83 = f32[8,128]{1,0:T(8,128)S(1)} custom-call(f32[1024,512]{1,0:T(8,128)S(1)} %get-tuple-element.69.refs_0_, f32[1024,1024]{1,0:T(8,128)S(1)} %get-tuple-element.70.refs_1_, f32[1024,512]{1,0:T(8,128)S(1)} %get-tuple-element.71.refs_2_, f32[16,128]{1,0:T(8,128)S(1)} %get-tuple-element.77.refs_3_, s32[16]{0:T(128)S(1)} %broadcast_select_fusion.4.refs_5_.refs_6_.refs_4_), custom_call_target="tpu_custom_call" | custom-call | tf_op jit(solution)/shard_map/pallas_call | solution.py:528
  173.5 2.6 %collective-permute-start.29 = (f32[16,128]{1,0:T(8,128)S(1)}, f32[16,128]{1,0:T(8,128)S(1)}, u32[]{:S(2)}, u32[]{:S(2)}) collective-permute-start(f32[16,128]{1,0:T(8,128)S(1)} %pad_maximum_fusion.8), channel_id=1, source_target_pairs={{0,3},{1,0},{2,1},{3,2},{4,7},{5,4},{6,5},{7,6},{8,11},{9,8},{10,9... | collective-permute-start | bytes 24584 | tf_op jit(solution)/shard_map/ppermute | solution.py:569
  176.1 1.0 collective-permute-done.27
  177.1 0.4 collective-permute-done.28
  177.5 0.3 collective-permute-done.29
  177.8 5.0 %collective-permute-start.30 = (f32[52,128]{1,0:T(8,128)S(1)}, f32[52,128]{1,0:T(8,128)S(1)}, u32[]{:S(2)}, u32[]{:S(2)}) collective-permute-start(f32[52,128]{1,0:T(8,128)S(1)} %pad_maximum_fusion.4), channel_id=1, source_target_pairs={{0,4},{4,0},{8,12},{12,8},{16,20},{20,16},{24,28},{28,24},{32,36},... | collective-permute-start | bytes 79880 | tf_op jit(solution)/shard_map/ppermute | solution.py:569
  182.9 0.9 collective-permute-done.30
  183.7 2.4 %shard_map.84 = f32[16,128]{1,0:T(8,128)S(1)} custom-call(f32[1024,512]{1,0:T(8,128)S(1)} %get-tuple-element.69.refs_0_, f32[1024,1024]{1,0:T(8,128)S(1)} %get-tuple-element.70.refs_1_, f32[1024,512]{1,0:T(8,128)S(1)} %get-tuple-element.71.refs_2_, f32[8,128]{1,0:T(8,128)S(1)} %get-tuple-element.99.refs_3_, s32[16]{0:T(128)S(1)} %broadcast_select_fusion.4.refs_5_.refs_6_.refs_4_), custom_call_target="tpu_custom_call" | custom-call | tf_op jit(solution)/shard_map/pallas_call | solution.py:528
  186.2 1.1 collective-permute-start.31
  187.3 1.8 collective-permute-start.32
  189.1 1.4 collective-permute-start.33
  190.5 1.2 collective-permute-done.32
  191.7 0.9 collective-permute-done.33
  192.7 0.6 collective-permute-start.34
  193.2 2.5 %collective-permute-start.35 = (f32[72,128]{1,0:T(8,128)S(1)}, f32[72,128]{1,0:T(8,128)S(1)}, u32[]{:S(2)}, u32[]{:S(2)}) collective-permute-start(f32[72,128]{1,0:T(8,128)S(1)} %pad_maximum_fusion.1), channel_id=1, source_target_pairs={{0,64},{4,68},{8,72},{12,76},{16,80},{20,84},{24,88},{28,92},{32,9... | collective-permute-start | bytes 110600 | tf_op jit(solution)/shard_map/ppermute | solution.py:569
  195.8 0.5 collective-permute-start.36
  196.2 0.5 collective-permute-done.34
  196.7 0.8 collective-permute-done.35
  197.5 1.3 collective-permute-done.36
  198.9 3.2 %collective-permute-start.37 = (f32[8,128]{1,0:T(8,128)S(1)}, f32[8,128]{1,0:T(8,128)S(1)}, u32[]{:S(2)}, u32[]{:S(2)}) collective-permute-start(f32[8,128]{1,0:T(8,128)S(1)} %bitcast_reduce_fusion.1), channel_id=1, source_target_pairs={{0,4},{4,0},{8,12},{12,8},{16,20},{20,16},{24,28},{28,24},{32,36},... | collective-permute-start | bytes 12296 | tf_op jit(solution)/shard_map/ppermute | solution.py:569
  202.1 0.6 bitcast_reduce_fusion
  202.8 0.2 collective-permute-done.37
  203.0 1.5 collective-permute-start.38
  204.5 1.8 collective-permute-start.39
  206.3 0.7 collective-permute-start.40
  207.0 1.5 collective-permute-done.39
  208.5 0.6 collective-permute-done.40
  209.1 1.2 fusion.13
  (94 shorter events, 1.8 us)
Async XLA Ops:
  3.4 48.8 %collective-permute-start.13 = (bf16[128,2048]{1,0:T(8,128)(2,1)S(1)}, bf16[128,2048]{1,0:T(8,128)(2,1)S(1)}, u32[]{:S(2)}, u32[]{:S(2)}) collective-permute-start(bf16[128,2048]{1,0:T(8,128)(2,1)S(1)} %get-tuple-element.61), channel_id=1, source_target_pairs={{0,8},{4,36},{8,16},{12,44},{16,24},{20,52},{24,0},{28,60},{32,40}... | collective-permute-start | bytes 1572872 | tf_op jit(solution)/shard_map/ppermute | solution.py:615
  5.9 46.3 %collective-permute-start.14 = (bf16[128,2048]{1,0:T(8,128)(2,1)S(1)}, bf16[128,2048]{1,0:T(8,128)(2,1)S(1)}, u32[]{:S(2)}, u32[]{:S(2)}) collective-permute-start(bf16[128,2048]{1,0:T(8,128)(2,1)S(1)} %get-tuple-element.61), channel_id=1, source_target_pairs={{0,16},{4,68},{8,24},{12,76},{16,0},{20,84},{24,8},{28,92},{32,48}... | collective-permute-start | bytes 1572872 | tf_op jit(solution)/shard_map/ppermute | solution.py:615
  9.2 43.1 %collective-permute-start.15 = (bf16[128,2048]{1,0:T(8,128)(2,1)S(1)}, bf16[128,2048]{1,0:T(8,128)(2,1)S(1)}, u32[]{:S(2)}, u32[]{:S(2)}) collective-permute-start(bf16[128,2048]{1,0:T(8,128)(2,1)S(1)} %get-tuple-element.61), channel_id=1, source_target_pairs={{0,24},{4,100},{8,0},{12,108},{16,8},{20,116},{24,16},{28,124},{32... | collective-permute-start | bytes 1572872 | tf_op jit(solution)/shard_map/ppermute | solution.py:615
  50.0 5.2 %collective-permute-start.2 = (f32[40,128]{1,0:T(8,128)S(1)}, f32[40,128]{1,0:T(8,128)S(1)}, u32[]{:S(2)}, u32[]{:S(2)}) collective-permute-start(f32[40,128]{1,0:T(8,128)S(1)} %pad_maximum_fusion.7), channel_id=1, source_target_pairs={{0,4},{4,0},{8,12},{12,8},{16,20},{20,16},{24,28},{28,24},{32,36},... | collective-permute-start | bytes 61448 | tf_op jit(solution)/shard_map/ppermute | solution.py:569
  50.9 4.3 %collective-permute-start = (f32[8,128]{1,0:T(8,128)S(1)}, f32[8,128]{1,0:T(8,128)S(1)}, u32[]{:S(2)}, u32[]{:S(2)}) collective-permute-start(f32[8,128]{1,0:T(8,128)S(1)} %get-tuple-element.52), channel_id=1, source_target_pairs={{0,1},{1,0},{2,3},{3,2},{4,5},{5,4},{6,7},{7,6},{8,9},{9,8},{10,11... | collective-permute-start | bytes 12296 | tf_op jit(solution)/shard_map/ppermute | solution.py:582
  52.3 35.8 %collective-permute-start.17 = (bf16[512,2048]{1,0:T(8,128)(2,1)S(1)}, bf16[512,2048]{1,0:T(8,128)(2,1)S(1)}, u32[]{:S(2)}, u32[]{:S(2)}) collective-permute-start(bf16[512,2048]{1,0:T(8,128)(2,1)S(1)} %constant_dynamic-update-slice_fusion.refs_2_), channel_id=1, source_target_pairs={{0,32},{4,12},{8,40},{12,20},{16,48},{20,28},{24,56},{28,4},{32,64... | collective-permute-start | bytes 6291464 | tf_op jit(solution)/shard_map/ppermute | solution.py:618
  53.0 35.5 %collective-permute-start.18 = (bf16[512,2048]{1,0:T(8,128)(2,1)S(1)}, bf16[512,2048]{1,0:T(8,128)(2,1)S(1)}, u32[]{:S(2)}, u32[]{:S(2)}) collective-permute-start(bf16[512,2048]{1,0:T(8,128)(2,1)S(1)} %constant_dynamic-update-slice_fusion.refs_2_), channel_id=1, source_target_pairs={{0,96},{4,28},{8,104},{12,4},{16,112},{20,12},{24,120},{28,20},{32... | collective-permute-start | bytes 6291464 | tf_op jit(solution)/shard_map/ppermute | solution.py:619
  55.2 24.5 %collective-permute-start.3 = (f32[56,128]{1,0:T(8,128)S(1)}, f32[56,128]{1,0:T(8,128)S(1)}, u32[]{:S(2)}, u32[]{:S(2)}) collective-permute-start(f32[56,128]{1,0:T(8,128)S(1)} %pad_maximum_fusion.2), channel_id=1, source_target_pairs={{0,8},{4,12},{8,16},{12,20},{16,24},{20,28},{24,0},{28,4},{32,40},... | collective-permute-start | bytes 86024 | tf_op jit(solution)/shard_map/ppermute | solution.py:569
  55.3 4.5 %collective-permute-start.1 = (f32[8,128]{1,0:T(8,128)S(1)}, f32[8,128]{1,0:T(8,128)S(1)}, u32[]{:S(2)}, u32[]{:S(2)}) collective-permute-start(f32[8,128]{1,0:T(8,128)S(1)} %pad_maximum_fusion.10), channel_id=1, source_target_pairs={{0,3},{1,2},{2,1},{3,0},{4,7},{5,6},{6,5},{7,4},{8,11},{9,10},{10,... | collective-permute-start | bytes 12296 | tf_op jit(solution)/shard_map/ppermute | solution.py:582
  57.2 62.3 %collective-permute-start.12 = (bf16[512,2048]{1,0:T(8,128)(2,1)S(1)}, bf16[512,2048]{1,0:T(8,128)(2,1)S(1)}, u32[]{:S(2)}, u32[]{:S(2)}) collective-permute-start(bf16[512,2048]{1,0:T(8,128)(2,1)S(1)} %get-tuple-element.39.refs_0_), channel_id=1, source_target_pairs={{0,4},{4,0},{8,12},{12,8},{16,20},{20,16},{24,28},{28,24},{32,36},... | collective-permute-start | bytes 6291464 | tf_op jit(solution)/shard_map/ppermute | solution.py:616
  59.8 20.6 %collective-permute-start.4 = (f32[56,128]{1,0:T(8,128)S(1)}, f32[56,128]{1,0:T(8,128)S(1)}, u32[]{:S(2)}, u32[]{:S(2)}) collective-permute-start(f32[56,128]{1,0:T(8,128)S(1)} %pad_maximum_fusion.2), channel_id=1, source_target_pairs={{0,16},{4,20},{8,24},{12,28},{16,0},{20,4},{24,8},{28,12},{32,48},... | collective-permute-start | bytes 86024 | tf_op jit(solution)/shard_map/ppermute | solution.py:569
  79.7 2.8 %collective-permute-start.5 = (f32[56,128]{1,0:T(8,128)S(1)}, f32[56,128]{1,0:T(8,128)S(1)}, u32[]{:S(2)}, u32[]{:S(2)}) collective-permute-start(f32[56,128]{1,0:T(8,128)S(1)} %pad_maximum_fusion.2), channel_id=1, source_target_pairs={{0,24},{4,28},{8,0},{12,4},{16,8},{20,12},{24,16},{28,20},{32,56},... | collective-permute-start | bytes 86024 | tf_op jit(solution)/shard_map/ppermute | solution.py:569
  82.5 6.2 %collective-permute-start.6 = (f32[56,128]{1,0:T(8,128)S(1)}, f32[56,128]{1,0:T(8,128)S(1)}, u32[]{:S(2)}, u32[]{:S(2)}) collective-permute-start(f32[56,128]{1,0:T(8,128)S(1)} %pad_maximum_fusion.3), channel_id=1, source_target_pairs={{0,32},{4,36},{8,40},{12,44},{16,48},{20,52},{24,56},{28,60},{32,6... | collective-permute-start | bytes 86024 | tf_op jit(solution)/shard_map/ppermute | solution.py:569
  84.2 7.2 %collective-permute-start.7 = (f32[56,128]{1,0:T(8,128)S(1)}, f32[56,128]{1,0:T(8,128)S(1)}, u32[]{:S(2)}, u32[]{:S(2)}) collective-permute-start(f32[56,128]{1,0:T(8,128)S(1)} %pad_maximum_fusion.3), channel_id=1, source_target_pairs={{0,64},{4,68},{8,72},{12,76},{16,80},{20,84},{24,88},{28,92},{32,9... | collective-permute-start | bytes 86024 | tf_op jit(solution)/shard_map/ppermute | solution.py:569
  88.1 3.3 %collective-permute-start.8 = (f32[56,128]{1,0:T(8,128)S(1)}, f32[56,128]{1,0:T(8,128)S(1)}, u32[]{:S(2)}, u32[]{:S(2)}) collective-permute-start(f32[56,128]{1,0:T(8,128)S(1)} %pad_maximum_fusion.3), channel_id=1, source_target_pairs={{0,96},{4,100},{8,104},{12,108},{16,112},{20,116},{24,120},{28,124... | collective-permute-start | bytes 86024 | tf_op jit(solution)/shard_map/ppermute | solution.py:569
  88.5 41.3 %collective-permute-start.19 = (bf16[256,2048]{1,0:T(8,128)(2,1)S(1)}, bf16[256,2048]{1,0:T(8,128)(2,1)S(1)}, u32[]{:S(2)}, u32[]{:S(2)}) collective-permute-start(bf16[256,2048]{1,0:T(8,128)(2,1)S(1)} %slice.309), channel_id=1, source_target_pairs={{0,32},{4,12},{8,40},{12,20},{16,48},{20,28},{24,56},{28,4},{32,64... | collective-permute-start | bytes 3145736 | tf_op jit(solution)/shard_map/ppermute | solution.py:620
  88.8 41.0 %collective-permute-start.20 = (bf16[256,2048]{1,0:T(8,128)(2,1)S(1)}, bf16[256,2048]{1,0:T(8,128)(2,1)S(1)}, u32[]{:S(2)}, u32[]{:S(2)}) collective-permute-start(bf16[256,2048]{1,0:T(8,128)(2,1)S(1)} %slice.310), channel_id=1, source_target_pairs={{0,96},{4,28},{8,104},{12,4},{16,112},{20,12},{24,120},{28,20},{32... | collective-permute-start | bytes 3145736 | tf_op jit(solution)/shard_map/ppermute | solution.py:621
  117.9 1.3 collective-permute-start.11
  118.0 1.5 collective-permute-start.16
  119.2 17.1 %collective-permute-start.9 = (f32[4,128]{1,0:T(4,128)S(1)}, f32[4,128]{1,0:T(4,128)S(1)}, u32[]{:S(2)}, u32[]{:S(2)}) collective-permute-start(f32[4,128]{1,0:T(4,128)S(1)} %get-tuple-element.59), channel_id=1, source_target_pairs={{0,1},{1,0},{2,3},{3,2},{4,5},{5,4},{6,7},{7,6},{8,9},{9,8},{10,11... | collective-permute-start | bytes 6152 | tf_op jit(solution)/shard_map/ppermute | solution.py:582
  133.6 5.3 %collective-permute-start.21 = (f32[48,128]{1,0:T(8,128)S(1)}, f32[48,128]{1,0:T(8,128)S(1)}, u32[]{:S(2)}, u32[]{:S(2)}) collective-permute-start(f32[48,128]{1,0:T(8,128)S(1)} %pad_maximum_fusion.5), channel_id=1, source_target_pairs={{0,8},{4,12},{8,16},{12,20},{16,24},{20,28},{24,0},{28,4},{32,40},... | collective-permute-start | bytes 73736 | tf_op jit(solution)/shard_map/ppermute | solution.py:569
  133.6 5.2 %collective-permute-start.22 = (f32[48,128]{1,0:T(8,128)S(1)}, f32[48,128]{1,0:T(8,128)S(1)}, u32[]{:S(2)}, u32[]{:S(2)}) collective-permute-start(f32[48,128]{1,0:T(8,128)S(1)} %pad_maximum_fusion.5), channel_id=1, source_target_pairs={{0,16},{4,20},{8,24},{12,28},{16,0},{20,4},{24,8},{28,12},{32,48},... | collective-permute-start | bytes 73736 | tf_op jit(solution)/shard_map/ppermute | solution.py:569
  135.7 3.2 %collective-permute-start.23 = (f32[48,128]{1,0:T(8,128)S(1)}, f32[48,128]{1,0:T(8,128)S(1)}, u32[]{:S(2)}, u32[]{:S(2)}) collective-permute-start(f32[48,128]{1,0:T(8,128)S(1)} %pad_maximum_fusion.5), channel_id=1, source_target_pairs={{0,24},{4,28},{8,0},{12,4},{16,8},{20,12},{24,16},{28,20},{32,56},... | collective-permute-start | bytes 73736 | tf_op jit(solution)/shard_map/ppermute | solution.py:569
  136.3 6.4 %collective-permute-start.10 = (f32[4,128]{1,0:T(4,128)S(1)}, f32[4,128]{1,0:T(4,128)S(1)}, u32[]{:S(2)}, u32[]{:S(2)}) collective-permute-start(f32[4,128]{1,0:T(4,128)S(1)} %multiply_add_fusion.6), channel_id=1, source_target_pairs={{0,3},{1,2},{2,1},{3,0},{4,7},{5,6},{6,5},{7,4},{8,11},{9,10},{10,... | collective-permute-start | bytes 6152 | tf_op jit(solution)/shard_map/ppermute | solution.py:582
  139.0 4.0 %collective-permute-start.24 = (f32[48,128]{1,0:T(8,128)S(1)}, f32[48,128]{1,0:T(8,128)S(1)}, u32[]{:S(2)}, u32[]{:S(2)}) collective-permute-start(f32[48,128]{1,0:T(8,128)S(1)} %pad_maximum_fusion.6), channel_id=1, source_target_pairs={{0,32},{4,36},{8,40},{12,44},{16,48},{20,52},{24,56},{28,60},{32,6... | collective-permute-start | bytes 73736 | tf_op jit(solution)/shard_map/ppermute | solution.py:569
  140.2 4.2 %collective-permute-start.25 = (f32[48,128]{1,0:T(8,128)S(1)}, f32[48,128]{1,0:T(8,128)S(1)}, u32[]{:S(2)}, u32[]{:S(2)}) collective-permute-start(f32[48,128]{1,0:T(8,128)S(1)} %pad_maximum_fusion.6), channel_id=1, source_target_pairs={{0,64},{4,68},{8,72},{12,76},{16,80},{20,84},{24,88},{28,92},{32,9... | collective-permute-start | bytes 73736 | tf_op jit(solution)/shard_map/ppermute | solution.py:569
  141.7 2.7 %collective-permute-start.26 = (f32[48,128]{1,0:T(8,128)S(1)}, f32[48,128]{1,0:T(8,128)S(1)}, u32[]{:S(2)}, u32[]{:S(2)}) collective-permute-start(f32[48,128]{1,0:T(8,128)S(1)} %pad_maximum_fusion.6), channel_id=1, source_target_pairs={{0,96},{4,100},{8,104},{12,108},{16,112},{20,116},{24,120},{28,124... | collective-permute-start | bytes 73736 | tf_op jit(solution)/shard_map/ppermute | solution.py:569
  173.3 3.8 %collective-permute-start.27 = (f32[16,128]{1,0:T(8,128)S(1)}, f32[16,128]{1,0:T(8,128)S(1)}, u32[]{:S(2)}, u32[]{:S(2)}) collective-permute-start(f32[16,128]{1,0:T(8,128)S(1)} %pad_maximum_fusion.8), channel_id=1, source_target_pairs={{0,1},{1,2},{2,3},{3,0},{4,5},{5,6},{6,7},{7,4},{8,9},{9,10},{10,1... | collective-permute-start | bytes 24584 | tf_op jit(solution)/shard_map/ppermute | solution.py:569
  173.4 4.1 %collective-permute-start.28 = (f32[16,128]{1,0:T(8,128)S(1)}, f32[16,128]{1,0:T(8,128)S(1)}, u32[]{:S(2)}, u32[]{:S(2)}) collective-permute-start(f32[16,128]{1,0:T(8,128)S(1)} %pad_maximum_fusion.8), channel_id=1, source_target_pairs={{0,2},{1,3},{2,0},{3,1},{4,6},{5,7},{6,4},{7,5},{8,10},{9,11},{10,... | collective-permute-start | bytes 24584 | tf_op jit(solution)/shard_map/ppermute | solution.py:569
  173.5 4.3 %collective-permute-start.29 = (f32[16,128]{1,0:T(8,128)S(1)}, f32[16,128]{1,0:T(8,128)S(1)}, u32[]{:S(2)}, u32[]{:S(2)}) collective-permute-start(f32[16,128]{1,0:T(8,128)S(1)} %pad_maximum_fusion.8), channel_id=1, source_target_pairs={{0,3},{1,0},{2,1},{3,2},{4,7},{5,4},{6,5},{7,6},{8,11},{9,8},{10,9... | collective-permute-start | bytes 24584 | tf_op jit(solution)/shard_map/ppermute | solution.py:569
  177.8 5.9 %collective-permute-start.30 = (f32[52,128]{1,0:T(8,128)S(1)}, f32[52,128]{1,0:T(8,128)S(1)}, u32[]{:S(2)}, u32[]{:S(2)}) collective-permute-start(f32[52,128]{1,0:T(8,128)S(1)} %pad_maximum_fusion.4), channel_id=1, source_target_pairs={{0,4},{4,0},{8,12},{12,8},{16,20},{20,16},{24,28},{28,24},{32,36},... | collective-permute-start | bytes 79880 | tf_op jit(solution)/shard_map/ppermute | solution.py:569
  183.7 18.4 %copy-start = (f32[4096]{0:T(1024)S(1)}, f32[4096]{0:T(1024)}, u32[]{:S(2)}) copy-start(f32[4096]{0:T(1024)} %param.9) | copy-start | bytes 49156
  186.2 4.3 %collective-permute-start.31 = (f32[72,128]{1,0:T(8,128)S(1)}, f32[72,128]{1,0:T(8,128)S(1)}, u32[]{:S(2)}, u32[]{:S(2)}) collective-permute-start(f32[72,128]{1,0:T(8,128)S(1)} %pad_maximum_fusion), channel_id=1, source_target_pairs={{0,8},{4,12},{8,16},{12,20},{16,24},{20,28},{24,0},{28,4},{32,40},... | collective-permute-start | bytes 110600 | tf_op jit(solution)/shard_map/ppermute | solution.py:569
  187.3 4.4 %collective-permute-start.32 = (f32[72,128]{1,0:T(8,128)S(1)}, f32[72,128]{1,0:T(8,128)S(1)}, u32[]{:S(2)}, u32[]{:S(2)}) collective-permute-start(f32[72,128]{1,0:T(8,128)S(1)} %pad_maximum_fusion), channel_id=1, source_target_pairs={{0,16},{4,20},{8,24},{12,28},{16,0},{20,4},{24,8},{28,12},{32,48},... | collective-permute-start | bytes 110600 | tf_op jit(solution)/shard_map/ppermute | solution.py:569
  189.1 3.5 %collective-permute-start.33 = (f32[72,128]{1,0:T(8,128)S(1)}, f32[72,128]{1,0:T(8,128)S(1)}, u32[]{:S(2)}, u32[]{:S(2)}) collective-permute-start(f32[72,128]{1,0:T(8,128)S(1)} %pad_maximum_fusion), channel_id=1, source_target_pairs={{0,24},{4,28},{8,0},{12,4},{16,8},{20,12},{24,16},{28,20},{32,56},... | collective-permute-start | bytes 110600 | tf_op jit(solution)/shard_map/ppermute | solution.py:569
  192.7 4.1 %collective-permute-start.34 = (f32[72,128]{1,0:T(8,128)S(1)}, f32[72,128]{1,0:T(8,128)S(1)}, u32[]{:S(2)}, u32[]{:S(2)}) collective-permute-start(f32[72,128]{1,0:T(8,128)S(1)} %pad_maximum_fusion.1), channel_id=1, source_target_pairs={{0,32},{4,36},{8,40},{12,44},{16,48},{20,52},{24,56},{28,60},{32,6... | collective-permute-start | bytes 110600 | tf_op jit(solution)/shard_map/ppermute | solution.py:569
  193.2 4.3 %collective-permute-start.35 = (f32[72,128]{1,0:T(8,128)S(1)}, f32[72,128]{1,0:T(8,128)S(1)}, u32[]{:S(2)}, u32[]{:S(2)}) collective-permute-start(f32[72,128]{1,0:T(8,128)S(1)} %pad_maximum_fusion.1), channel_id=1, source_target_pairs={{0,64},{4,68},{8,72},{12,76},{16,80},{20,84},{24,88},{28,92},{32,9... | collective-permute-start | bytes 110600 | tf_op jit(solution)/shard_map/ppermute | solution.py:569
  195.8 3.1 %collective-permute-start.36 = (f32[72,128]{1,0:T(8,128)S(1)}, f32[72,128]{1,0:T(8,128)S(1)}, u32[]{:S(2)}, u32[]{:S(2)}) collective-permute-start(f32[72,128]{1,0:T(8,128)S(1)} %pad_maximum_fusion.1), channel_id=1, source_target_pairs={{0,96},{4,100},{8,104},{12,108},{16,112},{20,116},{24,120},{28,124... | collective-permute-start | bytes 110600 | tf_op jit(solution)/shard_map/ppermute | solution.py:569
  198.9 4.0 %collective-permute-start.37 = (f32[8,128]{1,0:T(8,128)S(1)}, f32[8,128]{1,0:T(8,128)S(1)}, u32[]{:S(2)}, u32[]{:S(2)}) collective-permute-start(f32[8,128]{1,0:T(8,128)S(1)} %bitcast_reduce_fusion.1), channel_id=1, source_target_pairs={{0,4},{4,0},{8,12},{12,8},{16,20},{20,16},{24,28},{28,24},{32,36},... | collective-permute-start | bytes 12296 | tf_op jit(solution)/shard_map/ppermute | solution.py:569
  203.0 4.0 %collective-permute-start.38 = (f32[12,128]{1,0:T(8,128)S(1)}, f32[12,128]{1,0:T(8,128)S(1)}, u32[]{:S(2)}, u32[]{:S(2)}) collective-permute-start(f32[12,128]{1,0:T(8,128)S(1)} %pad_maximum_fusion.9), channel_id=1, source_target_pairs={{0,1},{1,2},{2,3},{3,0},{4,5},{5,6},{6,7},{7,4},{8,9},{9,10},{10,1... | collective-permute-start | bytes 18440 | tf_op jit(solution)/shard_map/ppermute | solution.py:569
  204.5 4.0 %collective-permute-start.39 = (f32[12,128]{1,0:T(8,128)S(1)}, f32[12,128]{1,0:T(8,128)S(1)}, u32[]{:S(2)}, u32[]{:S(2)}) collective-permute-start(f32[12,128]{1,0:T(8,128)S(1)} %pad_maximum_fusion.9), channel_id=1, source_target_pairs={{0,2},{1,3},{2,0},{3,1},{4,6},{5,7},{6,4},{7,5},{8,10},{9,11},{10,... | collective-permute-start | bytes 18440 | tf_op jit(solution)/shard_map/ppermute | solution.py:569
  206.3 2.8 %collective-permute-start.40 = (f32[12,128]{1,0:T(8,128)S(1)}, f32[12,128]{1,0:T(8,128)S(1)}, u32[]{:S(2)}, u32[]{:S(2)}) collective-permute-start(f32[12,128]{1,0:T(8,128)S(1)} %pad_maximum_fusion.9), channel_id=1, source_target_pairs={{0,3},{1,0},{2,1},{3,2},{4,7},{5,4},{6,5},{7,6},{8,11},{9,8},{10,9... | collective-permute-start | bytes 18440 | tf_op jit(solution)/shard_map/ppermute | solution.py:569

commit v5 on v4

--- a/solution.py
+++ b/solution.py
@@ -14,6 +14,7 @@
 LANES = 128
 TILE = 512
 ROWS = 32
+LEAD = 5
 LOW = 2.0**-80
 HIGH = 2.0**120
 
@@ -224,8 +225,9 @@
     return jnp.sum(jnp.sum(x, axis=0, keepdims=True), axis=1, keepdims=True)
 
 
-def first_kernel(offset, steps, *refs):
-    if offset == 0:
+def first_kernel(first_tile, steps, *refs):
+    leading = first_tile == 0
+    if leading:
         gen_ref, first_ref, gweight_ref, rweight_ref, ref_hbm, *refs = refs
         d_ref, hcol_ref, hrow_ref, mass_ref, ahead_ref, vs_ref, rowacc_ref, u_ref, colsum_ref, peak_ref, *refs = refs
         tile_ref, stage_ref, v_ref, sem = refs
@@ -234,11 +236,10 @@
         hcol0_ref, vs_ref, rowacc0_ref, u0_ref, colsum0_ref, peak_ref, *refs = refs
         d_ref, lrow_ref, lcol_ref, hcol_ref, tile_ref, stage_ref, v_ref, rowacc_ref, u_ref, colsum_ref, sem = refs
     rows, width = gen_ref.shape
-    nq, nc = rows // LANES, d_ref.shape[1] // LANES
+    nq = rows // LANES
     chunks = TILE // LANES
     half_scale = 0.5 * LOG2E / (EPS * width)
     dot_scale = LOG2E / (EPS * width)
-    first_tile = offset * steps
 
     def load(j):
         at = pl.ds(pl.multiple_of((first_tile + j) * TILE, TILE), TILE)
@@ -259,7 +260,7 @@
 
     whole = slice(0, TILE)
     load(1).start()
-    if offset == 0:
+    if leading:
         ahead = pltpu.make_async_copy(ref_hbm.at[steps * TILE : (steps + 1) * TILE, :], ahead_ref, sem.at[steps])
         for q, part in enumerate(norms(gen_ref, 0, nq, half_scale)):
             hrow_ref[q : q + 1, :] = part
@@ -271,11 +272,12 @@
     else:
         v_ref[...] = jnp.log2(hrow_ref[nq : 2 * nq, :]) - hrow_ref[0:nq, :]
         lrow_ref[nq : 2 * nq, :] = jnp.broadcast_to(total(rweight_ref[...]), (nq, LANES))
-        hcol_ref[0:nc, :] = hcol0_ref[...]
+        done = first_tile * chunks
+        hcol_ref[0:done, :] = hcol0_ref[...]
         rowacc_ref[...] = rowacc0_ref[...]
-        u_ref[0:nc, :] = u0_ref[...]
-        colsum_ref[0:nc, :] = colsum0_ref[...]
-        sums(steps - 1, True, before_ref, (steps - 1) * TILE, None)
+        u_ref[0:done, :] = u0_ref[...]
+        colsum_ref[0:done, :] = colsum0_ref[...]
+        sums(first_tile - 1, True, before_ref, (first_tile - 1) * TILE, None)
         product(0, first_ref, stage_ref, whole)
 
     def step(j, carry):
@@ -289,7 +291,7 @@
         product(j, tile_ref.at[j], stage_ref, whole)
         return carry
 
-    if offset == 0:
+    if leading:
         lax.fori_loop(1, steps - 1, step, 0)
         load(steps - 1).wait()
         ahead.start()
@@ -303,11 +305,13 @@
         finish([before_ref, d_ref], u_ref, v_ref, vs_ref, rowacc_ref, colsum_ref, peak_ref, lrow_ref, lcol_ref)
 
 
-def first_pass(offset, pieces, gen, first, ref, *more):
+def first_pass(gen, first, ref, *more):
     rows, width = gen.shape
-    cols = ref.shape[0] // pieces
-    steps = cols // TILE
-    nq, nc = rows // LANES, cols // LANES
+    nq, tiles = rows // LANES, ref.shape[0] // TILE
+    leading = len(more) == 2
+    first_tile, steps = (0, LEAD) if leading else (LEAD, tiles - LEAD)
+    cols = steps * TILE
+    nc, all_nc = cols // LANES, ref.shape[0] // LANES
     vmem = pl.BlockSpec(memory_space=pltpu.VMEM)
     hbm = pl.BlockSpec(memory_space=pltpu.HBM)
     vec = lambda n: jax.ShapeDtypeStruct((n, LANES), F32)
@@ -317,7 +321,7 @@
         pltpu.VMEM((rows, TILE), F32),
         pltpu.VMEM((nq, LANES), F32),
     ]
-    if offset == 0:
+    if leading:
         gweight, rweight = more
         operands = [vmem_array(gen), vmem_array(first), gweight, rweight, hbm_array(ref)]
         outs = (
@@ -329,20 +333,21 @@
         rweight, hrow, before, hcol, vs, rowacc, u, colsum, peak = more
         operands = [vmem_array(gen), vmem_array(first), rweight, hrow, hbm_array(ref), vmem_array(before)]
         operands += [hcol, vmem_array(vs), vmem_array(rowacc), u, colsum, peak]
-        outs = (pltpu.VMEM((rows, cols), F32), vec(2 * nq), vec(2 * nc), vec(2 * nc))
+        outs = (pltpu.VMEM((rows, cols), F32), vec(2 * nq), vec(all_nc), vec(all_nc))
         specs = [vmem] * 4 + [hbm] + [vmem] * 7
         scratch += [
             pltpu.VMEM((rows, LANES), F32),
-            pltpu.VMEM((2 * nc, LANES), F32),
-            pltpu.VMEM((2 * nc, LANES), F32),
+            pltpu.VMEM((all_nc, LANES), F32),
+            pltpu.VMEM((all_nc, LANES), F32),
         ]
     return pl.pallas_call(
-        functools.partial(first_kernel, offset, steps),
+        functools.partial(first_kernel, first_tile, steps),
         in_specs=specs,
         out_shape=outs,
         out_specs=(vmem,) * len(outs),
         scratch_shapes=scratch + [pltpu.SemaphoreType.DMA((steps + 1,))],
-        compiler_params=pltpu.CompilerParams(vmem_limit_bytes=16 << 20),
+        compiler_params=pltpu.CompilerParams(vmem_limit_bytes=20 << 20),
+        name="cross_first_0" if leading else "cross_first_1",
     )(*operands)
 
 
@@ -556,9 +561,9 @@
         return out
 
     core_stage = [gen_perm(lambda z, y, c: (z, y, c + 1))]
-    y_stage = [gen_perm(lambda z, y, c: (z, y + k, c)) for k in (1, 2, 3)]
-    z_stage = [gen_perm(lambda z, y, c: (z + k, y, c)) for k in (1, 2, 3)]
-    ref_stage = [[(i, (i + k) % n_ref) for i in range(n_ref)] for k in (1, 2, 3)]
+    y_stage = [gen_perm(lambda z, y, c: (z, y + k, c)) for k in (2, 1, 3)]
+    z_stage = [gen_perm(lambda z, y, c: (z + k, y, c)) for k in (2, 1, 3)]
+    ref_stage = [[(i, (i + k) % n_ref) for i in range(n_ref)] for k in (2, 1, 3)]
     first_axis = {k: gen_perm(lambda z, y, c: (z, y + k, c) if c == 0 else (z + k, y, c)) for k in (1, 2, 3)}
     second_axis = {k: gen_perm(lambda z, y, c: (z + k, y, c) if c == 0 else (z, y + k, c)) for k in (1, 3)}
     order = [(0, 0), (0, 1), (0, 2), (0, 3)]
@@ -612,17 +617,19 @@
             picked = jnp.sum(jnp.where(at_zy > 0, cols, 0.0), axis=0, keepdims=True)
             return jnp.where(at_x > 0, picked, 0.0)
 
-        got = [lax.ppermute(own, "gen", first_axis[k]) for k in (1, 2, 3)]
+        got = {}
+        for k in (1, 3, 2):
+            got[k] = lax.ppermute(own, "gen", first_axis[k])
         mate = lax.ppermute(held, "gen", core_stage[0])
-        near = jnp.concatenate([own] + got, axis=0)
+        near = jnp.concatenate([own, got[1], got[2], got[3]], axis=0)
         up = lax.ppermute(near, "gen", second_axis[1])
         down = lax.ppermute(near, "gen", second_axis[3])
         low_far = lax.ppermute(up[: 2 * LANES], "gen", second_axis[1])
         high_far = lax.ppermute(down[2 * LANES :], "gen", second_axis[3])
 
-        d0, hcol, mine, gmass, ahead, *carried = first_pass(0, 2, held, tile0, ref_features, wg, wr)
+        d0, hcol, mine, gmass, ahead, *carried = first_pass(held, tile0, ref_features, wg, wr)
         theirs = lax.ppermute(mine, "gen", core_stage[0])
-        d1, row_part, lcol, hcol = first_pass(1, 2, held, ahead, ref_features, wr, mine, d0, hcol, *carried)
+        d1, row_part, lcol, hcol = first_pass(held, ahead, ref_features, wr, mine, d0, hcol, *carried)
         hrow = mine[:nq]
         weight = jnp.concatenate([wg, theirs[nq:]], axis=0)
         e0, z1_0, hs, ws = self_first(held, mate, [near], mine, theirs, place, 0)

time: 211 us -> 211 us (level)
  transfers between devices with their start and end apart: 41 -> 41, of which waited for: 18 -> 15; matrix products, arithmetic and copies ran while one was open for 1% -> 1% of each run, Pallas kernels for 38% -> 38%
where the time goes in v5:
time: 211 us
  Pallas kernels  114 us (54%)
  starting transfers between devices  61.9 us (29%)
  waiting for transfers between devices  30.3 us (14%)
  other arithmetic  2.55 us (1%)
    pallas_call x2, Pallas kernels, next_pass(): pl.pallas_call(functools.partial(next_kernel, len(parts)), in_specs=[vmem...  53.2 us
    ppermute x28, starting transfers between devices, shift(): return [lax.ppermute(value, axis, perm) for perm in perms]  40.1 us
    pallas_call x2, Pallas kernels, first_pass(): pl.pallas_call(functools.partial(first_kernel, first_tile, steps), in_spe...  40.1 us
    ppermute x28, waiting for transfers between devices, shift(): return [lax.ppermute(value, axis, perm) for perm in perms]  30.3 us
    pallas_call x3, Pallas kernels, self_first(): pl.pallas_call(functools.partial(self_first_kernel, len(sources), first),...  14 us
    ppermute x3, starting transfers between devices, run(): got[k] = lax.ppermute(own, 'gen', first_axis[k])  6.55 us
    ppermute x4, starting transfers between devices, doubled(): lax.ppermute(value, 'ref', [(i, i ^ flip) for i in range(n_ref)])  5.92 us
    pallas_call x2, Pallas kernels, self_apply(): pl.pallas_call(functools.partial(kernel, len(parts)), in_specs=[vmem] * (...  4.55 us
  transfers between devices with their start and end apart: 41, of which 15 were waited for; matrix products, arithmetic and copies ran while one was open for 1% of the time, Pallas kernels for 38%

profile of v5, /device:TPU:1, one launch (start us, length us, event | category | flops | bytes accessed | tf_op | source)
XLA Modules:
  0.0 210.7 jit_solution(2531598178857937390)
XLA Ops:
  0.9 2.5 %entry.1 = (bf16[128,2048]{1,0:T(8,128)(2,1)S(1)}, bf16[512,2048]{1,0:T(8,128)(2,1)S(1)}, bf16[512,2048]{1,0:T(8,128)(2,1)S(1)}, f32[4,128]{1,0:T(4,128)S(1)}, f32[32,128]{1,0:T(8,128)S(1)}) custom-call(bf16[512,2048]{1,0:T(8,128)(2,1)} %gen_hbm.1, bf16[4096,2048]{1,0:T(8,128)(2,1)} %refs_4_.3, f32[4,128]{1,0:T(4,128)} %bitcast.22, f32[32,128]{1,0:T(8,128)} %bitcast.21), custom_call_target="tpu_custom_call" | custom-call | tf_op jit(solution)/shard_map/entry/pallas_call | solution.py:207
  3.4 2.5 %collective-permute-start.13 = (bf16[128,2048]{1,0:T(8,128)(2,1)S(1)}, bf16[128,2048]{1,0:T(8,128)(2,1)S(1)}, u32[]{:S(2)}, u32[]{:S(2)}) collective-permute-start(bf16[128,2048]{1,0:T(8,128)(2,1)S(1)} %get-tuple-element.61), channel_id=1, source_target_pairs={{0,8},{4,36},{8,16},{12,44},{16,24},{20,52},{24,0},{28,60},{32,40}... | collective-permute-start | bytes 1572872 | tf_op jit(solution)/shard_map/ppermute | solution.py:622
  5.9 3.3 %collective-permute-start.14 = (bf16[128,2048]{1,0:T(8,128)(2,1)S(1)}, bf16[128,2048]{1,0:T(8,128)(2,1)S(1)}, u32[]{:S(2)}, u32[]{:S(2)}) collective-permute-start(bf16[128,2048]{1,0:T(8,128)(2,1)S(1)} %get-tuple-element.61), channel_id=1, source_target_pairs={{0,16},{4,68},{8,24},{12,76},{16,0},{20,84},{24,8},{28,92},{32,48}... | collective-permute-start | bytes 1572872 | tf_op jit(solution)/shard_map/ppermute | solution.py:622
  9.2 0.7 collective-permute-start.15
  9.9 9.0 %cross_first_0.1 = (f32[512,2560]{1,0:T(8,128)S(1)}, f32[20,128]{1,0:T(8,128)S(1)}, f32[8,128]{1,0:T(8,128)S(1)}, f32[8,128]{1,0:T(8,128)S(1)}, bf16[512,2048]{1...) custom-call(bf16[512,2048]{1,0:T(8,128)(2,1)S(1)} %get-tuple-element, ...), custom_call_target="tpu_custom_call" | custom-call | tf_op jit(solution)/shard_map/cross_first_0/pallas_call | solution.py:343
  18.9 31.1 %cross_first_1.1 = (f32[512,1536]{1,0:T(8,128)S(1)}, f32[8,128]{1,0:T(8,128)S(1)}, f32[32,128]{1,0:T(8,128)S(1)}, f32[32,128]{1,0:T(8,128)S(1)}) custom-call(bf16[512,2048]{1,0:T(8,128)(2,1)S(1)} %get-tuple-element.39.refs_0_, bf16[512,2048]{1,0:T(8,128)(2,1)S(1)} %get-tuple-element.44.refs_1_, f32[32,128]{1,0:T(8,128)S(1)} %get-tuple-element.42.refs_3_.refs_2_, ...), custom_call_target="tpu_custom_call" | custom-call | tf_op jit(solution)/shard_map/cross_first_1/pallas_call | solution.py:343
  50.0 0.9 collective-permute-start.2
  50.9 1.2 collective-permute-start
  52.4 0.6 collective-permute-start.17
  53.0 2.2 %collective-permute-start.18 = (bf16[512,2048]{1,0:T(8,128)(2,1)S(1)}, bf16[512,2048]{1,0:T(8,128)(2,1)S(1)}, u32[]{:S(2)}, u32[]{:S(2)}) collective-permute-start(bf16[512,2048]{1,0:T(8,128)(2,1)S(1)} %constant_dynamic-update-slice_fusion.refs_2_), channel_id=1, source_target_pairs={{0,96},{4,28},{8,104},{12,4},{16,112},{20,12},{24,120},{28,20},{32... | collective-permute-start | bytes 6291464 | tf_op jit(solution)/shard_map/ppermute | solution.py:626
  55.3 1.0 collective-permute-start.3
  56.3 1.9 collective-permute-start.1
  58.2 2.9 %collective-permute-start.12 = (bf16[512,2048]{1,0:T(8,128)(2,1)S(1)}, bf16[512,2048]{1,0:T(8,128)(2,1)S(1)}, u32[]{:S(2)}, u32[]{:S(2)}) collective-permute-start(bf16[512,2048]{1,0:T(8,128)(2,1)S(1)} %get-tuple-element.39.refs_0_), channel_id=1, source_target_pairs={{0,4},{4,0},{8,12},{12,8},{16,20},{20,16},{24,28},{28,24},{32,36},... | collective-permute-start | bytes 6291464 | tf_op jit(solution)/shard_map/ppermute | solution.py:623
  61.2 0.4 collective-permute-start.4
  61.6 18.4 %collective-permute-done.3 = f32[56,128]{1,0:T(8,128)S(1)} collective-permute-done((f32[56,128]{1,0:T(8,128)S(1)}, f32[56,128]{1,0:T(8,128)S(1)}, u32[]{:S(2)}, u32[]{:S(2)}) %collective-permute-start.3) | collective-permute-done | bytes 28704 | tf_op jit(solution)/shard_map/ppermute | solution.py:574
  79.9 1.4 collective-permute-start.5
  81.4 1.3 collective-permute-done.5
  82.7 3.2 %collective-permute-start.6 = (f32[56,128]{1,0:T(8,128)S(1)}, f32[56,128]{1,0:T(8,128)S(1)}, u32[]{:S(2)}, u32[]{:S(2)}) collective-permute-start(f32[56,128]{1,0:T(8,128)S(1)} %pad_maximum_fusion.3), channel_id=1, source_target_pairs={{0,64},{4,68},{8,72},{12,76},{16,80},{20,84},{24,88},{28,92},{32,9... | collective-permute-start | bytes 86024 | tf_op jit(solution)/shard_map/ppermute | solution.py:574
  85.9 0.7 collective-permute-start.7
  86.7 1.9 collective-permute-start.8
  88.7 0.9 collective-permute-start.19
  89.7 2.2 %collective-permute-start.20 = (bf16[256,2048]{1,0:T(8,128)(2,1)S(1)}, bf16[256,2048]{1,0:T(8,128)(2,1)S(1)}, u32[]{:S(2)}, u32[]{:S(2)}) collective-permute-start(bf16[256,2048]{1,0:T(8,128)(2,1)S(1)} %slice.310), channel_id=1, source_target_pairs={{0,96},{4,28},{8,104},{12,4},{16,112},{20,12},{24,120},{28,20},{32... | collective-permute-start | bytes 3145736 | tf_op jit(solution)/shard_map/ppermute | solution.py:628
  92.0 26.5 %shard_map.76 = (f32[4,128]{1,0:T(4,128)S(1)}, f32[32,128]{1,0:T(8,128)S(1)}) custom-call(f32[512,2560]{1,0:T(8,128)S(1)} %get-tuple-element.45.refs_5_.refs_0_, f32[512,1536]{1,0:T(8,128)S(1)} %get-tuple-element.53.refs_1_, f32[32,128]{1,0:T(8,128)S(1)} %get-tuple-element.85.refs_2_, f32[4,128]{1,0:T(4,128)S(1)} %get-tuple-element.83.refs_3_), custom_call_target="tpu_custom_call" | custom-call | tf_op jit(solution)/shard_map/pallas_call | solution.py:380
  118.6 0.5 collective-permute-start.16
  119.1 0.7 collective-permute-done.11
  119.8 0.3 collective-permute-start.9
  120.1 3.8 %shard_map.77 = (f32[1024,512]{1,0:T(8,128)S(1)}, f32[16,128]{1,0:T(8,128)S(1)}, f32[1024,128]{1,0:T(8,128)S(1)}, f32[1024,128]{1,0:T(8,128)S(1)}) custom-call(bf16[512,2048]{1,0:T(8,128)(2,1)S(1)} %get-tuple-element.39.refs_0_, bf16[512,2048]{1,0:T(8,128)(2,1)S(1)} %collective-permute-done.12.refs_1_, ...), custom_call_target="tpu_custom_call" | custom-call | tf_op jit(solution)/shard_map/pallas_call | solution.py:461
  123.9 6.5 %shard_map.78 = (f32[1024,1024]{1,0:T(8,128)S(1)}, f32[16,128]{1,0:T(8,128)S(1)}) custom-call(bf16[512,2048]{1,0:T(8,128)(2,1)S(1)} %get-tuple-element.39.refs_0_, bf16[512,2048]{1,0:T(8,128)(2,1)S(1)} %collective-permute-done.12.refs_1_, bf16[512,2048]{1,0:T(8,128)(2,1)S(1)} %collective-permute-done.17.refs_2_, ...), custom_call_target="tpu_custom_call" | custom-call | tf_op jit(solution)/shard_map/pallas_call | solution.py:461
  130.3 3.8 %shard_map.79 = (f32[1024,512]{1,0:T(8,128)S(1)}, f32[16,128]{1,0:T(8,128)S(1)}) custom-call(bf16[512,2048]{1,0:T(8,128)(2,1)S(1)} %get-tuple-element.39.refs_0_, bf16[512,2048]{1,0:T(8,128)(2,1)S(1)} %collective-permute-done.12.refs_1_, bf16[256,2048]{1,0:T(8,128)(2,1)S(1)} %collective-permute-done.19.refs_2_, ...), custom_call_target="tpu_custom_call" | custom-call | tf_op jit(solution)/shard_map/pallas_call | solution.py:461
  134.1 1.3 collective-permute-start.21
  135.4 0.8 collective-permute-start.22
  136.3 1.8 collective-permute-start.23
  138.1 2.6 %collective-permute-start.10 = (f32[4,128]{1,0:T(4,128)S(1)}, f32[4,128]{1,0:T(4,128)S(1)}, u32[]{:S(2)}, u32[]{:S(2)}) collective-permute-start(f32[4,128]{1,0:T(4,128)S(1)} %multiply_add_fusion.6), channel_id=1, source_target_pairs={{0,3},{1,2},{2,1},{3,0},{4,7},{5,6},{6,5},{7,4},{8,11},{9,10},{10,... | collective-permute-start | bytes 6152 | tf_op jit(solution)/shard_map/ppermute | solution.py:587
  140.8 0.4 collective-permute-start.24
  141.2 1.7 collective-permute-start.25
  142.9 1.0 collective-permute-start.26
  143.9 1.1 collective-permute-done.24
  145.0 0.2 collective-permute-done.25
  145.3 0.3 collective-permute-done.26
  145.6 26.7 %shard_map.80 = (f32[4,128]{1,0:T(4,128)S(1)}, f32[32,128]{1,0:T(8,128)S(1)}) custom-call(f32[512,2560]{1,0:T(8,128)S(1)} %get-tuple-element.45.refs_5_.refs_0_, f32[512,1536]{1,0:T(8,128)S(1)} %get-tuple-element.53.refs_1_, f32[32,128]{1,0:T(8,128)S(1)} %get-tuple-element.81.refs_2_, f32[4,128]{1,0:T(4,128)S(1)} %get-tuple-element.79.refs_3_), custom_call_target="tpu_custom_call" | custom-call | tf_op jit(solution)/shard_map/pallas_call | solution.py:380
  172.4 2.1 %shard_map.81 = f32[8,128]{1,0:T(8,128)S(1)} custom-call(f32[1024,512]{1,0:T(8,128)S(1)} %get-tuple-element.69.refs_0_, f32[1024,1024]{1,0:T(8,128)S(1)} %get-tuple-element.70.refs_1_, f32[1024,512]{1,0:T(8,128)S(1)} %get-tuple-element.71.refs_2_, f32[16,128]{1,0:T(8,128)S(1)} %get-tuple-element.77.refs_3_, s32[16]{0:T(128)S(1)} %broadcast_select_fusion.4.refs_5_.refs_6_.refs_4_), custom_call_target="tpu_custom_call" | custom-call | tf_op jit(solution)/shard_map/pallas_call | solution.py:533
  174.7 2.7 %collective-permute-start.29 = (f32[16,128]{1,0:T(8,128)S(1)}, f32[16,128]{1,0:T(8,128)S(1)}, u32[]{:S(2)}, u32[]{:S(2)}) collective-permute-start(f32[16,128]{1,0:T(8,128)S(1)} %pad_maximum_fusion.8), channel_id=1, source_target_pairs={{0,3},{1,0},{2,1},{3,2},{4,7},{5,4},{6,5},{7,6},{8,11},{9,8},{10,9... | collective-permute-start | bytes 24584 | tf_op jit(solution)/shard_map/ppermute | solution.py:574
  177.4 1.2 collective-permute-done.27
  178.7 4.6 %collective-permute-start.30 = (f32[52,128]{1,0:T(8,128)S(1)}, f32[52,128]{1,0:T(8,128)S(1)}, u32[]{:S(2)}, u32[]{:S(2)}) collective-permute-start(f32[52,128]{1,0:T(8,128)S(1)} %pad_maximum_fusion.4), channel_id=1, source_target_pairs={{0,4},{4,0},{8,12},{12,8},{16,20},{20,16},{24,28},{28,24},{32,36},... | collective-permute-start | bytes 79880 | tf_op jit(solution)/shard_map/ppermute | solution.py:574
  183.3 0.9 collective-permute-done.30
  184.2 2.4 %shard_map.82 = f32[16,128]{1,0:T(8,128)S(1)} custom-call(f32[1024,512]{1,0:T(8,128)S(1)} %get-tuple-element.69.refs_0_, f32[1024,1024]{1,0:T(8,128)S(1)} %get-tuple-element.70.refs_1_, f32[1024,512]{1,0:T(8,128)S(1)} %get-tuple-element.71.refs_2_, f32[8,128]{1,0:T(8,128)S(1)} %get-tuple-element.99.refs_3_, s32[16]{0:T(128)S(1)} %broadcast_select_fusion.4.refs_5_.refs_6_.refs_4_), custom_call_target="tpu_custom_call" | custom-call | tf_op jit(solution)/shard_map/pallas_call | solution.py:533
  186.7 1.0 collective-permute-start.31
  187.6 1.5 collective-permute-start.32
  189.1 1.2 collective-permute-start.33
  190.3 0.7 collective-permute-done.31
  191.0 1.1 collective-permute-done.32
  192.2 2.7 %collective-permute-start.34 = (f32[72,128]{1,0:T(8,128)S(1)}, f32[72,128]{1,0:T(8,128)S(1)}, u32[]{:S(2)}, u32[]{:S(2)}) collective-permute-start(f32[72,128]{1,0:T(8,128)S(1)} %pad_maximum_fusion.1), channel_id=1, source_target_pairs={{0,64},{4,68},{8,72},{12,76},{16,80},{20,84},{24,88},{28,92},{32,9... | collective-permute-start | bytes 110600 | tf_op jit(solution)/shard_map/ppermute | solution.py:574
  194.9 1.5 collective-permute-start.35
  196.3 1.2 collective-permute-start.36
  197.6 1.7 collective-permute-done.35
  199.4 3.4 %collective-permute-start.37 = (f32[8,128]{1,0:T(8,128)S(1)}, f32[8,128]{1,0:T(8,128)S(1)}, u32[]{:S(2)}, u32[]{:S(2)}) collective-permute-start(f32[8,128]{1,0:T(8,128)S(1)} %bitcast_reduce_fusion.1), channel_id=1, source_target_pairs={{0,4},{4,0},{8,12},{12,8},{16,20},{20,16},{24,28},{28,24},{32,36},... | collective-permute-start | bytes 12296 | tf_op jit(solution)/shard_map/ppermute | solution.py:574
  202.8 0.6 bitcast_reduce_fusion
  203.6 0.8 collective-permute-start.38
  204.4 2.3 %collective-permute-start.39 = (f32[12,128]{1,0:T(8,128)S(1)}, f32[12,128]{1,0:T(8,128)S(1)}, u32[]{:S(2)}, u32[]{:S(2)}) collective-permute-start(f32[12,128]{1,0:T(8,128)S(1)} %pad_maximum_fusion.9), channel_id=1, source_target_pairs={{0,1},{1,2},{2,3},{3,0},{4,5},{5,6},{6,7},{7,4},{8,9},{9,10},{10,1... | collective-permute-start | bytes 18440 | tf_op jit(solution)/shard_map/ppermute | solution.py:574
  206.7 0.4 collective-permute-start.40
  207.1 0.6 collective-permute-done.38
  207.7 0.7 collective-permute-done.39
  208.4 1.1 collective-permute-done.40
  209.5 1.2 fusion.13
  (94 shorter events, 1.7 us)
Async XLA Ops:
  3.4 48.8 %collective-permute-start.13 = (bf16[128,2048]{1,0:T(8,128)(2,1)S(1)}, bf16[128,2048]{1,0:T(8,128)(2,1)S(1)}, u32[]{:S(2)}, u32[]{:S(2)}) collective-permute-start(bf16[128,2048]{1,0:T(8,128)(2,1)S(1)} %get-tuple-element.61), channel_id=1, source_target_pairs={{0,8},{4,36},{8,16},{12,44},{16,24},{20,52},{24,0},{28,60},{32,40}... | collective-permute-start | bytes 1572872 | tf_op jit(solution)/shard_map/ppermute | solution.py:622
  5.9 46.4 %collective-permute-start.14 = (bf16[128,2048]{1,0:T(8,128)(2,1)S(1)}, bf16[128,2048]{1,0:T(8,128)(2,1)S(1)}, u32[]{:S(2)}, u32[]{:S(2)}) collective-permute-start(bf16[128,2048]{1,0:T(8,128)(2,1)S(1)} %get-tuple-element.61), channel_id=1, source_target_pairs={{0,16},{4,68},{8,24},{12,76},{16,0},{20,84},{24,8},{28,92},{32,48}... | collective-permute-start | bytes 1572872 | tf_op jit(solution)/shard_map/ppermute | solution.py:622
  9.2 43.1 %collective-permute-start.15 = (bf16[128,2048]{1,0:T(8,128)(2,1)S(1)}, bf16[128,2048]{1,0:T(8,128)(2,1)S(1)}, u32[]{:S(2)}, u32[]{:S(2)}) collective-permute-start(bf16[128,2048]{1,0:T(8,128)(2,1)S(1)} %get-tuple-element.61), channel_id=1, source_target_pairs={{0,24},{4,100},{8,0},{12,108},{16,8},{20,116},{24,16},{28,124},{32... | collective-permute-start | bytes 1572872 | tf_op jit(solution)/shard_map/ppermute | solution.py:622
  50.0 5.2 %collective-permute-start.2 = (f32[40,128]{1,0:T(8,128)S(1)}, f32[40,128]{1,0:T(8,128)S(1)}, u32[]{:S(2)}, u32[]{:S(2)}) collective-permute-start(f32[40,128]{1,0:T(8,128)S(1)} %pad_maximum_fusion.7), channel_id=1, source_target_pairs={{0,4},{4,0},{8,12},{12,8},{16,20},{20,16},{24,28},{28,24},{32,36},... | collective-permute-start | bytes 61448 | tf_op jit(solution)/shard_map/ppermute | solution.py:574
  50.9 4.3 %collective-permute-start = (f32[8,128]{1,0:T(8,128)S(1)}, f32[8,128]{1,0:T(8,128)S(1)}, u32[]{:S(2)}, u32[]{:S(2)}) collective-permute-start(f32[8,128]{1,0:T(8,128)S(1)} %get-tuple-element.52), channel_id=1, source_target_pairs={{0,1},{1,0},{2,3},{3,2},{4,5},{5,4},{6,7},{7,6},{8,9},{9,8},{10,11... | collective-permute-start | bytes 12296 | tf_op jit(solution)/shard_map/ppermute | solution.py:587
  52.4 34.3 %collective-permute-start.17 = (bf16[512,2048]{1,0:T(8,128)(2,1)S(1)}, bf16[512,2048]{1,0:T(8,128)(2,1)S(1)}, u32[]{:S(2)}, u32[]{:S(2)}) collective-permute-start(bf16[512,2048]{1,0:T(8,128)(2,1)S(1)} %constant_dynamic-update-slice_fusion.refs_2_), channel_id=1, source_target_pairs={{0,32},{4,12},{8,40},{12,20},{16,48},{20,28},{24,56},{28,4},{32,64... | collective-permute-start | bytes 6291464 | tf_op jit(solution)/shard_map/ppermute | solution.py:625
  53.0 35.7 %collective-permute-start.18 = (bf16[512,2048]{1,0:T(8,128)(2,1)S(1)}, bf16[512,2048]{1,0:T(8,128)(2,1)S(1)}, u32[]{:S(2)}, u32[]{:S(2)}) collective-permute-start(bf16[512,2048]{1,0:T(8,128)(2,1)S(1)} %constant_dynamic-update-slice_fusion.refs_2_), channel_id=1, source_target_pairs={{0,96},{4,28},{8,104},{12,4},{16,112},{20,12},{24,120},{28,20},{32... | collective-permute-start | bytes 6291464 | tf_op jit(solution)/shard_map/ppermute | solution.py:626
  55.3 24.7 %collective-permute-start.3 = (f32[56,128]{1,0:T(8,128)S(1)}, f32[56,128]{1,0:T(8,128)S(1)}, u32[]{:S(2)}, u32[]{:S(2)}) collective-permute-start(f32[56,128]{1,0:T(8,128)S(1)} %pad_maximum_fusion.2), channel_id=1, source_target_pairs={{0,16},{4,20},{8,24},{12,28},{16,0},{20,4},{24,8},{28,12},{32,48},... | collective-permute-start | bytes 86024 | tf_op jit(solution)/shard_map/ppermute | solution.py:574
  56.3 4.8 %collective-permute-start.1 = (f32[8,128]{1,0:T(8,128)S(1)}, f32[8,128]{1,0:T(8,128)S(1)}, u32[]{:S(2)}, u32[]{:S(2)}) collective-permute-start(f32[8,128]{1,0:T(8,128)S(1)} %pad_maximum_fusion.10), channel_id=1, source_target_pairs={{0,3},{1,2},{2,1},{3,0},{4,7},{5,6},{6,5},{7,4},{8,11},{9,10},{10,... | collective-permute-start | bytes 12296 | tf_op jit(solution)/shard_map/ppermute | solution.py:587
  58.2 61.8 %collective-permute-start.12 = (bf16[512,2048]{1,0:T(8,128)(2,1)S(1)}, bf16[512,2048]{1,0:T(8,128)(2,1)S(1)}, u32[]{:S(2)}, u32[]{:S(2)}) collective-permute-start(bf16[512,2048]{1,0:T(8,128)(2,1)S(1)} %get-tuple-element.39.refs_0_), channel_id=1, source_target_pairs={{0,4},{4,0},{8,12},{12,8},{16,20},{20,16},{24,28},{28,24},{32,36},... | collective-permute-start | bytes 6291464 | tf_op jit(solution)/shard_map/ppermute | solution.py:623
  61.2 20.2 %collective-permute-start.4 = (f32[56,128]{1,0:T(8,128)S(1)}, f32[56,128]{1,0:T(8,128)S(1)}, u32[]{:S(2)}, u32[]{:S(2)}) collective-permute-start(f32[56,128]{1,0:T(8,128)S(1)} %pad_maximum_fusion.2), channel_id=1, source_target_pairs={{0,8},{4,12},{8,16},{12,20},{16,24},{20,28},{24,0},{28,4},{32,40},... | collective-permute-start | bytes 86024 | tf_op jit(solution)/shard_map/ppermute | solution.py:574
  79.9 2.7 %collective-permute-start.5 = (f32[56,128]{1,0:T(8,128)S(1)}, f32[56,128]{1,0:T(8,128)S(1)}, u32[]{:S(2)}, u32[]{:S(2)}) collective-permute-start(f32[56,128]{1,0:T(8,128)S(1)} %pad_maximum_fusion.2), channel_id=1, source_target_pairs={{0,24},{4,28},{8,0},{12,4},{16,8},{20,12},{24,16},{28,20},{32,56},... | collective-permute-start | bytes 86024 | tf_op jit(solution)/shard_map/ppermute | solution.py:574
  82.7 7.0 %collective-permute-start.6 = (f32[56,128]{1,0:T(8,128)S(1)}, f32[56,128]{1,0:T(8,128)S(1)}, u32[]{:S(2)}, u32[]{:S(2)}) collective-permute-start(f32[56,128]{1,0:T(8,128)S(1)} %pad_maximum_fusion.3), channel_id=1, source_target_pairs={{0,64},{4,68},{8,72},{12,76},{16,80},{20,84},{24,88},{28,92},{32,9... | collective-permute-start | bytes 86024 | tf_op jit(solution)/shard_map/ppermute | solution.py:574
  85.9 6.0 %collective-permute-start.7 = (f32[56,128]{1,0:T(8,128)S(1)}, f32[56,128]{1,0:T(8,128)S(1)}, u32[]{:S(2)}, u32[]{:S(2)}) collective-permute-start(f32[56,128]{1,0:T(8,128)S(1)} %pad_maximum_fusion.3), channel_id=1, source_target_pairs={{0,32},{4,36},{8,40},{12,44},{16,48},{20,52},{24,56},{28,60},{32,6... | collective-permute-start | bytes 86024 | tf_op jit(solution)/shard_map/ppermute | solution.py:574
  86.7 5.3 %collective-permute-start.8 = (f32[56,128]{1,0:T(8,128)S(1)}, f32[56,128]{1,0:T(8,128)S(1)}, u32[]{:S(2)}, u32[]{:S(2)}) collective-permute-start(f32[56,128]{1,0:T(8,128)S(1)} %pad_maximum_fusion.3), channel_id=1, source_target_pairs={{0,96},{4,100},{8,104},{12,108},{16,112},{20,116},{24,120},{28,124... | collective-permute-start | bytes 86024 | tf_op jit(solution)/shard_map/ppermute | solution.py:574
  88.7 41.6 %collective-permute-start.19 = (bf16[256,2048]{1,0:T(8,128)(2,1)S(1)}, bf16[256,2048]{1,0:T(8,128)(2,1)S(1)}, u32[]{:S(2)}, u32[]{:S(2)}) collective-permute-start(bf16[256,2048]{1,0:T(8,128)(2,1)S(1)} %slice.309), channel_id=1, source_target_pairs={{0,32},{4,12},{8,40},{12,20},{16,48},{20,28},{24,56},{28,4},{32,64... | collective-permute-start | bytes 3145736 | tf_op jit(solution)/shard_map/ppermute | solution.py:627
  89.7 40.6 %collective-permute-start.20 = (bf16[256,2048]{1,0:T(8,128)(2,1)S(1)}, bf16[256,2048]{1,0:T(8,128)(2,1)S(1)}, u32[]{:S(2)}, u32[]{:S(2)}) collective-permute-start(bf16[256,2048]{1,0:T(8,128)(2,1)S(1)} %slice.310), channel_id=1, source_target_pairs={{0,96},{4,28},{8,104},{12,4},{16,112},{20,12},{24,120},{28,20},{32... | collective-permute-start | bytes 3145736 | tf_op jit(solution)/shard_map/ppermute | solution.py:628
  118.5 1.3 collective-permute-start.11
  118.6 1.5 collective-permute-start.16
  119.8 18.3 %collective-permute-start.9 = (f32[4,128]{1,0:T(4,128)S(1)}, f32[4,128]{1,0:T(4,128)S(1)}, u32[]{:S(2)}, u32[]{:S(2)}) collective-permute-start(f32[4,128]{1,0:T(4,128)S(1)} %get-tuple-element.59), channel_id=1, source_target_pairs={{0,1},{1,0},{2,3},{3,2},{4,5},{5,4},{6,7},{7,6},{8,9},{9,8},{10,11... | collective-permute-start | bytes 6152 | tf_op jit(solution)/shard_map/ppermute | solution.py:587
  134.1 6.6 %collective-permute-start.21 = (f32[48,128]{1,0:T(8,128)S(1)}, f32[48,128]{1,0:T(8,128)S(1)}, u32[]{:S(2)}, u32[]{:S(2)}) collective-permute-start(f32[48,128]{1,0:T(8,128)S(1)} %pad_maximum_fusion.5), channel_id=1, source_target_pairs={{0,16},{4,20},{8,24},{12,28},{16,0},{20,4},{24,8},{28,12},{32,48},... | collective-permute-start | bytes 73736 | tf_op jit(solution)/shard_map/ppermute | solution.py:574
  135.4 5.3 %collective-permute-start.22 = (f32[48,128]{1,0:T(8,128)S(1)}, f32[48,128]{1,0:T(8,128)S(1)}, u32[]{:S(2)}, u32[]{:S(2)}) collective-permute-start(f32[48,128]{1,0:T(8,128)S(1)} %pad_maximum_fusion.5), channel_id=1, source_target_pairs={{0,8},{4,12},{8,16},{12,20},{16,24},{20,28},{24,0},{28,4},{32,40},... | collective-permute-start | bytes 73736 | tf_op jit(solution)/shard_map/ppermute | solution.py:574
  136.3 4.4 %collective-permute-start.23 = (f32[48,128]{1,0:T(8,128)S(1)}, f32[48,128]{1,0:T(8,128)S(1)}, u32[]{:S(2)}, u32[]{:S(2)}) collective-permute-start(f32[48,128]{1,0:T(8,128)S(1)} %pad_maximum_fusion.5), channel_id=1, source_target_pairs={{0,24},{4,28},{8,0},{12,4},{16,8},{20,12},{24,16},{28,20},{32,56},... | collective-permute-start | bytes 73736 | tf_op jit(solution)/shard_map/ppermute | solution.py:574
  138.1 5.8 %collective-permute-start.10 = (f32[4,128]{1,0:T(4,128)S(1)}, f32[4,128]{1,0:T(4,128)S(1)}, u32[]{:S(2)}, u32[]{:S(2)}) collective-permute-start(f32[4,128]{1,0:T(4,128)S(1)} %multiply_add_fusion.6), channel_id=1, source_target_pairs={{0,3},{1,2},{2,1},{3,0},{4,7},{5,6},{6,5},{7,4},{8,11},{9,10},{10,... | collective-permute-start | bytes 6152 | tf_op jit(solution)/shard_map/ppermute | solution.py:587
  140.8 4.3 %collective-permute-start.24 = (f32[48,128]{1,0:T(8,128)S(1)}, f32[48,128]{1,0:T(8,128)S(1)}, u32[]{:S(2)}, u32[]{:S(2)}) collective-permute-start(f32[48,128]{1,0:T(8,128)S(1)} %pad_maximum_fusion.6), channel_id=1, source_target_pairs={{0,64},{4,68},{8,72},{12,76},{16,80},{20,84},{24,88},{28,92},{32,9... | collective-permute-start | bytes 73736 | tf_op jit(solution)/shard_map/ppermute | solution.py:574
  141.2 4.1 %collective-permute-start.25 = (f32[48,128]{1,0:T(8,128)S(1)}, f32[48,128]{1,0:T(8,128)S(1)}, u32[]{:S(2)}, u32[]{:S(2)}) collective-permute-start(f32[48,128]{1,0:T(8,128)S(1)} %pad_maximum_fusion.6), channel_id=1, source_target_pairs={{0,32},{4,36},{8,40},{12,44},{16,48},{20,52},{24,56},{28,60},{32,6... | collective-permute-start | bytes 73736 | tf_op jit(solution)/shard_map/ppermute | solution.py:574
  142.9 2.7 %collective-permute-start.26 = (f32[48,128]{1,0:T(8,128)S(1)}, f32[48,128]{1,0:T(8,128)S(1)}, u32[]{:S(2)}, u32[]{:S(2)}) collective-permute-start(f32[48,128]{1,0:T(8,128)S(1)} %pad_maximum_fusion.6), channel_id=1, source_target_pairs={{0,96},{4,100},{8,104},{12,108},{16,112},{20,116},{24,120},{28,124... | collective-permute-start | bytes 73736 | tf_op jit(solution)/shard_map/ppermute | solution.py:574
  174.6 4.1 %collective-permute-start.27 = (f32[16,128]{1,0:T(8,128)S(1)}, f32[16,128]{1,0:T(8,128)S(1)}, u32[]{:S(2)}, u32[]{:S(2)}) collective-permute-start(f32[16,128]{1,0:T(8,128)S(1)} %pad_maximum_fusion.8), channel_id=1, source_target_pairs={{0,2},{1,3},{2,0},{3,1},{4,6},{5,7},{6,4},{7,5},{8,10},{9,11},{10,... | collective-permute-start | bytes 24584 | tf_op jit(solution)/shard_map/ppermute | solution.py:574
  174.7 4.0 %collective-permute-start.28 = (f32[16,128]{1,0:T(8,128)S(1)}, f32[16,128]{1,0:T(8,128)S(1)}, u32[]{:S(2)}, u32[]{:S(2)}) collective-permute-start(f32[16,128]{1,0:T(8,128)S(1)} %pad_maximum_fusion.8), channel_id=1, source_target_pairs={{0,1},{1,2},{2,3},{3,0},{4,5},{5,6},{6,7},{7,4},{8,9},{9,10},{10,1... | collective-permute-start | bytes 24584 | tf_op jit(solution)/shard_map/ppermute | solution.py:574
  174.7 3.9 %collective-permute-start.29 = (f32[16,128]{1,0:T(8,128)S(1)}, f32[16,128]{1,0:T(8,128)S(1)}, u32[]{:S(2)}, u32[]{:S(2)}) collective-permute-start(f32[16,128]{1,0:T(8,128)S(1)} %pad_maximum_fusion.8), channel_id=1, source_target_pairs={{0,3},{1,0},{2,1},{3,2},{4,7},{5,4},{6,5},{7,6},{8,11},{9,8},{10,9... | collective-permute-start | bytes 24584 | tf_op jit(solution)/shard_map/ppermute | solution.py:574
  178.7 5.4 %collective-permute-start.30 = (f32[52,128]{1,0:T(8,128)S(1)}, f32[52,128]{1,0:T(8,128)S(1)}, u32[]{:S(2)}, u32[]{:S(2)}) collective-permute-start(f32[52,128]{1,0:T(8,128)S(1)} %pad_maximum_fusion.4), channel_id=1, source_target_pairs={{0,4},{4,0},{8,12},{12,8},{16,20},{20,16},{24,28},{28,24},{32,36},... | collective-permute-start | bytes 79880 | tf_op jit(solution)/shard_map/ppermute | solution.py:574
  184.1 18.6 %copy-start = (f32[4096]{0:T(1024)S(1)}, f32[4096]{0:T(1024)}, u32[]{:S(2)}) copy-start(f32[4096]{0:T(1024)} %param.9) | copy-start | bytes 49156
  186.7 4.4 %collective-permute-start.31 = (f32[72,128]{1,0:T(8,128)S(1)}, f32[72,128]{1,0:T(8,128)S(1)}, u32[]{:S(2)}, u32[]{:S(2)}) collective-permute-start(f32[72,128]{1,0:T(8,128)S(1)} %pad_maximum_fusion), channel_id=1, source_target_pairs={{0,16},{4,20},{8,24},{12,28},{16,0},{20,4},{24,8},{28,12},{32,48},... | collective-permute-start | bytes 110600 | tf_op jit(solution)/shard_map/ppermute | solution.py:574
  187.6 4.5 %collective-permute-start.32 = (f32[72,128]{1,0:T(8,128)S(1)}, f32[72,128]{1,0:T(8,128)S(1)}, u32[]{:S(2)}, u32[]{:S(2)}) collective-permute-start(f32[72,128]{1,0:T(8,128)S(1)} %pad_maximum_fusion), channel_id=1, source_target_pairs={{0,8},{4,12},{8,16},{12,20},{16,24},{20,28},{24,0},{28,4},{32,40},... | collective-permute-start | bytes 110600 | tf_op jit(solution)/shard_map/ppermute | solution.py:574
  189.1 3.0 %collective-permute-start.33 = (f32[72,128]{1,0:T(8,128)S(1)}, f32[72,128]{1,0:T(8,128)S(1)}, u32[]{:S(2)}, u32[]{:S(2)}) collective-permute-start(f32[72,128]{1,0:T(8,128)S(1)} %pad_maximum_fusion), channel_id=1, source_target_pairs={{0,24},{4,28},{8,0},{12,4},{16,8},{20,12},{24,16},{28,20},{32,56},... | collective-permute-start | bytes 110600 | tf_op jit(solution)/shard_map/ppermute | solution.py:574
  192.2 5.4 %collective-permute-start.34 = (f32[72,128]{1,0:T(8,128)S(1)}, f32[72,128]{1,0:T(8,128)S(1)}, u32[]{:S(2)}, u32[]{:S(2)}) collective-permute-start(f32[72,128]{1,0:T(8,128)S(1)} %pad_maximum_fusion.1), channel_id=1, source_target_pairs={{0,64},{4,68},{8,72},{12,76},{16,80},{20,84},{24,88},{28,92},{32,9... | collective-permute-start | bytes 110600 | tf_op jit(solution)/shard_map/ppermute | solution.py:574
  194.9 4.4 %collective-permute-start.35 = (f32[72,128]{1,0:T(8,128)S(1)}, f32[72,128]{1,0:T(8,128)S(1)}, u32[]{:S(2)}, u32[]{:S(2)}) collective-permute-start(f32[72,128]{1,0:T(8,128)S(1)} %pad_maximum_fusion.1), channel_id=1, source_target_pairs={{0,32},{4,36},{8,40},{12,44},{16,48},{20,52},{24,56},{28,60},{32,6... | collective-permute-start | bytes 110600 | tf_op jit(solution)/shard_map/ppermute | solution.py:574
  196.3 3.0 %collective-permute-start.36 = (f32[72,128]{1,0:T(8,128)S(1)}, f32[72,128]{1,0:T(8,128)S(1)}, u32[]{:S(2)}, u32[]{:S(2)}) collective-permute-start(f32[72,128]{1,0:T(8,128)S(1)} %pad_maximum_fusion.1), channel_id=1, source_target_pairs={{0,96},{4,100},{8,104},{12,108},{16,112},{20,116},{24,120},{28,124... | collective-permute-start | bytes 110600 | tf_op jit(solution)/shard_map/ppermute | solution.py:574
  199.4 4.2 %collective-permute-start.37 = (f32[8,128]{1,0:T(8,128)S(1)}, f32[8,128]{1,0:T(8,128)S(1)}, u32[]{:S(2)}, u32[]{:S(2)}) collective-permute-start(f32[8,128]{1,0:T(8,128)S(1)} %bitcast_reduce_fusion.1), channel_id=1, source_target_pairs={{0,4},{4,0},{8,12},{12,8},{16,20},{20,16},{24,28},{28,24},{32,36},... | collective-permute-start | bytes 12296 | tf_op jit(solution)/shard_map/ppermute | solution.py:574
  203.6 4.1 %collective-permute-start.38 = (f32[12,128]{1,0:T(8,128)S(1)}, f32[12,128]{1,0:T(8,128)S(1)}, u32[]{:S(2)}, u32[]{:S(2)}) collective-permute-start(f32[12,128]{1,0:T(8,128)S(1)} %pad_maximum_fusion.9), channel_id=1, source_target_pairs={{0,2},{1,3},{2,0},{3,1},{4,6},{5,7},{6,4},{7,5},{8,10},{9,11},{10,... | collective-permute-start | bytes 18440 | tf_op jit(solution)/shard_map/ppermute | solution.py:574
  204.4 4.0 %collective-permute-start.39 = (f32[12,128]{1,0:T(8,128)S(1)}, f32[12,128]{1,0:T(8,128)S(1)}, u32[]{:S(2)}, u32[]{:S(2)}) collective-permute-start(f32[12,128]{1,0:T(8,128)S(1)} %pad_maximum_fusion.9), channel_id=1, source_target_pairs={{0,1},{1,2},{2,3},{3,0},{4,5},{5,6},{6,7},{7,4},{8,9},{9,10},{10,1... | collective-permute-start | bytes 18440 | tf_op jit(solution)/shard_map/ppermute | solution.py:574
  206.7 2.8 %collective-permute-start.40 = (f32[12,128]{1,0:T(8,128)S(1)}, f32[12,128]{1,0:T(8,128)S(1)}, u32[]{:S(2)}, u32[]{:S(2)}) collective-permute-start(f32[12,128]{1,0:T(8,128)S(1)} %pad_maximum_fusion.9), channel_id=1, source_target_pairs={{0,3},{1,0},{2,1},{3,2},{4,7},{5,4},{6,5},{7,6},{8,11},{9,8},{10,9... | collective-permute-start | bytes 18440 | tf_op jit(solution)/shard_map/ppermute | solution.py:574

commit v6 on v5

--- a/solution.py
+++ b/solution.py
@@ -14,7 +14,7 @@
 LANES = 128
 TILE = 512
 ROWS = 32
-LEAD = 5
+LEAD = 6
 LOW = 2.0**-80
 HIGH = 2.0**120
 
@@ -57,20 +57,21 @@
 
 def sweep(d_ref, base, chunks, u, vs_ref, rowacc_ref, straight=False, keep=None):
     rows = d_ref.shape[0]
+    u = [jnp.broadcast_to(part, (8, LANES))[None] for part in u]
 
     def body(r, cols):
         at = row_block(r)
-        vs = vs_ref[at, :]
-        racc = rowacc_ref[at, :]
+        vs = vs_ref[at, :].reshape(ROWS // 8, 8, LANES)
+        racc = rowacc_ref[at, :].reshape(ROWS // 8, 8, LANES)
         out = []
         for c in range(chunks):
             d = d_ref[at, pl.ds(base + c * LANES, LANES)]
             if keep is not None:
                 keep[0][at, pl.ds(pl.multiple_of(keep[1] + c * LANES, LANES), LANES)] = d
-            p = jnp.exp2((d + u[c]) + vs)
+            p = jnp.exp2((d.reshape(ROWS // 8, 8, LANES) + u[c]) + vs)
             racc = racc + p
-            out.append(cols[c] + jnp.sum(p.reshape(ROWS // 8, 8, LANES), axis=0))
-        rowacc_ref[at, :] = racc
+            out.append(cols[c] + jnp.sum(p, axis=0))
+        rowacc_ref[at, :] = racc.reshape(ROWS, LANES)
         return tuple(out)
 
     cols = (jnp.zeros((8, LANES), F32),) * chunks
@@ -470,59 +471,48 @@
 def self_cols_kernel(count, *refs):
     w_ref, place_ref, z_ref, ws_ref = refs[count:]
     rows = refs[0].shape[0]
-    chunks = 256 // LANES
+    chunks = TILE // LANES
     spread(w_ref, ws_ref, rows // LANES)
-    zero = jnp.zeros((8, LANES), F32)
     first = 0
     for e_ref in refs[:count]:
-        steps = e_ref.shape[1] // 256
-
-        def tile(t, carry):
-            base = pl.multiple_of(t * 256, 256)
+        for base in range(0, e_ref.shape[1], TILE):
 
             def body(r, acc):
-                at = pl.ds(pl.multiple_of(r * ROWS, ROWS), ROWS)
+                at = row_block(r)
                 ws = ws_ref[at, :]
                 out = []
                 for c in range(chunks):
-                    e = e_ref[at, pl.ds(base + c * LANES, LANES)] * ws
+                    e = e_ref[at, base + c * LANES : base + (c + 1) * LANES] * ws
                     out.append(acc[c] + jnp.sum(e.reshape(ROWS // 8, 8, LANES), axis=0))
                 return tuple(out)
 
-            acc = lax.fori_loop(0, rows // ROWS, body, (zero,) * chunks, unroll=4)
+            acc = lax.fori_loop(0, rows // ROWS, body, (jnp.zeros((8, LANES), F32),) * chunks, unroll=4)
             for c in range(chunks):
-                z_ref[pl.ds(place_ref[first + t * chunks + c], 1), :] = jnp.sum(acc[c], axis=0, keepdims=True)
-            return carry
-
-        lax.fori_loop(0, steps, tile, 0)
-        first += steps * chunks
+                z_ref[pl.ds(place_ref[first + c], 1), :] = jnp.sum(acc[c], axis=0, keepdims=True)
+            first += chunks
 
 
 def self_rows_kernel(count, *refs):
     w_ref, place_ref, y_ref, rowacc_ref = refs[count:]
     rows = refs[0].shape[0]
-    chunks = 512 // LANES
-    rowacc_ref[...] = jnp.zeros_like(rowacc_ref)
     first = 0
-    for e_ref in refs[:count]:
-        steps = e_ref.shape[1] // 512
-
-        def tile(t, carry):
-            base = pl.multiple_of(t * 512, 512)
-            w = [w_ref[pl.ds(place_ref[first + t * chunks + c], 1), :] for c in range(chunks)]
-
-            def body(r, carry):
-                at = pl.ds(pl.multiple_of(r * ROWS, ROWS), ROWS)
-                acc = rowacc_ref[at, :]
-                for c in range(chunks):
-                    acc = acc + e_ref[at, pl.ds(base + c * LANES, LANES)] * w[c]
-                rowacc_ref[at, :] = acc
-                return carry
-
-            return lax.fori_loop(0, rows // ROWS, body, carry, unroll=4)
-
-        lax.fori_loop(0, steps, tile, 0)
-        first += steps * chunks
+    for at_e, e_ref in enumerate(refs[:count]):
+        chunks = e_ref.shape[1] // LANES
+        w = [
+            jnp.broadcast_to(w_ref[pl.ds(place_ref[first + c], 1), :], (8, LANES))[None] for c in range(chunks)
+        ]
+
+        def body(r, carry):
+            at = row_block(r)
+            parts = [
+                e_ref[at, c * LANES : (c + 1) * LANES].reshape(ROWS // 8, 8, LANES) * w[c] for c in range(chunks)
+            ]
+            acc = sum(parts[1:], parts[0]).reshape(ROWS, LANES)
+            rowacc_ref[at, :] = acc if at_e == 0 else rowacc_ref[at, :] + acc
+            return carry
+
+        lax.fori_loop(0, rows // ROWS, body, 0, unroll=4)
+        first += chunks
     for q in range(rows // LANES):
         y_ref[q : q + 1, :] = lane_fold(rowacc_ref[q * LANES : (q + 1) * LANES, :], jnp.sum)
 
@@ -561,9 +551,9 @@
         return out
 
     core_stage = [gen_perm(lambda z, y, c: (z, y, c + 1))]
-    y_stage = [gen_perm(lambda z, y, c: (z, y + k, c)) for k in (2, 1, 3)]
-    z_stage = [gen_perm(lambda z, y, c: (z + k, y, c)) for k in (2, 1, 3)]
-    ref_stage = [[(i, (i + k) % n_ref) for i in range(n_ref)] for k in (2, 1, 3)]
+    y_stage = [gen_perm(lambda z, y, c: (z, y + k, c)) for k in (1, 2, 3)]
+    z_stage = [gen_perm(lambda z, y, c: (z + k, y, c)) for k in (1, 2, 3)]
+    ref_stage = [[(i, (i + k) % n_ref) for i in range(n_ref)] for k in (1, 2, 3)]
     first_axis = {k: gen_perm(lambda z, y, c: (z, y + k, c) if c == 0 else (z + k, y, c)) for k in (1, 2, 3)}
     second_axis = {k: gen_perm(lambda z, y, c: (z + k, y, c) if c == 0 else (z, y + k, c)) for k in (1, 3)}
     order = [(0, 0), (0, 1), (0, 2), (0, 3)]

time: 211 us -> 210 us (level)
  transfers between devices with their start and end apart: 41 -> 41, of which waited for: 15 -> 18; matrix products, arithmetic and copies ran while one was open for 1% -> 1% of each run, Pallas kernels for 38% -> 39%
where the time goes in v6:
time: 210 us; the launch traced here: 209 us
  Pallas kernels  113 us (54%)
  starting transfers between devices  60.2 us (29%)
  waiting for transfers between devices  31.8 us (15%)
  other arithmetic  2.56 us (1%)
    pallas_call x2, Pallas kernels, next_pass(): pl.pallas_call(functools.partial(next_kernel, len(parts)), in_specs=[vmem...  53.2 us
    pallas_call x2, Pallas kernels, first_pass(): pl.pallas_call(functools.partial(first_kernel, first_tile, steps), in_spe...  40.2 us
    ppermute x28, starting transfers between devices, shift(): return [lax.ppermute(value, axis, perm) for perm in perms]  39.1 us
    ppermute x28, waiting for transfers between devices, shift(): return [lax.ppermute(value, axis, perm) for perm in perms]  31.7 us
    pallas_call x3, Pallas kernels, self_first(): pl.pallas_call(functools.partial(self_first_kernel, len(sources), first),...  14 us
    ppermute x3, starting transfers between devices, run(): got[k] = lax.ppermute(own, 'gen', first_axis[k])  6.55 us
    ppermute x4, starting transfers between devices, doubled(): lax.ppermute(value, 'ref', [(i, i ^ flip) for i in range(n_ref)])  5.92 us
  transfers between devices with their start and end apart: 41, of which 18 were waited for; matrix products, arithmetic and copies ran while one was open for 1% of the time, Pallas kernels for 39%

profile of v6, /device:TPU:1, one launch (start us, length us, event | category | flops | bytes accessed | tf_op | source)
XLA Modules:
  0.0 209.0 jit_solution(7986620838289618863)
XLA Ops:
  0.9 2.5 %entry.1 = (bf16[128,2048]{1,0:T(8,128)(2,1)S(1)}, bf16[512,2048]{1,0:T(8,128)(2,1)S(1)}, bf16[512,2048]{1,0:T(8,128)(2,1)S(1)}, f32[4,128]{1,0:T(4,128)S(1)}, f32[32,128]{1,0:T(8,128)S(1)}) custom-call(bf16[512,2048]{1,0:T(8,128)(2,1)} %gen_hbm.1, bf16[4096,2048]{1,0:T(8,128)(2,1)} %refs_4_.3, f32[4,128]{1,0:T(4,128)} %bitcast.22, f32[32,128]{1,0:T(8,128)} %bitcast.21), custom_call_target="tpu_custom_call" | custom-call | tf_op jit(solution)/shard_map/entry/pallas_call | solution.py:208
  3.4 2.5 %collective-permute-start.13 = (bf16[128,2048]{1,0:T(8,128)(2,1)S(1)}, bf16[128,2048]{1,0:T(8,128)(2,1)S(1)}, u32[]{:S(2)}, u32[]{:S(2)}) collective-permute-start(bf16[128,2048]{1,0:T(8,128)(2,1)S(1)} %get-tuple-element.61), channel_id=1, source_target_pairs={{0,8},{4,36},{8,16},{12,44},{16,24},{20,52},{24,0},{28,60},{32,40}... | collective-permute-start | bytes 1572872 | tf_op jit(solution)/shard_map/ppermute | solution.py:612
  5.9 3.3 %collective-permute-start.14 = (bf16[128,2048]{1,0:T(8,128)(2,1)S(1)}, bf16[128,2048]{1,0:T(8,128)(2,1)S(1)}, u32[]{:S(2)}, u32[]{:S(2)}) collective-permute-start(bf16[128,2048]{1,0:T(8,128)(2,1)S(1)} %get-tuple-element.61), channel_id=1, source_target_pairs={{0,16},{4,68},{8,24},{12,76},{16,0},{20,84},{24,8},{28,92},{32,48}... | collective-permute-start | bytes 1572872 | tf_op jit(solution)/shard_map/ppermute | solution.py:612
  9.2 0.7 collective-permute-start.15
  9.9 10.9 %cross_first_0.1 = (f32[512,3072]{1,0:T(8,128)S(1)}, f32[24,128]{1,0:T(8,128)S(1)}, f32[8,128]{1,0:T(8,128)S(1)}, f32[8,128]{1,0:T(8,128)S(1)}, bf16[512,2048]{1...) custom-call(bf16[512,2048]{1,0:T(8,128)(2,1)S(1)} %get-tuple-element, ...), custom_call_target="tpu_custom_call" | custom-call | tf_op jit(solution)/shard_map/cross_first_0/pallas_call | solution.py:344
  20.8 29.3 %cross_first_1.1 = (f32[512,1024]{1,0:T(8,128)S(1)}, f32[8,128]{1,0:T(8,128)S(1)}, f32[32,128]{1,0:T(8,128)S(1)}, f32[32,128]{1,0:T(8,128)S(1)}) custom-call(bf16[512,2048]{1,0:T(8,128)(2,1)S(1)} %get-tuple-element.39.refs_0_, bf16[512,2048]{1,0:T(8,128)(2,1)S(1)} %get-tuple-element.44.refs_1_, f32[32,128]{1,0:T(8,128)S(1)} %get-tuple-element.42.refs_3_.refs_2_, ...), custom_call_target="tpu_custom_call" | custom-call | tf_op jit(solution)/shard_map/cross_first_1/pallas_call | solution.py:344
  50.1 0.9 collective-permute-start.2
  51.0 1.2 collective-permute-start
  52.5 0.6 collective-permute-start.17
  53.1 2.2 %collective-permute-start.18 = (bf16[512,2048]{1,0:T(8,128)(2,1)S(1)}, bf16[512,2048]{1,0:T(8,128)(2,1)S(1)}, u32[]{:S(2)}, u32[]{:S(2)}) collective-permute-start(bf16[512,2048]{1,0:T(8,128)(2,1)S(1)} %constant_dynamic-update-slice_fusion.refs_2_), channel_id=1, source_target_pairs={{0,96},{4,28},{8,104},{12,4},{16,112},{20,12},{24,120},{28,20},{32... | collective-permute-start | bytes 6291464 | tf_op jit(solution)/shard_map/ppermute | solution.py:616
  55.5 1.9 collective-permute-start.1
  57.4 2.6 %collective-permute-start.12 = (bf16[512,2048]{1,0:T(8,128)(2,1)S(1)}, bf16[512,2048]{1,0:T(8,128)(2,1)S(1)}, u32[]{:S(2)}, u32[]{:S(2)}) collective-permute-start(bf16[512,2048]{1,0:T(8,128)(2,1)S(1)} %get-tuple-element.39.refs_0_), channel_id=1, source_target_pairs={{0,4},{4,0},{8,12},{12,8},{16,20},{20,16},{24,28},{28,24},{32,36},... | collective-permute-start | bytes 6291464 | tf_op jit(solution)/shard_map/ppermute | solution.py:613
  60.0 2.3 %collective-permute-start.4 = (f32[56,128]{1,0:T(8,128)S(1)}, f32[56,128]{1,0:T(8,128)S(1)}, u32[]{:S(2)}, u32[]{:S(2)}) collective-permute-start(f32[56,128]{1,0:T(8,128)S(1)} %pad_maximum_fusion.2), channel_id=1, source_target_pairs={{0,16},{4,20},{8,24},{12,28},{16,0},{20,4},{24,8},{28,12},{32,48},... | collective-permute-start | bytes 86024 | tf_op jit(solution)/shard_map/ppermute | solution.py:564
  62.3 17.6 %collective-permute-done.3 = f32[56,128]{1,0:T(8,128)S(1)} collective-permute-done((f32[56,128]{1,0:T(8,128)S(1)}, f32[56,128]{1,0:T(8,128)S(1)}, u32[]{:S(2)}, u32[]{:S(2)}) %collective-permute-start.3) | collective-permute-done | bytes 28704 | tf_op jit(solution)/shard_map/ppermute | solution.py:564
  79.9 0.8 collective-permute-start.5
  80.7 2.0 collective-permute-done.5
  82.7 1.7 collective-permute-start.6
  84.4 3.9 %collective-permute-start.7 = (f32[56,128]{1,0:T(8,128)S(1)}, f32[56,128]{1,0:T(8,128)S(1)}, u32[]{:S(2)}, u32[]{:S(2)}) collective-permute-start(f32[56,128]{1,0:T(8,128)S(1)} %pad_maximum_fusion.3), channel_id=1, source_target_pairs={{0,64},{4,68},{8,72},{12,76},{16,80},{20,84},{24,88},{28,92},{32,9... | collective-permute-start | bytes 86024 | tf_op jit(solution)/shard_map/ppermute | solution.py:564
  88.3 0.3 collective-permute-start.8
  88.9 2.6 %collective-permute-start.20 = (bf16[256,2048]{1,0:T(8,128)(2,1)S(1)}, bf16[256,2048]{1,0:T(8,128)(2,1)S(1)}, u32[]{:S(2)}, u32[]{:S(2)}) collective-permute-start(bf16[256,2048]{1,0:T(8,128)(2,1)S(1)} %slice.310), channel_id=1, source_target_pairs={{0,96},{4,28},{8,104},{12,4},{16,112},{20,12},{24,120},{28,20},{32... | collective-permute-start | bytes 3145736 | tf_op jit(solution)/shard_map/ppermute | solution.py:618
  91.7 26.5 %shard_map.76 = (f32[4,128]{1,0:T(4,128)S(1)}, f32[32,128]{1,0:T(8,128)S(1)}) custom-call(f32[512,3072]{1,0:T(8,128)S(1)} %get-tuple-element.45.refs_5_.refs_0_, f32[512,1024]{1,0:T(8,128)S(1)} %get-tuple-element.53.refs_1_, f32[32,128]{1,0:T(8,128)S(1)} %get-tuple-element.85.refs_2_, f32[4,128]{1,0:T(4,128)S(1)} %get-tuple-element.83.refs_3_), custom_call_target="tpu_custom_call" | custom-call | tf_op jit(solution)/shard_map/pallas_call | solution.py:381
  118.2 0.5 collective-permute-start.16
  118.7 0.7 collective-permute-done.11
  119.4 0.3 collective-permute-start.9
  119.7 3.8 %shard_map.77 = (f32[1024,512]{1,0:T(8,128)S(1)}, f32[16,128]{1,0:T(8,128)S(1)}, f32[1024,128]{1,0:T(8,128)S(1)}, f32[1024,128]{1,0:T(8,128)S(1)}) custom-call(bf16[512,2048]{1,0:T(8,128)(2,1)S(1)} %get-tuple-element.39.refs_0_, bf16[512,2048]{1,0:T(8,128)(2,1)S(1)} %collective-permute-done.12.refs_1_, ...), custom_call_target="tpu_custom_call" | custom-call | tf_op jit(solution)/shard_map/pallas_call | solution.py:462
  123.5 6.5 %shard_map.78 = (f32[1024,1024]{1,0:T(8,128)S(1)}, f32[16,128]{1,0:T(8,128)S(1)}) custom-call(bf16[512,2048]{1,0:T(8,128)(2,1)S(1)} %get-tuple-element.39.refs_0_, bf16[512,2048]{1,0:T(8,128)(2,1)S(1)} %collective-permute-done.12.refs_1_, bf16[512,2048]{1,0:T(8,128)(2,1)S(1)} %collective-permute-done.17.refs_2_, ...), custom_call_target="tpu_custom_call" | custom-call | tf_op jit(solution)/shard_map/pallas_call | solution.py:462
  130.0 3.8 %shard_map.79 = (f32[1024,512]{1,0:T(8,128)S(1)}, f32[16,128]{1,0:T(8,128)S(1)}) custom-call(bf16[512,2048]{1,0:T(8,128)(2,1)S(1)} %get-tuple-element.39.refs_0_, bf16[512,2048]{1,0:T(8,128)(2,1)S(1)} %collective-permute-done.12.refs_1_, bf16[256,2048]{1,0:T(8,128)(2,1)S(1)} %collective-permute-done.19.refs_2_, ...), custom_call_target="tpu_custom_call" | custom-call | tf_op jit(solution)/shard_map/pallas_call | solution.py:462
  133.9 2.1 collective-permute-start.22
  136.0 0.6 collective-permute-start.23
  136.6 2.6 %collective-permute-start.10 = (f32[4,128]{1,0:T(4,128)S(1)}, f32[4,128]{1,0:T(4,128)S(1)}, u32[]{:S(2)}, u32[]{:S(2)}) collective-permute-start(f32[4,128]{1,0:T(4,128)S(1)} %multiply_add_fusion.6), channel_id=1, source_target_pairs={{0,3},{1,2},{2,1},{3,0},{4,7},{5,6},{6,5},{7,4},{8,11},{9,10},{10,... | collective-permute-start | bytes 6152 | tf_op jit(solution)/shard_map/ppermute | solution.py:577
  139.2 1.2 collective-permute-start.24
  140.4 1.5 collective-permute-start.25
  142.0 1.0 collective-permute-start.26
  142.9 0.2 collective-permute-done.24
  143.2 1.4 collective-permute-done.25
  144.7 26.7 %shard_map.80 = (f32[4,128]{1,0:T(4,128)S(1)}, f32[32,128]{1,0:T(8,128)S(1)}) custom-call(f32[512,3072]{1,0:T(8,128)S(1)} %get-tuple-element.45.refs_5_.refs_0_, f32[512,1024]{1,0:T(8,128)S(1)} %get-tuple-element.53.refs_1_, f32[32,128]{1,0:T(8,128)S(1)} %get-tuple-element.81.refs_2_, f32[4,128]{1,0:T(4,128)S(1)} %get-tuple-element.79.refs_3_), custom_call_target="tpu_custom_call" | custom-call | tf_op jit(solution)/shard_map/pallas_call | solution.py:381
  171.5 1.5 shard_map.81
  173.1 2.6 %collective-permute-start.29 = (f32[16,128]{1,0:T(8,128)S(1)}, f32[16,128]{1,0:T(8,128)S(1)}, u32[]{:S(2)}, u32[]{:S(2)}) collective-permute-start(f32[16,128]{1,0:T(8,128)S(1)} %pad_maximum_fusion.8), channel_id=1, source_target_pairs={{0,3},{1,0},{2,1},{3,2},{4,7},{5,4},{6,5},{7,6},{8,11},{9,8},{10,9... | collective-permute-start | bytes 24584 | tf_op jit(solution)/shard_map/ppermute | solution.py:564
  175.7 1.0 collective-permute-done.27
  176.8 0.4 collective-permute-done.28
  177.1 0.3 collective-permute-done.29
  177.5 5.0 %collective-permute-start.30 = (f32[52,128]{1,0:T(8,128)S(1)}, f32[52,128]{1,0:T(8,128)S(1)}, u32[]{:S(2)}, u32[]{:S(2)}) collective-permute-start(f32[52,128]{1,0:T(8,128)S(1)} %pad_maximum_fusion.4), channel_id=1, source_target_pairs={{0,4},{4,0},{8,12},{12,8},{16,20},{20,16},{24,28},{28,24},{32,36},... | collective-permute-start | bytes 79880 | tf_op jit(solution)/shard_map/ppermute | solution.py:564
  182.5 0.9 collective-permute-done.30
  183.4 1.5 shard_map.82
  185.0 1.1 collective-permute-start.31
  186.1 1.8 collective-permute-start.32
  187.9 1.4 collective-permute-start.33
  189.3 1.2 collective-permute-done.32
  190.5 0.9 collective-permute-done.33
  191.4 0.6 collective-permute-start.34
  192.0 2.5 %collective-permute-start.35 = (f32[72,128]{1,0:T(8,128)S(1)}, f32[72,128]{1,0:T(8,128)S(1)}, u32[]{:S(2)}, u32[]{:S(2)}) collective-permute-start(f32[72,128]{1,0:T(8,128)S(1)} %pad_maximum_fusion.1), channel_id=1, source_target_pairs={{0,64},{4,68},{8,72},{12,76},{16,80},{20,84},{24,88},{28,92},{32,9... | collective-permute-start | bytes 110600 | tf_op jit(solution)/shard_map/ppermute | solution.py:564
  194.6 0.4 collective-permute-start.36
  195.0 0.5 collective-permute-done.34
  195.5 0.8 collective-permute-done.35
  196.3 1.3 collective-permute-done.36
  197.7 3.2 %collective-permute-start.37 = (f32[8,128]{1,0:T(8,128)S(1)}, f32[8,128]{1,0:T(8,128)S(1)}, u32[]{:S(2)}, u32[]{:S(2)}) collective-permute-start(f32[8,128]{1,0:T(8,128)S(1)} %bitcast_reduce_fusion.1), channel_id=1, source_target_pairs={{0,4},{4,0},{8,12},{12,8},{16,20},{20,16},{24,28},{28,24},{32,36},... | collective-permute-start | bytes 12296 | tf_op jit(solution)/shard_map/ppermute | solution.py:564
  200.9 0.6 bitcast_reduce_fusion
  201.6 0.2 collective-permute-done.37
  201.8 1.4 collective-permute-start.38
  203.2 1.8 collective-permute-start.39
  205.0 0.7 collective-permute-start.40
  205.7 1.5 collective-permute-done.39
  207.2 0.6 collective-permute-done.40
  207.8 1.2 fusion.13
  (94 shorter events, 1.9 us)
Async XLA Ops:
  3.4 48.9 %collective-permute-start.13 = (bf16[128,2048]{1,0:T(8,128)(2,1)S(1)}, bf16[128,2048]{1,0:T(8,128)(2,1)S(1)}, u32[]{:S(2)}, u32[]{:S(2)}) collective-permute-start(bf16[128,2048]{1,0:T(8,128)(2,1)S(1)} %get-tuple-element.61), channel_id=1, source_target_pairs={{0,8},{4,36},{8,16},{12,44},{16,24},{20,52},{24,0},{28,60},{32,40}... | collective-permute-start | bytes 1572872 | tf_op jit(solution)/shard_map/ppermute | solution.py:612
  5.9 46.5 %collective-permute-start.14 = (bf16[128,2048]{1,0:T(8,128)(2,1)S(1)}, bf16[128,2048]{1,0:T(8,128)(2,1)S(1)}, u32[]{:S(2)}, u32[]{:S(2)}) collective-permute-start(bf16[128,2048]{1,0:T(8,128)(2,1)S(1)} %get-tuple-element.61), channel_id=1, source_target_pairs={{0,16},{4,68},{8,24},{12,76},{16,0},{20,84},{24,8},{28,92},{32,48}... | collective-permute-start | bytes 1572872 | tf_op jit(solution)/shard_map/ppermute | solution.py:612
  9.2 43.2 %collective-permute-start.15 = (bf16[128,2048]{1,0:T(8,128)(2,1)S(1)}, bf16[128,2048]{1,0:T(8,128)(2,1)S(1)}, u32[]{:S(2)}, u32[]{:S(2)}) collective-permute-start(bf16[128,2048]{1,0:T(8,128)(2,1)S(1)} %get-tuple-element.61), channel_id=1, source_target_pairs={{0,24},{4,100},{8,0},{12,108},{16,8},{20,116},{24,16},{28,124},{32... | collective-permute-start | bytes 1572872 | tf_op jit(solution)/shard_map/ppermute | solution.py:612
  50.1 5.2 %collective-permute-start.2 = (f32[40,128]{1,0:T(8,128)S(1)}, f32[40,128]{1,0:T(8,128)S(1)}, u32[]{:S(2)}, u32[]{:S(2)}) collective-permute-start(f32[40,128]{1,0:T(8,128)S(1)} %pad_maximum_fusion.7), channel_id=1, source_target_pairs={{0,4},{4,0},{8,12},{12,8},{16,20},{20,16},{24,28},{28,24},{32,36},... | collective-permute-start | bytes 61448 | tf_op jit(solution)/shard_map/ppermute | solution.py:564
  51.0 4.3 %collective-permute-start = (f32[8,128]{1,0:T(8,128)S(1)}, f32[8,128]{1,0:T(8,128)S(1)}, u32[]{:S(2)}, u32[]{:S(2)}) collective-permute-start(f32[8,128]{1,0:T(8,128)S(1)} %get-tuple-element.52), channel_id=1, source_target_pairs={{0,1},{1,0},{2,3},{3,2},{4,5},{5,4},{6,7},{7,6},{8,9},{9,8},{10,11... | collective-permute-start | bytes 12296 | tf_op jit(solution)/shard_map/ppermute | solution.py:577
  52.5 35.8 %collective-permute-start.17 = (bf16[512,2048]{1,0:T(8,128)(2,1)S(1)}, bf16[512,2048]{1,0:T(8,128)(2,1)S(1)}, u32[]{:S(2)}, u32[]{:S(2)}) collective-permute-start(bf16[512,2048]{1,0:T(8,128)(2,1)S(1)} %constant_dynamic-update-slice_fusion.refs_2_), channel_id=1, source_target_pairs={{0,32},{4,12},{8,40},{12,20},{16,48},{20,28},{24,56},{28,4},{32,64... | collective-permute-start | bytes 6291464 | tf_op jit(solution)/shard_map/ppermute | solution.py:615
  53.1 35.5 %collective-permute-start.18 = (bf16[512,2048]{1,0:T(8,128)(2,1)S(1)}, bf16[512,2048]{1,0:T(8,128)(2,1)S(1)}, u32[]{:S(2)}, u32[]{:S(2)}) collective-permute-start(bf16[512,2048]{1,0:T(8,128)(2,1)S(1)} %constant_dynamic-update-slice_fusion.refs_2_), channel_id=1, source_target_pairs={{0,96},{4,28},{8,104},{12,4},{16,112},{20,12},{24,120},{28,20},{32... | collective-permute-start | bytes 6291464 | tf_op jit(solution)/shard_map/ppermute | solution.py:616
  55.4 24.5 %collective-permute-start.3 = (f32[56,128]{1,0:T(8,128)S(1)}, f32[56,128]{1,0:T(8,128)S(1)}, u32[]{:S(2)}, u32[]{:S(2)}) collective-permute-start(f32[56,128]{1,0:T(8,128)S(1)} %pad_maximum_fusion.2), channel_id=1, source_target_pairs={{0,8},{4,12},{8,16},{12,20},{16,24},{20,28},{24,0},{28,4},{32,40},... | collective-permute-start | bytes 86024 | tf_op jit(solution)/shard_map/ppermute | solution.py:564
  55.5 4.5 %collective-permute-start.1 = (f32[8,128]{1,0:T(8,128)S(1)}, f32[8,128]{1,0:T(8,128)S(1)}, u32[]{:S(2)}, u32[]{:S(2)}) collective-permute-start(f32[8,128]{1,0:T(8,128)S(1)} %pad_maximum_fusion.10), channel_id=1, source_target_pairs={{0,3},{1,2},{2,1},{3,0},{4,7},{5,6},{6,5},{7,4},{8,11},{9,10},{10,... | collective-permute-start | bytes 12296 | tf_op jit(solution)/shard_map/ppermute | solution.py:577
  57.4 62.3 %collective-permute-start.12 = (bf16[512,2048]{1,0:T(8,128)(2,1)S(1)}, bf16[512,2048]{1,0:T(8,128)(2,1)S(1)}, u32[]{:S(2)}, u32[]{:S(2)}) collective-permute-start(bf16[512,2048]{1,0:T(8,128)(2,1)S(1)} %get-tuple-element.39.refs_0_), channel_id=1, source_target_pairs={{0,4},{4,0},{8,12},{12,8},{16,20},{20,16},{24,28},{28,24},{32,36},... | collective-permute-start | bytes 6291464 | tf_op jit(solution)/shard_map/ppermute | solution.py:613
  60.0 20.7 %collective-permute-start.4 = (f32[56,128]{1,0:T(8,128)S(1)}, f32[56,128]{1,0:T(8,128)S(1)}, u32[]{:S(2)}, u32[]{:S(2)}) collective-permute-start(f32[56,128]{1,0:T(8,128)S(1)} %pad_maximum_fusion.2), channel_id=1, source_target_pairs={{0,16},{4,20},{8,24},{12,28},{16,0},{20,4},{24,8},{28,12},{32,48},... | collective-permute-start | bytes 86024 | tf_op jit(solution)/shard_map/ppermute | solution.py:564
  79.9 2.8 %collective-permute-start.5 = (f32[56,128]{1,0:T(8,128)S(1)}, f32[56,128]{1,0:T(8,128)S(1)}, u32[]{:S(2)}, u32[]{:S(2)}) collective-permute-start(f32[56,128]{1,0:T(8,128)S(1)} %pad_maximum_fusion.2), channel_id=1, source_target_pairs={{0,24},{4,28},{8,0},{12,4},{16,8},{20,12},{24,16},{28,20},{32,56},... | collective-permute-start | bytes 86024 | tf_op jit(solution)/shard_map/ppermute | solution.py:564
  82.7 6.2 %collective-permute-start.6 = (f32[56,128]{1,0:T(8,128)S(1)}, f32[56,128]{1,0:T(8,128)S(1)}, u32[]{:S(2)}, u32[]{:S(2)}) collective-permute-start(f32[56,128]{1,0:T(8,128)S(1)} %pad_maximum_fusion.3), channel_id=1, source_target_pairs={{0,32},{4,36},{8,40},{12,44},{16,48},{20,52},{24,56},{28,60},{32,6... | collective-permute-start | bytes 86024 | tf_op jit(solution)/shard_map/ppermute | solution.py:564
  84.4 7.1 %collective-permute-start.7 = (f32[56,128]{1,0:T(8,128)S(1)}, f32[56,128]{1,0:T(8,128)S(1)}, u32[]{:S(2)}, u32[]{:S(2)}) collective-permute-start(f32[56,128]{1,0:T(8,128)S(1)} %pad_maximum_fusion.3), channel_id=1, source_target_pairs={{0,64},{4,68},{8,72},{12,76},{16,80},{20,84},{24,88},{28,92},{32,9... | collective-permute-start | bytes 86024 | tf_op jit(solution)/shard_map/ppermute | solution.py:564
  88.3 3.3 %collective-permute-start.8 = (f32[56,128]{1,0:T(8,128)S(1)}, f32[56,128]{1,0:T(8,128)S(1)}, u32[]{:S(2)}, u32[]{:S(2)}) collective-permute-start(f32[56,128]{1,0:T(8,128)S(1)} %pad_maximum_fusion.3), channel_id=1, source_target_pairs={{0,96},{4,100},{8,104},{12,108},{16,112},{20,116},{24,120},{28,124... | collective-permute-start | bytes 86024 | tf_op jit(solution)/shard_map/ppermute | solution.py:564
  88.6 41.4 %collective-permute-start.19 = (bf16[256,2048]{1,0:T(8,128)(2,1)S(1)}, bf16[256,2048]{1,0:T(8,128)(2,1)S(1)}, u32[]{:S(2)}, u32[]{:S(2)}) collective-permute-start(bf16[256,2048]{1,0:T(8,128)(2,1)S(1)} %slice.309), channel_id=1, source_target_pairs={{0,32},{4,12},{8,40},{12,20},{16,48},{20,28},{24,56},{28,4},{32,64... | collective-permute-start | bytes 3145736 | tf_op jit(solution)/shard_map/ppermute | solution.py:617
  88.9 41.1 %collective-permute-start.20 = (bf16[256,2048]{1,0:T(8,128)(2,1)S(1)}, bf16[256,2048]{1,0:T(8,128)(2,1)S(1)}, u32[]{:S(2)}, u32[]{:S(2)}) collective-permute-start(bf16[256,2048]{1,0:T(8,128)(2,1)S(1)} %slice.310), channel_id=1, source_target_pairs={{0,96},{4,28},{8,104},{12,4},{16,112},{20,12},{24,120},{28,20},{32... | collective-permute-start | bytes 3145736 | tf_op jit(solution)/shard_map/ppermute | solution.py:618
  118.1 1.3 collective-permute-start.11
  118.2 1.5 collective-permute-start.16
  119.4 17.2 %collective-permute-start.9 = (f32[4,128]{1,0:T(4,128)S(1)}, f32[4,128]{1,0:T(4,128)S(1)}, u32[]{:S(2)}, u32[]{:S(2)}) collective-permute-start(f32[4,128]{1,0:T(4,128)S(1)} %get-tuple-element.59), channel_id=1, source_target_pairs={{0,1},{1,0},{2,3},{3,2},{4,5},{5,4},{6,7},{7,6},{8,9},{9,8},{10,11... | collective-permute-start | bytes 6152 | tf_op jit(solution)/shard_map/ppermute | solution.py:577
  133.8 5.3 %collective-permute-start.21 = (f32[48,128]{1,0:T(8,128)S(1)}, f32[48,128]{1,0:T(8,128)S(1)}, u32[]{:S(2)}, u32[]{:S(2)}) collective-permute-start(f32[48,128]{1,0:T(8,128)S(1)} %pad_maximum_fusion.5), channel_id=1, source_target_pairs={{0,8},{4,12},{8,16},{12,20},{16,24},{20,28},{24,0},{28,4},{32,40},... | collective-permute-start | bytes 73736 | tf_op jit(solution)/shard_map/ppermute | solution.py:564
  133.9 5.2 %collective-permute-start.22 = (f32[48,128]{1,0:T(8,128)S(1)}, f32[48,128]{1,0:T(8,128)S(1)}, u32[]{:S(2)}, u32[]{:S(2)}) collective-permute-start(f32[48,128]{1,0:T(8,128)S(1)} %pad_maximum_fusion.5), channel_id=1, source_target_pairs={{0,16},{4,20},{8,24},{12,28},{16,0},{20,4},{24,8},{28,12},{32,48},... | collective-permute-start | bytes 73736 | tf_op jit(solution)/shard_map/ppermute | solution.py:564
  136.0 3.2 %collective-permute-start.23 = (f32[48,128]{1,0:T(8,128)S(1)}, f32[48,128]{1,0:T(8,128)S(1)}, u32[]{:S(2)}, u32[]{:S(2)}) collective-permute-start(f32[48,128]{1,0:T(8,128)S(1)} %pad_maximum_fusion.5), channel_id=1, source_target_pairs={{0,24},{4,28},{8,0},{12,4},{16,8},{20,12},{24,16},{28,20},{32,56},... | collective-permute-start | bytes 73736 | tf_op jit(solution)/shard_map/ppermute | solution.py:564
  136.6 6.3 %collective-permute-start.10 = (f32[4,128]{1,0:T(4,128)S(1)}, f32[4,128]{1,0:T(4,128)S(1)}, u32[]{:S(2)}, u32[]{:S(2)}) collective-permute-start(f32[4,128]{1,0:T(4,128)S(1)} %multiply_add_fusion.6), channel_id=1, source_target_pairs={{0,3},{1,2},{2,1},{3,0},{4,7},{5,6},{6,5},{7,4},{8,11},{9,10},{10,... | collective-permute-start | bytes 6152 | tf_op jit(solution)/shard_map/ppermute | solution.py:577
  139.2 4.0 %collective-permute-start.24 = (f32[48,128]{1,0:T(8,128)S(1)}, f32[48,128]{1,0:T(8,128)S(1)}, u32[]{:S(2)}, u32[]{:S(2)}) collective-permute-start(f32[48,128]{1,0:T(8,128)S(1)} %pad_maximum_fusion.6), channel_id=1, source_target_pairs={{0,32},{4,36},{8,40},{12,44},{16,48},{20,52},{24,56},{28,60},{32,6... | collective-permute-start | bytes 73736 | tf_op jit(solution)/shard_map/ppermute | solution.py:564
  140.4 4.2 %collective-permute-start.25 = (f32[48,128]{1,0:T(8,128)S(1)}, f32[48,128]{1,0:T(8,128)S(1)}, u32[]{:S(2)}, u32[]{:S(2)}) collective-permute-start(f32[48,128]{1,0:T(8,128)S(1)} %pad_maximum_fusion.6), channel_id=1, source_target_pairs={{0,64},{4,68},{8,72},{12,76},{16,80},{20,84},{24,88},{28,92},{32,9... | collective-permute-start | bytes 73736 | tf_op jit(solution)/shard_map/ppermute | solution.py:564
  142.0 2.7 %collective-permute-start.26 = (f32[48,128]{1,0:T(8,128)S(1)}, f32[48,128]{1,0:T(8,128)S(1)}, u32[]{:S(2)}, u32[]{:S(2)}) collective-permute-start(f32[48,128]{1,0:T(8,128)S(1)} %pad_maximum_fusion.6), channel_id=1, source_target_pairs={{0,96},{4,100},{8,104},{12,108},{16,112},{20,116},{24,120},{28,124... | collective-permute-start | bytes 73736 | tf_op jit(solution)/shard_map/ppermute | solution.py:564
  173.0 3.8 %collective-permute-start.27 = (f32[16,128]{1,0:T(8,128)S(1)}, f32[16,128]{1,0:T(8,128)S(1)}, u32[]{:S(2)}, u32[]{:S(2)}) collective-permute-start(f32[16,128]{1,0:T(8,128)S(1)} %pad_maximum_fusion.8), channel_id=1, source_target_pairs={{0,1},{1,2},{2,3},{3,0},{4,5},{5,6},{6,7},{7,4},{8,9},{9,10},{10,1... | collective-permute-start | bytes 24584 | tf_op jit(solution)/shard_map/ppermute | solution.py:564
  173.1 4.1 %collective-permute-start.28 = (f32[16,128]{1,0:T(8,128)S(1)}, f32[16,128]{1,0:T(8,128)S(1)}, u32[]{:S(2)}, u32[]{:S(2)}) collective-permute-start(f32[16,128]{1,0:T(8,128)S(1)} %pad_maximum_fusion.8), channel_id=1, source_target_pairs={{0,2},{1,3},{2,0},{3,1},{4,6},{5,7},{6,4},{7,5},{8,10},{9,11},{10,... | collective-permute-start | bytes 24584 | tf_op jit(solution)/shard_map/ppermute | solution.py:564
  173.1 4.3 %collective-permute-start.29 = (f32[16,128]{1,0:T(8,128)S(1)}, f32[16,128]{1,0:T(8,128)S(1)}, u32[]{:S(2)}, u32[]{:S(2)}) collective-permute-start(f32[16,128]{1,0:T(8,128)S(1)} %pad_maximum_fusion.8), channel_id=1, source_target_pairs={{0,3},{1,0},{2,1},{3,2},{4,7},{5,4},{6,5},{7,6},{8,11},{9,8},{10,9... | collective-permute-start | bytes 24584 | tf_op jit(solution)/shard_map/ppermute | solution.py:564
  177.5 5.9 %collective-permute-start.30 = (f32[52,128]{1,0:T(8,128)S(1)}, f32[52,128]{1,0:T(8,128)S(1)}, u32[]{:S(2)}, u32[]{:S(2)}) collective-permute-start(f32[52,128]{1,0:T(8,128)S(1)} %pad_maximum_fusion.4), channel_id=1, source_target_pairs={{0,4},{4,0},{8,12},{12,8},{16,20},{20,16},{24,28},{28,24},{32,36},... | collective-permute-start | bytes 79880 | tf_op jit(solution)/shard_map/ppermute | solution.py:564
  183.4 17.6 %copy-start = (f32[4096]{0:T(1024)S(1)}, f32[4096]{0:T(1024)}, u32[]{:S(2)}) copy-start(f32[4096]{0:T(1024)} %param.9) | copy-start | bytes 49156
  185.0 4.3 %collective-permute-start.31 = (f32[72,128]{1,0:T(8,128)S(1)}, f32[72,128]{1,0:T(8,128)S(1)}, u32[]{:S(2)}, u32[]{:S(2)}) collective-permute-start(f32[72,128]{1,0:T(8,128)S(1)} %pad_maximum_fusion), channel_id=1, source_target_pairs={{0,8},{4,12},{8,16},{12,20},{16,24},{20,28},{24,0},{28,4},{32,40},... | collective-permute-start | bytes 110600 | tf_op jit(solution)/shard_map/ppermute | solution.py:564
  186.1 4.4 %collective-permute-start.32 = (f32[72,128]{1,0:T(8,128)S(1)}, f32[72,128]{1,0:T(8,128)S(1)}, u32[]{:S(2)}, u32[]{:S(2)}) collective-permute-start(f32[72,128]{1,0:T(8,128)S(1)} %pad_maximum_fusion), channel_id=1, source_target_pairs={{0,16},{4,20},{8,24},{12,28},{16,0},{20,4},{24,8},{28,12},{32,48},... | collective-permute-start | bytes 110600 | tf_op jit(solution)/shard_map/ppermute | solution.py:564
  187.9 3.5 %collective-permute-start.33 = (f32[72,128]{1,0:T(8,128)S(1)}, f32[72,128]{1,0:T(8,128)S(1)}, u32[]{:S(2)}, u32[]{:S(2)}) collective-permute-start(f32[72,128]{1,0:T(8,128)S(1)} %pad_maximum_fusion), channel_id=1, source_target_pairs={{0,24},{4,28},{8,0},{12,4},{16,8},{20,12},{24,16},{28,20},{32,56},... | collective-permute-start | bytes 110600 | tf_op jit(solution)/shard_map/ppermute | solution.py:564
  191.4 4.1 %collective-permute-start.34 = (f32[72,128]{1,0:T(8,128)S(1)}, f32[72,128]{1,0:T(8,128)S(1)}, u32[]{:S(2)}, u32[]{:S(2)}) collective-permute-start(f32[72,128]{1,0:T(8,128)S(1)} %pad_maximum_fusion.1), channel_id=1, source_target_pairs={{0,32},{4,36},{8,40},{12,44},{16,48},{20,52},{24,56},{28,60},{32,6... | collective-permute-start | bytes 110600 | tf_op jit(solution)/shard_map/ppermute | solution.py:564
  192.0 4.3 %collective-permute-start.35 = (f32[72,128]{1,0:T(8,128)S(1)}, f32[72,128]{1,0:T(8,128)S(1)}, u32[]{:S(2)}, u32[]{:S(2)}) collective-permute-start(f32[72,128]{1,0:T(8,128)S(1)} %pad_maximum_fusion.1), channel_id=1, source_target_pairs={{0,64},{4,68},{8,72},{12,76},{16,80},{20,84},{24,88},{28,92},{32,9... | collective-permute-start | bytes 110600 | tf_op jit(solution)/shard_map/ppermute | solution.py:564
  194.6 3.1 %collective-permute-start.36 = (f32[72,128]{1,0:T(8,128)S(1)}, f32[72,128]{1,0:T(8,128)S(1)}, u32[]{:S(2)}, u32[]{:S(2)}) collective-permute-start(f32[72,128]{1,0:T(8,128)S(1)} %pad_maximum_fusion.1), channel_id=1, source_target_pairs={{0,96},{4,100},{8,104},{12,108},{16,112},{20,116},{24,120},{28,124... | collective-permute-start | bytes 110600 | tf_op jit(solution)/shard_map/ppermute | solution.py:564
  197.7 4.0 %collective-permute-start.37 = (f32[8,128]{1,0:T(8,128)S(1)}, f32[8,128]{1,0:T(8,128)S(1)}, u32[]{:S(2)}, u32[]{:S(2)}) collective-permute-start(f32[8,128]{1,0:T(8,128)S(1)} %bitcast_reduce_fusion.1), channel_id=1, source_target_pairs={{0,4},{4,0},{8,12},{12,8},{16,20},{20,16},{24,28},{28,24},{32,36},... | collective-permute-start | bytes 12296 | tf_op jit(solution)/shard_map/ppermute | solution.py:564
  201.8 3.9 %collective-permute-start.38 = (f32[12,128]{1,0:T(8,128)S(1)}, f32[12,128]{1,0:T(8,128)S(1)}, u32[]{:S(2)}, u32[]{:S(2)}) collective-permute-start(f32[12,128]{1,0:T(8,128)S(1)} %pad_maximum_fusion.9), channel_id=1, source_target_pairs={{0,1},{1,2},{2,3},{3,0},{4,5},{5,6},{6,7},{7,4},{8,9},{9,10},{10,1... | collective-permute-start | bytes 18440 | tf_op jit(solution)/shard_map/ppermute | solution.py:564
  203.2 4.0 %collective-permute-start.39 = (f32[12,128]{1,0:T(8,128)S(1)}, f32[12,128]{1,0:T(8,128)S(1)}, u32[]{:S(2)}, u32[]{:S(2)}) collective-permute-start(f32[12,128]{1,0:T(8,128)S(1)} %pad_maximum_fusion.9), channel_id=1, source_target_pairs={{0,2},{1,3},{2,0},{3,1},{4,6},{5,7},{6,4},{7,5},{8,10},{9,11},{10,... | collective-permute-start | bytes 18440 | tf_op jit(solution)/shard_map/ppermute | solution.py:564
  205.0 2.8 %collective-permute-start.40 = (f32[12,128]{1,0:T(8,128)S(1)}, f32[12,128]{1,0:T(8,128)S(1)}, u32[]{:S(2)}, u32[]{:S(2)}) collective-permute-start(f32[12,128]{1,0:T(8,128)S(1)} %pad_maximum_fusion.9), channel_id=1, source_target_pairs={{0,3},{1,0},{2,1},{3,2},{4,7},{5,4},{6,5},{7,6},{8,11},{9,8},{10,9... | collective-permute-start | bytes 18440 | tf_op jit(solution)/shard_map/ppermute | solution.py:564

commit v7 on v6

--- a/solution.py
+++ b/solution.py
@@ -611,19 +611,22 @@
         for k in (1, 3, 2):
             got[k] = lax.ppermute(own, "gen", first_axis[k])
         mate = lax.ppermute(held, "gen", core_stage[0])
-        near = jnp.concatenate([own, got[1], got[2], got[3]], axis=0)
-        up = lax.ppermute(near, "gen", second_axis[1])
-        down = lax.ppermute(near, "gen", second_axis[3])
-        low_far = lax.ppermute(up[: 2 * LANES], "gen", second_axis[1])
-        high_far = lax.ppermute(down[2 * LANES :], "gen", second_axis[3])
+        low = jnp.concatenate([own, got[1]], axis=0)
+        high = jnp.concatenate([got[2], got[3]], axis=0)
+        low_up = lax.ppermute(low, "gen", second_axis[1])
+        high_down = lax.ppermute(high, "gen", second_axis[3])
+        high_up = lax.ppermute(high, "gen", second_axis[1])
+        low_down = lax.ppermute(low, "gen", second_axis[3])
+        low_far = lax.ppermute(low_up, "gen", second_axis[1])
+        high_far = lax.ppermute(high_down, "gen", second_axis[3])
 
         d0, hcol, mine, gmass, ahead, *carried = first_pass(held, tile0, ref_features, wg, wr)
         theirs = lax.ppermute(mine, "gen", core_stage[0])
         d1, row_part, lcol, hcol = first_pass(held, ahead, ref_features, wr, mine, d0, hcol, *carried)
         hrow = mine[:nq]
         weight = jnp.concatenate([wg, theirs[nq:]], axis=0)
-        e0, z1_0, hs, ws = self_first(held, mate, [near], mine, theirs, place, 0)
-        e1, z1_1 = self_first(held, mate, [up, down], hs, ws, place, 4)
+        e0, z1_0, hs, ws = self_first(held, mate, [low, high], mine, theirs, place, 0)
+        e1, z1_1 = self_first(held, mate, [low_up, high_up, low_down, high_down], hs, ws, place, 4)
         e2, z1_2 = self_first(held, mate, [low_far, high_far], hs, ws, place, 12)
         e = [e0, e1, e2]
 

time: 210 us -> 212 us (level)
  starting transfers between devices: 60.2 us -> 62.9 us
    ppermute x28, waiting for transfers between devices: 31.7 us -> 16.7 us  [shift(): return [lax.ppermute(value, axis, perm) for perm in perms]]
    ppermute x4 -> x6, waiting for transfers between devices: 0.01 us -> 11.9 us  [the longest x1 7.1 us: run(): high_up = lax.ppermute(high, 'gen', second_axis[1])]
    ppermute x28, starting transfers between devices: 39.1 us -> 44.3 us  [shift(): return [lax.ppermute(value, axis, perm) for perm in perms]]
    ppermute x4 -> x6, starting transfers between devices: 5.48 us -> 5.68 us  [the longest x1 2.67 us: run(): low_down = lax.ppermute(low, 'gen', second_axis[3])]
  transfers between devices with their start and end apart: 41 -> 43, of which waited for: 18 -> 25; matrix products, arithmetic and copies ran while one was open for 1% -> 1% of each run, Pallas kernels for 39% -> 38%
where the time goes in v7:
time: 212 us
  Pallas kernels  113 us (53%)
  starting transfers between devices  62.9 us (30%)
  waiting for transfers between devices  31.9 us (15%)
  other arithmetic  2.56 us (1%)
    pallas_call x2, Pallas kernels, next_pass(): pl.pallas_call(functools.partial(next_kernel, len(parts)), in_specs=[vmem...  53.2 us
    ppermute x28, starting transfers between devices, shift(): return [lax.ppermute(value, axis, perm) for perm in perms]  44.3 us
    pallas_call x2, Pallas kernels, first_pass(): pl.pallas_call(functools.partial(first_kernel, first_tile, steps), in_spe...  40.2 us
    ppermute x28, waiting for transfers between devices, shift(): return [lax.ppermute(value, axis, perm) for perm in perms]  16.7 us
    pallas_call x3, Pallas kernels, self_first(): pl.pallas_call(functools.partial(self_first_kernel, len(sources), first),...  14 us
    ppermute x1, waiting for transfers between devices, run(): high_up = lax.ppermute(high, 'gen', second_axis[1])  7.1 us
    ppermute x3, starting transfers between devices, run(): got[k] = lax.ppermute(own, 'gen', first_axis[k])  6.3 us
  transfers between devices with their start and end apart: 43, of which 25 were waited for; matrix products, arithmetic and copies ran while one was open for 1% of the time, Pallas kernels for 38%

profile of v7, /device:TPU:1, one launch (start us, length us, event | category | flops | bytes accessed | tf_op | source)
XLA Modules:
  0.0 211.5 jit_solution(16062730645825836113)
XLA Ops:
  0.9 2.5 %entry.1 = (bf16[128,2048]{1,0:T(8,128)(2,1)S(1)}, bf16[512,2048]{1,0:T(8,128)(2,1)S(1)}, bf16[512,2048]{1,0:T(8,128)(2,1)S(1)}, f32[4,128]{1,0:T(4,128)S(1)}, f32[32,128]{1,0:T(8,128)S(1)}) custom-call(bf16[512,2048]{1,0:T(8,128)(2,1)} %gen_hbm.1, bf16[4096,2048]{1,0:T(8,128)(2,1)} %refs_4_.3, f32[4,128]{1,0:T(4,128)} %bitcast.22, f32[32,128]{1,0:T(8,128)} %bitcast.21), custom_call_target="tpu_custom_call" | custom-call | tf_op jit(solution)/shard_map/entry/pallas_call | solution.py:208
  3.4 4.5 %collective-permute-start.14 = (bf16[128,2048]{1,0:T(8,128)(2,1)S(1)}, bf16[128,2048]{1,0:T(8,128)(2,1)S(1)}, u32[]{:S(2)}, u32[]{:S(2)}) collective-permute-start(bf16[128,2048]{1,0:T(8,128)(2,1)S(1)} %get-tuple-element.61), channel_id=1, source_target_pairs={{0,16},{4,68},{8,24},{12,76},{16,0},{20,84},{24,8},{28,92},{32,48}... | collective-permute-start | bytes 1572872 | tf_op jit(solution)/shard_map/ppermute | solution.py:612
  7.9 0.4 collective-permute-start.15
  8.3 10.9 %cross_first_0.1 = (f32[512,3072]{1,0:T(8,128)S(1)}, f32[24,128]{1,0:T(8,128)S(1)}, f32[8,128]{1,0:T(8,128)S(1)}, f32[8,128]{1,0:T(8,128)S(1)}, bf16[512,2048]{1...) custom-call(bf16[512,2048]{1,0:T(8,128)(2,1)S(1)} %get-tuple-element, ...), custom_call_target="tpu_custom_call" | custom-call | tf_op jit(solution)/shard_map/cross_first_0/pallas_call | solution.py:344
  19.2 29.3 %cross_first_1.1 = (f32[512,1024]{1,0:T(8,128)S(1)}, f32[8,128]{1,0:T(8,128)S(1)}, f32[32,128]{1,0:T(8,128)S(1)}, f32[32,128]{1,0:T(8,128)S(1)}) custom-call(bf16[512,2048]{1,0:T(8,128)(2,1)S(1)} %get-tuple-element.39.refs_0_, bf16[512,2048]{1,0:T(8,128)(2,1)S(1)} %get-tuple-element.44.refs_1_, f32[32,128]{1,0:T(8,128)S(1)} %get-tuple-element.42.refs_3_.refs_2_, ...), custom_call_target="tpu_custom_call" | custom-call | tf_op jit(solution)/shard_map/cross_first_1/pallas_call | solution.py:344
  48.5 1.0 collective-permute-start.2
  49.5 1.2 collective-permute-start
  50.8 1.2 collective-permute-done
  52.0 2.6 %collective-permute-start.1 = (f32[8,128]{1,0:T(8,128)S(1)}, f32[8,128]{1,0:T(8,128)S(1)}, u32[]{:S(2)}, u32[]{:S(2)}) collective-permute-start(f32[8,128]{1,0:T(8,128)S(1)} %pad_maximum_fusion.10), channel_id=1, source_target_pairs={{0,3},{1,2},{2,1},{3,0},{4,7},{5,6},{6,5},{7,4},{8,11},{9,10},{10,... | collective-permute-start | bytes 12296 | tf_op jit(solution)/shard_map/ppermute | solution.py:577
  54.6 0.8 collective-permute-start.3
  55.3 2.4 %collective-permute-start.4 = (f32[56,128]{1,0:T(8,128)S(1)}, f32[56,128]{1,0:T(8,128)S(1)}, u32[]{:S(2)}, u32[]{:S(2)}) collective-permute-start(f32[56,128]{1,0:T(8,128)S(1)} %pad_maximum_fusion.2), channel_id=1, source_target_pairs={{0,16},{4,20},{8,24},{12,28},{16,0},{20,4},{24,8},{28,12},{32,48},... | collective-permute-start | bytes 86024 | tf_op jit(solution)/shard_map/ppermute | solution.py:564
  57.8 1.1 collective-permute-start.5
  58.9 1.4 collective-permute-start.13
  60.2 2.4 %collective-permute-start.12 = (bf16[512,2048]{1,0:T(8,128)(2,1)S(1)}, bf16[512,2048]{1,0:T(8,128)(2,1)S(1)}, u32[]{:S(2)}, u32[]{:S(2)}) collective-permute-start(bf16[512,2048]{1,0:T(8,128)(2,1)S(1)} %get-tuple-element.39.refs_0_), channel_id=1, source_target_pairs={{0,4},{4,0},{8,12},{12,8},{16,20},{20,16},{24,28},{28,24},{32,36},... | collective-permute-start | bytes 6291464 | tf_op jit(solution)/shard_map/ppermute | solution.py:613
  62.7 1.6 collective-permute-start.6
  64.3 3.3 %collective-permute-start.7 = (f32[56,128]{1,0:T(8,128)S(1)}, f32[56,128]{1,0:T(8,128)S(1)}, u32[]{:S(2)}, u32[]{:S(2)}) collective-permute-start(f32[56,128]{1,0:T(8,128)S(1)} %pad_maximum_fusion.3), channel_id=1, source_target_pairs={{0,64},{4,68},{8,72},{12,76},{16,80},{20,84},{24,88},{28,92},{32,9... | collective-permute-start | bytes 86024 | tf_op jit(solution)/shard_map/ppermute | solution.py:564
  67.7 0.8 collective-permute-start.8
  68.5 1.0 collective-permute-done.13
  69.5 1.0 collective-permute-start.20
  70.6 0.5 collective-permute-start.17
  71.4 26.5 %shard_map.76 = (f32[4,128]{1,0:T(4,128)S(1)}, f32[32,128]{1,0:T(8,128)S(1)}) custom-call(f32[512,3072]{1,0:T(8,128)S(1)} %get-tuple-element.45.refs_5_.refs_0_, f32[512,1024]{1,0:T(8,128)S(1)} %get-tuple-element.53.refs_1_, f32[32,128]{1,0:T(8,128)S(1)} %get-tuple-element.85.refs_2_, f32[4,128]{1,0:T(4,128)S(1)} %get-tuple-element.83.refs_3_), custom_call_target="tpu_custom_call" | custom-call | tf_op jit(solution)/shard_map/pallas_call | solution.py:381
  97.9 4.6 %collective-permute-start.11 = (f32[32,128]{1,0:T(8,128)S(1)}, f32[32,128]{1,0:T(8,128)S(1)}, u32[]{:S(2)}, u32[]{:S(2)}) collective-permute-start(f32[32,128]{1,0:T(8,128)S(1)} %get-tuple-element.60), channel_id=1, source_target_pairs={{0,4},{4,0},{8,12},{12,8},{16,20},{20,16},{24,28},{28,24},{32,36},... | collective-permute-start | bytes 49160 | tf_op jit(solution)/shard_map/ppermute | solution.py:564
  102.6 1.1 collective-permute-done.16.refs_5_
  103.7 2.7 %collective-permute-start.19 = (bf16[256,2048]{1,0:T(8,128)(2,1)S(1)}, bf16[256,2048]{1,0:T(8,128)(2,1)S(1)}, u32[]{:S(2)}, u32[]{:S(2)}) collective-permute-start(bf16[256,2048]{1,0:T(8,128)(2,1)S(1)} %constant_dynamic-update-slice_fusion.refs_2_), channel_id=1, source_target_pairs={{0,96},{4,28},{8,104},{12,4},{16,112},{20,12},{24,120},{28,20},{32... | collective-permute-start | bytes 3145736 | tf_op jit(solution)/shard_map/ppermute | solution.py:619
  106.4 1.4 collective-permute-start.21
  108.0 3.8 %shard_map.77 = (f32[1024,512]{1,0:T(8,128)S(1)}, f32[16,128]{1,0:T(8,128)S(1)}, f32[1024,128]{1,0:T(8,128)S(1)}, f32[1024,128]{1,0:T(8,128)S(1)}) custom-call(bf16[512,2048]{1,0:T(8,128)(2,1)S(1)} %get-tuple-element.39.refs_0_, bf16[512,2048]{1,0:T(8,128)(2,1)S(1)} %collective-permute-done.12.refs_1_, ...), custom_call_target="tpu_custom_call" | custom-call | tf_op jit(solution)/shard_map/pallas_call | solution.py:462
  111.7 7.1 %collective-permute-done.18.refs_3_ = bf16[256,2048]{1,0:T(8,128)(2,1)S(1)} collective-permute-done((bf16[256,2048]{1,0:T(8,128)(2,1)S(1)}, bf16[256,2048]{1,0:T(8,128)(2,1)S(1)}, u32[]{:S(2)}, u32[]{:S(2)}) %collective-permute-start.18) | collective-permute-done | bytes 1048608 | tf_op jit(solution)/shard_map/ppermute | solution.py:618
  118.8 6.4 %shard_map.78 = (f32[1024,1024]{1,0:T(8,128)S(1)}, f32[16,128]{1,0:T(8,128)S(1)}) custom-call(bf16[512,2048]{1,0:T(8,128)(2,1)S(1)} %get-tuple-element.39.refs_0_, bf16[512,2048]{1,0:T(8,128)(2,1)S(1)} %collective-permute-done.12.refs_1_, bf16[256,2048]{1,0:T(8,128)(2,1)S(1)} %collective-permute-done.17.refs_2_, ...), custom_call_target="tpu_custom_call" | custom-call | tf_op jit(solution)/shard_map/pallas_call | solution.py:462
  125.3 4.0 %collective-permute-done.22.refs_3_ = bf16[256,2048]{1,0:T(8,128)(2,1)S(1)} collective-permute-done((bf16[256,2048]{1,0:T(8,128)(2,1)S(1)}, bf16[256,2048]{1,0:T(8,128)(2,1)S(1)}, u32[]{:S(2)}, u32[]{:S(2)}) %collective-permute-start.22) | collective-permute-done | bytes 1048608 | tf_op jit(solution)/shard_map/ppermute | solution.py:621
  129.3 0.7 collective-permute-done.21.refs_2_
  130.1 3.8 %shard_map.79 = (f32[1024,512]{1,0:T(8,128)S(1)}, f32[16,128]{1,0:T(8,128)S(1)}) custom-call(bf16[512,2048]{1,0:T(8,128)(2,1)S(1)} %get-tuple-element.39.refs_0_, bf16[512,2048]{1,0:T(8,128)(2,1)S(1)} %collective-permute-done.12.refs_1_, bf16[256,2048]{1,0:T(8,128)(2,1)S(1)} %collective-permute-done.21.refs_2_, ...), custom_call_target="tpu_custom_call" | custom-call | tf_op jit(solution)/shard_map/pallas_call | solution.py:462
  133.9 3.6 %collective-permute-start.24 = (f32[48,128]{1,0:T(8,128)S(1)}, f32[48,128]{1,0:T(8,128)S(1)}, u32[]{:S(2)}, u32[]{:S(2)}) collective-permute-start(f32[48,128]{1,0:T(8,128)S(1)} %pad_maximum_fusion.5), channel_id=1, source_target_pairs={{0,16},{4,20},{8,24},{12,28},{16,0},{20,4},{24,8},{28,12},{32,48},... | collective-permute-start | bytes 73736 | tf_op jit(solution)/shard_map/ppermute | solution.py:564
  137.8 1.2 collective-permute-done.24
  139.0 1.8 collective-permute-done.25
  140.9 3.8 %collective-permute-start.27 = (f32[48,128]{1,0:T(8,128)S(1)}, f32[48,128]{1,0:T(8,128)S(1)}, u32[]{:S(2)}, u32[]{:S(2)}) collective-permute-start(f32[48,128]{1,0:T(8,128)S(1)} %pad_maximum_fusion.6), channel_id=1, source_target_pairs={{0,64},{4,68},{8,72},{12,76},{16,80},{20,84},{24,88},{28,92},{32,9... | collective-permute-start | bytes 73736 | tf_op jit(solution)/shard_map/ppermute | solution.py:564
  144.7 1.4 collective-permute-done.27
  146.1 1.5 collective-permute-done.28
  147.7 26.7 %shard_map.80 = (f32[4,128]{1,0:T(4,128)S(1)}, f32[32,128]{1,0:T(8,128)S(1)}) custom-call(f32[512,3072]{1,0:T(8,128)S(1)} %get-tuple-element.45.refs_5_.refs_0_, f32[512,1024]{1,0:T(8,128)S(1)} %get-tuple-element.53.refs_1_, f32[32,128]{1,0:T(8,128)S(1)} %get-tuple-element.81.refs_2_, f32[4,128]{1,0:T(4,128)S(1)} %get-tuple-element.79.refs_3_), custom_call_target="tpu_custom_call" | custom-call | tf_op jit(solution)/shard_map/pallas_call | solution.py:381
  174.4 1.5 shard_map.81
  176.1 2.6 %collective-permute-start.31 = (f32[16,128]{1,0:T(8,128)S(1)}, f32[16,128]{1,0:T(8,128)S(1)}, u32[]{:S(2)}, u32[]{:S(2)}) collective-permute-start(f32[16,128]{1,0:T(8,128)S(1)} %pad_maximum_fusion.8), channel_id=1, source_target_pairs={{0,3},{1,0},{2,1},{3,2},{4,7},{5,4},{6,5},{7,6},{8,11},{9,8},{10,9... | collective-permute-start | bytes 24584 | tf_op jit(solution)/shard_map/ppermute | solution.py:564
  178.7 1.0 collective-permute-done.29
  179.7 0.4 collective-permute-done.30
  180.1 0.3 collective-permute-done.31
  180.4 3.9 %collective-permute-start.32 = (f32[52,128]{1,0:T(8,128)S(1)}, f32[52,128]{1,0:T(8,128)S(1)}, u32[]{:S(2)}, u32[]{:S(2)}) collective-permute-start(f32[52,128]{1,0:T(8,128)S(1)} %pad_maximum_fusion.4), channel_id=1, source_target_pairs={{0,4},{4,0},{8,12},{12,8},{16,20},{20,16},{24,28},{28,24},{32,36},... | collective-permute-start | bytes 79880 | tf_op jit(solution)/shard_map/ppermute | solution.py:564
  184.3 0.9 collective-permute-done.32
  185.2 1.5 shard_map.82
  186.8 1.3 collective-permute-start.33
  188.1 2.1 collective-permute-start.34
  190.2 0.4 collective-permute-start.35
  190.6 0.3 collective-permute-done.33
  190.9 1.8 collective-permute-done.34
  192.8 0.6 collective-permute-done.35
  193.5 3.2 %collective-permute-start.37 = (f32[72,128]{1,0:T(8,128)S(1)}, f32[72,128]{1,0:T(8,128)S(1)}, u32[]{:S(2)}, u32[]{:S(2)}) collective-permute-start(f32[72,128]{1,0:T(8,128)S(1)} %pad_maximum_fusion.1), channel_id=1, source_target_pairs={{0,64},{4,68},{8,72},{12,76},{16,80},{20,84},{24,88},{28,92},{32,9... | collective-permute-start | bytes 110600 | tf_op jit(solution)/shard_map/ppermute | solution.py:564
  196.8 0.7 collective-permute-done.36
  197.5 1.0 collective-permute-done.37
  198.5 1.4 collective-permute-done.38
  199.9 3.3 %collective-permute-start.39 = (f32[8,128]{1,0:T(8,128)S(1)}, f32[8,128]{1,0:T(8,128)S(1)}, u32[]{:S(2)}, u32[]{:S(2)}) collective-permute-start(f32[8,128]{1,0:T(8,128)S(1)} %bitcast_reduce_fusion.1), channel_id=1, source_target_pairs={{0,4},{4,0},{8,12},{12,8},{16,20},{20,16},{24,28},{28,24},{32,36},... | collective-permute-start | bytes 12296 | tf_op jit(solution)/shard_map/ppermute | solution.py:564
  203.1 0.6 bitcast_reduce_fusion
  204.0 1.7 collective-permute-start.40
  205.7 1.8 collective-permute-start.41
  207.5 0.7 collective-permute-start.42
  208.2 1.5 collective-permute-done.41
  209.7 0.6 collective-permute-done.42
  210.3 1.2 fusion.13
  (96 shorter events, 2.5 us)
Async XLA Ops:
  3.4 60.9 %collective-permute-start.14 = (bf16[128,2048]{1,0:T(8,128)(2,1)S(1)}, bf16[128,2048]{1,0:T(8,128)(2,1)S(1)}, u32[]{:S(2)}, u32[]{:S(2)}) collective-permute-start(bf16[128,2048]{1,0:T(8,128)(2,1)S(1)} %get-tuple-element.61), channel_id=1, source_target_pairs={{0,16},{4,68},{8,24},{12,76},{16,0},{20,84},{24,8},{28,92},{32,48}... | collective-permute-start | bytes 1572872 | tf_op jit(solution)/shard_map/ppermute | solution.py:612
  7.9 59.8 %collective-permute-start.15 = (bf16[128,2048]{1,0:T(8,128)(2,1)S(1)}, bf16[128,2048]{1,0:T(8,128)(2,1)S(1)}, u32[]{:S(2)}, u32[]{:S(2)}) collective-permute-start(bf16[128,2048]{1,0:T(8,128)(2,1)S(1)} %get-tuple-element.61), channel_id=1, source_target_pairs={{0,24},{4,100},{8,0},{12,108},{16,8},{20,116},{24,16},{28,124},{32... | collective-permute-start | bytes 1572872 | tf_op jit(solution)/shard_map/ppermute | solution.py:612
  48.5 6.0 %collective-permute-start.2 = (f32[40,128]{1,0:T(8,128)S(1)}, f32[40,128]{1,0:T(8,128)S(1)}, u32[]{:S(2)}, u32[]{:S(2)}) collective-permute-start(f32[40,128]{1,0:T(8,128)S(1)} %pad_maximum_fusion.7), channel_id=1, source_target_pairs={{0,4},{4,0},{8,12},{12,8},{16,20},{20,16},{24,28},{28,24},{32,36},... | collective-permute-start | bytes 61448 | tf_op jit(solution)/shard_map/ppermute | solution.py:564
  49.5 2.5 %collective-permute-start = (f32[8,128]{1,0:T(8,128)S(1)}, f32[8,128]{1,0:T(8,128)S(1)}, u32[]{:S(2)}, u32[]{:S(2)}) collective-permute-start(f32[8,128]{1,0:T(8,128)S(1)} %get-tuple-element.52), channel_id=1, source_target_pairs={{0,1},{1,0},{2,3},{3,2},{4,5},{5,4},{6,7},{7,6},{8,9},{9,8},{10,11... | collective-permute-start | bytes 12296 | tf_op jit(solution)/shard_map/ppermute | solution.py:577
  52.0 5.8 %collective-permute-start.1 = (f32[8,128]{1,0:T(8,128)S(1)}, f32[8,128]{1,0:T(8,128)S(1)}, u32[]{:S(2)}, u32[]{:S(2)}) collective-permute-start(f32[8,128]{1,0:T(8,128)S(1)} %pad_maximum_fusion.10), channel_id=1, source_target_pairs={{0,3},{1,2},{2,1},{3,0},{4,7},{5,6},{6,5},{7,4},{8,11},{9,10},{10,... | collective-permute-start | bytes 12296 | tf_op jit(solution)/shard_map/ppermute | solution.py:577
  54.6 4.3 %collective-permute-start.3 = (f32[56,128]{1,0:T(8,128)S(1)}, f32[56,128]{1,0:T(8,128)S(1)}, u32[]{:S(2)}, u32[]{:S(2)}) collective-permute-start(f32[56,128]{1,0:T(8,128)S(1)} %pad_maximum_fusion.2), channel_id=1, source_target_pairs={{0,8},{4,12},{8,16},{12,20},{16,24},{20,28},{24,0},{28,4},{32,40},... | collective-permute-start | bytes 86024 | tf_op jit(solution)/shard_map/ppermute | solution.py:564
  55.3 4.9 %collective-permute-start.4 = (f32[56,128]{1,0:T(8,128)S(1)}, f32[56,128]{1,0:T(8,128)S(1)}, u32[]{:S(2)}, u32[]{:S(2)}) collective-permute-start(f32[56,128]{1,0:T(8,128)S(1)} %pad_maximum_fusion.2), channel_id=1, source_target_pairs={{0,16},{4,20},{8,24},{12,28},{16,0},{20,4},{24,8},{28,12},{32,48},... | collective-permute-start | bytes 86024 | tf_op jit(solution)/shard_map/ppermute | solution.py:564
  57.8 4.9 %collective-permute-start.5 = (f32[56,128]{1,0:T(8,128)S(1)}, f32[56,128]{1,0:T(8,128)S(1)}, u32[]{:S(2)}, u32[]{:S(2)}) collective-permute-start(f32[56,128]{1,0:T(8,128)S(1)} %pad_maximum_fusion.2), channel_id=1, source_target_pairs={{0,24},{4,28},{8,0},{12,4},{16,8},{20,12},{24,16},{28,20},{32,56},... | collective-permute-start | bytes 86024 | tf_op jit(solution)/shard_map/ppermute | solution.py:564
  58.9 10.7 %collective-permute-start.13 = (bf16[128,2048]{1,0:T(8,128)(2,1)S(1)}, bf16[128,2048]{1,0:T(8,128)(2,1)S(1)}, u32[]{:S(2)}, u32[]{:S(2)}) collective-permute-start(bf16[128,2048]{1,0:T(8,128)(2,1)S(1)} %get-tuple-element.61), channel_id=1, source_target_pairs={{0,8},{4,36},{8,16},{12,44},{16,24},{20,52},{24,0},{28,60},{32,40}... | collective-permute-start | bytes 1572872 | tf_op jit(solution)/shard_map/ppermute | solution.py:612
  60.2 47.6 %collective-permute-start.12 = (bf16[512,2048]{1,0:T(8,128)(2,1)S(1)}, bf16[512,2048]{1,0:T(8,128)(2,1)S(1)}, u32[]{:S(2)}, u32[]{:S(2)}) collective-permute-start(bf16[512,2048]{1,0:T(8,128)(2,1)S(1)} %get-tuple-element.39.refs_0_), channel_id=1, source_target_pairs={{0,4},{4,0},{8,12},{12,8},{16,20},{20,16},{24,28},{28,24},{32,36},... | collective-permute-start | bytes 6291464 | tf_op jit(solution)/shard_map/ppermute | solution.py:613
  62.7 7.9 %collective-permute-start.6 = (f32[56,128]{1,0:T(8,128)S(1)}, f32[56,128]{1,0:T(8,128)S(1)}, u32[]{:S(2)}, u32[]{:S(2)}) collective-permute-start(f32[56,128]{1,0:T(8,128)S(1)} %pad_maximum_fusion.3), channel_id=1, source_target_pairs={{0,32},{4,36},{8,40},{12,44},{16,48},{20,52},{24,56},{28,60},{32,6... | collective-permute-start | bytes 86024 | tf_op jit(solution)/shard_map/ppermute | solution.py:564
  64.3 7.0 %collective-permute-start.7 = (f32[56,128]{1,0:T(8,128)S(1)}, f32[56,128]{1,0:T(8,128)S(1)}, u32[]{:S(2)}, u32[]{:S(2)}) collective-permute-start(f32[56,128]{1,0:T(8,128)S(1)} %pad_maximum_fusion.3), channel_id=1, source_target_pairs={{0,64},{4,68},{8,72},{12,76},{16,80},{20,84},{24,88},{28,92},{32,9... | collective-permute-start | bytes 86024 | tf_op jit(solution)/shard_map/ppermute | solution.py:564
  67.7 3.7 %collective-permute-start.8 = (f32[56,128]{1,0:T(8,128)S(1)}, f32[56,128]{1,0:T(8,128)S(1)}, u32[]{:S(2)}, u32[]{:S(2)}) collective-permute-start(f32[56,128]{1,0:T(8,128)S(1)} %pad_maximum_fusion.3), channel_id=1, source_target_pairs={{0,96},{4,100},{8,104},{12,108},{16,112},{20,116},{24,120},{28,124... | collective-permute-start | bytes 86024 | tf_op jit(solution)/shard_map/ppermute | solution.py:564
  69.5 36.8 %collective-permute-start.20 = (bf16[256,2048]{1,0:T(8,128)(2,1)S(1)}, bf16[256,2048]{1,0:T(8,128)(2,1)S(1)}, u32[]{:S(2)}, u32[]{:S(2)}) collective-permute-start(bf16[256,2048]{1,0:T(8,128)(2,1)S(1)} %constant_dynamic-update-slice_fusion.2.refs_3_), channel_id=1, source_target_pairs={{0,96},{4,28},{8,104},{12,4},{16,112},{20,12},{24,120},{28,20},{32... | collective-permute-start | bytes 3145736 | tf_op jit(solution)/shard_map/ppermute | solution.py:617
  70.6 35.8 %collective-permute-start.17 = (bf16[256,2048]{1,0:T(8,128)(2,1)S(1)}, bf16[256,2048]{1,0:T(8,128)(2,1)S(1)}, u32[]{:S(2)}, u32[]{:S(2)}) collective-permute-start(bf16[256,2048]{1,0:T(8,128)(2,1)S(1)} %constant_dynamic-update-slice_fusion.refs_2_), channel_id=1, source_target_pairs={{0,32},{4,12},{8,40},{12,20},{16,48},{20,28},{24,56},{28,4},{32,64... | collective-permute-start | bytes 3145736 | tf_op jit(solution)/shard_map/ppermute | solution.py:616
  97.9 5.8 %collective-permute-start.11 = (f32[32,128]{1,0:T(8,128)S(1)}, f32[32,128]{1,0:T(8,128)S(1)}, u32[]{:S(2)}, u32[]{:S(2)}) collective-permute-start(f32[32,128]{1,0:T(8,128)S(1)} %get-tuple-element.60), channel_id=1, source_target_pairs={{0,4},{4,0},{8,12},{12,8},{16,20},{20,16},{24,28},{28,24},{32,36},... | collective-permute-start | bytes 49160 | tf_op jit(solution)/shard_map/ppermute | solution.py:564
  102.5 1.2 collective-permute-start.16
  103.7 15.2 %collective-permute-start.18 = (bf16[256,2048]{1,0:T(8,128)(2,1)S(1)}, bf16[256,2048]{1,0:T(8,128)(2,1)S(1)}, u32[]{:S(2)}, u32[]{:S(2)}) collective-permute-start(bf16[256,2048]{1,0:T(8,128)(2,1)S(1)} %constant_dynamic-update-slice_fusion.2.refs_3_), channel_id=1, source_target_pairs={{0,32},{4,12},{8,40},{12,20},{16,48},{20,28},{24,56},{28,4},{32,64... | collective-permute-start | bytes 3145736 | tf_op jit(solution)/shard_map/ppermute | solution.py:618
  103.7 15.2 %collective-permute-start.19 = (bf16[256,2048]{1,0:T(8,128)(2,1)S(1)}, bf16[256,2048]{1,0:T(8,128)(2,1)S(1)}, u32[]{:S(2)}, u32[]{:S(2)}) collective-permute-start(bf16[256,2048]{1,0:T(8,128)(2,1)S(1)} %constant_dynamic-update-slice_fusion.refs_2_), channel_id=1, source_target_pairs={{0,96},{4,28},{8,104},{12,4},{16,112},{20,12},{24,120},{28,20},{32... | collective-permute-start | bytes 3145736 | tf_op jit(solution)/shard_map/ppermute | solution.py:619
  106.4 23.0 %collective-permute-start.22 = (bf16[256,2048]{1,0:T(8,128)(2,1)S(1)}, bf16[256,2048]{1,0:T(8,128)(2,1)S(1)}, u32[]{:S(2)}, u32[]{:S(2)}) collective-permute-start(bf16[256,2048]{1,0:T(8,128)(2,1)S(1)} %collective-permute-done.20.refs_5_), channel_id=1, source_target_pairs={{0,96},{4,28},{8,104},{12,4},{16,112},{20,12},{24,120},{28,20},{32... | collective-permute-start | bytes 3145736 | tf_op jit(solution)/shard_map/ppermute | solution.py:621
  106.4 23.6 %collective-permute-start.21 = (bf16[256,2048]{1,0:T(8,128)(2,1)S(1)}, bf16[256,2048]{1,0:T(8,128)(2,1)S(1)}, u32[]{:S(2)}, u32[]{:S(2)}) collective-permute-start(bf16[256,2048]{1,0:T(8,128)(2,1)S(1)} %collective-permute-done.17.refs_2_), channel_id=1, source_target_pairs={{0,32},{4,12},{8,40},{12,20},{16,48},{20,28},{24,56},{28,4},{32,64... | collective-permute-start | bytes 3145736 | tf_op jit(solution)/shard_map/ppermute | solution.py:620
  107.9 29.6 %collective-permute-start.9 = (f32[4,128]{1,0:T(4,128)S(1)}, f32[4,128]{1,0:T(4,128)S(1)}, u32[]{:S(2)}, u32[]{:S(2)}) collective-permute-start(f32[4,128]{1,0:T(4,128)S(1)} %get-tuple-element.59), channel_id=1, source_target_pairs={{0,1},{1,0},{2,3},{3,2},{4,5},{5,4},{6,7},{7,6},{8,9},{9,8},{10,11... | collective-permute-start | bytes 6152 | tf_op jit(solution)/shard_map/ppermute | solution.py:577
  133.9 4.0 %collective-permute-start.23 = (f32[48,128]{1,0:T(8,128)S(1)}, f32[48,128]{1,0:T(8,128)S(1)}, u32[]{:S(2)}, u32[]{:S(2)}) collective-permute-start(f32[48,128]{1,0:T(8,128)S(1)} %pad_maximum_fusion.5), channel_id=1, source_target_pairs={{0,8},{4,12},{8,16},{12,20},{16,24},{20,28},{24,0},{28,4},{32,40},... | collective-permute-start | bytes 73736 | tf_op jit(solution)/shard_map/ppermute | solution.py:564
  133.9 5.0 %collective-permute-start.24 = (f32[48,128]{1,0:T(8,128)S(1)}, f32[48,128]{1,0:T(8,128)S(1)}, u32[]{:S(2)}, u32[]{:S(2)}) collective-permute-start(f32[48,128]{1,0:T(8,128)S(1)} %pad_maximum_fusion.5), channel_id=1, source_target_pairs={{0,16},{4,20},{8,24},{12,28},{16,0},{20,4},{24,8},{28,12},{32,48},... | collective-permute-start | bytes 73736 | tf_op jit(solution)/shard_map/ppermute | solution.py:564
  137.5 3.2 %collective-permute-start.25 = (f32[48,128]{1,0:T(8,128)S(1)}, f32[48,128]{1,0:T(8,128)S(1)}, u32[]{:S(2)}, u32[]{:S(2)}) collective-permute-start(f32[48,128]{1,0:T(8,128)S(1)} %pad_maximum_fusion.5), channel_id=1, source_target_pairs={{0,24},{4,28},{8,0},{12,4},{16,8},{20,12},{24,16},{28,20},{32,56},... | collective-permute-start | bytes 73736 | tf_op jit(solution)/shard_map/ppermute | solution.py:564
  137.5 7.1 %collective-permute-start.10 = (f32[4,128]{1,0:T(4,128)S(1)}, f32[4,128]{1,0:T(4,128)S(1)}, u32[]{:S(2)}, u32[]{:S(2)}) collective-permute-start(f32[4,128]{1,0:T(4,128)S(1)} %multiply_add_fusion.6), channel_id=1, source_target_pairs={{0,3},{1,2},{2,1},{3,0},{4,7},{5,6},{6,5},{7,4},{8,11},{9,10},{10,... | collective-permute-start | bytes 6152 | tf_op jit(solution)/shard_map/ppermute | solution.py:577
  140.8 4.0 %collective-permute-start.26 = (f32[48,128]{1,0:T(8,128)S(1)}, f32[48,128]{1,0:T(8,128)S(1)}, u32[]{:S(2)}, u32[]{:S(2)}) collective-permute-start(f32[48,128]{1,0:T(8,128)S(1)} %pad_maximum_fusion.6), channel_id=1, source_target_pairs={{0,32},{4,36},{8,40},{12,44},{16,48},{20,52},{24,56},{28,60},{32,6... | collective-permute-start | bytes 73736 | tf_op jit(solution)/shard_map/ppermute | solution.py:564
  140.9 5.2 %collective-permute-start.27 = (f32[48,128]{1,0:T(8,128)S(1)}, f32[48,128]{1,0:T(8,128)S(1)}, u32[]{:S(2)}, u32[]{:S(2)}) collective-permute-start(f32[48,128]{1,0:T(8,128)S(1)} %pad_maximum_fusion.6), channel_id=1, source_target_pairs={{0,64},{4,68},{8,72},{12,76},{16,80},{20,84},{24,88},{28,92},{32,9... | collective-permute-start | bytes 73736 | tf_op jit(solution)/shard_map/ppermute | solution.py:564
  144.6 3.0 %collective-permute-start.28 = (f32[48,128]{1,0:T(8,128)S(1)}, f32[48,128]{1,0:T(8,128)S(1)}, u32[]{:S(2)}, u32[]{:S(2)}) collective-permute-start(f32[48,128]{1,0:T(8,128)S(1)} %pad_maximum_fusion.6), channel_id=1, source_target_pairs={{0,96},{4,100},{8,104},{12,108},{16,112},{20,116},{24,120},{28,124... | collective-permute-start | bytes 73736 | tf_op jit(solution)/shard_map/ppermute | solution.py:564
  175.9 3.8 %collective-permute-start.29 = (f32[16,128]{1,0:T(8,128)S(1)}, f32[16,128]{1,0:T(8,128)S(1)}, u32[]{:S(2)}, u32[]{:S(2)}) collective-permute-start(f32[16,128]{1,0:T(8,128)S(1)} %pad_maximum_fusion.8), channel_id=1, source_target_pairs={{0,1},{1,2},{2,3},{3,0},{4,5},{5,6},{6,7},{7,4},{8,9},{9,10},{10,1... | collective-permute-start | bytes 24584 | tf_op jit(solution)/shard_map/ppermute | solution.py:564
  176.0 4.1 %collective-permute-start.30 = (f32[16,128]{1,0:T(8,128)S(1)}, f32[16,128]{1,0:T(8,128)S(1)}, u32[]{:S(2)}, u32[]{:S(2)}) collective-permute-start(f32[16,128]{1,0:T(8,128)S(1)} %pad_maximum_fusion.8), channel_id=1, source_target_pairs={{0,2},{1,3},{2,0},{3,1},{4,6},{5,7},{6,4},{7,5},{8,10},{9,11},{10,... | collective-permute-start | bytes 24584 | tf_op jit(solution)/shard_map/ppermute | solution.py:564
  176.1 4.3 %collective-permute-start.31 = (f32[16,128]{1,0:T(8,128)S(1)}, f32[16,128]{1,0:T(8,128)S(1)}, u32[]{:S(2)}, u32[]{:S(2)}) collective-permute-start(f32[16,128]{1,0:T(8,128)S(1)} %pad_maximum_fusion.8), channel_id=1, source_target_pairs={{0,3},{1,0},{2,1},{3,2},{4,7},{5,4},{6,5},{7,6},{8,11},{9,8},{10,9... | collective-permute-start | bytes 24584 | tf_op jit(solution)/shard_map/ppermute | solution.py:564
  180.4 4.8 %collective-permute-start.32 = (f32[52,128]{1,0:T(8,128)S(1)}, f32[52,128]{1,0:T(8,128)S(1)}, u32[]{:S(2)}, u32[]{:S(2)}) collective-permute-start(f32[52,128]{1,0:T(8,128)S(1)} %pad_maximum_fusion.4), channel_id=1, source_target_pairs={{0,4},{4,0},{8,12},{12,8},{16,20},{20,16},{24,28},{28,24},{32,36},... | collective-permute-start | bytes 79880 | tf_op jit(solution)/shard_map/ppermute | solution.py:564
  185.2 18.0 %copy-start = (f32[4096]{0:T(1024)S(1)}, f32[4096]{0:T(1024)}, u32[]{:S(2)}) copy-start(f32[4096]{0:T(1024)} %param.9) | copy-start | bytes 49156
  186.8 4.1 %collective-permute-start.33 = (f32[72,128]{1,0:T(8,128)S(1)}, f32[72,128]{1,0:T(8,128)S(1)}, u32[]{:S(2)}, u32[]{:S(2)}) collective-permute-start(f32[72,128]{1,0:T(8,128)S(1)} %pad_maximum_fusion), channel_id=1, source_target_pairs={{0,8},{4,12},{8,16},{12,20},{16,24},{20,28},{24,0},{28,4},{32,40},... | collective-permute-start | bytes 110600 | tf_op jit(solution)/shard_map/ppermute | solution.py:564
  188.1 4.6 %collective-permute-start.34 = (f32[72,128]{1,0:T(8,128)S(1)}, f32[72,128]{1,0:T(8,128)S(1)}, u32[]{:S(2)}, u32[]{:S(2)}) collective-permute-start(f32[72,128]{1,0:T(8,128)S(1)} %pad_maximum_fusion), channel_id=1, source_target_pairs={{0,16},{4,20},{8,24},{12,28},{16,0},{20,4},{24,8},{28,12},{32,48},... | collective-permute-start | bytes 110600 | tf_op jit(solution)/shard_map/ppermute | solution.py:564
  190.2 3.1 %collective-permute-start.35 = (f32[72,128]{1,0:T(8,128)S(1)}, f32[72,128]{1,0:T(8,128)S(1)}, u32[]{:S(2)}, u32[]{:S(2)}) collective-permute-start(f32[72,128]{1,0:T(8,128)S(1)} %pad_maximum_fusion), channel_id=1, source_target_pairs={{0,24},{4,28},{8,0},{12,4},{16,8},{20,12},{24,16},{28,20},{32,56},... | collective-permute-start | bytes 110600 | tf_op jit(solution)/shard_map/ppermute | solution.py:564
  193.4 4.1 %collective-permute-start.36 = (f32[72,128]{1,0:T(8,128)S(1)}, f32[72,128]{1,0:T(8,128)S(1)}, u32[]{:S(2)}, u32[]{:S(2)}) collective-permute-start(f32[72,128]{1,0:T(8,128)S(1)} %pad_maximum_fusion.1), channel_id=1, source_target_pairs={{0,32},{4,36},{8,40},{12,44},{16,48},{20,52},{24,56},{28,60},{32,6... | collective-permute-start | bytes 110600 | tf_op jit(solution)/shard_map/ppermute | solution.py:564
  193.5 5.0 %collective-permute-start.37 = (f32[72,128]{1,0:T(8,128)S(1)}, f32[72,128]{1,0:T(8,128)S(1)}, u32[]{:S(2)}, u32[]{:S(2)}) collective-permute-start(f32[72,128]{1,0:T(8,128)S(1)} %pad_maximum_fusion.1), channel_id=1, source_target_pairs={{0,64},{4,68},{8,72},{12,76},{16,80},{20,84},{24,88},{28,92},{32,9... | collective-permute-start | bytes 110600 | tf_op jit(solution)/shard_map/ppermute | solution.py:564
  196.7 3.1 %collective-permute-start.38 = (f32[72,128]{1,0:T(8,128)S(1)}, f32[72,128]{1,0:T(8,128)S(1)}, u32[]{:S(2)}, u32[]{:S(2)}) collective-permute-start(f32[72,128]{1,0:T(8,128)S(1)} %pad_maximum_fusion.1), channel_id=1, source_target_pairs={{0,96},{4,100},{8,104},{12,108},{16,112},{20,116},{24,120},{28,124... | collective-permute-start | bytes 110600 | tf_op jit(solution)/shard_map/ppermute | solution.py:564
  199.9 4.1 %collective-permute-start.39 = (f32[8,128]{1,0:T(8,128)S(1)}, f32[8,128]{1,0:T(8,128)S(1)}, u32[]{:S(2)}, u32[]{:S(2)}) collective-permute-start(f32[8,128]{1,0:T(8,128)S(1)} %bitcast_reduce_fusion.1), channel_id=1, source_target_pairs={{0,4},{4,0},{8,12},{12,8},{16,20},{20,16},{24,28},{28,24},{32,36},... | collective-permute-start | bytes 12296 | tf_op jit(solution)/shard_map/ppermute | solution.py:564
  204.0 4.2 %collective-permute-start.40 = (f32[12,128]{1,0:T(8,128)S(1)}, f32[12,128]{1,0:T(8,128)S(1)}, u32[]{:S(2)}, u32[]{:S(2)}) collective-permute-start(f32[12,128]{1,0:T(8,128)S(1)} %pad_maximum_fusion.9), channel_id=1, source_target_pairs={{0,1},{1,2},{2,3},{3,0},{4,5},{5,6},{6,7},{7,4},{8,9},{9,10},{10,1... | collective-permute-start | bytes 18440 | tf_op jit(solution)/shard_map/ppermute | solution.py:564
  205.7 4.0 %collective-permute-start.41 = (f32[12,128]{1,0:T(8,128)S(1)}, f32[12,128]{1,0:T(8,128)S(1)}, u32[]{:S(2)}, u32[]{:S(2)}) collective-permute-start(f32[12,128]{1,0:T(8,128)S(1)} %pad_maximum_fusion.9), channel_id=1, source_target_pairs={{0,2},{1,3},{2,0},{3,1},{4,6},{5,7},{6,4},{7,5},{8,10},{9,11},{10,... | collective-permute-start | bytes 18440 | tf_op jit(solution)/shard_map/ppermute | solution.py:564
  207.5 2.8 %collective-permute-start.42 = (f32[12,128]{1,0:T(8,128)S(1)}, f32[12,128]{1,0:T(8,128)S(1)}, u32[]{:S(2)}, u32[]{:S(2)}) collective-permute-start(f32[12,128]{1,0:T(8,128)S(1)} %pad_maximum_fusion.9), channel_id=1, source_target_pairs={{0,3},{1,0},{2,1},{3,2},{4,7},{5,4},{6,5},{7,6},{8,11},{9,8},{10,9... | collective-permute-start | bytes 18440 | tf_op jit(solution)/shard_map/ppermute | solution.py:564

commit v8 on v7

--- a/solution.py
+++ b/solution.py
@@ -555,7 +555,7 @@
     z_stage = [gen_perm(lambda z, y, c: (z + k, y, c)) for k in (1, 2, 3)]
     ref_stage = [[(i, (i + k) % n_ref) for i in range(n_ref)] for k in (1, 2, 3)]
     first_axis = {k: gen_perm(lambda z, y, c: (z, y + k, c) if c == 0 else (z + k, y, c)) for k in (1, 2, 3)}
-    second_axis = {k: gen_perm(lambda z, y, c: (z + k, y, c) if c == 0 else (z, y + k, c)) for k in (1, 3)}
+    second_axis = {k: gen_perm(lambda z, y, c: (z + k, y, c) if c == 0 else (z, y + k, c)) for k in (1, 2, 3)}
     order = [(0, 0), (0, 1), (0, 2), (0, 3)]
     order += [(1, 0), (1, 1), (1, 2), (1, 3), (3, 0), (3, 1), (3, 2), (3, 3)]
     order += [(2, 0), (2, 1), (2, 2), (2, 3)]
@@ -634,8 +634,8 @@
         col_part = jnp.concatenate([lcol, gmass], axis=0)
         col_part = stage(col_part, "gen", core_stage, nc)
         col_part = jnp.concatenate([col_part, to_cols(wg)], axis=0)
-        col_part = stage(col_part, "gen", y_stage, nc)
-        col_part = stage(col_part, "gen", z_stage, nc)
+        col_part = stage(col_part, "gen", list(first_axis.values()), nc)
+        col_part = stage(col_part, "gen", list(second_axis.values()), nc)
         gmass = col_part[nc : nc + 1]
         rmass = row_part[nq : nq + 1]
         wcols = col_part[nc + 8 :] / gmass

time: 212 us -> 213 us (level)
  transfers between devices with their start and end apart: 43 -> 43, of which waited for: 25 -> 26; matrix products, arithmetic and copies ran while one was open for 1% -> 1% of each run, Pallas kernels for 38% -> 38%
where the time goes in v8:
time: 213 us
  Pallas kernels  113 us (53%)
  starting transfers between devices  62.8 us (29%)
  waiting for transfers between devices  33.3 us (16%)
  other arithmetic  2.56 us (1%)
    pallas_call x2, Pallas kernels, next_pass(): pl.pallas_call(functools.partial(next_kernel, len(parts)), in_specs=[vmem...  53.2 us
    ppermute x28, starting transfers between devices, shift(): return [lax.ppermute(value, axis, perm) for perm in perms]  45.8 us
    pallas_call x2, Pallas kernels, first_pass(): pl.pallas_call(functools.partial(first_kernel, first_tile, steps), in_spe...  40.2 us
    ppermute x28, waiting for transfers between devices, shift(): return [lax.ppermute(value, axis, perm) for perm in perms]  16.7 us
    pallas_call x3, Pallas kernels, self_first(): pl.pallas_call(functools.partial(self_first_kernel, len(sources), first),...  14 us
    ppermute x1, waiting for transfers between devices, run(): high_up = lax.ppermute(high, 'gen', second_axis[1])  7.1 us
    ppermute x3, starting transfers between devices, run(): got[k] = lax.ppermute(own, 'gen', first_axis[k])  5.67 us
  transfers between devices with their start and end apart: 43, of which 26 were waited for; matrix products, arithmetic and copies ran while one was open for 1% of the time, Pallas kernels for 38%

profile of v8, /device:TPU:1, one launch (start us, length us, event | category | flops | bytes accessed | tf_op | source)
XLA Modules:
  0.0 212.9 jit_solution(7871224991679207410)
XLA Ops:
  0.9 2.5 %entry.1 = (bf16[128,2048]{1,0:T(8,128)(2,1)S(1)}, bf16[512,2048]{1,0:T(8,128)(2,1)S(1)}, bf16[512,2048]{1,0:T(8,128)(2,1)S(1)}, f32[4,128]{1,0:T(4,128)S(1)}, f32[32,128]{1,0:T(8,128)S(1)}) custom-call(bf16[512,2048]{1,0:T(8,128)(2,1)} %gen_hbm.1, bf16[4096,2048]{1,0:T(8,128)(2,1)} %refs_4_.3, f32[4,128]{1,0:T(4,128)} %bitcast.22, f32[32,128]{1,0:T(8,128)} %bitcast.21), custom_call_target="tpu_custom_call" | custom-call | tf_op jit(solution)/shard_map/entry/pallas_call | solution.py:208
  3.4 4.5 %collective-permute-start.14 = (bf16[128,2048]{1,0:T(8,128)(2,1)S(1)}, bf16[128,2048]{1,0:T(8,128)(2,1)S(1)}, u32[]{:S(2)}, u32[]{:S(2)}) collective-permute-start(bf16[128,2048]{1,0:T(8,128)(2,1)S(1)} %get-tuple-element.61), channel_id=1, source_target_pairs={{0,16},{4,68},{8,24},{12,76},{16,0},{20,84},{24,8},{28,92},{32,48}... | collective-permute-start | bytes 1572872 | tf_op jit(solution)/shard_map/ppermute | solution.py:612
  7.9 0.4 collective-permute-start.15
  8.3 10.9 %cross_first_0.1 = (f32[512,3072]{1,0:T(8,128)S(1)}, f32[24,128]{1,0:T(8,128)S(1)}, f32[8,128]{1,0:T(8,128)S(1)}, f32[8,128]{1,0:T(8,128)S(1)}, bf16[512,2048]{1...) custom-call(bf16[512,2048]{1,0:T(8,128)(2,1)S(1)} %get-tuple-element, ...), custom_call_target="tpu_custom_call" | custom-call | tf_op jit(solution)/shard_map/cross_first_0/pallas_call | solution.py:344
  19.2 29.3 %cross_first_1.1 = (f32[512,1024]{1,0:T(8,128)S(1)}, f32[8,128]{1,0:T(8,128)S(1)}, f32[32,128]{1,0:T(8,128)S(1)}, f32[32,128]{1,0:T(8,128)S(1)}) custom-call(bf16[512,2048]{1,0:T(8,128)(2,1)S(1)} %get-tuple-element.39.refs_0_, bf16[512,2048]{1,0:T(8,128)(2,1)S(1)} %get-tuple-element.44.refs_1_, f32[32,128]{1,0:T(8,128)S(1)} %get-tuple-element.42.refs_3_.refs_2_, ...), custom_call_target="tpu_custom_call" | custom-call | tf_op jit(solution)/shard_map/cross_first_1/pallas_call | solution.py:344
  48.5 1.0 collective-permute-start.2
  49.5 1.2 collective-permute-start
  50.8 1.2 collective-permute-done
  52.0 2.6 %collective-permute-start.1 = (f32[8,128]{1,0:T(8,128)S(1)}, f32[8,128]{1,0:T(8,128)S(1)}, u32[]{:S(2)}, u32[]{:S(2)}) collective-permute-start(f32[8,128]{1,0:T(8,128)S(1)} %pad_maximum_fusion.10), channel_id=1, source_target_pairs={{0,3},{1,2},{2,1},{3,0},{4,7},{5,6},{6,5},{7,4},{8,11},{9,10},{10,... | collective-permute-start | bytes 12296 | tf_op jit(solution)/shard_map/ppermute | solution.py:577
  54.6 1.7 collective-permute-start.3
  56.3 3.3 %collective-permute-start.4 = (f32[56,128]{1,0:T(8,128)S(1)}, f32[56,128]{1,0:T(8,128)S(1)}, u32[]{:S(2)}, u32[]{:S(2)}) collective-permute-start(f32[56,128]{1,0:T(8,128)S(1)} %pad_maximum_fusion.2), channel_id=1, source_target_pairs={{0,16},{4,68},{8,24},{12,76},{16,0},{20,84},{24,8},{28,92},{32,48}... | collective-permute-start | bytes 86024 | tf_op jit(solution)/shard_map/ppermute | solution.py:564
  59.6 0.7 collective-permute-start.5
  60.3 0.7 collective-permute-start.13
  61.2 1.5 collective-permute-start.12
  62.7 1.5 collective-permute-start.6
  64.2 1.6 collective-permute-start.7
  65.9 1.7 collective-permute-start.8
  67.6 2.5 %collective-permute-done.13 = bf16[128,2048]{1,0:T(8,128)(2,1)S(1)} collective-permute-done((bf16[128,2048]{1,0:T(8,128)(2,1)S(1)}, bf16[128,2048]{1,0:T(8,128)(2,1)S(1)}, u32[]{:S(2)}, u32[]{:S(2)}) %collective-permute-start.13) | collective-permute-done | bytes 524320 | tf_op jit(solution)/shard_map/ppermute | solution.py:612
  70.2 1.5 collective-permute-start.17
  71.9 26.5 %shard_map.76 = (f32[4,128]{1,0:T(4,128)S(1)}, f32[32,128]{1,0:T(8,128)S(1)}) custom-call(f32[512,3072]{1,0:T(8,128)S(1)} %get-tuple-element.45.refs_5_.refs_0_, f32[512,1024]{1,0:T(8,128)S(1)} %get-tuple-element.53.refs_1_, f32[32,128]{1,0:T(8,128)S(1)} %get-tuple-element.85.refs_2_, f32[4,128]{1,0:T(4,128)S(1)} %get-tuple-element.83.refs_3_), custom_call_target="tpu_custom_call" | custom-call | tf_op jit(solution)/shard_map/pallas_call | solution.py:381
  98.3 5.5 %collective-permute-start.11 = (f32[32,128]{1,0:T(8,128)S(1)}, f32[32,128]{1,0:T(8,128)S(1)}, u32[]{:S(2)}, u32[]{:S(2)}) collective-permute-start(f32[32,128]{1,0:T(8,128)S(1)} %get-tuple-element.60), channel_id=1, source_target_pairs={{0,4},{4,0},{8,12},{12,8},{16,20},{20,16},{24,28},{28,24},{32,36},... | collective-permute-start | bytes 49160 | tf_op jit(solution)/shard_map/ppermute | solution.py:564
  104.0 1.1 collective-permute-done.16.refs_5_
  105.0 2.7 %collective-permute-start.19 = (bf16[256,2048]{1,0:T(8,128)(2,1)S(1)}, bf16[256,2048]{1,0:T(8,128)(2,1)S(1)}, u32[]{:S(2)}, u32[]{:S(2)}) collective-permute-start(bf16[256,2048]{1,0:T(8,128)(2,1)S(1)} %constant_dynamic-update-slice_fusion.refs_2_), channel_id=1, source_target_pairs={{0,96},{4,28},{8,104},{12,4},{16,112},{20,12},{24,120},{28,20},{32... | collective-permute-start | bytes 3145736 | tf_op jit(solution)/shard_map/ppermute | solution.py:619
  107.8 1.4 collective-permute-start.21
  109.3 3.8 %shard_map.77 = (f32[1024,512]{1,0:T(8,128)S(1)}, f32[16,128]{1,0:T(8,128)S(1)}, f32[1024,128]{1,0:T(8,128)S(1)}, f32[1024,128]{1,0:T(8,128)S(1)}) custom-call(bf16[512,2048]{1,0:T(8,128)(2,1)S(1)} %get-tuple-element.39.refs_0_, bf16[512,2048]{1,0:T(8,128)(2,1)S(1)} %collective-permute-done.12.refs_1_, ...), custom_call_target="tpu_custom_call" | custom-call | tf_op jit(solution)/shard_map/pallas_call | solution.py:462
  113.1 7.1 %collective-permute-done.18.refs_3_ = bf16[256,2048]{1,0:T(8,128)(2,1)S(1)} collective-permute-done((bf16[256,2048]{1,0:T(8,128)(2,1)S(1)}, bf16[256,2048]{1,0:T(8,128)(2,1)S(1)}, u32[]{:S(2)}, u32[]{:S(2)}) %collective-permute-start.18) | collective-permute-done | bytes 1048608 | tf_op jit(solution)/shard_map/ppermute | solution.py:618
  120.2 6.5 %shard_map.78 = (f32[1024,1024]{1,0:T(8,128)S(1)}, f32[16,128]{1,0:T(8,128)S(1)}) custom-call(bf16[512,2048]{1,0:T(8,128)(2,1)S(1)} %get-tuple-element.39.refs_0_, bf16[512,2048]{1,0:T(8,128)(2,1)S(1)} %collective-permute-done.12.refs_1_, bf16[256,2048]{1,0:T(8,128)(2,1)S(1)} %collective-permute-done.17.refs_2_, ...), custom_call_target="tpu_custom_call" | custom-call | tf_op jit(solution)/shard_map/pallas_call | solution.py:462
  126.7 4.0 %collective-permute-done.22.refs_3_ = bf16[256,2048]{1,0:T(8,128)(2,1)S(1)} collective-permute-done((bf16[256,2048]{1,0:T(8,128)(2,1)S(1)}, bf16[256,2048]{1,0:T(8,128)(2,1)S(1)}, u32[]{:S(2)}, u32[]{:S(2)}) %collective-permute-start.22) | collective-permute-done | bytes 1048608 | tf_op jit(solution)/shard_map/ppermute | solution.py:621
  130.7 0.7 collective-permute-done.21.refs_2_
  131.4 3.8 %shard_map.79 = (f32[1024,512]{1,0:T(8,128)S(1)}, f32[16,128]{1,0:T(8,128)S(1)}) custom-call(bf16[512,2048]{1,0:T(8,128)(2,1)S(1)} %get-tuple-element.39.refs_0_, bf16[512,2048]{1,0:T(8,128)(2,1)S(1)} %collective-permute-done.12.refs_1_, bf16[256,2048]{1,0:T(8,128)(2,1)S(1)} %collective-permute-done.21.refs_2_, ...), custom_call_target="tpu_custom_call" | custom-call | tf_op jit(solution)/shard_map/pallas_call | solution.py:462
  135.3 3.6 %collective-permute-start.24 = (f32[48,128]{1,0:T(8,128)S(1)}, f32[48,128]{1,0:T(8,128)S(1)}, u32[]{:S(2)}, u32[]{:S(2)}) collective-permute-start(f32[48,128]{1,0:T(8,128)S(1)} %pad_maximum_fusion.5), channel_id=1, source_target_pairs={{0,16},{4,20},{8,24},{12,28},{16,0},{20,4},{24,8},{28,12},{32,48},... | collective-permute-start | bytes 73736 | tf_op jit(solution)/shard_map/ppermute | solution.py:564
  138.9 0.2 collective-permute-start.10
  139.2 1.2 collective-permute-done.24
  140.3 1.8 collective-permute-done.25
  142.2 3.8 %collective-permute-start.27 = (f32[48,128]{1,0:T(8,128)S(1)}, f32[48,128]{1,0:T(8,128)S(1)}, u32[]{:S(2)}, u32[]{:S(2)}) collective-permute-start(f32[48,128]{1,0:T(8,128)S(1)} %pad_maximum_fusion.6), channel_id=1, source_target_pairs={{0,64},{4,68},{8,72},{12,76},{16,80},{20,84},{24,88},{28,92},{32,9... | collective-permute-start | bytes 73736 | tf_op jit(solution)/shard_map/ppermute | solution.py:564
  146.1 1.4 collective-permute-done.27
  147.5 1.5 collective-permute-done.28
  149.1 26.7 %shard_map.80 = (f32[4,128]{1,0:T(4,128)S(1)}, f32[32,128]{1,0:T(8,128)S(1)}) custom-call(f32[512,3072]{1,0:T(8,128)S(1)} %get-tuple-element.45.refs_5_.refs_0_, f32[512,1024]{1,0:T(8,128)S(1)} %get-tuple-element.53.refs_1_, f32[32,128]{1,0:T(8,128)S(1)} %get-tuple-element.81.refs_2_, f32[4,128]{1,0:T(4,128)S(1)} %get-tuple-element.79.refs_3_), custom_call_target="tpu_custom_call" | custom-call | tf_op jit(solution)/shard_map/pallas_call | solution.py:381
  175.8 1.5 shard_map.81
  177.5 2.6 %collective-permute-start.31 = (f32[16,128]{1,0:T(8,128)S(1)}, f32[16,128]{1,0:T(8,128)S(1)}, u32[]{:S(2)}, u32[]{:S(2)}) collective-permute-start(f32[16,128]{1,0:T(8,128)S(1)} %pad_maximum_fusion.8), channel_id=1, source_target_pairs={{0,3},{1,0},{2,1},{3,2},{4,7},{5,4},{6,5},{7,6},{8,11},{9,8},{10,9... | collective-permute-start | bytes 24584 | tf_op jit(solution)/shard_map/ppermute | solution.py:564
  180.0 1.0 collective-permute-done.29
  181.1 0.4 collective-permute-done.30
  181.5 0.3 collective-permute-done.31
  181.8 3.9 %collective-permute-start.32 = (f32[52,128]{1,0:T(8,128)S(1)}, f32[52,128]{1,0:T(8,128)S(1)}, u32[]{:S(2)}, u32[]{:S(2)}) collective-permute-start(f32[52,128]{1,0:T(8,128)S(1)} %pad_maximum_fusion.4), channel_id=1, source_target_pairs={{0,4},{4,0},{8,12},{12,8},{16,20},{20,16},{24,28},{28,24},{32,36},... | collective-permute-start | bytes 79880 | tf_op jit(solution)/shard_map/ppermute | solution.py:564
  185.7 0.9 collective-permute-done.32
  186.6 1.5 shard_map.82
  188.2 1.3 collective-permute-start.33
  189.5 2.1 collective-permute-start.34
  191.6 0.4 collective-permute-start.35
  192.0 0.3 collective-permute-done.33
  192.3 1.8 collective-permute-done.34
  194.1 0.6 collective-permute-done.35
  194.8 3.2 %collective-permute-start.37 = (f32[72,128]{1,0:T(8,128)S(1)}, f32[72,128]{1,0:T(8,128)S(1)}, u32[]{:S(2)}, u32[]{:S(2)}) collective-permute-start(f32[72,128]{1,0:T(8,128)S(1)} %pad_maximum_fusion.1), channel_id=1, source_target_pairs={{0,64},{4,68},{8,72},{12,76},{16,80},{20,84},{24,88},{28,92},{32,9... | collective-permute-start | bytes 110600 | tf_op jit(solution)/shard_map/ppermute | solution.py:564
  198.1 0.7 collective-permute-done.36
  198.9 1.0 collective-permute-done.37
  199.8 1.4 collective-permute-done.38
  201.3 3.3 %collective-permute-start.39 = (f32[8,128]{1,0:T(8,128)S(1)}, f32[8,128]{1,0:T(8,128)S(1)}, u32[]{:S(2)}, u32[]{:S(2)}) collective-permute-start(f32[8,128]{1,0:T(8,128)S(1)} %bitcast_reduce_fusion.1), channel_id=1, source_target_pairs={{0,4},{4,0},{8,12},{12,8},{16,20},{20,16},{24,28},{28,24},{32,36},... | collective-permute-start | bytes 12296 | tf_op jit(solution)/shard_map/ppermute | solution.py:564
  204.5 0.6 bitcast_reduce_fusion
  205.4 1.7 collective-permute-start.40
  207.1 1.8 collective-permute-start.41
  208.9 0.7 collective-permute-start.42
  209.6 1.5 collective-permute-done.41
  211.1 0.6 collective-permute-done.42
  211.7 1.2 fusion.13
  (96 shorter events, 2.2 us)
Async XLA Ops:
  3.4 60.8 %collective-permute-start.14 = (bf16[128,2048]{1,0:T(8,128)(2,1)S(1)}, bf16[128,2048]{1,0:T(8,128)(2,1)S(1)}, u32[]{:S(2)}, u32[]{:S(2)}) collective-permute-start(bf16[128,2048]{1,0:T(8,128)(2,1)S(1)} %get-tuple-element.61), channel_id=1, source_target_pairs={{0,16},{4,68},{8,24},{12,76},{16,0},{20,84},{24,8},{28,92},{32,48}... | collective-permute-start | bytes 1572872 | tf_op jit(solution)/shard_map/ppermute | solution.py:612
  7.9 58.0 %collective-permute-start.15 = (bf16[128,2048]{1,0:T(8,128)(2,1)S(1)}, bf16[128,2048]{1,0:T(8,128)(2,1)S(1)}, u32[]{:S(2)}, u32[]{:S(2)}) collective-permute-start(bf16[128,2048]{1,0:T(8,128)(2,1)S(1)} %get-tuple-element.61), channel_id=1, source_target_pairs={{0,24},{4,100},{8,0},{12,108},{16,8},{20,116},{24,16},{28,124},{32... | collective-permute-start | bytes 1572872 | tf_op jit(solution)/shard_map/ppermute | solution.py:612
  48.5 6.0 %collective-permute-start.2 = (f32[40,128]{1,0:T(8,128)S(1)}, f32[40,128]{1,0:T(8,128)S(1)}, u32[]{:S(2)}, u32[]{:S(2)}) collective-permute-start(f32[40,128]{1,0:T(8,128)S(1)} %pad_maximum_fusion.7), channel_id=1, source_target_pairs={{0,4},{4,0},{8,12},{12,8},{16,20},{20,16},{24,28},{28,24},{32,36},... | collective-permute-start | bytes 61448 | tf_op jit(solution)/shard_map/ppermute | solution.py:564
  49.5 2.5 %collective-permute-start = (f32[8,128]{1,0:T(8,128)S(1)}, f32[8,128]{1,0:T(8,128)S(1)}, u32[]{:S(2)}, u32[]{:S(2)}) collective-permute-start(f32[8,128]{1,0:T(8,128)S(1)} %get-tuple-element.52), channel_id=1, source_target_pairs={{0,1},{1,0},{2,3},{3,2},{4,5},{5,4},{6,7},{7,6},{8,9},{9,8},{10,11... | collective-permute-start | bytes 12296 | tf_op jit(solution)/shard_map/ppermute | solution.py:577
  52.0 7.6 %collective-permute-start.1 = (f32[8,128]{1,0:T(8,128)S(1)}, f32[8,128]{1,0:T(8,128)S(1)}, u32[]{:S(2)}, u32[]{:S(2)}) collective-permute-start(f32[8,128]{1,0:T(8,128)S(1)} %pad_maximum_fusion.10), channel_id=1, source_target_pairs={{0,3},{1,2},{2,1},{3,0},{4,7},{5,6},{6,5},{7,4},{8,11},{9,10},{10,... | collective-permute-start | bytes 12296 | tf_op jit(solution)/shard_map/ppermute | solution.py:577
  54.6 5.7 %collective-permute-start.3 = (f32[56,128]{1,0:T(8,128)S(1)}, f32[56,128]{1,0:T(8,128)S(1)}, u32[]{:S(2)}, u32[]{:S(2)}) collective-permute-start(f32[56,128]{1,0:T(8,128)S(1)} %pad_maximum_fusion.2), channel_id=1, source_target_pairs={{0,8},{4,36},{8,16},{12,44},{16,24},{20,52},{24,0},{28,60},{32,40}... | collective-permute-start | bytes 86024 | tf_op jit(solution)/shard_map/ppermute | solution.py:564
  56.3 4.9 %collective-permute-start.4 = (f32[56,128]{1,0:T(8,128)S(1)}, f32[56,128]{1,0:T(8,128)S(1)}, u32[]{:S(2)}, u32[]{:S(2)}) collective-permute-start(f32[56,128]{1,0:T(8,128)S(1)} %pad_maximum_fusion.2), channel_id=1, source_target_pairs={{0,16},{4,68},{8,24},{12,76},{16,0},{20,84},{24,8},{28,92},{32,48}... | collective-permute-start | bytes 86024 | tf_op jit(solution)/shard_map/ppermute | solution.py:564
  59.6 3.1 %collective-permute-start.5 = (f32[56,128]{1,0:T(8,128)S(1)}, f32[56,128]{1,0:T(8,128)S(1)}, u32[]{:S(2)}, u32[]{:S(2)}) collective-permute-start(f32[56,128]{1,0:T(8,128)S(1)} %pad_maximum_fusion.2), channel_id=1, source_target_pairs={{0,24},{4,100},{8,0},{12,108},{16,8},{20,116},{24,16},{28,124},{32... | collective-permute-start | bytes 86024 | tf_op jit(solution)/shard_map/ppermute | solution.py:564
  60.3 9.8 %collective-permute-start.13 = (bf16[128,2048]{1,0:T(8,128)(2,1)S(1)}, bf16[128,2048]{1,0:T(8,128)(2,1)S(1)}, u32[]{:S(2)}, u32[]{:S(2)}) collective-permute-start(bf16[128,2048]{1,0:T(8,128)(2,1)S(1)} %get-tuple-element.61), channel_id=1, source_target_pairs={{0,8},{4,36},{8,16},{12,44},{16,24},{20,52},{24,0},{28,60},{32,40}... | collective-permute-start | bytes 1572872 | tf_op jit(solution)/shard_map/ppermute | solution.py:612
  61.2 48.1 %collective-permute-start.12 = (bf16[512,2048]{1,0:T(8,128)(2,1)S(1)}, bf16[512,2048]{1,0:T(8,128)(2,1)S(1)}, u32[]{:S(2)}, u32[]{:S(2)}) collective-permute-start(bf16[512,2048]{1,0:T(8,128)(2,1)S(1)} %get-tuple-element.39.refs_0_), channel_id=1, source_target_pairs={{0,4},{4,0},{8,12},{12,8},{16,20},{20,16},{24,28},{28,24},{32,36},... | collective-permute-start | bytes 6291464 | tf_op jit(solution)/shard_map/ppermute | solution.py:613
  62.7 7.5 %collective-permute-start.6 = (f32[56,128]{1,0:T(8,128)S(1)}, f32[56,128]{1,0:T(8,128)S(1)}, u32[]{:S(2)}, u32[]{:S(2)}) collective-permute-start(f32[56,128]{1,0:T(8,128)S(1)} %pad_maximum_fusion.3), channel_id=1, source_target_pairs={{0,32},{4,12},{8,40},{12,20},{16,48},{20,28},{24,56},{28,4},{32,64... | collective-permute-start | bytes 86024 | tf_op jit(solution)/shard_map/ppermute | solution.py:564
  64.2 7.6 %collective-permute-start.7 = (f32[56,128]{1,0:T(8,128)S(1)}, f32[56,128]{1,0:T(8,128)S(1)}, u32[]{:S(2)}, u32[]{:S(2)}) collective-permute-start(f32[56,128]{1,0:T(8,128)S(1)} %pad_maximum_fusion.3), channel_id=1, source_target_pairs={{0,64},{4,20},{8,72},{12,28},{16,80},{20,4},{24,88},{28,12},{32,96... | collective-permute-start | bytes 86024 | tf_op jit(solution)/shard_map/ppermute | solution.py:564
  65.9 5.9 %collective-permute-start.8 = (f32[56,128]{1,0:T(8,128)S(1)}, f32[56,128]{1,0:T(8,128)S(1)}, u32[]{:S(2)}, u32[]{:S(2)}) collective-permute-start(f32[56,128]{1,0:T(8,128)S(1)} %pad_maximum_fusion.3), channel_id=1, source_target_pairs={{0,96},{4,28},{8,104},{12,4},{16,112},{20,12},{24,120},{28,20},{32... | collective-permute-start | bytes 86024 | tf_op jit(solution)/shard_map/ppermute | solution.py:564
  70.2 37.5 %collective-permute-start.20 = (bf16[256,2048]{1,0:T(8,128)(2,1)S(1)}, bf16[256,2048]{1,0:T(8,128)(2,1)S(1)}, u32[]{:S(2)}, u32[]{:S(2)}) collective-permute-start(bf16[256,2048]{1,0:T(8,128)(2,1)S(1)} %constant_dynamic-update-slice_fusion.2.refs_3_), channel_id=1, source_target_pairs={{0,96},{4,28},{8,104},{12,4},{16,112},{20,12},{24,120},{28,20},{32... | collective-permute-start | bytes 3145736 | tf_op jit(solution)/shard_map/ppermute | solution.py:617
  70.2 37.6 %collective-permute-start.17 = (bf16[256,2048]{1,0:T(8,128)(2,1)S(1)}, bf16[256,2048]{1,0:T(8,128)(2,1)S(1)}, u32[]{:S(2)}, u32[]{:S(2)}) collective-permute-start(bf16[256,2048]{1,0:T(8,128)(2,1)S(1)} %constant_dynamic-update-slice_fusion.refs_2_), channel_id=1, source_target_pairs={{0,32},{4,12},{8,40},{12,20},{16,48},{20,28},{24,56},{28,4},{32,64... | collective-permute-start | bytes 3145736 | tf_op jit(solution)/shard_map/ppermute | solution.py:616
  98.3 6.7 %collective-permute-start.11 = (f32[32,128]{1,0:T(8,128)S(1)}, f32[32,128]{1,0:T(8,128)S(1)}, u32[]{:S(2)}, u32[]{:S(2)}) collective-permute-start(f32[32,128]{1,0:T(8,128)S(1)} %get-tuple-element.60), channel_id=1, source_target_pairs={{0,4},{4,0},{8,12},{12,8},{16,20},{20,16},{24,28},{28,24},{32,36},... | collective-permute-start | bytes 49160 | tf_op jit(solution)/shard_map/ppermute | solution.py:564
  103.9 1.2 collective-permute-start.16
  105.0 15.2 %collective-permute-start.18 = (bf16[256,2048]{1,0:T(8,128)(2,1)S(1)}, bf16[256,2048]{1,0:T(8,128)(2,1)S(1)}, u32[]{:S(2)}, u32[]{:S(2)}) collective-permute-start(bf16[256,2048]{1,0:T(8,128)(2,1)S(1)} %constant_dynamic-update-slice_fusion.2.refs_3_), channel_id=1, source_target_pairs={{0,32},{4,12},{8,40},{12,20},{16,48},{20,28},{24,56},{28,4},{32,64... | collective-permute-start | bytes 3145736 | tf_op jit(solution)/shard_map/ppermute | solution.py:618
  105.0 15.2 %collective-permute-start.19 = (bf16[256,2048]{1,0:T(8,128)(2,1)S(1)}, bf16[256,2048]{1,0:T(8,128)(2,1)S(1)}, u32[]{:S(2)}, u32[]{:S(2)}) collective-permute-start(bf16[256,2048]{1,0:T(8,128)(2,1)S(1)} %constant_dynamic-update-slice_fusion.refs_2_), channel_id=1, source_target_pairs={{0,96},{4,28},{8,104},{12,4},{16,112},{20,12},{24,120},{28,20},{32... | collective-permute-start | bytes 3145736 | tf_op jit(solution)/shard_map/ppermute | solution.py:619
  107.7 23.0 %collective-permute-start.22 = (bf16[256,2048]{1,0:T(8,128)(2,1)S(1)}, bf16[256,2048]{1,0:T(8,128)(2,1)S(1)}, u32[]{:S(2)}, u32[]{:S(2)}) collective-permute-start(bf16[256,2048]{1,0:T(8,128)(2,1)S(1)} %collective-permute-done.20.refs_5_), channel_id=1, source_target_pairs={{0,96},{4,28},{8,104},{12,4},{16,112},{20,12},{24,120},{28,20},{32... | collective-permute-start | bytes 3145736 | tf_op jit(solution)/shard_map/ppermute | solution.py:621
  107.8 23.6 %collective-permute-start.21 = (bf16[256,2048]{1,0:T(8,128)(2,1)S(1)}, bf16[256,2048]{1,0:T(8,128)(2,1)S(1)}, u32[]{:S(2)}, u32[]{:S(2)}) collective-permute-start(bf16[256,2048]{1,0:T(8,128)(2,1)S(1)} %collective-permute-done.17.refs_2_), channel_id=1, source_target_pairs={{0,32},{4,12},{8,40},{12,20},{16,48},{20,28},{24,56},{28,4},{32,64... | collective-permute-start | bytes 3145736 | tf_op jit(solution)/shard_map/ppermute | solution.py:620
  109.2 29.6 %collective-permute-start.9 = (f32[4,128]{1,0:T(4,128)S(1)}, f32[4,128]{1,0:T(4,128)S(1)}, u32[]{:S(2)}, u32[]{:S(2)}) collective-permute-start(f32[4,128]{1,0:T(4,128)S(1)} %get-tuple-element.59), channel_id=1, source_target_pairs={{0,1},{1,0},{2,3},{3,2},{4,5},{5,4},{6,7},{7,6},{8,9},{9,8},{10,11... | collective-permute-start | bytes 6152 | tf_op jit(solution)/shard_map/ppermute | solution.py:577
  135.2 4.0 %collective-permute-start.23 = (f32[48,128]{1,0:T(8,128)S(1)}, f32[48,128]{1,0:T(8,128)S(1)}, u32[]{:S(2)}, u32[]{:S(2)}) collective-permute-start(f32[48,128]{1,0:T(8,128)S(1)} %pad_maximum_fusion.5), channel_id=1, source_target_pairs={{0,8},{4,12},{8,16},{12,20},{16,24},{20,28},{24,0},{28,4},{32,40},... | collective-permute-start | bytes 73736 | tf_op jit(solution)/shard_map/ppermute | solution.py:564
  135.3 5.0 %collective-permute-start.24 = (f32[48,128]{1,0:T(8,128)S(1)}, f32[48,128]{1,0:T(8,128)S(1)}, u32[]{:S(2)}, u32[]{:S(2)}) collective-permute-start(f32[48,128]{1,0:T(8,128)S(1)} %pad_maximum_fusion.5), channel_id=1, source_target_pairs={{0,16},{4,20},{8,24},{12,28},{16,0},{20,4},{24,8},{28,12},{32,48},... | collective-permute-start | bytes 73736 | tf_op jit(solution)/shard_map/ppermute | solution.py:564
  138.9 3.2 %collective-permute-start.25 = (f32[48,128]{1,0:T(8,128)S(1)}, f32[48,128]{1,0:T(8,128)S(1)}, u32[]{:S(2)}, u32[]{:S(2)}) collective-permute-start(f32[48,128]{1,0:T(8,128)S(1)} %pad_maximum_fusion.5), channel_id=1, source_target_pairs={{0,24},{4,28},{8,0},{12,4},{16,8},{20,12},{24,16},{28,20},{32,56},... | collective-permute-start | bytes 73736 | tf_op jit(solution)/shard_map/ppermute | solution.py:564
  138.9 7.1 %collective-permute-start.10 = (f32[4,128]{1,0:T(4,128)S(1)}, f32[4,128]{1,0:T(4,128)S(1)}, u32[]{:S(2)}, u32[]{:S(2)}) collective-permute-start(f32[4,128]{1,0:T(4,128)S(1)} %multiply_add_fusion.6), channel_id=1, source_target_pairs={{0,3},{1,2},{2,1},{3,0},{4,7},{5,6},{6,5},{7,4},{8,11},{9,10},{10,... | collective-permute-start | bytes 6152 | tf_op jit(solution)/shard_map/ppermute | solution.py:577
  142.2 4.0 %collective-permute-start.26 = (f32[48,128]{1,0:T(8,128)S(1)}, f32[48,128]{1,0:T(8,128)S(1)}, u32[]{:S(2)}, u32[]{:S(2)}) collective-permute-start(f32[48,128]{1,0:T(8,128)S(1)} %pad_maximum_fusion.6), channel_id=1, source_target_pairs={{0,32},{4,36},{8,40},{12,44},{16,48},{20,52},{24,56},{28,60},{32,6... | collective-permute-start | bytes 73736 | tf_op jit(solution)/shard_map/ppermute | solution.py:564
  142.2 5.3 %collective-permute-start.27 = (f32[48,128]{1,0:T(8,128)S(1)}, f32[48,128]{1,0:T(8,128)S(1)}, u32[]{:S(2)}, u32[]{:S(2)}) collective-permute-start(f32[48,128]{1,0:T(8,128)S(1)} %pad_maximum_fusion.6), channel_id=1, source_target_pairs={{0,64},{4,68},{8,72},{12,76},{16,80},{20,84},{24,88},{28,92},{32,9... | collective-permute-start | bytes 73736 | tf_op jit(solution)/shard_map/ppermute | solution.py:564
  146.0 3.0 %collective-permute-start.28 = (f32[48,128]{1,0:T(8,128)S(1)}, f32[48,128]{1,0:T(8,128)S(1)}, u32[]{:S(2)}, u32[]{:S(2)}) collective-permute-start(f32[48,128]{1,0:T(8,128)S(1)} %pad_maximum_fusion.6), channel_id=1, source_target_pairs={{0,96},{4,100},{8,104},{12,108},{16,112},{20,116},{24,120},{28,124... | collective-permute-start | bytes 73736 | tf_op jit(solution)/shard_map/ppermute | solution.py:564
  177.3 3.8 %collective-permute-start.29 = (f32[16,128]{1,0:T(8,128)S(1)}, f32[16,128]{1,0:T(8,128)S(1)}, u32[]{:S(2)}, u32[]{:S(2)}) collective-permute-start(f32[16,128]{1,0:T(8,128)S(1)} %pad_maximum_fusion.8), channel_id=1, source_target_pairs={{0,1},{1,2},{2,3},{3,0},{4,5},{5,6},{6,7},{7,4},{8,9},{9,10},{10,1... | collective-permute-start | bytes 24584 | tf_op jit(solution)/shard_map/ppermute | solution.py:564
  177.4 4.1 %collective-permute-start.30 = (f32[16,128]{1,0:T(8,128)S(1)}, f32[16,128]{1,0:T(8,128)S(1)}, u32[]{:S(2)}, u32[]{:S(2)}) collective-permute-start(f32[16,128]{1,0:T(8,128)S(1)} %pad_maximum_fusion.8), channel_id=1, source_target_pairs={{0,2},{1,3},{2,0},{3,1},{4,6},{5,7},{6,4},{7,5},{8,10},{9,11},{10,... | collective-permute-start | bytes 24584 | tf_op jit(solution)/shard_map/ppermute | solution.py:564
  177.5 4.3 %collective-permute-start.31 = (f32[16,128]{1,0:T(8,128)S(1)}, f32[16,128]{1,0:T(8,128)S(1)}, u32[]{:S(2)}, u32[]{:S(2)}) collective-permute-start(f32[16,128]{1,0:T(8,128)S(1)} %pad_maximum_fusion.8), channel_id=1, source_target_pairs={{0,3},{1,0},{2,1},{3,2},{4,7},{5,4},{6,5},{7,6},{8,11},{9,8},{10,9... | collective-permute-start | bytes 24584 | tf_op jit(solution)/shard_map/ppermute | solution.py:564
  181.8 4.8 %collective-permute-start.32 = (f32[52,128]{1,0:T(8,128)S(1)}, f32[52,128]{1,0:T(8,128)S(1)}, u32[]{:S(2)}, u32[]{:S(2)}) collective-permute-start(f32[52,128]{1,0:T(8,128)S(1)} %pad_maximum_fusion.4), channel_id=1, source_target_pairs={{0,4},{4,0},{8,12},{12,8},{16,20},{20,16},{24,28},{28,24},{32,36},... | collective-permute-start | bytes 79880 | tf_op jit(solution)/shard_map/ppermute | solution.py:564
  186.6 18.0 %copy-start = (f32[4096]{0:T(1024)S(1)}, f32[4096]{0:T(1024)}, u32[]{:S(2)}) copy-start(f32[4096]{0:T(1024)} %param.9) | copy-start | bytes 49156
  188.2 4.1 %collective-permute-start.33 = (f32[72,128]{1,0:T(8,128)S(1)}, f32[72,128]{1,0:T(8,128)S(1)}, u32[]{:S(2)}, u32[]{:S(2)}) collective-permute-start(f32[72,128]{1,0:T(8,128)S(1)} %pad_maximum_fusion), channel_id=1, source_target_pairs={{0,8},{4,12},{8,16},{12,20},{16,24},{20,28},{24,0},{28,4},{32,40},... | collective-permute-start | bytes 110600 | tf_op jit(solution)/shard_map/ppermute | solution.py:564
  189.5 4.6 %collective-permute-start.34 = (f32[72,128]{1,0:T(8,128)S(1)}, f32[72,128]{1,0:T(8,128)S(1)}, u32[]{:S(2)}, u32[]{:S(2)}) collective-permute-start(f32[72,128]{1,0:T(8,128)S(1)} %pad_maximum_fusion), channel_id=1, source_target_pairs={{0,16},{4,20},{8,24},{12,28},{16,0},{20,4},{24,8},{28,12},{32,48},... | collective-permute-start | bytes 110600 | tf_op jit(solution)/shard_map/ppermute | solution.py:564
  191.6 3.1 %collective-permute-start.35 = (f32[72,128]{1,0:T(8,128)S(1)}, f32[72,128]{1,0:T(8,128)S(1)}, u32[]{:S(2)}, u32[]{:S(2)}) collective-permute-start(f32[72,128]{1,0:T(8,128)S(1)} %pad_maximum_fusion), channel_id=1, source_target_pairs={{0,24},{4,28},{8,0},{12,4},{16,8},{20,12},{24,16},{28,20},{32,56},... | collective-permute-start | bytes 110600 | tf_op jit(solution)/shard_map/ppermute | solution.py:564
  194.8 4.1 %collective-permute-start.36 = (f32[72,128]{1,0:T(8,128)S(1)}, f32[72,128]{1,0:T(8,128)S(1)}, u32[]{:S(2)}, u32[]{:S(2)}) collective-permute-start(f32[72,128]{1,0:T(8,128)S(1)} %pad_maximum_fusion.1), channel_id=1, source_target_pairs={{0,32},{4,36},{8,40},{12,44},{16,48},{20,52},{24,56},{28,60},{32,6... | collective-permute-start | bytes 110600 | tf_op jit(solution)/shard_map/ppermute | solution.py:564
  194.8 5.0 %collective-permute-start.37 = (f32[72,128]{1,0:T(8,128)S(1)}, f32[72,128]{1,0:T(8,128)S(1)}, u32[]{:S(2)}, u32[]{:S(2)}) collective-permute-start(f32[72,128]{1,0:T(8,128)S(1)} %pad_maximum_fusion.1), channel_id=1, source_target_pairs={{0,64},{4,68},{8,72},{12,76},{16,80},{20,84},{24,88},{28,92},{32,9... | collective-permute-start | bytes 110600 | tf_op jit(solution)/shard_map/ppermute | solution.py:564
  198.1 3.1 %collective-permute-start.38 = (f32[72,128]{1,0:T(8,128)S(1)}, f32[72,128]{1,0:T(8,128)S(1)}, u32[]{:S(2)}, u32[]{:S(2)}) collective-permute-start(f32[72,128]{1,0:T(8,128)S(1)} %pad_maximum_fusion.1), channel_id=1, source_target_pairs={{0,96},{4,100},{8,104},{12,108},{16,112},{20,116},{24,120},{28,124... | collective-permute-start | bytes 110600 | tf_op jit(solution)/shard_map/ppermute | solution.py:564
  201.3 4.1 %collective-permute-start.39 = (f32[8,128]{1,0:T(8,128)S(1)}, f32[8,128]{1,0:T(8,128)S(1)}, u32[]{:S(2)}, u32[]{:S(2)}) collective-permute-start(f32[8,128]{1,0:T(8,128)S(1)} %bitcast_reduce_fusion.1), channel_id=1, source_target_pairs={{0,4},{4,0},{8,12},{12,8},{16,20},{20,16},{24,28},{28,24},{32,36},... | collective-permute-start | bytes 12296 | tf_op jit(solution)/shard_map/ppermute | solution.py:564
  205.4 4.2 %collective-permute-start.40 = (f32[12,128]{1,0:T(8,128)S(1)}, f32[12,128]{1,0:T(8,128)S(1)}, u32[]{:S(2)}, u32[]{:S(2)}) collective-permute-start(f32[12,128]{1,0:T(8,128)S(1)} %pad_maximum_fusion.9), channel_id=1, source_target_pairs={{0,1},{1,2},{2,3},{3,0},{4,5},{5,6},{6,7},{7,4},{8,9},{9,10},{10,1... | collective-permute-start | bytes 18440 | tf_op jit(solution)/shard_map/ppermute | solution.py:564
  207.1 4.0 %collective-permute-start.41 = (f32[12,128]{1,0:T(8,128)S(1)}, f32[12,128]{1,0:T(8,128)S(1)}, u32[]{:S(2)}, u32[]{:S(2)}) collective-permute-start(f32[12,128]{1,0:T(8,128)S(1)} %pad_maximum_fusion.9), channel_id=1, source_target_pairs={{0,2},{1,3},{2,0},{3,1},{4,6},{5,7},{6,4},{7,5},{8,10},{9,11},{10,... | collective-permute-start | bytes 18440 | tf_op jit(solution)/shard_map/ppermute | solution.py:564
  208.9 2.8 %collective-permute-start.42 = (f32[12,128]{1,0:T(8,128)S(1)}, f32[12,128]{1,0:T(8,128)S(1)}, u32[]{:S(2)}, u32[]{:S(2)}) collective-permute-start(f32[12,128]{1,0:T(8,128)S(1)} %pad_maximum_fusion.9), channel_id=1, source_target_pairs={{0,3},{1,0},{2,1},{3,2},{4,7},{5,4},{6,5},{7,6},{8,11},{9,8},{10,9... | collective-permute-start | bytes 18440 | tf_op jit(solution)/shard_map/ppermute | solution.py:564
